TPU v7x, 512 devices: a whole 4x8x8 slice. The times are simulated.
512 devices in a mesh: tm: 32 (over x, z), space: 16 (over y, core).
Axes of the slice: x: 4, y: 8, z: 8, core: 2. Of those that a mesh axis runs over, the one named last changes fastest.
Arguments:
- inverse_factor: bfloat16 [32, 2048, 2048], P('tm', None, 'space'), as said below
- arrow_factor: bfloat16 [32, 64, 2048], P('tm', None, 'space'), may hold values from -6 to 6
- decay: float32 [32, 2048], P('tm'), may hold values from 0 to 1
- tip_inverse: float32 [64, 64], replicated, may hold values from -0.75 to 0.75
- sigma_end: float32 [2048, 2048], P(None, 'space'), may hold values from -2.7 to 2.7, as said below
- arrow_end: float32 [2048, 64], P('space'), may hold values from -6 to 6
Outputs:
- sigmas: float32 [32, 2048, 2048], P('tm', None, 'space')
- arrows: float32 [32, 2048, 64], P('tm', 'space')
Inputs may be any that keep to these rules, and one draw needn't show every extreme that they name: `inverse_factor`: each K_t is lower triangular with a positive diagonal. `sigma_end`: symmetric.
All inputs are finite; a program needn't handle non-finite values.
Results may differ from a plain program's by a relative error of at most 0.0003.
Values may be sent and summed in bfloat16 or wider, within the bound.
No kernel may reach another device: no remote copies, remote signals or barrier semaphores. Data moves between devices by JAX's collectives and lax.ppermute only.
A program may use at most 128 MiB of HBM per device.

v0:
```python
import jax
import jax.numpy as jnp
from jax import lax
from jax.sharding import PartitionSpec as P


def prefix(array, axis, combine, identity):
    devices, position = (lax.axis_size(axis), lax.axis_index(axis))
    everything = jax.tree.map(lambda part: lax.all_gather(part, axis), array)
    start = jax.tree.map(
        lambda part, zero: jnp.broadcast_to(jnp.asarray(zero, part.dtype), part.shape),
        array,
        identity,
    )

    def hop(k, before):
        at = devices - 1 - k
        reached = at > position
        new = combine(before, jax.tree.map(lambda part: part[at], everything))
        return jax.tree.map(lambda a, b: jnp.where(reached, a, b), new, before)

    return lax.fori_loop(0, devices, hop, start)


def column_products(left, right):
    return lax.dot_general(
        left, right, (((0,), (0,)), ((), ())), preferred_element_type=jnp.float32
    )


def compose(earlier, later):
    falloff_later, own_after, sigma_after, arrow_after = earlier
    lower_factor_current, own_here, sigma_here, border_column_current = later
    return (
        lower_factor_current * falloff_later,
        own_here * own_after,
        sigma_here + lower_factor_current[:, None] * own_here[None, :] * sigma_after,
        border_column_current + own_here[:, None] * arrow_after,
    )


def body(inverse_factor, arrow_factor, decay, tip_inverse, sigma_end, arrow_end):
    highest = lax.Precision.HIGHEST
    factor_cols = inverse_factor[0]
    order = factor_cols.shape[0]
    width = factor_cols.shape[1]
    panel_index = lax.axis_index("space")
    precision_panel = column_products(
        lax.all_gather(factor_cols, "space", axis=1, tiled=True), factor_cols
    )
    decay_all = decay[0]
    self_falloff = lax.dynamic_slice_in_dim(decay_all, panel_index * width, width)
    arrow_local = arrow_factor[0]
    arrow_wide = arrow_local.astype(jnp.float32)
    cross = lax.psum_scatter(
        lax.dot_general(
            precision_panel,
            arrow_wide,
            (((1,), (1,)), ((), ())),
            precision=highest,
            preferred_element_type=jnp.float32,
        ),
        "space",
        scatter_dimension=0,
        tiled=True,
    )
    own_arrow = -jnp.dot(cross, tip_inverse, precision=highest)
    arrow_cols_count = tip_inverse.shape[0]
    identity_matrix = (
        jnp.ones((order,), jnp.float32),
        jnp.ones((width,), jnp.float32),
        jnp.zeros((order, width), jnp.float32),
        jnp.zeros((width, arrow_cols_count), jnp.float32),
    )
    mine = (decay_all, self_falloff, precision_panel, own_arrow)
    later_decay, later_own, later_sigma, later_arrow = prefix(mine, "tm", compose, identity_matrix)
    covariance_following = later_sigma + later_decay[:, None] * later_own[None, :] * sigma_end
    spike_ahead = later_arrow + later_own[:, None] * arrow_end
    sigma_block = (
        precision_panel + decay_all[:, None] * self_falloff[None, :] * covariance_following
    )
    arrow_block = own_arrow + self_falloff[:, None] * spike_ahead
    return (sigma_block[None], arrow_block[None])


def solution(mesh):
    placed = (
        P("tm", None, "space"),
        P("tm", None, "space"),
        P("tm", None),
        P(),
        P(None, "space"),
        P("space", None),
    )
    return jax.shard_map(
        body,
        mesh=mesh,
        in_specs=placed,
        out_specs=(P("tm", None, "space"), P("tm", "space", None)),
        check_vma=False,
    )
```

profile of v0, /device:TPU:1, one launch (start us, length us, event | category | flops | bytes accessed | tf_op | source)
XLA Modules:
  0.0 611.4 jit_solution(3542080441122480926)
XLA Ops:
  8.0 76.7 %all-gather.9.cloned.1.call-done = bf16[1,2048,2048]{2,1,0:T(8,128)(2,1)} async-done(((bf16[1,2048,128]{2,1,0:T(8,128)(2,1)}), bf16[1,2048,2048]{2,1,0:T(8,128)(2,1)}) %all-gather.9.cloned.1.call-update) | async-done | bytes 8388624 | tf_op jit(solution)/shard_map/all_gather | solution.py:49
  84.7 5.8 fusion.3
  92.2 54.2 %reduce-scatter.2.cloned.1.call-done = f32[128,64]{1,0:T(8,128)} async-done(((f32[2048,64]{1,0:T(8,128)}), f32[128,64]{1,0:T(8,128)}) %reduce-scatter.2.cloned.1.call-update) | async-done | bytes 32784 | tf_op jit(solution)/shard_map/reduce_scatter | solution.py:55
  148.8 37.9 %all-gather.3 = f32[32,1,2048]{2,1,0:T(1,128)S(1)} all-gather(f32[1,1,2048]{2,1,0:T(1,128)S(1)} %bitcast.51), channel_id=1, replica_groups=mesh['tm'=32,'space'=16] {'tm'}, dimensions={0}, use_global_device_ids=true | all-gather | bytes 270336 | tf_op jit(solution)/shard_map/all_gather | solution.py:9
  187.4 33.0 %all-gather.4 = f32[32,1,128]{2,1,0:T(1,128)} all-gather(f32[1,1,128]{2,1,0:T(1,128)S(1)} %get-tuple-element.327), channel_id=1, replica_groups=mesh['tm'=32,'space'=16] {'tm'}, dimensions={0}, use_global_device_ids=true | all-gather | bytes 16896 | tf_op jit(solution)/shard_map/all_gather | solution.py:9
  220.4 4.0 all-gather.13.cloned.1.call-done
  224.4 3.1 copy.12
  227.5 243.0 %all-gather.11.cloned.1.call-done = f32[65536,128]{1,0:T(8,128)} async-done(((f32[2048,128]{1,0:T(8,128)}), f32[65536,128]{1,0:T(8,128)}) %all-gather.11.cloned.1.call-update) | async-done | bytes 33554448 | tf_op jit(solution)/shard_map/all_gather | solution.py:9
  470.5 130.7 %while.22 = (s32[]{:T(128)}, f32[2048]{0:T(1024)S(1)}, f32[128]{0:T(128)}, f32[2048,128]{1,0:T(8,128)S(1)}, f32[128,64]{1,0:T(8,128)S(1)}, /*index=5*/s32[]{:T(1...) while((s32[]{:T(128)}, f32[2048]{0:T(1024)S(1)}, ...), condition=%wide.region_2.3_spmd.clone, body=%wide.region_1.2_spmd.clone.sunk | while | flops 1350024 | bytes 3296485 | solution.py:22
  472.9 1.8 fusion.16
  477.0 1.8 fusion.16
  481.1 1.8 fusion.16
  485.2 1.8 fusion.16
  489.3 1.8 fusion.16
  493.3 1.8 fusion.16
  497.4 1.8 fusion.16
  501.5 1.8 fusion.16
  505.6 1.8 fusion.16
  509.7 1.8 fusion.16
  513.8 1.8 fusion.16
  517.8 1.8 fusion.16
  521.9 1.8 fusion.16
  526.0 1.8 fusion.16
  602.7 2.2 add_bitcast_fusion
  (178 shorter events, 111.0 us)
Async XLA Ops:
  7.2 139.2 %copy-start = (f32[64,64]{1,0:T(8,128)S(1)}, f32[64,64]{1,0:T(8,128)}, u32[]{:S(2)}) copy-start(f32[64,64]{1,0:T(8,128)} %param.11) | copy-start | bytes 49156
  7.2 83.3 %copy-start.6 = (bf16[1,64,128]{2,1,0:T(8,128)(2,1)S(1)}, bf16[1,64,128]{2,1,0:T(8,128)(2,1)}, u32[]{:S(2)}) copy-start(bf16[1,64,128]{2,1,0:T(8,128)(2,1)} %param.9) | copy-start | bytes 49156
  7.2 77.5 %all-gather.9.cloned.1.call-start = ((), (), s32[]{:S(2)}) async-start(), calls=%async_computation.2 | async-start | bytes 8912896 | tf_op jit(solution)/shard_map/all_gather | solution.py:49
  7.9 140.9 %copy-start.5 = (f32[1,2048]{1,0:T(1,128)S(1)}, f32[1,2048]{1,0:T(1,128)}, u32[]{:S(2)}) copy-start(f32[1,2048]{1,0:T(1,128)} %param.10) | copy-start | bytes 24580
  7.9 138.5 %reduce-scatter.2.cloned.1.call-start = ((), (), s32[]{:S(2)}) async-start(), calls=%async_computation.1 | async-start | bytes 1114112 | tf_op jit(solution)/shard_map/reduce_scatter | solution.py:55
  90.5 57.7 %copy-start.1 = (f32[2048,128]{1,0:T(8,128)}, f32[2048,128]{1,0:T(8,128)S(1)}, u32[]{:S(2)}) copy-start(f32[2048,128]{1,0:T(8,128)S(1)} %fusion.3) | copy-start | bytes 3145732
  92.1 132.3 %all-gather.13.cloned.1.call-start = ((), (), s32[]{:S(2)}) async-start(), calls=%async_computation.4 | async-start | bytes 1081344 | tf_op jit(solution)/shard_map/all_gather | solution.py:9
  148.1 322.3 %all-gather.11.cloned.1.call-start = ((), (), s32[]{:S(2)}) async-start(), calls=%async_computation.3 | async-start | bytes 34603008 | tf_op jit(solution)/shard_map/all_gather | solution.py:9
  470.5 130.8 %copy-start.4 = (f32[128,64]{0,1:T(8,128)S(1)}, f32[128,64]{0,1:T(8,128)}, u32[]{:S(2)}) copy-start(f32[128,64]{0,1:T(8,128)} %convolution_negate_fusion) | copy-start | bytes 98308
  470.5 132.2 %copy-start.2 = (f32[2048,128]{1,0:T(8,128)S(1)}, f32[2048,128]{1,0:T(8,128)}, u32[]{:S(2)}) copy-start(f32[2048,128]{1,0:T(8,128)} %copy-done.1) | copy-start | bytes 3145732
  470.5 132.2 %copy-start.3 = (f32[2048,128]{1,0:T(8,128)S(1)}, f32[2048,128]{1,0:T(8,128)}, u32[]{:S(2)}) copy-start(f32[2048,128]{1,0:T(8,128)} %param.12) | copy-start | bytes 3145732
Sparse Core Ops, SparseCore 0:
  10.1 74.5 all-gather.8
  92.2 54.1 reduce-scatter.1
  150.5 73.8 all-gather.12
  228.5 241.9 all-gather.10
where the time goes:
time: 615 us; the launch traced here: 611 us
  waiting for transfers between devices  379 us (62%)
  other arithmetic  132 us (21%)
  blocking collectives  70.9 us (12%)
  between operations  13.9 us (2%)
  matrix products  9.12 us (1%)
    all_gather x2, waiting for transfers between devices, prefix(): everything = jax.tree.map(lambda part: lax.all_gather(part, axis), array)  247 us
    select_n x128, other arithmetic, hop(): return jax.tree.map(lambda a, b: jnp.where(reached, a, b), new, before)  129 us
    all_gather x1, waiting for transfers between devices, body(): lax.all_gather(factor_cols, 'space', axis=1, tiled=True)  76.7 us
    all_gather x2, blocking collectives, prefix(): everything = jax.tree.map(lambda part: lax.all_gather(part, axis), array)  70.9 us
    reduce_scatter x1, waiting for transfers between devices, body(): lax.psum_scatter(lax.dot_general(precision_panel, arrow_wide, (((1,), (1,...  54.2 us
  transfers between devices with their start and end apart: 4, of which 4 were waited for; matrix products, arithmetic and copies ran while one was open for 1% of the time, Pallas kernels for 0%

commit v1 on v0

v1 whole, which is shorter than its diff:
```python
import jax
import jax.numpy as jnp
from jax import lax
from jax.experimental import pallas as pl
from jax.experimental.pallas import tpu as pltpu
from jax.sharding import PartitionSpec as P

PAD = 8


def split3(x):
    hi = x.astype(jnp.bfloat16)
    rest = x - hi.astype(jnp.float32)
    mid = rest.astype(jnp.bfloat16)
    low = (rest - mid.astype(jnp.float32)).astype(jnp.bfloat16)
    return hi, mid, low


def panel_kernel(order, arrow, pieces, gathered, mine, tip_t, decay_rows, decay_cols, out, total):
    step = pl.program_id(0)
    width = mine.shape[1]
    rows = order // pieces
    per = width // rows

    @pl.when(step == 0)
    def _():
        total[...] = jnp.zeros_like(total)

    tile = lax.dot_general(
        gathered[0, :order, :], mine[...], (((0,), (0,)), ((), ())), preferred_element_type=jnp.float32
    )
    out[pl.ds(step * per, per), :rows, :] = tile.reshape(per, rows, width)
    border = gathered[0, order:, :]
    acc = total[...]
    for part in split3(tile):
        acc = acc + jnp.dot(border, part, preferred_element_type=jnp.float32)
    total[...] = acc

    @pl.when(step == pl.num_programs(0) - 1)
    def _():
        own = -jnp.dot(
            tip_t[...], total[...], precision=lax.Precision.HIGHEST, preferred_element_type=jnp.float32
        )
        share = arrow // pieces
        for r in range(pieces):
            out[r, rows : rows + share, :] = own[r * share : (r + 1) * share, :]
            out[r, rows + share : rows + share + 1, :] = decay_rows[r : r + 1, :]
            out[r, rows + share + 1 : rows + share + 2, :] = decay_cols[...]
            out[r, rows + share + 2 :, :] = jnp.zeros((PAD - share - 2, width), jnp.float32)


def scan_kernel(rows, share, got, end, out, turned):
    pieces = got.shape[0]
    width = got.shape[2]
    for s in range(pieces):
        turned[s : s + 1, :] = got[s, rows + share : rows + share + 1, :]
    columns = turned[...].T
    carry = end[...]
    tail = jnp.where(lax.broadcasted_iota(jnp.int32, (PAD, width), 0) < share, 1.0, 0.0)
    for s in range(pieces - 1, -1, -1):
        by_row = jnp.concatenate([jnp.broadcast_to(columns[:rows, s : s + 1], (rows, width)), tail], axis=0)
        by_col = got[s, rows + share + 1 : rows + share + 2, :]
        carry = got[s] + by_row * by_col * carry
        out[s] = carry


def body(inverse_factor, arrow_factor, decay, tip_inverse, sigma_end, arrow_end):
    factor_cols = inverse_factor[0]
    order, width = factor_cols.shape
    arrow = tip_inverse.shape[0]
    pieces = lax.axis_size("tm")
    rows, share = order // pieces, arrow // pieces
    column_at = lax.axis_index("space")
    piece_at = lax.axis_index("tm")

    gathered = lax.all_gather(jnp.concatenate([factor_cols, arrow_factor[0]], axis=0), "space", axis=0)
    panels = gathered.shape[0]
    decay_rows = jnp.pad(decay[0].reshape(pieces, rows), ((0, 0), (0, width - rows)))
    decay_cols = lax.dynamic_slice_in_dim(decay, column_at * width, width, axis=1)
    whole = lambda shape: pl.BlockSpec(shape, lambda i: (0,) * len(shape))
    send = pl.pallas_call(
        lambda *refs: panel_kernel(order, arrow, pieces, *refs),
        grid=(panels,),
        out_shape=jax.ShapeDtypeStruct((pieces, rows + PAD, width), jnp.float32),
        in_specs=[
            pl.BlockSpec((1, order + arrow, width), lambda i: (i, 0, 0)),
            whole((order, width)),
            whole((arrow, arrow)),
            whole((pieces, width)),
            whole((1, width)),
        ],
        out_specs=whole((pieces, rows + PAD, width)),
        scratch_shapes=[pltpu.VMEM((arrow, width), jnp.float32)],
        name="panel",
    )(gathered, factor_cols, tip_inverse.T, decay_rows, decay_cols)

    got = lax.all_to_all(send, "tm", 0, 0, tiled=True)
    end = jnp.concatenate(
        [
            lax.dynamic_slice_in_dim(sigma_end, piece_at * rows, rows, axis=0),
            lax.dynamic_slice_in_dim(arrow_end.T, piece_at * share, share, axis=0),
            jnp.zeros((PAD - share, width), jnp.float32),
        ],
        axis=0,
    )
    done = pl.pallas_call(
        lambda *refs: scan_kernel(rows, share, *refs),
        out_shape=jax.ShapeDtypeStruct(got.shape, jnp.float32),
        scratch_shapes=[pltpu.VMEM((pieces, width), jnp.float32)],
        name="suffix",
    )(got, end)
    back = lax.all_to_all(done, "tm", 0, 0, tiled=True)
    sigma = back[:, :rows].reshape(order, width)
    arrows = back[:, rows : rows + share].reshape(arrow, width).T
    return sigma[None], arrows[None]


def solution(mesh):
    placed = (
        P("tm", None, "space"),
        P("tm", None, "space"),
        P("tm", None),
        P(),
        P(None, "space"),
        P("space", None),
    )
    return jax.shard_map(
        body,
        mesh=mesh,
        in_specs=placed,
        out_specs=(P("tm", None, "space"), P("tm", "space", None)),
        check_vma=False,
    )
```

time: 615 us -> 182 us (0.30)
  the two profiles are of different devices: /device:TPU:1 before, /device:TPU:24 now
where the time goes in v1:
time: 182 us; the launch traced here: 181 us
  waiting for transfers between devices  92.4 us (51%)
  blocking collectives  37.6 us (21%)
  Pallas kernels  17.4 us (10%)
  between operations  14.1 us (8%)
  starting transfers between devices  10.2 us (6%)
  local copies, waits for them, and re-layouts  5.89 us (3%)
  other arithmetic  3.24 us (2%)
    all_gather x1, waiting for transfers between devices, body(): lax.all_gather(jnp.concatenate([factor_cols, arrow_factor[0]], axis=0), '...  62.2 us
    all_to_all x1, blocking collectives, body(): back = lax.all_to_all(done, 'tm', 0, 0, tiled=True)  37.6 us
    all_to_all x1, waiting for transfers between devices, body(): got = lax.all_to_all(send, 'tm', 0, 0, tiled=True)  30.2 us
    pallas_call x1, Pallas kernels, body(): pl.pallas_call(lambda *refs: panel_kernel(order, arrow, pieces, *refs), g...  14.6 us
    all_to_all x1, starting transfers between devices, body(): got = lax.all_to_all(send, 'tm', 0, 0, tiled=True)  10.2 us
  transfers between devices with their start and end apart: 2, of which 2 were waited for; matrix products, arithmetic and copies ran while one was open for 2% of the time, Pallas kernels for 0%

profile of v1, /device:TPU:24, one launch (start us, length us, event | category | flops | bytes accessed | tf_op | source)
XLA Modules:
  0.0 180.9 jit_solution(5794091297694584502)
XLA Ops:
  7.2 0.0 copy-start
  7.2 0.0 copy-start.2
  7.2 0.0 all-gather.3.cloned.1.call-start
  7.2 2.0 %pad_maximum_fusion = bf16[2112,128]{1,0:T(8,128)(2,1)} fusion(bf16[64,128]{1,0:T(8,128)(2,1)} %bitcast.18, bf16[2048,128]{1,0:T(8,128)(2,1)} %bitcast.13), kind=kLoop, calls=%fused_computation | loop fusion | flops 1081344 | bytes 1081344 | tf_op jit(solution)/shard_map/concatenate | solution.py:76
  9.2 0.0 all-gather.3.cloned.1.call-update
  9.3 0.7 copy.8
  10.0 0.5 broadcast.7
  10.5 0.0 copy-done.3
  10.5 0.6 reduce.3
  11.0 0.1 reshape_squeeze.3
  11.1 0.6 pad.4.refs_3_
  11.7 0.5 constant_dynamic-slice_fusion.1.refs_4_
  12.2 62.2 %all-gather.3.cloned.1.call-done = bf16[33792,128]{1,0:T(8,128)(2,1)} async-done(((bf16[2112,128]{1,0:T(8,128)(2,1)}), bf16[33792,128]{1,0:T(8,128)(2,1)}) %all-gather.3.cloned.1.call-update) | async-done | bytes 8650768 | tf_op jit(solution)/shard_map/all_gather | solution.py:76
  74.4 14.6 %panel.1 = f32[32,72,128]{2,1,0:T(8,128)} custom-call(bf16[16,2112,128]{2,1,0:T(8,128)(2,1)} %bitcast.12, bf16[2048,128]{1,0:T(8,128)(2,1)} %bitcast.14, f32[64,64]{1,0:T(8,128)} %bitcast.16, f32[32,128]{1,0:T(8,128)} %pad.4.refs_3_, f32[1,128]{1,0:T(1,128)} %constant_dynamic-slice_fusion.1.refs_4_), custom_call_target="tpu_custom_call" | custom-call | tf_op jit(solution)/shard_map/panel/pallas_call | solution.py:81
  89.0 10.2 %all-to-all-start = ((f32[32,72,128]{2,1,0:T(8,128)}), f32[32,72,128]{2,1,0:T(8,128)S(1)}, u32[]{:S(2)}, u32[]{:S(2)}) async-start(f32[32,72,128]{2,1,0:T(8,128)} %panel.1), calls=%async_computation | async-start | bytes 2359296 | tf_op jit(solution)/shard_map/all_to_all | solution.py:97
  99.2 0.1 pad.7.clone
  99.3 0.7 dynamic-slice_bitcast_fusion
  100.0 0.7 maximum_maximum_fusion.refs_1_
  100.7 30.2 %all-to-all-done.refs_0_ = f32[32,72,128]{2,1,0:T(8,128)S(1)} async-done(((f32[32,72,128]{2,1,0:T(8,128)}), f32[32,72,128]{2,1,0:T(8,128)S(1)}, u32[]{:S(2)}, u32[]{:S(2)}) %all-to-all-start) | async-done | bytes 1179680 | tf_op jit(solution)/shard_map/all_to_all | solution.py:97
  130.9 1.0 copy-done.1
  131.9 2.8 %suffix.1 = f32[32,72,128]{2,1,0:T(8,128)} custom-call(f32[32,72,128]{2,1,0:T(8,128)} %copy-done.1, f32[72,128]{1,0:T(8,128)} %maximum_maximum_fusion.refs_1_), custom_call_target="tpu_custom_call" | custom-call | tf_op jit(solution)/shard_map/suffix/pallas_call | solution.py:106
  134.7 37.6 %all_to_all.10 = f32[32,72,128]{2,1,0:T(8,128)S(1)} all-to-all(f32[32,72,128]{2,1,0:T(8,128)} %suffix.1), channel_id=1, replica_groups=mesh['tm'=32,'space'=16] {'tm'}, dimensions={0} | all-to-all | bytes 2359296 | tf_op jit(solution)/shard_map/all_to_all | solution.py:112
  172.3 1.1 slice.8
  173.4 0.6 slice.9
  (6 shorter events, 0.0 us)
Async XLA Ops:
  7.2 92.8 %copy-start = (f32[2048,128]{1,0:T(8,128)S(1)}, f32[2048,128]{1,0:T(8,128)}, u32[]{:S(2)}) copy-start(f32[2048,128]{1,0:T(8,128)} %param.10) | copy-start | bytes 3145732
  7.2 2.1 %copy-start.2 = (f32[64,64]{1,0:T(8,128)S(1)}, f32[64,64]{1,0:T(8,128)}, u32[]{:S(2)}) copy-start(f32[64,64]{1,0:T(8,128)} %param.9) | copy-start | bytes 49156
  7.2 3.3 %copy-start.3 = (f32[1,2048]{1,0:T(1,128)S(1)}, f32[1,2048]{1,0:T(1,128)}, u32[]{:S(2)}) copy-start(f32[1,2048]{1,0:T(1,128)} %param.8) | copy-start | bytes 24580
  7.2 67.2 %all-gather.3.cloned.1.call-start = ((), (), s32[]{:S(2)}) async-start(), calls=%async_computation.2 | async-start | bytes 9191424 | tf_op jit(solution)/shard_map/all_gather | solution.py:76
  89.0 41.9 %all-to-all-start = ((f32[32,72,128]{2,1,0:T(8,128)}), f32[32,72,128]{2,1,0:T(8,128)S(1)}, u32[]{:S(2)}, u32[]{:S(2)}) async-start(f32[32,72,128]{2,1,0:T(8,128)} %panel.1), calls=%async_computation | async-start | bytes 2359296 | tf_op jit(solution)/shard_map/all_to_all | solution.py:97
  130.9 1.0 copy-start.1
Sparse Core Ops, SparseCore 0:
  10.7 63.6 all-gather.2

commit v2 on v1

v2 whole, which is shorter than its diff:
```python
import jax
import jax.numpy as jnp
from jax import lax
from jax.experimental import pallas as pl
from jax.experimental.pallas import tpu as pltpu
from jax.sharding import PartitionSpec as P

CORNER = 4
PAD = 8
TOP = 14.0


def whole(shape):
    return pl.BlockSpec(shape, lambda i: (0,) * len(shape))


def split3(x):
    hi = x.astype(jnp.bfloat16)
    rest = x - hi.astype(jnp.float32)
    mid = rest.astype(jnp.bfloat16)
    low = (rest - mid.astype(jnp.float32)).astype(jnp.bfloat16)
    return hi, mid, low


def dot(a, b):
    return jnp.dot(a, b, preferred_element_type=jnp.float32)


def border_times(border, tile):
    hi, mid, low = split3(tile)
    return dot(border, hi) + dot(border, mid) + dot(border, low)


def exponent(x):
    largest = jnp.max(jnp.abs(x), axis=0, keepdims=True)
    return jnp.ceil(jnp.log2(jnp.maximum(largest, 2.0**-100)))


def encode(panel, pair):
    at = lax.broadcasted_iota(jnp.int32, pair.shape, 0)
    level, pair_level = exponent(panel), exponent(pair)
    scaled = pair * jnp.exp2(TOP - pair_level)
    high = scaled.astype(jnp.bfloat16).astype(jnp.float32)
    tail = jnp.where(at < 2, high, jnp.where(at < 4, scaled - high, 0.0))
    tail = jnp.where(at == 4, level, jnp.where(at == 5, pair_level, tail))
    return panel * jnp.exp2(TOP - level), tail


def decode(message, rows):
    tail = message[rows:, :]
    at = lax.broadcasted_iota(jnp.int32, tail.shape, 0)
    panel = message[:rows, :] * jnp.exp2(tail[4:5, :] - TOP)
    both = tail + jnp.where(at < 2, jnp.roll(tail, -2, axis=0), jnp.roll(tail, 2, axis=0))
    return panel, jnp.where(at < 4, both * jnp.exp2(tail[5:6, :] - TOP), 0.0)


def doubled(pair):
    return jnp.concatenate([pair, pair, jnp.zeros((PAD - 4, pair.shape[1]), jnp.float32)], axis=0)


def panel_kernel(cut, rows, at, gathered, mine_t, own_top, *refs):
    tops = (own_top, *refs[: CORNER - 1])
    tip_t, out, total = refs[CORNER - 1 :]
    step = pl.program_id(0)
    group, depth, width = gathered.shape[0], mine_t.shape[1] - cut, mine_t.shape[0]
    per = width // rows

    @pl.when(step == 0)
    def _():
        total[...] = jnp.zeros_like(total)

    for q in range(0, group, 2):
        pair = jnp.concatenate([gathered[q, :depth], gathered[q + 1, :depth]], axis=1)
        border = jnp.concatenate([gathered[q, depth:], gathered[q + 1, depth:]], axis=1)
        tile = dot(mine_t[:, cut:], pair).T
        out[pl.ds((step * group + q) * per, 2 * per), :rows, :] = tile.reshape(2 * per, rows, width)
        total[...] += border_times(border, tile)

    @pl.when(step == 0)
    def _():
        for other, top in enumerate(tops):
            panel = other ^ (at[0] & (CORNER - 1))
            tile = dot(mine_t[:, :cut], top[...]).T
            out[pl.ds(panel * per, per), :rows, :] += tile.reshape(per, rows, width)
            total[...] += border_times(gathered[panel, depth:], tile)

    @pl.when(step == pl.num_programs(0) - 1)
    def _():
        own = -jnp.dot(
            tip_t[...], total[...], precision=lax.Precision.HIGHEST, preferred_element_type=jnp.float32
        )
        for r in range(out.shape[0]):
            panel, tail = encode(out[r, :rows, :], doubled(own[2 * r : 2 * r + 2, :]))
            out[r, :rows, :] = panel
            out[r, rows:, :] = tail


def scan_kernel(rows, got, decays, end, out, turned):
    pieces, _, width = got.shape
    for s in range(pieces):
        turned[s : s + 1, :] = decays[s, 0:1, :]
    columns = turned[...].T[:rows, :]
    carry, pair = end[:rows, :], end[rows:, :]
    for s in range(pieces - 1, -1, -1):
        out[s, :rows, :], out[s, rows:, :] = encode(carry, pair)
        if s == 0:
            break
        panel, arrow = decode(got[s], rows)
        by_col = decays[s, 1:2, :]
        by_row = jnp.broadcast_to(columns[:, s : s + 1], (rows, width))
        carry = panel + by_row * by_col * carry
        pair = arrow + by_col * pair


def last_kernel(rows, sent, got, decay_rows, by_col, sigma, arrows):
    columns = decay_rows[...].T[:rows, :]
    for r in range(sent.shape[0]):
        panel, arrow = decode(sent[r], rows)
        later, later_arrow = decode(got[r], rows)
        by_row = jnp.broadcast_to(columns[:, r : r + 1], panel.shape)
        sigma[r * rows : (r + 1) * rows, :] = panel + by_row * by_col[...] * later
        arrows[2 * r : 2 * r + 2, :] = (arrow + by_col[...] * later_arrow)[:2, :]


def body(inverse_factor, arrow_factor, decay, tip_inverse, sigma_end, arrow_end):
    factor_cols = inverse_factor[0]
    order, width = factor_cols.shape
    arrow = tip_inverse.shape[0]
    pieces = lax.axis_size("tm")
    cut = CORNER * width
    rows, share = order // pieces, arrow // pieces
    column_at = lax.axis_index("space")
    piece_at = lax.axis_index("tm")

    gathered = lax.all_gather(jnp.concatenate([factor_cols[cut:], arrow_factor[0]], axis=0), "space", axis=0)
    panels, tall = gathered.shape[:2]
    top = factor_cols[:cut]
    tops = [top] + [
        lax.ppermute(top, "space", [(q, q ^ other) for q in range(CORNER)]) for other in range(1, CORNER)
    ]
    decay_rows = jnp.pad(decay[0].reshape(pieces, rows), ((0, 0), (0, width - rows)))
    by_col = lax.dynamic_slice_in_dim(decay, column_at * width, width, axis=1)
    decays = jnp.concatenate(
        [
            decay_rows[:, None],
            jnp.broadcast_to(by_col[None], (pieces, 1, width)),
            jnp.zeros((pieces, PAD - 2, width), jnp.float32),
        ],
        axis=1,
    )
    gathered, decays = lax.optimization_barrier(
        (gathered, lax.all_to_all(decays, "tm", 0, 0, tiled=True))
    )
    pair_end = lax.dynamic_slice_in_dim(arrow_end.T, piece_at * share, share, axis=0)
    end = jnp.concatenate(
        [
            lax.dynamic_slice_in_dim(sigma_end, piece_at * rows, rows, axis=0),
            pair_end,
            pair_end,
            jnp.zeros((PAD - 2 * share, width), jnp.float32),
        ],
        axis=0,
    )

    group = 4
    message = jax.ShapeDtypeStruct((pieces, rows + PAD, width), jnp.float32)
    sent = pl.pallas_call(
        lambda *refs: panel_kernel(cut, rows, *refs),
        grid=(panels // group,),
        out_shape=message,
        in_specs=[
            pl.BlockSpec(memory_space=pltpu.SMEM),
            pl.BlockSpec((group, tall, width), lambda i: (i, 0, 0)),
            whole((width, order)),
            *[whole((cut, width)) for _ in range(CORNER)],
            whole((arrow, arrow)),
        ],
        out_specs=whole(message.shape),
        scratch_shapes=[pltpu.VMEM((arrow, width), jnp.float32)],
        name="panel",
    )(column_at.reshape(1), gathered, factor_cols.T, *tops, tip_inverse.T)

    def exchange(values):
        moved = lax.all_to_all(values.astype(jnp.float16), "tm", 0, 0, tiled=True)
        return moved.astype(jnp.float32)

    ahead = pl.pallas_call(
        lambda *refs: scan_kernel(rows, *refs),
        out_shape=message,
        scratch_shapes=[pltpu.VMEM((pieces, width), jnp.float32)],
        name="suffix",
    )(exchange(sent), decays, end)
    sigma, arrows = pl.pallas_call(
        lambda *refs: last_kernel(rows, *refs),
        out_shape=(
            jax.ShapeDtypeStruct((order, width), jnp.float32),
            jax.ShapeDtypeStruct((arrow, width), jnp.float32),
        ),
        name="last",
    )(sent, exchange(ahead), decay_rows, by_col)
    return sigma[None], arrows.T[None]


def solution(mesh):
    placed = (
        P("tm", None, "space"),
        P("tm", None, "space"),
        P("tm", None),
        P(),
        P(None, "space"),
        P("space", None),
    )
    return jax.shard_map(
        body,
        mesh=mesh,
        in_specs=placed,
        out_specs=(P("tm", None, "space"), P("tm", "space", None)),
        check_vma=False,
    )
```

time: 182 us -> 151 us (0.83)
  the two profiles are of different devices: /device:TPU:24 before, /device:TPU:64 now
where the time goes in v2:
time: 151 us; the launch traced here: 150 us
  waiting for transfers between devices  70 us (46%)
  starting transfers between devices  35.4 us (23%)
  Pallas kernels  14.6 us (10%)
  between operations  14.2 us (9%)
  other arithmetic  10.2 us (7%)
  local copies, waits for them, and re-layouts  5.67 us (4%)
    all_to_all x2, waiting for transfers between devices, exchange(): moved = lax.all_to_all(values.astype(jnp.float16), 'tm', 0, 0, tiled=True)  36 us
    all_gather x1, waiting for transfers between devices, body(): lax.all_gather(jnp.concatenate([factor_cols[cut:], arrow_factor[0]], axis...  33.5 us
    all_to_all x2, starting transfers between devices, exchange(): moved = lax.all_to_all(values.astype(jnp.float16), 'tm', 0, 0, tiled=True)  15.2 us
    all_to_all x1, starting transfers between devices, body(): lax.all_to_all(decays, 'tm', 0, 0, tiled=True)  12.6 us
    pallas_call x1, Pallas kernels, body(): pl.pallas_call(lambda *refs: panel_kernel(cut, rows, *refs), grid=(panels...  8.58 us
    ppermute x3, starting transfers between devices, body(): lax.ppermute(top, 'space', [(q, q ^ other) for q in range(CORNER)])  7.59 us
    convert_element_type x2, other arithmetic, exchange(): moved = lax.all_to_all(values.astype(jnp.float16), 'tm', 0, 0, tiled=True)  4.33 us
    pallas_call x1, Pallas kernels, body(): pl.pallas_call(lambda *refs: last_kernel(rows, *refs), out_shape=(jax.Sha...  3.09 us
  transfers between devices with their start and end apart: 7, of which 4 were waited for; matrix products, arithmetic and copies ran while one was open for 4% of the time, Pallas kernels for 0%

profile of v2, /device:TPU:64, one launch (start us, length us, event | category | flops | bytes accessed | tf_op | source)
XLA Modules:
  0.0 150.0 jit_solution(3687541433388873689)
XLA Ops:
  7.2 1.1 slice_bitcast_fusion
  8.4 1.5 %pad_maximum_fusion = bf16[1600,128]{1,0:T(8,128)(2,1)} fusion(bf16[64,128]{1,0:T(8,128)(2,1)} %bitcast.26, bf16[1536,128]{1,0:T(8,128)(2,1)S(1)} %slice_bitcast_fusion), kind=kLoop, calls=%fused_computation | loop fusion | flops 819200 | bytes 819200 | tf_op jit(solution)/shard_map/concatenate | solution.py:135
  10.4 0.7 reduce.3
  11.3 0.7 maximum_maximum_fusion
  12.0 12.6 %all-to-all-start = ((f32[32,8,128]{2,1,0:T(8,128)}), f32[32,8,128]{2,1,0:T(8,128)S(1)}, u32[]{:S(2)}, u32[]{:S(2)}) async-start(f32[32,8,128]{2,1,0:T(8,128)} %maximum_maximum_fusion), calls=%async_computation | async-start | bytes 262144 | tf_op jit(solution)/shard_map/all_to_all | solution.py:152
  24.6 1.9 %collective-permute-start = (bf16[512,128]{1,0:T(8,128)(2,1)S(1)}, bf16[512,128]{1,0:T(8,128)(2,1)S(1)}, u32[]{:S(2)}, u32[]{:S(2)}) collective-permute-start(bf16[512,128]{1,0:T(8,128)(2,1)S(1)} %slice_bitcast_fusion.1.refs_3_), channel_id=1, source_target_pairs={{0,1},{1,0},{2,3},{3,2},{16,17},{17,16},{18,19},{19,18},{32,33},{3... | collective-permute-start | bytes 393224 | tf_op jit(solution)/shard_map/ppermute | solution.py:139
  26.6 3.5 %collective-permute-start.1 = (bf16[512,128]{1,0:T(8,128)(2,1)S(1)}, bf16[512,128]{1,0:T(8,128)(2,1)S(1)}, u32[]{:S(2)}, u32[]{:S(2)}) collective-permute-start(bf16[512,128]{1,0:T(8,128)(2,1)S(1)} %slice_bitcast_fusion.1.refs_3_), channel_id=1, source_target_pairs={{0,2},{1,3},{2,0},{3,1},{16,18},{17,19},{18,16},{19,17},{32,34},{3... | collective-permute-start | bytes 393224 | tf_op jit(solution)/shard_map/ppermute | solution.py:139
  30.1 2.2 %collective-permute-start.2 = (bf16[512,128]{1,0:T(8,128)(2,1)S(1)}, bf16[512,128]{1,0:T(8,128)(2,1)S(1)}, u32[]{:S(2)}, u32[]{:S(2)}) collective-permute-start(bf16[512,128]{1,0:T(8,128)(2,1)S(1)} %slice_bitcast_fusion.1.refs_3_), channel_id=1, source_target_pairs={{0,3},{1,2},{2,1},{3,0},{16,19},{17,18},{18,17},{19,16},{32,35},{3... | collective-permute-start | bytes 393224 | tf_op jit(solution)/shard_map/ppermute | solution.py:139
  32.2 1.0 copy.9
  33.3 0.7 copy.10
  34.4 33.5 %all-gather.3.cloned.1.call-done = bf16[25600,128]{1,0:T(8,128)(2,1)} async-done(((bf16[1600,128]{1,0:T(8,128)(2,1)}), bf16[25600,128]{1,0:T(8,128)(2,1)}) %all-gather.3.cloned.1.call-update) | async-done | bytes 6553616 | tf_op jit(solution)/shard_map/all_gather | solution.py:135
  68.7 8.6 %panel.1.refs_0_ = f32[32,72,128]{2,1,0:T(8,128)} custom-call(s32[1]{0:T(128)} %bitcast.refs_0_, bf16[16,1600,128]{2,1,0:T(8,128)(2,1)} %bitcast.22, bf16[128,2048]{1,0:T(8,128)(2,1)} %bitcast.23, bf16[512,128]{1,0:T(8,128)(2,1)} %copy-done.2, bf16[512,128]{1,0:T(8,128)(2,1)} %copy-done.5, bf16[512,128]{1,0:T(8,128)(2,1)} %copy-done.6, ...), custom_call_target="tpu_custom_call" | custom-call | tf_op jit(solution)/shard_map/panel/pallas_call | solution.py:167
  77.3 2.2 %convert_element_type.14 = f16[32,72,128]{2,1,0:T(8,128)(2,1)} convert(f32[32,72,128]{2,1,0:T(8,128)} %panel.1.refs_0_) | non-fusion elementwise | flops 294912 | bytes 1769472 | tf_op jit(solution)/shard_map/convert_element_type | solution.py:184
  79.5 10.3 %all-to-all-start.1 = ((f16[32,72,128]{2,1,0:T(8,128)(2,1)}), f16[32,72,128]{2,1,0:T(8,128)(2,1)S(1)}, u32[]{:S(2)}, u32[]{:S(2)}) async-start(f16[32,72,128]{2,1,0:T(8,128)(2,1)} %convert_element_type.14), calls=%async_computation.1 | async-start | bytes 1179648 | tf_op jit(solution)/shard_map/all_to_all | solution.py:184
  89.9 0.7 dynamic-slice_bitcast_fusion
  90.6 0.7 maximum_maximum_fusion.1.refs_2_
  91.3 17.9 %all-to-all-done.1 = f16[32,72,128]{2,1,0:T(8,128)(2,1)S(1)} async-done(((f16[32,72,128]{2,1,0:T(8,128)(2,1)}), f16[32,72,128]{2,1,0:T(8,128)(2,1)S(1)}, u32[]{:S(2)}, u32[]{:S(2)}) %all-to-all-start.1) | async-done | bytes 589856 | tf_op jit(solution)/shard_map/all_to_all | solution.py:184
  109.2 1.1 convert_element_type.15.refs_0_
  110.3 2.9 %suffix.1 = f32[32,72,128]{2,1,0:T(8,128)} custom-call(f32[32,72,128]{2,1,0:T(8,128)} %convert_element_type.15.refs_0_, f32[32,8,128]{2,1,0:T(8,128)} %copy-done.3, f32[72,128]{1,0:T(8,128)} %maximum_maximum_fusion.1.refs_2_), custom_call_target="tpu_custom_call" | custom-call | tf_op jit(solution)/shard_map/suffix/pallas_call | solution.py:187
  113.2 2.2 %convert_element_type.16 = f16[32,72,128]{2,1,0:T(8,128)(2,1)} convert(f32[32,72,128]{2,1,0:T(8,128)} %suffix.1) | non-fusion elementwise | flops 294912 | bytes 1769472 | tf_op jit(solution)/shard_map/convert_element_type | solution.py:184
  115.4 4.9 %all-to-all-start.2 = ((f16[32,72,128]{2,1,0:T(8,128)(2,1)}), f16[32,72,128]{2,1,0:T(8,128)(2,1)S(1)}, u32[]{:S(2)}, u32[]{:S(2)}) async-start(f16[32,72,128]{2,1,0:T(8,128)(2,1)} %convert_element_type.16), calls=%async_computation.2 | async-start | bytes 1179648 | tf_op jit(solution)/shard_map/all_to_all | solution.py:184
  120.9 18.1 %all-to-all-done.2 = f16[32,72,128]{2,1,0:T(8,128)(2,1)S(1)} async-done(((f16[32,72,128]{2,1,0:T(8,128)(2,1)}), f16[32,72,128]{2,1,0:T(8,128)(2,1)S(1)}, u32[]{:S(2)}, u32[]{:S(2)}) %all-to-all-start.2) | async-done | bytes 589856 | tf_op jit(solution)/shard_map/all_to_all | solution.py:184
  139.0 1.1 convert_element_type.17.refs_1_
  140.1 3.1 %last.1 = (f32[2048,128]{1,0:T(8,128)}, f32[64,128]{1,0:T(8,128)}) custom-call(f32[32,72,128]{2,1,0:T(8,128)} %panel.1.refs_0_, f32[32,72,128]{2,1,0:T(8,128)} %convert_element_type.17.refs_1_, f32[32,128]{1,0:T(8,128)} %copy-done.4, f32[1,128]{1,0:T(1,128)} %constant_dynamic-slice_fusion.1.refs_3_), custom_call_target="tpu_custom_call" | custom-call | tf_op jit(solution)/shard_map/last/pallas_call | solution.py:193
  (38 shorter events, 2.6 us)
Async XLA Ops:
  7.2 83.4 %copy-start = (f32[2048,128]{1,0:T(8,128)S(1)}, f32[2048,128]{1,0:T(8,128)}, u32[]{:S(2)}) copy-start(f32[2048,128]{1,0:T(8,128)} %param.10) | copy-start | bytes 3145732
  7.2 17.4 %copy-start.1 = (bf16[1,2048,128]{2,1,0:T(8,128)(2,1)S(1)}, bf16[1,2048,128]{2,1,0:T(8,128)(2,1)}, u32[]{:S(2)}) copy-start(bf16[1,2048,128]{2,1,0:T(8,128)(2,1)} %param.6) | copy-start | bytes 1572868
  7.2 3.2 %copy-start.9 = (f32[1,2048]{1,0:T(1,128)S(1)}, f32[1,2048]{1,0:T(1,128)}, u32[]{:S(2)}) copy-start(f32[1,2048]{1,0:T(1,128)} %param.8) | copy-start | bytes 24580
  7.2 60.7 %all-gather.3.cloned.1.call-start = ((), (), s32[]{:S(2)}) async-start(), calls=%async_computation.3 | async-start | bytes 6963200 | tf_op jit(solution)/shard_map/all_gather | solution.py:135
  9.9 23.4 %copy-start.8 = (f32[64,64]{1,0:T(8,128)S(1)}, f32[64,64]{1,0:T(8,128)}, u32[]{:S(2)}) copy-start(f32[64,64]{1,0:T(8,128)} %param.9) | copy-start | bytes 49156
  11.2 66.1 %copy-start.4 = (f32[32,128]{1,0:T(8,128)}, f32[32,128]{1,0:T(8,128)S(1)}, u32[]{:S(2)}) copy-start(f32[32,128]{1,0:T(8,128)S(1)} %pad.4.refs_2_) | copy-start | bytes 49156
  12.0 22.4 %all-to-all-start = ((f32[32,8,128]{2,1,0:T(8,128)}), f32[32,8,128]{2,1,0:T(8,128)S(1)}, u32[]{:S(2)}, u32[]{:S(2)}) async-start(f32[32,8,128]{2,1,0:T(8,128)} %maximum_maximum_fusion), calls=%async_computation | async-start | bytes 262144 | tf_op jit(solution)/shard_map/all_to_all | solution.py:152
  24.6 43.3 %copy-start.2 = (bf16[512,128]{1,0:T(8,128)(2,1)}, bf16[512,128]{1,0:T(8,128)(2,1)S(1)}, u32[]{:S(2)}) copy-start(bf16[512,128]{1,0:T(8,128)(2,1)S(1)} %slice_bitcast_fusion.1.refs_3_) | copy-start | bytes 393220
  24.6 43.3 %collective-permute-start = (bf16[512,128]{1,0:T(8,128)(2,1)S(1)}, bf16[512,128]{1,0:T(8,128)(2,1)S(1)}, u32[]{:S(2)}, u32[]{:S(2)}) collective-permute-start(bf16[512,128]{1,0:T(8,128)(2,1)S(1)} %slice_bitcast_fusion.1.refs_3_), channel_id=1, source_target_pairs={{0,1},{1,0},{2,3},{3,2},{16,17},{17,16},{18,19},{19,18},{32,33},{3... | collective-permute-start | bytes 393224 | tf_op jit(solution)/shard_map/ppermute | solution.py:139
  26.6 41.4 %collective-permute-start.1 = (bf16[512,128]{1,0:T(8,128)(2,1)S(1)}, bf16[512,128]{1,0:T(8,128)(2,1)S(1)}, u32[]{:S(2)}, u32[]{:S(2)}) collective-permute-start(bf16[512,128]{1,0:T(8,128)(2,1)S(1)} %slice_bitcast_fusion.1.refs_3_), channel_id=1, source_target_pairs={{0,2},{1,3},{2,0},{3,1},{16,18},{17,19},{18,16},{19,17},{32,34},{3... | collective-permute-start | bytes 393224 | tf_op jit(solution)/shard_map/ppermute | solution.py:139
  30.1 37.9 %collective-permute-start.2 = (bf16[512,128]{1,0:T(8,128)(2,1)S(1)}, bf16[512,128]{1,0:T(8,128)(2,1)S(1)}, u32[]{:S(2)}, u32[]{:S(2)}) collective-permute-start(bf16[512,128]{1,0:T(8,128)(2,1)S(1)} %slice_bitcast_fusion.1.refs_3_), channel_id=1, source_target_pairs={{0,3},{1,2},{2,1},{3,0},{16,19},{17,18},{18,17},{19,16},{32,35},{3... | collective-permute-start | bytes 393224 | tf_op jit(solution)/shard_map/ppermute | solution.py:139
  34.4 42.9 %copy-start.3 = (f32[32,8,128]{2,1,0:T(8,128)}, f32[32,8,128]{2,1,0:T(8,128)S(1)}, u32[]{:S(2)}) copy-start(f32[32,8,128]{2,1,0:T(8,128)S(1)} %all-to-all-done.refs_1_) | copy-start | bytes 393220
  67.9 0.7 copy-start.5
  67.9 0.7 copy-start.6
  67.9 0.8 copy-start.7
  79.5 29.7 %all-to-all-start.1 = ((f16[32,72,128]{2,1,0:T(8,128)(2,1)}), f16[32,72,128]{2,1,0:T(8,128)(2,1)S(1)}, u32[]{:S(2)}, u32[]{:S(2)}) async-start(f16[32,72,128]{2,1,0:T(8,128)(2,1)} %convert_element_type.14), calls=%async_computation.1 | async-start | bytes 1179648 | tf_op jit(solution)/shard_map/all_to_all | solution.py:184
  115.4 23.6 %all-to-all-start.2 = ((f16[32,72,128]{2,1,0:T(8,128)(2,1)}), f16[32,72,128]{2,1,0:T(8,128)(2,1)S(1)}, u32[]{:S(2)}, u32[]{:S(2)}) async-start(f16[32,72,128]{2,1,0:T(8,128)(2,1)} %convert_element_type.16), calls=%async_computation.2 | async-start | bytes 1179648 | tf_op jit(solution)/shard_map/all_to_all | solution.py:184
Sparse Core Ops, SparseCore 0:
  10.2 57.7 all-gather.2

commit v3 on v2

v3 whole, which is shorter than its diff:
```python
import jax
import jax.numpy as jnp
from jax import lax
from jax.experimental import pallas as pl
from jax.experimental.pallas import tpu as pltpu
from jax.sharding import PartitionSpec as P

CORES = 2
PAD = 8
TOP = 14.0
DECAY = 1024.0


def split3(x):
    hi = x.astype(jnp.bfloat16)
    rest = x - hi.astype(jnp.float32)
    mid = rest.astype(jnp.bfloat16)
    low = (rest - mid.astype(jnp.float32)).astype(jnp.bfloat16)
    return hi, mid, low


def dot(a, b):
    return jnp.dot(a, b, preferred_element_type=jnp.float32)


def border_times(border, tile):
    hi, mid, low = split3(tile)
    return dot(border, hi) + dot(border, mid) + dot(border, low)


def exponent(x):
    largest = jnp.max(jnp.abs(x), axis=0, keepdims=True)
    return jnp.ceil(jnp.log2(jnp.maximum(largest, 2.0**-100)))


def squared(x, level):
    unit = x * jnp.exp2(TOP / 2 - level)
    return unit * jnp.abs(unit)


def rooted(x, level):
    root = jnp.sqrt(jnp.abs(x))
    return jnp.where(x < 0, -root, root) * jnp.exp2(level - TOP / 2)


def encode(panel, pair, extra):
    at = lax.broadcasted_iota(jnp.int32, pair.shape, 0)
    level, pair_level = exponent(panel), exponent(pair)
    tail = jnp.where(at < 2, squared(pair, pair_level), extra)
    tail = jnp.where(at == 2, level, jnp.where(at == 3, pair_level, tail))
    return squared(panel, level), tail


def decode(message, rows):
    tail = message[rows:, :]
    at = lax.broadcasted_iota(jnp.int32, tail.shape, 0)
    panel = rooted(message[:rows, :], tail[2:3, :])
    return panel, jnp.where(at < 2, rooted(tail, tail[3:4, :]), 0.0)


def own_kernel(mine, other, mine_top, other_top, tile, both_t, total):
    tall = mine.shape[0]
    depth = both_t.shape[1]
    turned = jnp.concatenate([mine[:depth, :].T, other[:depth, :].T], axis=0)
    top = jnp.concatenate([mine_top[...].T, other_top[...].T], axis=0)
    both_t[...] = turned
    got = dot(turned, mine[:depth, :]) + dot(top, mine_top[...])
    tile[...] = got
    border = jnp.concatenate([mine[depth:tall, :], other[depth:tall, :]], axis=1)
    total[...] = jnp.concatenate([border_times(border, got), jnp.zeros(total.shape[:1] + got.shape[1:])], axis=1)


def far_tiles(panels, both_t, before):
    depth = both_t.shape[1]
    tall = panels[0].shape[0]
    joined = jnp.concatenate([p[:depth, :] for p in panels], axis=1)
    border = jnp.concatenate([p[depth:tall, :] for p in panels], axis=1)
    tile = dot(both_t[...], joined).T
    return tile, before[...] + border_times(border, tile)


def far_kernel(first, second, both_t, before, keep, give, total):
    tile, total[...] = far_tiles((first, second), both_t, before)
    width = keep.shape[1]
    keep[...] = tile[:, :width]
    give[...] = tile[:, width:]


def farthest_kernel(first, both_t, before, keep, give):
    tile, total = far_tiles((first,), both_t, before)
    width = keep.shape[1]
    count = tile.shape[0]
    keep[:count, :] = tile[:, :width]
    keep[count:, :] = total[:, :width]
    give[:count, :] = tile[:, width:]
    give[count:, :] = total[:, width:]


def message_kernel(rows, chips, at, own, *refs):
    hops = (len(refs) - 4) // 2
    kept, given = refs[:hops], refs[hops : 2 * hops]
    tip_t, decay_rows, decay_cols, out = refs[2 * hops :]
    width = own.shape[1]
    per = width // rows
    chip, core = at[0] // CORES, at[0] % CORES
    way = 1 - 2 * core

    def put(block, hop, parity):
        spot = lax.rem(chip + hop + chips, chips) * CORES + parity
        out[pl.ds(spot * per, per), :rows, :] = block.reshape(per, rows, width)

    put(own[:width, :], 0, core)
    put(own[width:, :], 0, 1 - core)
    for s in range(hops):
        hop = (s + 1) * way
        put(kept[s][:width, :], -hop, core)
        put(given[s][:width, :], hop, 1 - core)
        if s < hops - 1:
            put(kept[s][width:, :], -hop, 1 - core)
            put(given[s][width:, :], hop, core)
    total = kept[-1][width:, :] + given[-1][width:, :]
    arrow = -jnp.dot(tip_t[...], total, precision=lax.Precision.HIGHEST, preferred_element_type=jnp.float32)
    fill = jnp.zeros((PAD - 2, width), jnp.float32)
    cols = decay_cols[...]
    place = lax.broadcasted_iota(jnp.int32, cols.shape, 0)
    for r in range(out.shape[0]):
        extra = jnp.where(place == 4, decay_rows[r : r + 1, :], cols)
        pair = jnp.concatenate([arrow[2 * r : 2 * r + 2, :], fill], axis=0)
        out[r, :rows, :], out[r, rows:, :] = encode(out[r, :rows, :], pair, extra)


def scan_kernel(rows, got, end, out, turned):
    pieces, _, width = got.shape
    for s in range(pieces):
        turned[s : s + 1, :] = got[s, rows + 4 : rows + 5, :]
    columns = turned[...].T
    columns = (columns[:rows, :] + columns[rows : 2 * rows, :] * (1 / 256)) * (1 / DECAY)
    carry, pair = end[:rows, :], end[rows:, :]
    for s in range(pieces - 1, -1, -1):
        out[s, :rows, :], out[s, rows:, :] = encode(carry, pair, jnp.zeros_like(pair))
        if s == 0:
            break
        panel, arrow = decode(got[s], rows)
        by_col = (got[s, rows + 5 : rows + 6, :] + got[s, rows + 6 : rows + 7, :] * (1 / 256)) * (1 / DECAY)
        by_row = jnp.broadcast_to(columns[:, s : s + 1], (rows, width))
        carry = panel + by_row * by_col * carry
        pair = arrow + by_col * pair


def last_kernel(rows, sent, got, decay_rows, by_col, sigma, arrows):
    columns = decay_rows[...].T[:rows, :]
    for r in range(sent.shape[0]):
        panel, arrow = decode(sent[r], rows)
        later, later_arrow = decode(got[r], rows)
        by_row = jnp.broadcast_to(columns[:, r : r + 1], panel.shape)
        sigma[r * rows : (r + 1) * rows, :] = panel + by_row * by_col[...] * later
        arrows[2 * r : 2 * r + 2, :] = (arrow + by_col[...] * later_arrow)[:2, :]


def two_parts(decay):
    scaled = decay * DECAY
    high = lax.reduce_precision(scaled, 8, 7)
    return high, (scaled - high) * 256


def body(inverse_factor, arrow_factor, decay, tip_inverse, sigma_end, arrow_end):
    factor_cols = inverse_factor[0]
    order, width = factor_cols.shape
    arrow = tip_inverse.shape[0]
    pieces, devices = lax.axis_size("tm"), lax.axis_size("space")
    chips, cut = devices // CORES, CORES * width
    rows, share = order // pieces, arrow // pieces
    column_at = lax.axis_index("space")
    piece_at = lax.axis_index("tm")
    swapped = [(p, p ^ 1) for p in range(devices)]
    around = [
        (p, (p // CORES + 1 - 2 * (p % CORES)) % chips * CORES + p % CORES) for p in range(devices)
    ]
    depth = order - cut
    tall = depth + arrow
    f32 = lambda *shape: jax.ShapeDtypeStruct(shape, jnp.float32)

    def pack_kernel(cols, border, out):
        out[:depth, :] = cols[cut:, :]
        out[depth:, :] = border[...]

    mine = pl.pallas_call(
        pack_kernel, out_shape=jax.ShapeDtypeStruct((tall, width), jnp.bfloat16), name="pack"
    )(factor_cols, arrow_factor[0])
    top = factor_cols[:cut]
    first = [lax.ppermute(mine, "space", around)]
    other = lax.ppermute(mine, "space", swapped)
    other_top = lax.ppermute(top, "space", swapped)
    second = [lax.ppermute(other, "space", around)]
    hops = chips // 2
    for s in range(1, hops):
        first.append(lax.ppermute(first[-1], "space", around))
        if s < hops - 1:
            second.append(lax.ppermute(second[-1], "space", around))

    own, both_t, total = pl.pallas_call(
        own_kernel,
        out_shape=(
            f32(CORES * width, width),
            jax.ShapeDtypeStruct((CORES * width, depth), jnp.bfloat16),
            f32(arrow, CORES * width),
        ),
        name="own",
    )(mine, other, top, other_top)
    kept, given = [], []
    for s in range(hops - 1):
        keep, give, total = pl.pallas_call(
            far_kernel,
            out_shape=(f32(2 * width, width), f32(2 * width, width), f32(arrow, CORES * width)),
            name="far",
        )(first[s], second[s], both_t, total)
        kept.append(keep)
        given.append(lax.ppermute(give, "space", swapped))
    keep, give = pl.pallas_call(
        farthest_kernel, out_shape=(f32(width + arrow, width), f32(width + arrow, width)), name="farthest"
    )(first[-1], both_t, total)
    kept.append(keep)
    given.append(lax.ppermute(give, "space", swapped))

    by_col = lax.dynamic_slice_in_dim(decay, column_at * width, width, axis=1)
    decay_rows = decay[0].reshape(pieces, rows)
    row_parts = jnp.concatenate(two_parts(decay_rows), axis=1)
    row_parts = jnp.pad(row_parts, ((0, 0), (0, width - 2 * rows)))
    col_parts = jnp.pad(jnp.concatenate(two_parts(by_col), axis=0), ((5, PAD - 7), (0, 0)))
    message = f32(pieces, rows + PAD, width)
    vmem, smem = pl.BlockSpec(memory_space=pltpu.VMEM), pl.BlockSpec(memory_space=pltpu.SMEM)
    sent = pl.pallas_call(
        lambda *refs: message_kernel(rows, chips, *refs),
        out_shape=message,
        in_specs=[smem] + [vmem] * (2 * hops + 4),
        name="message",
    )(column_at.reshape(1), own, *kept, *given, tip_inverse.T, row_parts, col_parts)

    def exchange(values):
        moved = lax.all_to_all(values.astype(jnp.float16), "tm", 0, 0, tiled=True)
        return moved.astype(jnp.float32)

    end = jnp.concatenate(
        [
            lax.dynamic_slice_in_dim(sigma_end, piece_at * rows, rows, axis=0),
            lax.dynamic_slice_in_dim(arrow_end.T, piece_at * share, share, axis=0),
            jnp.zeros((PAD - share, width), jnp.float32),
        ],
        axis=0,
    )
    ahead = pl.pallas_call(
        lambda *refs: scan_kernel(rows, *refs),
        out_shape=message,
        scratch_shapes=[pltpu.VMEM((pieces, width), jnp.float32)],
        name="suffix",
    )(exchange(sent), end)
    sigma, arrows = pl.pallas_call(
        lambda *refs: last_kernel(rows, *refs),
        out_shape=(f32(order, width), f32(arrow, width)),
        name="last",
    )(sent, exchange(ahead), jnp.pad(decay_rows, ((0, 0), (0, width - rows))), by_col)
    return sigma[None], arrows.T[None]


def solution(mesh):
    placed = (
        P("tm", None, "space"),
        P("tm", None, "space"),
        P("tm", None),
        P(),
        P(None, "space"),
        P("space", None),
    )
    return jax.shard_map(
        body,
        mesh=mesh,
        in_specs=placed,
        out_specs=(P("tm", None, "space"), P("tm", "space", None)),
        check_vma=False,
    )
```

time: 151 us -> 146 us (0.967)
  the two profiles are of different devices: /device:TPU:64 before, /device:TPU:24 now
where the time goes in v3:
time: 146 us; the launch traced here: 144 us
  starting transfers between devices  61.9 us (42%)
  waiting for transfers between devices  40.5 us (28%)
  Pallas kernels  25.5 us (17%)
  other arithmetic  10.5 us (7%)
  local copies, waits for them, and re-layouts  5.01 us (3%)
    all_to_all x2, waiting for transfers between devices, exchange(): moved = lax.all_to_all(values.astype(jnp.float16), 'tm', 0, 0, tiled=True)  35 us
    all_to_all x2, starting transfers between devices, exchange(): moved = lax.all_to_all(values.astype(jnp.float16), 'tm', 0, 0, tiled=True)  19 us
    ppermute x3, starting transfers between devices, body(): first.append(lax.ppermute(first[-1], 'space', around))  16.1 us
    ppermute x4, starting transfers between devices, body(): given.append(lax.ppermute(give, 'space', swapped))  8.75 us
    pallas_call x3, Pallas kernels, body(): pl.pallas_call(far_kernel, out_shape=(f32(2 * width, width), f32(2 * widt...  8.64 us
    ppermute x2, starting transfers between devices, body(): second.append(lax.ppermute(second[-1], 'space', around))  6.98 us
    ppermute x1, starting transfers between devices, body(): first = [lax.ppermute(mine, 'space', around)]  4.69 us
    convert_element_type x2, other arithmetic, exchange(): moved = lax.all_to_all(values.astype(jnp.float16), 'tm', 0, 0, tiled=True)  4.32 us
  transfers between devices with their start and end apart: 15, of which 5 were waited for; matrix products, arithmetic and copies ran while one was open for 5% of the time, Pallas kernels for 10%

profile of v3, /device:TPU:24, one launch (start us, length us, event | category | flops | bytes accessed | tf_op | source)
XLA Modules:
  0.0 144.4 jit_solution(5482660451166578769)
XLA Ops:
  0.6 2.0 %pack.1.mine = bf16[1856,128]{1,0:T(8,128)(2,1)} custom-call(bf16[2048,128]{1,0:T(8,128)(2,1)} %bitcast.12, bf16[64,128]{1,0:T(8,128)(2,1)} %bitcast.14), custom_call_target="tpu_custom_call" | custom-call | tf_op jit(solution)/shard_map/pack/pallas_call | solution.py:187
  4.5 4.7 %collective-permute-start.2 = (bf16[1856,128]{1,0:T(8,128)(2,1)}, bf16[1856,128]{1,0:T(8,128)(2,1)S(1)}, u32[]{:S(2)}, u32[]{:S(2)}) collective-permute-start(bf16[1856,128]{1,0:T(8,128)(2,1)} %pack.1.mine), channel_id=1, source_target_pairs={{0,2},{1,15},{2,4},{3,1},{4,6},{5,3},{6,8},{7,5},{8,10},{9,7},{10,... | collective-permute-start | bytes 1425416 | tf_op jit(solution)/shard_map/ppermute | solution.py:191
  9.2 2.6 %collective-permute-start.3 = (bf16[1856,128]{1,0:T(8,128)(2,1)S(1)}, bf16[1856,128]{1,0:T(8,128)(2,1)S(1)}, u32[]{:S(2)}, u32[]{:S(2)}) collective-permute-start(bf16[1856,128]{1,0:T(8,128)(2,1)S(1)} %collective-permute-done.other), channel_id=1, source_target_pairs={{0,2},{1,15},{2,4},{3,1},{4,6},{5,3},{6,8},{7,5},{8,10},{9,7},{10,... | collective-permute-start | bytes 1425416 | tf_op jit(solution)/shard_map/ppermute | solution.py:194
  11.8 3.9 %collective-permute-done.2.first = bf16[1856,128]{1,0:T(8,128)(2,1)S(1)} collective-permute-done((bf16[1856,128]{1,0:T(8,128)(2,1)}, bf16[1856,128]{1,0:T(8,128)(2,1)S(1)}, u32[]{:S(2)}, u32[]{:S(2)}) %collective-permute-start.2) | collective-permute-done | bytes 475168 | tf_op jit(solution)/shard_map/ppermute | solution.py:191
  15.7 5.5 %collective-permute-start.4 = (bf16[1856,128]{1,0:T(8,128)(2,1)S(1)}, bf16[1856,128]{1,0:T(8,128)(2,1)S(1)}, u32[]{:S(2)}, u32[]{:S(2)}) collective-permute-start(bf16[1856,128]{1,0:T(8,128)(2,1)S(1)} %collective-permute-done.2.first), channel_id=1, source_target_pairs={{0,2},{1,15},{2,4},{3,1},{4,6},{5,3},{6,8},{7,5},{8,10},{9,7},{10,... | collective-permute-start | bytes 1425416 | tf_op jit(solution)/shard_map/ppermute | solution.py:197
  21.2 5.1 %collective-permute-start.5 = (bf16[1856,128]{1,0:T(8,128)(2,1)S(1)}, bf16[1856,128]{1,0:T(8,128)(2,1)}, u32[]{:S(2)}, u32[]{:S(2)}) collective-permute-start(bf16[1856,128]{1,0:T(8,128)(2,1)S(1)} %collective-permute-done.3.second), channel_id=1, source_target_pairs={{0,2},{1,15},{2,4},{3,1},{4,6},{5,3},{6,8},{7,5},{8,10},{9,7},{10,... | collective-permute-start | bytes 1425416 | tf_op jit(solution)/shard_map/ppermute | solution.py:199
  27.3 5.6 %collective-permute-start.6 = (bf16[1856,128]{1,0:T(8,128)(2,1)S(1)}, bf16[1856,128]{1,0:T(8,128)(2,1)S(1)}, u32[]{:S(2)}, u32[]{:S(2)}) collective-permute-start(bf16[1856,128]{1,0:T(8,128)(2,1)S(1)} %collective-permute-done.4.first), channel_id=1, source_target_pairs={{0,2},{1,15},{2,4},{3,1},{4,6},{5,3},{6,8},{7,5},{8,10},{9,7},{10,... | collective-permute-start | bytes 1425416 | tf_op jit(solution)/shard_map/ppermute | solution.py:197
  39.6 5.1 %collective-permute-start.8 = (bf16[1856,128]{1,0:T(8,128)(2,1)S(1)}, bf16[1856,128]{1,0:T(8,128)(2,1)S(1)}, u32[]{:S(2)}, u32[]{:S(2)}) collective-permute-start(bf16[1856,128]{1,0:T(8,128)(2,1)S(1)} %collective-permute-done.6.first), channel_id=1, source_target_pairs={{0,2},{1,15},{2,4},{3,1},{4,6},{5,3},{6,8},{7,5},{8,10},{9,7},{10,... | collective-permute-start | bytes 1425416 | tf_op jit(solution)/shard_map/ppermute | solution.py:197
  45.4 2.5 %own.1 = (f32[256,128]{1,0:T(8,128)}, bf16[256,1792]{1,0:T(8,128)(2,1)}, f32[64,256]{1,0:T(8,128)}) custom-call(bf16[1856,128]{1,0:T(8,128)(2,1)} %pack.1.mine, bf16[1856,128]{1,0:T(8,128)(2,1)} %copy-done.2, bf16[256,128]{1,0:T(8,128)(2,1)} %copy-done.7, bf16[256,128]{1,0:T(8,128)(2,1)} %collective-permute-done.1.other_top), custom_call_target="tpu_custom_call" | custom-call | tf_op jit(solution)/shard_map/own/pallas_call | solution.py:201
  47.9 2.9 %far.3 = (f32[256,128]{1,0:T(8,128)}, f32[256,128]{1,0:T(8,128)}, f32[64,256]{1,0:T(8,128)}) custom-call(bf16[1856,128]{1,0:T(8,128)(2,1)} %copy-done.4, bf16[1856,128]{1,0:T(8,128)(2,1)} %copy-done.6, bf16[256,1792]{1,0:T(8,128)(2,1)} %get-tuple-element.19.both_t, f32[64,256]{1,0:T(8,128)} %get-tuple-element.20.before), custom_call_target="tpu_custom_call" | custom-call | tf_op jit(solution)/shard_map/far/pallas_call | solution.py:212
  52.7 2.9 %far.4 = (f32[256,128]{1,0:T(8,128)}, f32[256,128]{1,0:T(8,128)}, f32[64,256]{1,0:T(8,128)}) custom-call(bf16[1856,128]{1,0:T(8,128)(2,1)} %copy-done.5, bf16[1856,128]{1,0:T(8,128)(2,1)} %collective-permute-done.5.second, bf16[256,1792]{1,0:T(8,128)(2,1)} %get-tuple-element.19.both_t, f32[64,256]{1,0:T(8,128)} %get-tuple-element.22.before), custom_call_target="tpu_custom_call" | custom-call | tf_op jit(solution)/shard_map/far/pallas_call | solution.py:212
  55.6 2.5 %collective-permute-start.10 = (f32[256,128]{1,0:T(8,128)}, f32[256,128]{1,0:T(8,128)S(1)}, u32[]{:S(2)}, u32[]{:S(2)}) collective-permute-start(f32[256,128]{1,0:T(8,128)} %get-tuple-element.29), channel_id=1, source_target_pairs={{0,1},{1,0},{2,3},{3,2},{4,5},{5,4},{6,7},{7,6},{8,9},{9,8},{10,11... | collective-permute-start | bytes 393224 | tf_op jit(solution)/shard_map/ppermute | solution.py:218
  58.1 2.9 %far.5 = (f32[256,128]{1,0:T(8,128)}, f32[256,128]{1,0:T(8,128)}, f32[64,256]{1,0:T(8,128)}) custom-call(bf16[1856,128]{1,0:T(8,128)(2,1)} %copy-done.3, bf16[1856,128]{1,0:T(8,128)(2,1)} %collective-permute-done.7.second, bf16[256,1792]{1,0:T(8,128)(2,1)} %get-tuple-element.19.both_t, f32[64,256]{1,0:T(8,128)} %get-tuple-element.24.before), custom_call_target="tpu_custom_call" | custom-call | tf_op jit(solution)/shard_map/far/pallas_call | solution.py:212
  65.1 2.6 %farthest.1 = (f32[192,128]{1,0:T(8,128)}, f32[192,128]{1,0:T(8,128)}) custom-call(bf16[1856,128]{1,0:T(8,128)(2,1)} %copy-done.1, bf16[256,1792]{1,0:T(8,128)(2,1)} %get-tuple-element.19.both_t, f32[64,256]{1,0:T(8,128)} %get-tuple-element.26.before), custom_call_target="tpu_custom_call" | custom-call | tf_op jit(solution)/shard_map/farthest/pallas_call | solution.py:219
  67.7 2.4 %collective-permute-start.12 = (f32[192,128]{1,0:T(8,128)}, f32[192,128]{1,0:T(8,128)S(1)}, u32[]{:S(2)}, u32[]{:S(2)}) collective-permute-start(f32[192,128]{1,0:T(8,128)} %get-tuple-element.31), channel_id=1, source_target_pairs={{0,1},{1,0},{2,3},{3,2},{4,5},{5,4},{6,7},{7,6},{8,9},{9,8},{10,11... | collective-permute-start | bytes 294920 | tf_op jit(solution)/shard_map/ppermute | solution.py:223
  72.0 2.7 %message.1.refs_0_ = f32[32,72,128]{2,1,0:T(8,128)} custom-call(s32[1]{0:T(128)} %bitcast.refs_0_, f32[256,128]{1,0:T(8,128)} %get-tuple-element.18.refs_1_, f32[256,128]{1,0:T(8,128)} %get-tuple-element.21.refs_2_, f32[256,128]{1,0:T(8,128)} %get-tuple-element.23.refs_3_, f32[256,128]{1,0:T(8,128)} %get-tuple-element.25.refs_4_, ...), custom_call_target="tpu_custom_call" | custom-call | tf_op jit(solution)/shard_map/message/pallas_call | solution.py:232
  74.7 2.2 %convert_element_type.16 = f16[32,72,128]{2,1,0:T(8,128)(2,1)} convert(f32[32,72,128]{2,1,0:T(8,128)} %message.1.refs_0_) | non-fusion elementwise | flops 294912 | bytes 1769472 | tf_op jit(solution)/shard_map/convert_element_type | solution.py:240
  76.9 13.2 %all-to-all-start = ((f16[32,72,128]{2,1,0:T(8,128)(2,1)}), f16[32,72,128]{2,1,0:T(8,128)(2,1)S(1)}, u32[]{:S(2)}, u32[]{:S(2)}) async-start(f16[32,72,128]{2,1,0:T(8,128)(2,1)} %convert_element_type.16), calls=%async_computation | async-start | bytes 1179648 | tf_op jit(solution)/shard_map/all_to_all | solution.py:240
  91.5 17.1 %all-to-all-done = f16[32,72,128]{2,1,0:T(8,128)(2,1)S(1)} async-done(((f16[32,72,128]{2,1,0:T(8,128)(2,1)}), f16[32,72,128]{2,1,0:T(8,128)(2,1)S(1)}, u32[]{:S(2)}, u32[]{:S(2)}) %all-to-all-start) | async-done | bytes 589856 | tf_op jit(solution)/shard_map/all_to_all | solution.py:240
  109.7 3.3 %suffix.1 = f32[32,72,128]{2,1,0:T(8,128)} custom-call(f32[32,72,128]{2,1,0:T(8,128)} %convert_element_type.17.refs_0_, f32[72,128]{1,0:T(8,128)} %maximum_maximum_fusion.refs_1_), custom_call_target="tpu_custom_call" | custom-call | tf_op jit(solution)/shard_map/suffix/pallas_call | solution.py:251
  113.0 2.2 %convert_element_type.18 = f16[32,72,128]{2,1,0:T(8,128)(2,1)} convert(f32[32,72,128]{2,1,0:T(8,128)} %suffix.1) | non-fusion elementwise | flops 294912 | bytes 1769472 | tf_op jit(solution)/shard_map/convert_element_type | solution.py:240
  115.2 5.8 %all-to-all-start.1 = ((f16[32,72,128]{2,1,0:T(8,128)(2,1)}), f16[32,72,128]{2,1,0:T(8,128)(2,1)S(1)}, u32[]{:S(2)}, u32[]{:S(2)}) async-start(f16[32,72,128]{2,1,0:T(8,128)(2,1)} %convert_element_type.18), calls=%async_computation.1 | async-start | bytes 1179648 | tf_op jit(solution)/shard_map/all_to_all | solution.py:240
  121.6 17.9 %all-to-all-done.1 = f16[32,72,128]{2,1,0:T(8,128)(2,1)S(1)} async-done(((f16[32,72,128]{2,1,0:T(8,128)(2,1)}), f16[32,72,128]{2,1,0:T(8,128)(2,1)S(1)}, u32[]{:S(2)}, u32[]{:S(2)}) %all-to-all-start.1) | async-done | bytes 589856 | tf_op jit(solution)/shard_map/all_to_all | solution.py:240
  140.6 3.7 %last.1 = (f32[2048,128]{1,0:T(8,128)}, f32[64,128]{1,0:T(8,128)}) custom-call(f32[32,72,128]{2,1,0:T(8,128)} %message.1.refs_0_, f32[32,72,128]{2,1,0:T(8,128)} %convert_element_type.19.refs_1_, f32[32,128]{1,0:T(8,128)} %pad.9.refs_2_, f32[1,128]{1,0:T(1,128)} %copy-done.13), custom_call_target="tpu_custom_call" | custom-call | tf_op jit(solution)/shard_map/last/pallas_call | solution.py:257
  (63 shorter events, 22.4 us)
Async XLA Ops:
  0.6 90.2 %copy-start = (f32[2048,128]{1,0:T(8,128)S(1)}, f32[2048,128]{1,0:T(8,128)}, u32[]{:S(2)}) copy-start(f32[2048,128]{1,0:T(8,128)} %param.10) | copy-start | bytes 3145732
  2.6 6.6 %collective-permute-start = (bf16[1856,128]{1,0:T(8,128)(2,1)}, bf16[1856,128]{1,0:T(8,128)(2,1)S(1)}, u32[]{:S(2)}, u32[]{:S(2)}) collective-permute-start(bf16[1856,128]{1,0:T(8,128)(2,1)} %pack.1.mine), channel_id=1, source_target_pairs={{0,1},{1,0},{2,3},{3,2},{4,5},{5,4},{6,7},{7,6},{8,9},{9,8},{10,11... | collective-permute-start | bytes 1425416 | tf_op jit(solution)/shard_map/ppermute | solution.py:192
  4.5 11.2 %collective-permute-start.2 = (bf16[1856,128]{1,0:T(8,128)(2,1)}, bf16[1856,128]{1,0:T(8,128)(2,1)S(1)}, u32[]{:S(2)}, u32[]{:S(2)}) collective-permute-start(bf16[1856,128]{1,0:T(8,128)(2,1)} %pack.1.mine), channel_id=1, source_target_pairs={{0,2},{1,15},{2,4},{3,1},{4,6},{5,3},{6,8},{7,5},{8,10},{9,7},{10,... | collective-permute-start | bytes 1425416 | tf_op jit(solution)/shard_map/ppermute | solution.py:191
  9.2 36.2 %copy-start.2 = (bf16[1856,128]{1,0:T(8,128)(2,1)}, bf16[1856,128]{1,0:T(8,128)(2,1)S(1)}, u32[]{:S(2)}) copy-start(bf16[1856,128]{1,0:T(8,128)(2,1)S(1)} %collective-permute-done.other) | copy-start | bytes 1425412
  9.2 11.9 %collective-permute-start.3 = (bf16[1856,128]{1,0:T(8,128)(2,1)S(1)}, bf16[1856,128]{1,0:T(8,128)(2,1)S(1)}, u32[]{:S(2)}, u32[]{:S(2)}) collective-permute-start(bf16[1856,128]{1,0:T(8,128)(2,1)S(1)} %collective-permute-done.other), channel_id=1, source_target_pairs={{0,2},{1,15},{2,4},{3,1},{4,6},{5,3},{6,8},{7,5},{8,10},{9,7},{10,... | collective-permute-start | bytes 1425416 | tf_op jit(solution)/shard_map/ppermute | solution.py:194
  15.7 32.2 %copy-start.4 = (bf16[1856,128]{1,0:T(8,128)(2,1)}, bf16[1856,128]{1,0:T(8,128)(2,1)S(1)}, u32[]{:S(2)}) copy-start(bf16[1856,128]{1,0:T(8,128)(2,1)S(1)} %collective-permute-done.2.first) | copy-start | bytes 1425412
  15.7 11.6 %collective-permute-start.4 = (bf16[1856,128]{1,0:T(8,128)(2,1)S(1)}, bf16[1856,128]{1,0:T(8,128)(2,1)S(1)}, u32[]{:S(2)}, u32[]{:S(2)}) collective-permute-start(bf16[1856,128]{1,0:T(8,128)(2,1)S(1)} %collective-permute-done.2.first), channel_id=1, source_target_pairs={{0,2},{1,15},{2,4},{3,1},{4,6},{5,3},{6,8},{7,5},{8,10},{9,7},{10,... | collective-permute-start | bytes 1425416 | tf_op jit(solution)/shard_map/ppermute | solution.py:197
  21.2 18.4 %copy-start.6 = (bf16[1856,128]{1,0:T(8,128)(2,1)}, bf16[1856,128]{1,0:T(8,128)(2,1)S(1)}, u32[]{:S(2)}) copy-start(bf16[1856,128]{1,0:T(8,128)(2,1)S(1)} %collective-permute-done.3.second) | copy-start | bytes 1425412
  21.2 16.5 %collective-permute-start.5 = (bf16[1856,128]{1,0:T(8,128)(2,1)S(1)}, bf16[1856,128]{1,0:T(8,128)(2,1)}, u32[]{:S(2)}, u32[]{:S(2)}) collective-permute-start(bf16[1856,128]{1,0:T(8,128)(2,1)S(1)} %collective-permute-done.3.second), channel_id=1, source_target_pairs={{0,2},{1,15},{2,4},{3,1},{4,6},{5,3},{6,8},{7,5},{8,10},{9,7},{10,... | collective-permute-start | bytes 1425416 | tf_op jit(solution)/shard_map/ppermute | solution.py:199
  27.3 23.5 %copy-start.5 = (bf16[1856,128]{1,0:T(8,128)(2,1)}, bf16[1856,128]{1,0:T(8,128)(2,1)S(1)}, u32[]{:S(2)}) copy-start(bf16[1856,128]{1,0:T(8,128)(2,1)S(1)} %collective-permute-done.4.first) | copy-start | bytes 1425412
  27.3 12.3 %collective-permute-start.6 = (bf16[1856,128]{1,0:T(8,128)(2,1)S(1)}, bf16[1856,128]{1,0:T(8,128)(2,1)S(1)}, u32[]{:S(2)}, u32[]{:S(2)}) collective-permute-start(bf16[1856,128]{1,0:T(8,128)(2,1)S(1)} %collective-permute-done.4.first), channel_id=1, source_target_pairs={{0,2},{1,15},{2,4},{3,1},{4,6},{5,3},{6,8},{7,5},{8,10},{9,7},{10,... | collective-permute-start | bytes 1425416 | tf_op jit(solution)/shard_map/ppermute | solution.py:197
  33.8 11.6 %copy-start.7 = (bf16[256,128]{1,0:T(8,128)(2,1)}, bf16[256,128]{1,0:T(8,128)(2,1)S(1)}, u32[]{:S(2)}) copy-start(bf16[256,128]{1,0:T(8,128)(2,1)S(1)} %slice_bitcast_fusion.mine_top) | copy-start | bytes 196612
  33.8 11.6 %collective-permute-start.1 = (bf16[256,128]{1,0:T(8,128)(2,1)S(1)}, bf16[256,128]{1,0:T(8,128)(2,1)}, u32[]{:S(2)}, u32[]{:S(2)}) collective-permute-start(bf16[256,128]{1,0:T(8,128)(2,1)S(1)} %slice_bitcast_fusion.mine_top), channel_id=1, source_target_pairs={{0,1},{1,0},{2,3},{3,2},{4,5},{5,4},{6,7},{7,6},{8,9},{9,8},{10,11... | collective-permute-start | bytes 196616 | tf_op jit(solution)/shard_map/ppermute | solution.py:193
  37.6 20.5 %collective-permute-start.7 = (bf16[1856,128]{1,0:T(8,128)(2,1)}, bf16[1856,128]{1,0:T(8,128)(2,1)}, u32[]{:S(2)}, u32[]{:S(2)}) collective-permute-start(bf16[1856,128]{1,0:T(8,128)(2,1)} %collective-permute-done.5.second), channel_id=1, source_target_pairs={{0,2},{1,15},{2,4},{3,1},{4,6},{5,3},{6,8},{7,5},{8,10},{9,7},{10,... | collective-permute-start | bytes 1425416 | tf_op jit(solution)/shard_map/ppermute | solution.py:199
  39.6 11.2 %copy-start.3 = (bf16[1856,128]{1,0:T(8,128)(2,1)}, bf16[1856,128]{1,0:T(8,128)(2,1)S(1)}, u32[]{:S(2)}) copy-start(bf16[1856,128]{1,0:T(8,128)(2,1)S(1)} %collective-permute-done.6.first) | copy-start | bytes 1425412
  39.6 24.7 %collective-permute-start.8 = (bf16[1856,128]{1,0:T(8,128)(2,1)S(1)}, bf16[1856,128]{1,0:T(8,128)(2,1)S(1)}, u32[]{:S(2)}, u32[]{:S(2)}) collective-permute-start(bf16[1856,128]{1,0:T(8,128)(2,1)S(1)} %collective-permute-done.6.first), channel_id=1, source_target_pairs={{0,2},{1,15},{2,4},{3,1},{4,6},{5,3},{6,8},{7,5},{8,10},{9,7},{10,... | collective-permute-start | bytes 1425416 | tf_op jit(solution)/shard_map/ppermute | solution.py:197
  45.4 5.4 %copy-start.13 = (f32[1,128]{1,0:T(1,128)}, f32[1,128]{1,0:T(1,128)S(1)}, u32[]{:S(2)}) copy-start(f32[1,128]{1,0:T(1,128)S(1)} %get-tuple-element.35.refs_3_) | copy-start | bytes 1540
  50.8 19.9 %collective-permute-start.9 = (f32[256,128]{1,0:T(8,128)}, f32[256,128]{1,0:T(8,128)S(1)}, u32[]{:S(2)}, u32[]{:S(2)}) collective-permute-start(f32[256,128]{1,0:T(8,128)} %get-tuple-element.28), channel_id=1, source_target_pairs={{0,1},{1,0},{2,3},{3,2},{4,5},{5,4},{6,7},{7,6},{8,9},{9,8},{10,11... | collective-permute-start | bytes 393224 | tf_op jit(solution)/shard_map/ppermute | solution.py:218
  55.6 8.0 %copy-start.12 = (f32[64,64]{1,0:T(8,128)S(1)}, f32[64,64]{1,0:T(8,128)}, u32[]{:S(2)}) copy-start(f32[64,64]{1,0:T(8,128)} %param.9) | copy-start | bytes 49156
  55.6 15.1 %collective-permute-start.10 = (f32[256,128]{1,0:T(8,128)}, f32[256,128]{1,0:T(8,128)S(1)}, u32[]{:S(2)}, u32[]{:S(2)}) collective-permute-start(f32[256,128]{1,0:T(8,128)} %get-tuple-element.29), channel_id=1, source_target_pairs={{0,1},{1,0},{2,3},{3,2},{4,5},{5,4},{6,7},{7,6},{8,9},{9,8},{10,11... | collective-permute-start | bytes 393224 | tf_op jit(solution)/shard_map/ppermute | solution.py:218
  61.0 10.3 %collective-permute-start.11 = (f32[256,128]{1,0:T(8,128)}, f32[256,128]{1,0:T(8,128)S(1)}, u32[]{:S(2)}, u32[]{:S(2)}) collective-permute-start(f32[256,128]{1,0:T(8,128)} %get-tuple-element.30), channel_id=1, source_target_pairs={{0,1},{1,0},{2,3},{3,2},{4,5},{5,4},{6,7},{7,6},{8,9},{9,8},{10,11... | collective-permute-start | bytes 393224 | tf_op jit(solution)/shard_map/ppermute | solution.py:218
  67.7 3.5 %collective-permute-start.12 = (f32[192,128]{1,0:T(8,128)}, f32[192,128]{1,0:T(8,128)S(1)}, u32[]{:S(2)}, u32[]{:S(2)}) collective-permute-start(f32[192,128]{1,0:T(8,128)} %get-tuple-element.31), channel_id=1, source_target_pairs={{0,1},{1,0},{2,3},{3,2},{4,5},{5,4},{6,7},{7,6},{8,9},{9,8},{10,11... | collective-permute-start | bytes 294920 | tf_op jit(solution)/shard_map/ppermute | solution.py:223
  76.9 31.8 %all-to-all-start = ((f16[32,72,128]{2,1,0:T(8,128)(2,1)}), f16[32,72,128]{2,1,0:T(8,128)(2,1)S(1)}, u32[]{:S(2)}, u32[]{:S(2)}) async-start(f16[32,72,128]{2,1,0:T(8,128)(2,1)} %convert_element_type.16), calls=%async_computation | async-start | bytes 1179648 | tf_op jit(solution)/shard_map/all_to_all | solution.py:240
  115.2 24.3 %all-to-all-start.1 = ((f16[32,72,128]{2,1,0:T(8,128)(2,1)}), f16[32,72,128]{2,1,0:T(8,128)(2,1)S(1)}, u32[]{:S(2)}, u32[]{:S(2)}) async-start(f16[32,72,128]{2,1,0:T(8,128)(2,1)} %convert_element_type.18), calls=%async_computation.1 | async-start | bytes 1179648 | tf_op jit(solution)/shard_map/all_to_all | solution.py:240
  (5 other events, 3.4 us)

commit v4 on v3

--- a/solution.py
+++ b/solution.py
@@ -96,10 +96,9 @@
     give[count:, :] = total[:, width:]
 
 
-def message_kernel(rows, chips, at, own, *refs):
-    hops = (len(refs) - 4) // 2
+def message_kernel(rows, chips, hops, at, own, *refs):
     kept, given = refs[:hops], refs[hops : 2 * hops]
-    tip_t, decay_rows, decay_cols, out = refs[2 * hops :]
+    tip_t, decay_rows, decay_cols, out, copied, own_arrow, plain, done = refs[2 * hops :]
     width = own.shape[1]
     per = width // rows
     chip, core = at[0] // CORES, at[0] % CORES
@@ -107,7 +106,7 @@
 
     def put(block, hop, parity):
         spot = lax.rem(chip + hop + chips, chips) * CORES + parity
-        out[pl.ds(spot * per, per), :rows, :] = block.reshape(per, rows, width)
+        plain[pl.ds(spot * per, per), :, :] = block.reshape(per, rows, width)
 
     put(own[:width, :], 0, core)
     put(own[width:, :], 0, 1 - core)
@@ -118,15 +117,19 @@
         if s < hops - 1:
             put(kept[s][width:, :], -hop, 1 - core)
             put(given[s][width:, :], hop, core)
+    copy = pltpu.make_async_copy(plain, copied, done)
+    copy.start()
     total = kept[-1][width:, :] + given[-1][width:, :]
     arrow = -jnp.dot(tip_t[...], total, precision=lax.Precision.HIGHEST, preferred_element_type=jnp.float32)
+    own_arrow[...] = arrow
     fill = jnp.zeros((PAD - 2, width), jnp.float32)
     cols = decay_cols[...]
     place = lax.broadcasted_iota(jnp.int32, cols.shape, 0)
     for r in range(out.shape[0]):
         extra = jnp.where(place == 4, decay_rows[r : r + 1, :], cols)
         pair = jnp.concatenate([arrow[2 * r : 2 * r + 2, :], fill], axis=0)
-        out[r, :rows, :], out[r, rows:, :] = encode(out[r, :rows, :], pair, extra)
+        out[r, :rows, :], out[r, rows:, :] = encode(plain[r], pair, extra)
+    copy.wait()
 
 
 def scan_kernel(rows, got, end, out, turned):
@@ -147,20 +150,39 @@
         pair = arrow + by_col * pair
 
 
-def last_kernel(rows, sent, got, decay_rows, by_col, sigma, arrows):
+def last_kernel(rows, plain, own_arrow, got, decay_rows, by_col, sigma, arrows):
     columns = decay_rows[...].T[:rows, :]
-    for r in range(sent.shape[0]):
-        panel, arrow = decode(sent[r], rows)
+    for r in range(plain.shape[0]):
         later, later_arrow = decode(got[r], rows)
-        by_row = jnp.broadcast_to(columns[:, r : r + 1], panel.shape)
-        sigma[r * rows : (r + 1) * rows, :] = panel + by_row * by_col[...] * later
-        arrows[2 * r : 2 * r + 2, :] = (arrow + by_col[...] * later_arrow)[:2, :]
+        by_row = jnp.broadcast_to(columns[:, r : r + 1], later.shape)
+        sigma[r * rows : (r + 1) * rows, :] = plain[r] + by_row * by_col[...] * later
+        pair = slice(2 * r, 2 * r + 2)
+        arrows[pair, :] = own_arrow[pair, :] + by_col[...] * later_arrow[:2, :]
 
 
 def two_parts(decay):
     scaled = decay * DECAY
     high = lax.reduce_precision(scaled, 8, 7)
     return high, (scaled - high) * 256
+
+
+VMEM = pl.BlockSpec(memory_space=pltpu.VMEM)
+SMEM = pl.BlockSpec(memory_space=pltpu.SMEM)
+
+
+def near(x):
+    return pltpu.with_memory_space_constraint(x, pltpu.VMEM)
+
+
+def held(kernel, name, results, *operands, scratch=()):
+    return pl.pallas_call(
+        kernel,
+        out_shape=tuple(pltpu.VMEM(shape, dtype) for shape, dtype in results),
+        in_specs=[VMEM] * len(operands),
+        out_specs=(VMEM,) * len(results),
+        scratch_shapes=scratch,
+        name=name,
+    )(*map(near, operands))
 
 
 def body(inverse_factor, arrow_factor, decay, tip_inverse, sigma_end, arrow_end):
@@ -176,49 +198,47 @@
     around = [
         (p, (p // CORES + 1 - 2 * (p % CORES)) % chips * CORES + p % CORES) for p in range(devices)
     ]
-    depth = order - cut
-    tall = depth + arrow
-    f32 = lambda *shape: jax.ShapeDtypeStruct(shape, jnp.float32)
-
-    def pack_kernel(cols, border, out):
+    depth, both = order - cut, CORES * width
+    tall, hops = depth + arrow, chips // 2
+    f32, bf16 = jnp.float32, jnp.bfloat16
+
+    def pack_kernel(cols, border, out, top):
         out[:depth, :] = cols[cut:, :]
         out[depth:, :] = border[...]
-
-    mine = pl.pallas_call(
-        pack_kernel, out_shape=jax.ShapeDtypeStruct((tall, width), jnp.bfloat16), name="pack"
+        top[...] = cols[:cut, :]
+
+    mine, top = pl.pallas_call(
+        pack_kernel,
+        out_shape=(pltpu.VMEM((tall, width), bf16), pltpu.VMEM((cut, width), bf16)),
+        in_specs=[VMEM, VMEM],
+        out_specs=(VMEM, VMEM),
+        name="pack",
     )(factor_cols, arrow_factor[0])
-    top = factor_cols[:cut]
-    first = [lax.ppermute(mine, "space", around)]
+    first = lax.ppermute(mine, "space", around)
     other = lax.ppermute(mine, "space", swapped)
     other_top = lax.ppermute(top, "space", swapped)
-    second = [lax.ppermute(other, "space", around)]
-    hops = chips // 2
-    for s in range(1, hops):
-        first.append(lax.ppermute(first[-1], "space", around))
-        if s < hops - 1:
-            second.append(lax.ppermute(second[-1], "space", around))
-
+    second = lax.ppermute(other, "space", around)
     own, both_t, total = pl.pallas_call(
         own_kernel,
-        out_shape=(
-            f32(CORES * width, width),
-            jax.ShapeDtypeStruct((CORES * width, depth), jnp.bfloat16),
-            f32(arrow, CORES * width),
-        ),
+        out_shape=tuple(map(jax.ShapeDtypeStruct, ((both, width), (both, depth), (arrow, both)), (f32, bf16, f32))),
         name="own",
     )(mine, other, top, other_top)
     kept, given = [], []
+    second, total = lax.optimization_barrier((second, total))
     for s in range(hops - 1):
+        next_first = lax.ppermute(first, "space", around)
+        next_second = lax.ppermute(second, "space", around) if s < hops - 2 else None
         keep, give, total = pl.pallas_call(
             far_kernel,
-            out_shape=(f32(2 * width, width), f32(2 * width, width), f32(arrow, CORES * width)),
+            out_shape=[jax.ShapeDtypeStruct(shape, f32) for shape in ((both, width), (both, width), (arrow, both))],
             name="far",
-        )(first[s], second[s], both_t, total)
+        )(first, second, both_t, total)
         kept.append(keep)
         given.append(lax.ppermute(give, "space", swapped))
-    keep, give = pl.pallas_call(
-        farthest_kernel, out_shape=(f32(width + arrow, width), f32(width + arrow, width)), name="farthest"
-    )(first[-1], both_t, total)
+        first, second = next_first, next_second
+        if s < hops - 2:
+            first, total = lax.optimization_barrier((first, total))
+    keep, give = held(farthest_kernel, "farthest", (((width + arrow, width), f32),) * 2, first, both_t, total)
     kept.append(keep)
     given.append(lax.ppermute(give, "space", swapped))
 
@@ -227,14 +247,20 @@
     row_parts = jnp.concatenate(two_parts(decay_rows), axis=1)
     row_parts = jnp.pad(row_parts, ((0, 0), (0, width - 2 * rows)))
     col_parts = jnp.pad(jnp.concatenate(two_parts(by_col), axis=0), ((5, PAD - 7), (0, 0)))
-    message = f32(pieces, rows + PAD, width)
-    vmem, smem = pl.BlockSpec(memory_space=pltpu.VMEM), pl.BlockSpec(memory_space=pltpu.SMEM)
-    sent = pl.pallas_call(
-        lambda *refs: message_kernel(rows, chips, *refs),
-        out_shape=message,
-        in_specs=[smem] + [vmem] * (2 * hops + 4),
+    message = ((pieces, rows + PAD, width), f32)
+    pairs = [*kept[:-1], near(kept[-1]), *given[:-1], near(given[-1])]
+    sent, plain, own_arrow = pl.pallas_call(
+        lambda *refs: message_kernel(rows, chips, hops, *refs),
+        out_shape=(
+            pltpu.VMEM(*message),
+            jax.ShapeDtypeStruct((pieces, rows, width), f32),
+            jax.ShapeDtypeStruct((arrow, width), f32),
+        ),
+        in_specs=[SMEM] + [VMEM] * (2 * hops + 4),
+        out_specs=(VMEM, pl.BlockSpec(memory_space=pl.ANY), VMEM),
+        scratch_shapes=[pltpu.VMEM((pieces, rows, width), f32), pltpu.SemaphoreType.DMA],
         name="message",
-    )(column_at.reshape(1), own, *kept, *given, tip_inverse.T, row_parts, col_parts)
+    )(column_at.reshape(1), own, *pairs, near(tip_inverse.T), near(row_parts), near(col_parts))
 
     def exchange(values):
         moved = lax.all_to_all(values.astype(jnp.float16), "tm", 0, 0, tiled=True)
@@ -248,17 +274,20 @@
         ],
         axis=0,
     )
-    ahead = pl.pallas_call(
+    (ahead,) = held(
         lambda *refs: scan_kernel(rows, *refs),
-        out_shape=message,
-        scratch_shapes=[pltpu.VMEM((pieces, width), jnp.float32)],
-        name="suffix",
-    )(exchange(sent), end)
+        "suffix",
+        (message,),
+        *(exchange(sent), end),
+        scratch=[pltpu.VMEM((pieces, width), f32)],
+    )
+    last = (plain, own_arrow, exchange(ahead), jnp.pad(decay_rows, ((0, 0), (0, width - rows))), by_col)
     sigma, arrows = pl.pallas_call(
         lambda *refs: last_kernel(rows, *refs),
-        out_shape=(f32(order, width), f32(arrow, width)),
+        out_shape=(jax.ShapeDtypeStruct((order, width), f32), jax.ShapeDtypeStruct((arrow, width), f32)),
+        in_specs=[VMEM] * len(last),
         name="last",
-    )(sent, exchange(ahead), jnp.pad(decay_rows, ((0, 0), (0, width - rows))), by_col)
+    )(*map(near, last))
     return sigma[None], arrows.T[None]
 
 

time: 146 us -> 129 us (0.88)
  the two profiles are of different devices: /device:TPU:24 before, /device:TPU:8 now
where the time goes in v4:
time: 129 us; the launch traced here: 128 us
  starting transfers between devices  53.6 us (42%)
  waiting for transfers between devices  47.6 us (37%)
  Pallas kernels  18.5 us (14%)
  other arithmetic  3.9 us (3%)
  local copies, waits for them, and re-layouts  2.96 us (2%)
    all_to_all x2, waiting for transfers between devices, exchange(): moved = lax.all_to_all(values.astype(jnp.float16), 'tm', 0, 0, tiled=True)  36.2 us
    all_to_all x2, starting transfers between devices, exchange(): moved = lax.all_to_all(values.astype(jnp.float16), 'tm', 0, 0, tiled=True)  16.4 us
    ppermute x4, starting transfers between devices, body(): given.append(lax.ppermute(give, 'space', swapped))  10.9 us
    ppermute x3, starting transfers between devices, body(): next_first = lax.ppermute(first, 'space', around)  10.3 us
    pallas_call x3, Pallas kernels, body(): pl.pallas_call(far_kernel, out_shape=[jax.ShapeDtypeStruct(shape, f32) fo...  8.63 us
    ppermute x1, waiting for transfers between devices, body(): first = lax.ppermute(mine, 'space', around)  7.46 us
    ppermute x2, starting transfers between devices, body(): lax.ppermute(second, 'space', around)  3.83 us
    ppermute x1, starting transfers between devices, body(): first = lax.ppermute(mine, 'space', around)  3.49 us
  transfers between devices with their start and end apart: 15, of which 6 were waited for; matrix products, arithmetic and copies ran while one was open for 2% of the time, Pallas kernels for 9%

profile of v4, /device:TPU:8, one launch (start us, length us, event | category | flops | bytes accessed | tf_op | source)
XLA Modules:
  0.0 127.7 jit_solution(3338581987754105937)
XLA Ops:
  1.8 1.9 %collective-permute-start = (bf16[1856,128]{1,0:T(8,128)(2,1)S(1)}, bf16[1856,128]{1,0:T(8,128)(2,1)S(1)}, u32[]{:S(2)}, u32[]{:S(2)}) collective-permute-start(bf16[1856,128]{1,0:T(8,128)(2,1)S(1)} %get-tuple-element.29.mine), channel_id=1, source_target_pairs={{0,1},{1,0},{2,3},{3,2},{4,5},{5,4},{6,7},{7,6},{8,9},{9,8},{10,11... | collective-permute-start | bytes 1425416 | tf_op jit(solution)/shard_map/ppermute | solution.py:218
  3.8 3.5 %collective-permute-start.2 = (bf16[1856,128]{1,0:T(8,128)(2,1)S(1)}, bf16[1856,128]{1,0:T(8,128)(2,1)}, u32[]{:S(2)}, u32[]{:S(2)}) collective-permute-start(bf16[1856,128]{1,0:T(8,128)(2,1)S(1)} %get-tuple-element.29.mine), channel_id=1, source_target_pairs={{0,2},{1,15},{2,4},{3,1},{4,6},{5,3},{6,8},{7,5},{8,10},{9,7},{10,... | collective-permute-start | bytes 1425416 | tf_op jit(solution)/shard_map/ppermute | solution.py:217
  7.3 3.5 %collective-permute-start.3 = (bf16[1856,128]{1,0:T(8,128)(2,1)S(1)}, bf16[1856,128]{1,0:T(8,128)(2,1)S(1)}, u32[]{:S(2)}, u32[]{:S(2)}) collective-permute-start(bf16[1856,128]{1,0:T(8,128)(2,1)S(1)} %collective-permute-done.other), channel_id=1, source_target_pairs={{0,2},{1,15},{2,4},{3,1},{4,6},{5,3},{6,8},{7,5},{8,10},{9,7},{10,... | collective-permute-start | bytes 1425416 | tf_op jit(solution)/shard_map/ppermute | solution.py:220
  10.8 7.5 %collective-permute-done.2.first = bf16[1856,128]{1,0:T(8,128)(2,1)} collective-permute-done((bf16[1856,128]{1,0:T(8,128)(2,1)S(1)}, bf16[1856,128]{1,0:T(8,128)(2,1)}, u32[]{:S(2)}, u32[]{:S(2)}) %collective-permute-start.2) | collective-permute-done | bytes 475168 | tf_op jit(solution)/shard_map/ppermute | solution.py:217
  18.2 1.9 %collective-permute-start.4 = (bf16[1856,128]{1,0:T(8,128)(2,1)}, bf16[1856,128]{1,0:T(8,128)(2,1)S(1)}, u32[]{:S(2)}, u32[]{:S(2)}) collective-permute-start(bf16[1856,128]{1,0:T(8,128)(2,1)} %collective-permute-done.2.first), channel_id=1, source_target_pairs={{0,2},{1,15},{2,4},{3,1},{4,6},{5,3},{6,8},{7,5},{8,10},{9,7},{10,... | collective-permute-start | bytes 1425416 | tf_op jit(solution)/shard_map/ppermute | solution.py:229
  20.1 3.3 %collective-permute-start.1 = (bf16[256,128]{1,0:T(8,128)(2,1)S(1)}, bf16[256,128]{1,0:T(8,128)(2,1)S(1)}, u32[]{:S(2)}, u32[]{:S(2)}) collective-permute-start(bf16[256,128]{1,0:T(8,128)(2,1)S(1)} %get-tuple-element.30.mine_top), channel_id=1, source_target_pairs={{0,1},{1,0},{2,3},{3,2},{4,5},{5,4},{6,7},{7,6},{8,9},{9,8},{10,11... | collective-permute-start | bytes 196616 | tf_op jit(solution)/shard_map/ppermute | solution.py:219
  24.9 2.5 %own.1 = (f32[256,128]{1,0:T(8,128)}, bf16[256,1792]{1,0:T(8,128)(2,1)}, f32[64,256]{1,0:T(8,128)}) custom-call(bf16[1856,128]{1,0:T(8,128)(2,1)} %copy-done.3, bf16[1856,128]{1,0:T(8,128)(2,1)} %copy-done.7, bf16[256,128]{1,0:T(8,128)(2,1)} %copy-done.4, bf16[256,128]{1,0:T(8,128)(2,1)} %copy-done.12), custom_call_target="tpu_custom_call" | custom-call | tf_op jit(solution)/shard_map/own/pallas_call | solution.py:221
  27.5 1.9 %collective-permute-start.5 = (bf16[1856,128]{1,0:T(8,128)(2,1)S(1)}, bf16[1856,128]{1,0:T(8,128)(2,1)}, u32[]{:S(2)}, u32[]{:S(2)}) collective-permute-start(bf16[1856,128]{1,0:T(8,128)(2,1)S(1)} %collective-permute-done.3.second), channel_id=1, source_target_pairs={{0,2},{1,15},{2,4},{3,1},{4,6},{5,3},{6,8},{7,5},{8,10},{9,7},{10,... | collective-permute-start | bytes 1425416 | tf_op jit(solution)/shard_map/ppermute | solution.py:230
  29.4 2.9 %far.3 = (f32[256,128]{1,0:T(8,128)}, f32[256,128]{1,0:T(8,128)}, f32[64,256]{1,0:T(8,128)}) custom-call(bf16[1856,128]{1,0:T(8,128)(2,1)} %collective-permute-done.2.first, bf16[1856,128]{1,0:T(8,128)(2,1)} %copy-done.10, bf16[256,1792]{1,0:T(8,128)(2,1)} %get-tuple-element.34.both_t, f32[64,256]{1,0:T(8,128)} %get-tuple-element.35.before), custom_call_target="tpu_custom_call" | custom-call | tf_op jit(solution)/shard_map/far/pallas_call | solution.py:231
  32.3 4.2 %collective-permute-start.6 = (bf16[1856,128]{1,0:T(8,128)(2,1)S(1)}, bf16[1856,128]{1,0:T(8,128)(2,1)S(1)}, u32[]{:S(2)}, u32[]{:S(2)}) collective-permute-start(bf16[1856,128]{1,0:T(8,128)(2,1)S(1)} %collective-permute-done.4.first), channel_id=1, source_target_pairs={{0,2},{1,15},{2,4},{3,1},{4,6},{5,3},{6,8},{7,5},{8,10},{9,7},{10,... | collective-permute-start | bytes 1425416 | tf_op jit(solution)/shard_map/ppermute | solution.py:229
  36.5 1.8 %collective-permute-done.5.second = bf16[1856,128]{1,0:T(8,128)(2,1)} collective-permute-done((bf16[1856,128]{1,0:T(8,128)(2,1)S(1)}, bf16[1856,128]{1,0:T(8,128)(2,1)}, u32[]{:S(2)}, u32[]{:S(2)}) %collective-permute-start.5) | collective-permute-done | bytes 475168 | tf_op jit(solution)/shard_map/ppermute | solution.py:230
  38.3 1.9 %collective-permute-start.7 = (bf16[1856,128]{1,0:T(8,128)(2,1)}, bf16[1856,128]{1,0:T(8,128)(2,1)}, u32[]{:S(2)}, u32[]{:S(2)}) collective-permute-start(bf16[1856,128]{1,0:T(8,128)(2,1)} %collective-permute-done.5.second), channel_id=1, source_target_pairs={{0,2},{1,15},{2,4},{3,1},{4,6},{5,3},{6,8},{7,5},{8,10},{9,7},{10,... | collective-permute-start | bytes 1425416 | tf_op jit(solution)/shard_map/ppermute | solution.py:230
  41.5 2.9 %far.4 = (f32[256,128]{1,0:T(8,128)}, f32[256,128]{1,0:T(8,128)}, f32[64,256]{1,0:T(8,128)}) custom-call(bf16[1856,128]{1,0:T(8,128)(2,1)} %copy-done.9, bf16[1856,128]{1,0:T(8,128)(2,1)} %collective-permute-done.5.second, bf16[256,1792]{1,0:T(8,128)(2,1)} %get-tuple-element.34.both_t, f32[64,256]{1,0:T(8,128)} %get-tuple-element.39.before), custom_call_target="tpu_custom_call" | custom-call | tf_op jit(solution)/shard_map/far/pallas_call | solution.py:231
  44.4 4.1 %collective-permute-start.8 = (bf16[1856,128]{1,0:T(8,128)(2,1)S(1)}, bf16[1856,128]{1,0:T(8,128)(2,1)S(1)}, u32[]{:S(2)}, u32[]{:S(2)}) collective-permute-start(bf16[1856,128]{1,0:T(8,128)(2,1)S(1)} %collective-permute-done.6.first), channel_id=1, source_target_pairs={{0,2},{1,15},{2,4},{3,1},{4,6},{5,3},{6,8},{7,5},{8,10},{9,7},{10,... | collective-permute-start | bytes 1425416 | tf_op jit(solution)/shard_map/ppermute | solution.py:229
  48.6 4.7 %collective-permute-start.9 = (f32[256,128]{1,0:T(8,128)}, f32[256,128]{1,0:T(8,128)S(1)}, u32[]{:S(2)}, u32[]{:S(2)}) collective-permute-start(f32[256,128]{1,0:T(8,128)} %get-tuple-element.47), channel_id=1, source_target_pairs={{0,1},{1,0},{2,3},{3,2},{4,5},{5,4},{6,7},{7,6},{8,9},{9,8},{10,11... | collective-permute-start | bytes 393224 | tf_op jit(solution)/shard_map/ppermute | solution.py:237
  53.3 1.9 %collective-permute-start.10 = (f32[256,128]{1,0:T(8,128)}, f32[256,128]{1,0:T(8,128)}, u32[]{:S(2)}, u32[]{:S(2)}) collective-permute-start(f32[256,128]{1,0:T(8,128)} %get-tuple-element.48), channel_id=1, source_target_pairs={{0,1},{1,0},{2,3},{3,2},{4,5},{5,4},{6,7},{7,6},{8,9},{9,8},{10,11... | collective-permute-start | bytes 393224 | tf_op jit(solution)/shard_map/ppermute | solution.py:237
  55.2 2.9 %far.5 = (f32[256,128]{1,0:T(8,128)}, f32[256,128]{1,0:T(8,128)}, f32[64,256]{1,0:T(8,128)}) custom-call(bf16[1856,128]{1,0:T(8,128)(2,1)} %copy-done.8, bf16[1856,128]{1,0:T(8,128)(2,1)} %collective-permute-done.7.second, bf16[256,1792]{1,0:T(8,128)(2,1)} %get-tuple-element.34.both_t, f32[64,256]{1,0:T(8,128)} %get-tuple-element.43.before), custom_call_target="tpu_custom_call" | custom-call | tf_op jit(solution)/shard_map/far/pallas_call | solution.py:231
  58.1 2.4 %collective-permute-start.11 = (f32[256,128]{1,0:T(8,128)}, f32[256,128]{1,0:T(8,128)}, u32[]{:S(2)}, u32[]{:S(2)}) collective-permute-start(f32[256,128]{1,0:T(8,128)} %get-tuple-element.49), channel_id=1, source_target_pairs={{0,1},{1,0},{2,3},{3,2},{4,5},{5,4},{6,7},{7,6},{8,9},{9,8},{10,11... | collective-permute-start | bytes 393224 | tf_op jit(solution)/shard_map/ppermute | solution.py:237
  62.2 1.9 %collective-permute-start.12 = (f32[192,128]{1,0:T(8,128)S(1)}, f32[192,128]{1,0:T(8,128)S(1)}, u32[]{:S(2)}, u32[]{:S(2)}) collective-permute-start(f32[192,128]{1,0:T(8,128)S(1)} %get-tuple-element.50), channel_id=1, source_target_pairs={{0,1},{1,0},{2,3},{3,2},{4,5},{5,4},{6,7},{7,6},{8,9},{9,8},{10,11... | collective-permute-start | bytes 294920 | tf_op jit(solution)/shard_map/ppermute | solution.py:243
  65.4 2.9 %message.1 = (f32[32,72,128]{2,1,0:T(8,128)S(1)}, f32[32,64,128]{2,1,0:T(8,128)}, f32[64,128]{1,0:T(8,128)}) custom-call(s32[1]{0:T(128)} %bitcast.refs_0_, f32[256,128]{1,0:T(8,128)} %get-tuple-element.31.refs_1_, f32[256,128]{1,0:T(8,128)} %get-tuple-element.36.refs_2_, f32[256,128]{1,0:T(8,128)} %get-tuple-element.40.refs_3_, ...), custom_call_target="tpu_custom_call" | custom-call | tf_op jit(solution)/shard_map/message/pallas_call | solution.py:252
  69.2 10.6 %all-to-all-start = ((f16[32,72,128]{2,1,0:T(8,128)(2,1)}), f16[32,72,128]{2,1,0:T(8,128)(2,1)S(1)}, u32[]{:S(2)}, u32[]{:S(2)}) async-start(f16[32,72,128]{2,1,0:T(8,128)(2,1)} %convert_element_type.16), calls=%async_computation | async-start | bytes 1179648 | tf_op jit(solution)/shard_map/all_to_all | solution.py:266
  80.7 17.7 %all-to-all-done = f16[32,72,128]{2,1,0:T(8,128)(2,1)S(1)} async-done(((f16[32,72,128]{2,1,0:T(8,128)(2,1)}), f16[32,72,128]{2,1,0:T(8,128)(2,1)S(1)}, u32[]{:S(2)}, u32[]{:S(2)}) %all-to-all-start) | async-done | bytes 589856 | tf_op jit(solution)/shard_map/all_to_all | solution.py:266
  100.5 5.9 %all-to-all-start.1 = ((f16[32,72,128]{2,1,0:T(8,128)(2,1)}), f16[32,72,128]{2,1,0:T(8,128)(2,1)}, u32[]{:S(2)}, u32[]{:S(2)}) async-start(f16[32,72,128]{2,1,0:T(8,128)(2,1)} %convert_element_type.18), calls=%async_computation.1 | async-start | bytes 1179648 | tf_op jit(solution)/shard_map/all_to_all | solution.py:266
  106.4 18.5 %all-to-all-done.1 = f16[32,72,128]{2,1,0:T(8,128)(2,1)} async-done(((f16[32,72,128]{2,1,0:T(8,128)(2,1)}), f16[32,72,128]{2,1,0:T(8,128)(2,1)}, u32[]{:S(2)}, u32[]{:S(2)}) %all-to-all-start.1) | async-done | bytes 589856 | tf_op jit(solution)/shard_map/all_to_all | solution.py:266
  (64 shorter events, 13.5 us)
Async XLA Ops:
  0.6 80.0 %copy-start = (f32[2048,128]{1,0:T(8,128)S(1)}, f32[2048,128]{1,0:T(8,128)}, u32[]{:S(2)}) copy-start(f32[2048,128]{1,0:T(8,128)} %param.10) | copy-start | bytes 3145732
  1.8 22.5 %copy-start.3 = (bf16[1856,128]{1,0:T(8,128)(2,1)}, bf16[1856,128]{1,0:T(8,128)(2,1)S(1)}, u32[]{:S(2)}) copy-start(bf16[1856,128]{1,0:T(8,128)(2,1)S(1)} %get-tuple-element.29.mine) | copy-start | bytes 1425412
  1.8 22.5 %copy-start.4 = (bf16[256,128]{1,0:T(8,128)(2,1)}, bf16[256,128]{1,0:T(8,128)(2,1)S(1)}, u32[]{:S(2)}) copy-start(bf16[256,128]{1,0:T(8,128)(2,1)S(1)} %get-tuple-element.30.mine_top) | copy-start | bytes 196612
  1.8 5.4 %collective-permute-start = (bf16[1856,128]{1,0:T(8,128)(2,1)S(1)}, bf16[1856,128]{1,0:T(8,128)(2,1)S(1)}, u32[]{:S(2)}, u32[]{:S(2)}) collective-permute-start(bf16[1856,128]{1,0:T(8,128)(2,1)S(1)} %get-tuple-element.29.mine), channel_id=1, source_target_pairs={{0,1},{1,0},{2,3},{3,2},{4,5},{5,4},{6,7},{7,6},{8,9},{9,8},{10,11... | collective-permute-start | bytes 1425416 | tf_op jit(solution)/shard_map/ppermute | solution.py:218
  3.8 14.5 %collective-permute-start.2 = (bf16[1856,128]{1,0:T(8,128)(2,1)S(1)}, bf16[1856,128]{1,0:T(8,128)(2,1)}, u32[]{:S(2)}, u32[]{:S(2)}) collective-permute-start(bf16[1856,128]{1,0:T(8,128)(2,1)S(1)} %get-tuple-element.29.mine), channel_id=1, source_target_pairs={{0,2},{1,15},{2,4},{3,1},{4,6},{5,3},{6,8},{7,5},{8,10},{9,7},{10,... | collective-permute-start | bytes 1425416 | tf_op jit(solution)/shard_map/ppermute | solution.py:217
  7.3 17.0 %copy-start.7 = (bf16[1856,128]{1,0:T(8,128)(2,1)}, bf16[1856,128]{1,0:T(8,128)(2,1)S(1)}, u32[]{:S(2)}) copy-start(bf16[1856,128]{1,0:T(8,128)(2,1)S(1)} %collective-permute-done.other) | copy-start | bytes 1425412
  7.3 20.2 %collective-permute-start.3 = (bf16[1856,128]{1,0:T(8,128)(2,1)S(1)}, bf16[1856,128]{1,0:T(8,128)(2,1)S(1)}, u32[]{:S(2)}, u32[]{:S(2)}) collective-permute-start(bf16[1856,128]{1,0:T(8,128)(2,1)S(1)} %collective-permute-done.other), channel_id=1, source_target_pairs={{0,2},{1,15},{2,4},{3,1},{4,6},{5,3},{6,8},{7,5},{8,10},{9,7},{10,... | collective-permute-start | bytes 1425416 | tf_op jit(solution)/shard_map/ppermute | solution.py:220
  18.2 14.1 %collective-permute-start.4 = (bf16[1856,128]{1,0:T(8,128)(2,1)}, bf16[1856,128]{1,0:T(8,128)(2,1)S(1)}, u32[]{:S(2)}, u32[]{:S(2)}) collective-permute-start(bf16[1856,128]{1,0:T(8,128)(2,1)} %collective-permute-done.2.first), channel_id=1, source_target_pairs={{0,2},{1,15},{2,4},{3,1},{4,6},{5,3},{6,8},{7,5},{8,10},{9,7},{10,... | collective-permute-start | bytes 1425416 | tf_op jit(solution)/shard_map/ppermute | solution.py:229
  20.1 4.2 %collective-permute-start.1 = (bf16[256,128]{1,0:T(8,128)(2,1)S(1)}, bf16[256,128]{1,0:T(8,128)(2,1)S(1)}, u32[]{:S(2)}, u32[]{:S(2)}) collective-permute-start(bf16[256,128]{1,0:T(8,128)(2,1)S(1)} %get-tuple-element.30.mine_top), channel_id=1, source_target_pairs={{0,1},{1,0},{2,3},{3,2},{4,5},{5,4},{6,7},{7,6},{8,9},{9,8},{10,11... | collective-permute-start | bytes 196616 | tf_op jit(solution)/shard_map/ppermute | solution.py:219
  27.4 12.8 %copy-start.14 = (f32[1,2048]{1,0:T(1,128)S(1)}, f32[1,2048]{1,0:T(1,128)}, u32[]{:S(2)}) copy-start(f32[1,2048]{1,0:T(1,128)} %param.8) | copy-start | bytes 24580
  27.5 10.9 %collective-permute-start.5 = (bf16[1856,128]{1,0:T(8,128)(2,1)S(1)}, bf16[1856,128]{1,0:T(8,128)(2,1)}, u32[]{:S(2)}, u32[]{:S(2)}) collective-permute-start(bf16[1856,128]{1,0:T(8,128)(2,1)S(1)} %collective-permute-done.3.second), channel_id=1, source_target_pairs={{0,2},{1,15},{2,4},{3,1},{4,6},{5,3},{6,8},{7,5},{8,10},{9,7},{10,... | collective-permute-start | bytes 1425416 | tf_op jit(solution)/shard_map/ppermute | solution.py:230
  32.3 12.1 %collective-permute-start.6 = (bf16[1856,128]{1,0:T(8,128)(2,1)S(1)}, bf16[1856,128]{1,0:T(8,128)(2,1)S(1)}, u32[]{:S(2)}, u32[]{:S(2)}) collective-permute-start(bf16[1856,128]{1,0:T(8,128)(2,1)S(1)} %collective-permute-done.4.first), channel_id=1, source_target_pairs={{0,2},{1,15},{2,4},{3,1},{4,6},{5,3},{6,8},{7,5},{8,10},{9,7},{10,... | collective-permute-start | bytes 1425416 | tf_op jit(solution)/shard_map/ppermute | solution.py:229
  38.3 16.9 %collective-permute-start.7 = (bf16[1856,128]{1,0:T(8,128)(2,1)}, bf16[1856,128]{1,0:T(8,128)(2,1)}, u32[]{:S(2)}, u32[]{:S(2)}) collective-permute-start(bf16[1856,128]{1,0:T(8,128)(2,1)} %collective-permute-done.5.second), channel_id=1, source_target_pairs={{0,2},{1,15},{2,4},{3,1},{4,6},{5,3},{6,8},{7,5},{8,10},{9,7},{10,... | collective-permute-start | bytes 1425416 | tf_op jit(solution)/shard_map/ppermute | solution.py:230
  44.4 16.2 %copy-start.13 = (f32[64,64]{1,0:T(8,128)S(1)}, f32[64,64]{1,0:T(8,128)}, u32[]{:S(2)}) copy-start(f32[64,64]{1,0:T(8,128)} %param.9) | copy-start | bytes 49156
  44.4 16.3 %copy-start.1 = (bf16[256,1792]{1,0:T(8,128)(2,1)S(1)}, bf16[256,1792]{1,0:T(8,128)(2,1)}, u32[]{:S(2)}) copy-start(bf16[256,1792]{1,0:T(8,128)(2,1)} %get-tuple-element.34.both_t) | copy-start | bytes 2752516
  44.4 16.3 %collective-permute-start.8 = (bf16[1856,128]{1,0:T(8,128)(2,1)S(1)}, bf16[1856,128]{1,0:T(8,128)(2,1)S(1)}, u32[]{:S(2)}, u32[]{:S(2)}) collective-permute-start(bf16[1856,128]{1,0:T(8,128)(2,1)S(1)} %collective-permute-done.6.first), channel_id=1, source_target_pairs={{0,2},{1,15},{2,4},{3,1},{4,6},{5,3},{6,8},{7,5},{8,10},{9,7},{10,... | collective-permute-start | bytes 1425416 | tf_op jit(solution)/shard_map/ppermute | solution.py:229
  48.6 15.6 %collective-permute-start.9 = (f32[256,128]{1,0:T(8,128)}, f32[256,128]{1,0:T(8,128)S(1)}, u32[]{:S(2)}, u32[]{:S(2)}) collective-permute-start(f32[256,128]{1,0:T(8,128)} %get-tuple-element.47), channel_id=1, source_target_pairs={{0,1},{1,0},{2,3},{3,2},{4,5},{5,4},{6,7},{7,6},{8,9},{9,8},{10,11... | collective-permute-start | bytes 393224 | tf_op jit(solution)/shard_map/ppermute | solution.py:237
  53.3 10.9 %collective-permute-start.10 = (f32[256,128]{1,0:T(8,128)}, f32[256,128]{1,0:T(8,128)}, u32[]{:S(2)}, u32[]{:S(2)}) collective-permute-start(f32[256,128]{1,0:T(8,128)} %get-tuple-element.48), channel_id=1, source_target_pairs={{0,1},{1,0},{2,3},{3,2},{4,5},{5,4},{6,7},{7,6},{8,9},{9,8},{10,11... | collective-permute-start | bytes 393224 | tf_op jit(solution)/shard_map/ppermute | solution.py:237
  58.1 7.3 %collective-permute-start.11 = (f32[256,128]{1,0:T(8,128)}, f32[256,128]{1,0:T(8,128)}, u32[]{:S(2)}, u32[]{:S(2)}) collective-permute-start(f32[256,128]{1,0:T(8,128)} %get-tuple-element.49), channel_id=1, source_target_pairs={{0,1},{1,0},{2,3},{3,2},{4,5},{5,4},{6,7},{7,6},{8,9},{9,8},{10,11... | collective-permute-start | bytes 393224 | tf_op jit(solution)/shard_map/ppermute | solution.py:237
  62.2 3.2 %collective-permute-start.12 = (f32[192,128]{1,0:T(8,128)S(1)}, f32[192,128]{1,0:T(8,128)S(1)}, u32[]{:S(2)}, u32[]{:S(2)}) collective-permute-start(f32[192,128]{1,0:T(8,128)S(1)} %get-tuple-element.50), channel_id=1, source_target_pairs={{0,1},{1,0},{2,3},{3,2},{4,5},{5,4},{6,7},{7,6},{8,9},{9,8},{10,11... | collective-permute-start | bytes 294920 | tf_op jit(solution)/shard_map/ppermute | solution.py:243
  69.2 29.2 %all-to-all-start = ((f16[32,72,128]{2,1,0:T(8,128)(2,1)}), f16[32,72,128]{2,1,0:T(8,128)(2,1)S(1)}, u32[]{:S(2)}, u32[]{:S(2)}) async-start(f16[32,72,128]{2,1,0:T(8,128)(2,1)} %convert_element_type.16), calls=%async_computation | async-start | bytes 1179648 | tf_op jit(solution)/shard_map/all_to_all | solution.py:266
  100.5 24.4 %all-to-all-start.1 = ((f16[32,72,128]{2,1,0:T(8,128)(2,1)}), f16[32,72,128]{2,1,0:T(8,128)(2,1)}, u32[]{:S(2)}, u32[]{:S(2)}) async-start(f16[32,72,128]{2,1,0:T(8,128)(2,1)} %convert_element_type.18), calls=%async_computation.1 | async-start | bytes 1179648 | tf_op jit(solution)/shard_map/all_to_all | solution.py:266
  106.4 19.7 %copy-start.2 = (f32[32,64,128]{2,1,0:T(8,128)S(1)}, f32[32,64,128]{2,1,0:T(8,128)}, u32[]{:S(2)}) copy-start(f32[32,64,128]{2,1,0:T(8,128)} %get-tuple-element.51.refs_0_) | copy-start | bytes 3145732
  106.4 19.6 %copy-start.6 = (f32[64,128]{1,0:T(8,128)S(1)}, f32[64,128]{1,0:T(8,128)}, u32[]{:S(2)}) copy-start(f32[64,128]{1,0:T(8,128)} %get-tuple-element.52.refs_1_) | copy-start | bytes 98308
  (6 other events, 24.7 us)

commit v5 on v4

--- a/solution.py
+++ b/solution.py
@@ -71,11 +71,11 @@
 
 
 def far_tiles(panels, both_t, before):
-    depth = both_t.shape[1]
     tall = panels[0].shape[0]
+    depth = tall - before.shape[0]
     joined = jnp.concatenate([p[:depth, :] for p in panels], axis=1)
     border = jnp.concatenate([p[depth:tall, :] for p in panels], axis=1)
-    tile = dot(both_t[...], joined).T
+    tile = dot(both_t[:, both_t.shape[1] - depth :], joined).T
     return tile, before[...] + border_times(border, tile)
 
 
@@ -220,19 +220,28 @@
     second = lax.ppermute(other, "space", around)
     own, both_t, total = pl.pallas_call(
         own_kernel,
-        out_shape=tuple(map(jax.ShapeDtypeStruct, ((both, width), (both, depth), (arrow, both)), (f32, bf16, f32))),
+        out_shape=(
+            jax.ShapeDtypeStruct((both, width), f32),
+            pltpu.VMEM((both, depth), bf16),
+            pltpu.VMEM((arrow, both), f32),
+        ),
+        in_specs=[VMEM] * 4,
+        out_specs=(VMEM,) * 3,
         name="own",
-    )(mine, other, top, other_top)
+    )(*map(near, (mine, other, top, other_top)))
     kept, given = [], []
     second, total = lax.optimization_barrier((second, total))
     for s in range(hops - 1):
-        next_first = lax.ppermute(first, "space", around)
-        next_second = lax.ppermute(second, "space", around) if s < hops - 2 else None
+        skip = cut * (s + 2) - (order + arrow - first.shape[0]) if s > 0 else 0
+        next_first = lax.ppermute(first[skip:], "space", around)
+        next_second = lax.ppermute(second[skip:], "space", around) if s < hops - 2 else None
         keep, give, total = pl.pallas_call(
             far_kernel,
-            out_shape=[jax.ShapeDtypeStruct(shape, f32) for shape in ((both, width), (both, width), (arrow, both))],
+            out_shape=(*[jax.ShapeDtypeStruct((both, width), f32)] * 2, pltpu.VMEM((arrow, both), f32)),
+            in_specs=[VMEM] * 4,
+            out_specs=(VMEM,) * 3,
             name="far",
-        )(first, second, both_t, total)
+        )(*map(near, (first, second, both_t, total)))
         kept.append(keep)
         given.append(lax.ppermute(give, "space", swapped))
         first, second = next_first, next_second
@@ -248,7 +257,6 @@
     row_parts = jnp.pad(row_parts, ((0, 0), (0, width - 2 * rows)))
     col_parts = jnp.pad(jnp.concatenate(two_parts(by_col), axis=0), ((5, PAD - 7), (0, 0)))
     message = ((pieces, rows + PAD, width), f32)
-    pairs = [*kept[:-1], near(kept[-1]), *given[:-1], near(given[-1])]
     sent, plain, own_arrow = pl.pallas_call(
         lambda *refs: message_kernel(rows, chips, hops, *refs),
         out_shape=(
@@ -260,7 +268,7 @@
         out_specs=(VMEM, pl.BlockSpec(memory_space=pl.ANY), VMEM),
         scratch_shapes=[pltpu.VMEM((pieces, rows, width), f32), pltpu.SemaphoreType.DMA],
         name="message",
-    )(column_at.reshape(1), own, *pairs, near(tip_inverse.T), near(row_parts), near(col_parts))
+    )(column_at.reshape(1), *map(near, (own, *kept, *given, tip_inverse.T, row_parts, col_parts)))
 
     def exchange(values):
         moved = lax.all_to_all(values.astype(jnp.float16), "tm", 0, 0, tiled=True)

time: 129 us -> 132 us (1.023)
  local copies, waits for them, and re-layouts: 2.96 us -> 16.1 us
  waiting for transfers between devices: 47.6 us -> 39.9 us
  Pallas kernels: 18.5 us -> 15.2 us
    unnamed x32 -> x40, local copies, waits for them, and re-layouts: 2.11 us -> 11 us
    ppermute x1, waiting for transfers between devices: 7.46 us -> 2.65 us  [body(): first = lax.ppermute(mine, 'space', around)]
    slice x0 -> x3, local copies, waits for them, and re-layouts: none -> 4.22 us  [the longest x2 2.46 us: body(): next_first = lax.ppermute(first[skip:], 'space', around)]
    all_to_all x2, starting transfers between devices: 16.4 us -> 19.2 us  [exchange(): moved = lax.all_to_all(values.astype(jnp.float16), 'tm', 0, 0, tiled=True)]
    ppermute x4, starting transfers between devices: 10.9 us -> 8.64 us  [body(): given.append(lax.ppermute(give, 'space', swapped))]
    pallas_call x4, Pallas kernels: 11.1 us -> 9.14 us  [the longest x3 6.99 us: body(): pl.pallas_call(far_kernel, out_shape=(*[jax.ShapeDtypeStruct((both, width...]
    ppermute x1, starting transfers between devices: 3.27 us -> 4.81 us  [body(): other_top = lax.ppermute(top, 'space', swapped)]
  transfers between devices with their start and end apart: 15 -> 15, of which waited for: 6 -> 5; matrix products, arithmetic and copies ran while one was open for 2% -> 5% of each run, Pallas kernels for 9% -> 7%
where the time goes in v5:
time: 132 us; the launch traced here: 130 us
  starting transfers between devices  54.4 us (41%)
  waiting for transfers between devices  39.9 us (30%)
  local copies, waits for them, and re-layouts  16.1 us (12%)
  Pallas kernels  15.2 us (12%)
  other arithmetic  3.89 us (3%)
    all_to_all x2, waiting for transfers between devices, exchange(): moved = lax.all_to_all(values.astype(jnp.float16), 'tm', 0, 0, tiled=True)  35.7 us
    all_to_all x2, starting transfers between devices, exchange(): moved = lax.all_to_all(values.astype(jnp.float16), 'tm', 0, 0, tiled=True)  19.2 us
    unnamed x40, local copies, waits for them, and re-layouts  11 us
    ppermute x3, starting transfers between devices, body(): next_first = lax.ppermute(first[skip:], 'space', around)  8.95 us
    ppermute x4, starting transfers between devices, body(): given.append(lax.ppermute(give, 'space', swapped))  8.64 us
    pallas_call x3, Pallas kernels, body(): pl.pallas_call(far_kernel, out_shape=(*[jax.ShapeDtypeStruct((both, width...  6.99 us
    ppermute x1, starting transfers between devices, body(): other_top = lax.ppermute(top, 'space', swapped)  4.81 us
    ppermute x2, starting transfers between devices, body(): lax.ppermute(second[skip:], 'space', around)  3.9 us
  transfers between devices with their start and end apart: 15, of which 5 were waited for; matrix products, arithmetic and copies ran while one was open for 5% of the time, Pallas kernels for 7%

profile of v5, /device:TPU:8, one launch (start us, length us, event | category | flops | bytes accessed | tf_op | source)
XLA Modules:
  0.0 130.5 jit_solution(7096142398397100185)
XLA Ops:
  1.8 1.9 %collective-permute-start = (bf16[1856,128]{1,0:T(8,128)(2,1)S(1)}, bf16[1856,128]{1,0:T(8,128)(2,1)}, u32[]{:S(2)}, u32[]{:S(2)}) collective-permute-start(bf16[1856,128]{1,0:T(8,128)(2,1)S(1)} %get-tuple-element.29.mine), channel_id=1, source_target_pairs={{0,1},{1,0},{2,3},{3,2},{4,5},{5,4},{6,7},{7,6},{8,9},{9,8},{10,11... | collective-permute-start | bytes 1425416 | tf_op jit(solution)/shard_map/ppermute | solution.py:218
  3.7 3.5 %collective-permute-start.2 = (bf16[1856,128]{1,0:T(8,128)(2,1)S(1)}, bf16[1856,128]{1,0:T(8,128)(2,1)}, u32[]{:S(2)}, u32[]{:S(2)}) collective-permute-start(bf16[1856,128]{1,0:T(8,128)(2,1)S(1)} %get-tuple-element.29.mine), channel_id=1, source_target_pairs={{0,2},{1,15},{2,4},{3,1},{4,6},{5,3},{6,8},{7,5},{8,10},{9,7},{10,... | collective-permute-start | bytes 1425416 | tf_op jit(solution)/shard_map/ppermute | solution.py:217
  7.2 3.5 %collective-permute-start.3 = (bf16[1856,128]{1,0:T(8,128)(2,1)}, bf16[1856,128]{1,0:T(8,128)(2,1)}, u32[]{:S(2)}, u32[]{:S(2)}) collective-permute-start(bf16[1856,128]{1,0:T(8,128)(2,1)} %collective-permute-done.other), channel_id=1, source_target_pairs={{0,2},{1,15},{2,4},{3,1},{4,6},{5,3},{6,8},{7,5},{8,10},{9,7},{10,... | collective-permute-start | bytes 1425416 | tf_op jit(solution)/shard_map/ppermute | solution.py:220
  10.7 4.8 %collective-permute-start.1 = (bf16[256,128]{1,0:T(8,128)(2,1)S(1)}, bf16[256,128]{1,0:T(8,128)(2,1)S(1)}, u32[]{:S(2)}, u32[]{:S(2)}) collective-permute-start(bf16[256,128]{1,0:T(8,128)(2,1)S(1)} %get-tuple-element.30.mine_top), channel_id=1, source_target_pairs={{0,1},{1,0},{2,3},{3,2},{4,5},{5,4},{6,7},{7,6},{8,9},{9,8},{10,11... | collective-permute-start | bytes 196616 | tf_op jit(solution)/shard_map/ppermute | solution.py:219
  15.6 2.6 %collective-permute-done.2.first = bf16[1856,128]{1,0:T(8,128)(2,1)} collective-permute-done((bf16[1856,128]{1,0:T(8,128)(2,1)S(1)}, bf16[1856,128]{1,0:T(8,128)(2,1)}, u32[]{:S(2)}, u32[]{:S(2)}) %collective-permute-start.2) | collective-permute-done | bytes 475168 | tf_op jit(solution)/shard_map/ppermute | solution.py:217
  18.2 1.9 %collective-permute-start.4 = (bf16[1856,128]{1,0:T(8,128)(2,1)}, bf16[1856,128]{1,0:T(8,128)(2,1)}, u32[]{:S(2)}, u32[]{:S(2)}) collective-permute-start(bf16[1856,128]{1,0:T(8,128)(2,1)} %collective-permute-done.2.first), channel_id=1, source_target_pairs={{0,2},{1,15},{2,4},{3,1},{4,6},{5,3},{6,8},{7,5},{8,10},{9,7},{10,... | collective-permute-start | bytes 1425416 | tf_op jit(solution)/shard_map/ppermute | solution.py:236
  20.1 2.1 %own.1 = (f32[256,128]{1,0:T(8,128)}, bf16[256,1792]{1,0:T(8,128)(2,1)S(1)}, f32[64,256]{1,0:T(8,128)S(1)}) custom-call(bf16[1856,128]{1,0:T(8,128)(2,1)S(1)} %get-tuple-element.29.mine, bf16[1856,128]{1,0:T(8,128)(2,1)} %collective-permute-done.other, bf16[256,128]{1,0:T(8,128)(2,1)S(1)} %get-tuple-element.30.mine_top, ...), custom_call_target="tpu_custom_call" | custom-call | tf_op jit(solution)/shard_map/own/pallas_call | solution.py:221
  23.3 1.9 %collective-permute-start.5 = (bf16[1856,128]{1,0:T(8,128)(2,1)}, bf16[1856,128]{1,0:T(8,128)(2,1)}, u32[]{:S(2)}, u32[]{:S(2)}) collective-permute-start(bf16[1856,128]{1,0:T(8,128)(2,1)} %collective-permute-done.3.second), channel_id=1, source_target_pairs={{0,2},{1,15},{2,4},{3,1},{4,6},{5,3},{6,8},{7,5},{8,10},{9,7},{10,... | collective-permute-start | bytes 1425416 | tf_op jit(solution)/shard_map/ppermute | solution.py:237
  26.4 2.4 %far.3 = (f32[256,128]{1,0:T(8,128)}, f32[256,128]{1,0:T(8,128)}, f32[64,256]{1,0:T(8,128)S(1)}) custom-call(bf16[1856,128]{1,0:T(8,128)(2,1)} %collective-permute-done.2.first, bf16[1856,128]{1,0:T(8,128)(2,1)} %collective-permute-done.3.second, bf16[256,1792]{1,0:T(8,128)(2,1)S(1)} %copy-done.2, f32[64,256]{1,0:T(8,128)S(1)} %get-tuple-element.35.before), custom_call_target="tpu_custom_call" | custom-call | tf_op jit(solution)/shard_map/far/pallas_call | solution.py:238
  30.3 1.7 %slice.9 = bf16[1344,128]{1,0:T(8,128)(2,1)} slice(bf16[1856,128]{1,0:T(8,128)(2,1)} %collective-permute-done.4.first), slice={[512:1856], [0:128]} | slice | bytes 688128 | tf_op jit(solution)/shard_map/slice | solution.py:236
  32.0 3.7 %collective-permute-start.6 = (bf16[1344,128]{1,0:T(8,128)(2,1)}, bf16[1344,128]{1,0:T(8,128)(2,1)S(1)}, u32[]{:S(2)}, u32[]{:S(2)}) collective-permute-start(bf16[1344,128]{1,0:T(8,128)(2,1)} %slice.9), channel_id=1, source_target_pairs={{0,2},{1,15},{2,4},{3,1},{4,6},{5,3},{6,8},{7,5},{8,10},{9,7},{10,... | collective-permute-start | bytes 1032200 | tf_op jit(solution)/shard_map/ppermute | solution.py:236
  37.0 1.8 %slice.12 = bf16[1344,128]{1,0:T(8,128)(2,1)} slice(bf16[1856,128]{1,0:T(8,128)(2,1)} %collective-permute-done.5.second), slice={[512:1856], [0:128]} | slice | bytes 688128 | tf_op jit(solution)/shard_map/slice | solution.py:237
  38.7 2.0 %collective-permute-start.7 = (bf16[1344,128]{1,0:T(8,128)(2,1)}, bf16[1344,128]{1,0:T(8,128)(2,1)}, u32[]{:S(2)}, u32[]{:S(2)}) collective-permute-start(bf16[1344,128]{1,0:T(8,128)(2,1)} %slice.12), channel_id=1, source_target_pairs={{0,2},{1,15},{2,4},{3,1},{4,6},{5,3},{6,8},{7,5},{8,10},{9,7},{10,... | collective-permute-start | bytes 1032200 | tf_op jit(solution)/shard_map/ppermute | solution.py:237
  40.8 2.4 %far.4 = (f32[256,128]{1,0:T(8,128)}, f32[256,128]{1,0:T(8,128)}, f32[64,256]{1,0:T(8,128)S(1)}) custom-call(bf16[1856,128]{1,0:T(8,128)(2,1)} %collective-permute-done.4.first, bf16[1856,128]{1,0:T(8,128)(2,1)} %collective-permute-done.5.second, bf16[256,1792]{1,0:T(8,128)(2,1)S(1)} %copy-done.2, f32[64,256]{1,0:T(8,128)S(1)} %get-tuple-element.39.before), custom_call_target="tpu_custom_call" | custom-call | tf_op jit(solution)/shard_map/far/pallas_call | solution.py:238
  43.9 3.3 %collective-permute-start.8 = (bf16[1088,128]{1,0:T(8,128)(2,1)}, bf16[1088,128]{1,0:T(8,128)(2,1)S(1)}, u32[]{:S(2)}, u32[]{:S(2)}) collective-permute-start(bf16[1088,128]{1,0:T(8,128)(2,1)} %slice.11), channel_id=1, source_target_pairs={{0,2},{1,15},{2,4},{3,1},{4,6},{5,3},{6,8},{7,5},{8,10},{9,7},{10,... | collective-permute-start | bytes 835592 | tf_op jit(solution)/shard_map/ppermute | solution.py:236
  47.3 1.9 %collective-permute-start.9 = (f32[256,128]{1,0:T(8,128)}, f32[256,128]{1,0:T(8,128)S(1)}, u32[]{:S(2)}, u32[]{:S(2)}) collective-permute-start(f32[256,128]{1,0:T(8,128)} %get-tuple-element.47), channel_id=1, source_target_pairs={{0,1},{1,0},{2,3},{3,2},{4,5},{5,4},{6,7},{7,6},{8,9},{9,8},{10,11... | collective-permute-start | bytes 393224 | tf_op jit(solution)/shard_map/ppermute | solution.py:246
  49.2 2.4 %collective-permute-start.10 = (f32[256,128]{1,0:T(8,128)}, f32[256,128]{1,0:T(8,128)S(1)}, u32[]{:S(2)}, u32[]{:S(2)}) collective-permute-start(f32[256,128]{1,0:T(8,128)} %get-tuple-element.48), channel_id=1, source_target_pairs={{0,1},{1,0},{2,3},{3,2},{4,5},{5,4},{6,7},{7,6},{8,9},{9,8},{10,11... | collective-permute-start | bytes 393224 | tf_op jit(solution)/shard_map/ppermute | solution.py:246
  51.6 2.1 %far.5 = (f32[256,128]{1,0:T(8,128)}, f32[256,128]{1,0:T(8,128)}, f32[64,256]{1,0:T(8,128)S(1)}) custom-call(bf16[1344,128]{1,0:T(8,128)(2,1)S(1)} %collective-permute-done.6.first, bf16[1344,128]{1,0:T(8,128)(2,1)} %collective-permute-done.7.second, bf16[256,1792]{1,0:T(8,128)(2,1)S(1)} %copy-done.2, f32[64,256]{1,0:T(8,128)S(1)} %get-tuple-element.43.before), custom_call_target="tpu_custom_call" | custom-call | tf_op jit(solution)/shard_map/far/pallas_call | solution.py:238
  53.8 1.9 %collective-permute-start.11 = (f32[256,128]{1,0:T(8,128)}, f32[256,128]{1,0:T(8,128)S(1)}, u32[]{:S(2)}, u32[]{:S(2)}) collective-permute-start(f32[256,128]{1,0:T(8,128)} %get-tuple-element.49), channel_id=1, source_target_pairs={{0,1},{1,0},{2,3},{3,2},{4,5},{5,4},{6,7},{7,6},{8,9},{9,8},{10,11... | collective-permute-start | bytes 393224 | tf_op jit(solution)/shard_map/ppermute | solution.py:246
  56.4 2.4 %collective-permute-start.12 = (f32[192,128]{1,0:T(8,128)S(1)}, f32[192,128]{1,0:T(8,128)S(1)}, u32[]{:S(2)}, u32[]{:S(2)}) collective-permute-start(f32[192,128]{1,0:T(8,128)S(1)} %get-tuple-element.50), channel_id=1, source_target_pairs={{0,1},{1,0},{2,3},{3,2},{4,5},{5,4},{6,7},{7,6},{8,9},{9,8},{10,11... | collective-permute-start | bytes 294920 | tf_op jit(solution)/shard_map/ppermute | solution.py:252
  69.8 13.2 %all-to-all-start = ((f16[32,72,128]{2,1,0:T(8,128)(2,1)}), f16[32,72,128]{2,1,0:T(8,128)(2,1)S(1)}, u32[]{:S(2)}, u32[]{:S(2)}) async-start(f16[32,72,128]{2,1,0:T(8,128)(2,1)} %convert_element_type.16), calls=%async_computation | async-start | bytes 1179648 | tf_op jit(solution)/shard_map/all_to_all | solution.py:274
  83.8 17.2 %all-to-all-done = f16[32,72,128]{2,1,0:T(8,128)(2,1)S(1)} async-done(((f16[32,72,128]{2,1,0:T(8,128)(2,1)}), f16[32,72,128]{2,1,0:T(8,128)(2,1)S(1)}, u32[]{:S(2)}, u32[]{:S(2)}) %all-to-all-start) | async-done | bytes 589856 | tf_op jit(solution)/shard_map/all_to_all | solution.py:274
  103.1 6.1 %all-to-all-start.1 = ((f16[32,72,128]{2,1,0:T(8,128)(2,1)}), f16[32,72,128]{2,1,0:T(8,128)(2,1)}, u32[]{:S(2)}, u32[]{:S(2)}) async-start(f16[32,72,128]{2,1,0:T(8,128)(2,1)} %convert_element_type.18), calls=%async_computation.1 | async-start | bytes 1179648 | tf_op jit(solution)/shard_map/all_to_all | solution.py:274
  109.2 18.5 %all-to-all-done.1 = f16[32,72,128]{2,1,0:T(8,128)(2,1)} async-done(((f16[32,72,128]{2,1,0:T(8,128)(2,1)}), f16[32,72,128]{2,1,0:T(8,128)(2,1)}, u32[]{:S(2)}, u32[]{:S(2)}) %all-to-all-start.1) | async-done | bytes 589856 | tf_op jit(solution)/shard_map/all_to_all | solution.py:274
  (75 shorter events, 24.1 us)
Async XLA Ops:
  0.6 83.1 %copy-start = (f32[2048,128]{1,0:T(8,128)S(1)}, f32[2048,128]{1,0:T(8,128)}, u32[]{:S(2)}) copy-start(f32[2048,128]{1,0:T(8,128)} %param.10) | copy-start | bytes 3145732
  1.8 5.4 %collective-permute-start = (bf16[1856,128]{1,0:T(8,128)(2,1)S(1)}, bf16[1856,128]{1,0:T(8,128)(2,1)}, u32[]{:S(2)}, u32[]{:S(2)}) collective-permute-start(bf16[1856,128]{1,0:T(8,128)(2,1)S(1)} %get-tuple-element.29.mine), channel_id=1, source_target_pairs={{0,1},{1,0},{2,3},{3,2},{4,5},{5,4},{6,7},{7,6},{8,9},{9,8},{10,11... | collective-permute-start | bytes 1425416 | tf_op jit(solution)/shard_map/ppermute | solution.py:218
  3.7 14.5 %collective-permute-start.2 = (bf16[1856,128]{1,0:T(8,128)(2,1)S(1)}, bf16[1856,128]{1,0:T(8,128)(2,1)}, u32[]{:S(2)}, u32[]{:S(2)}) collective-permute-start(bf16[1856,128]{1,0:T(8,128)(2,1)S(1)} %get-tuple-element.29.mine), channel_id=1, source_target_pairs={{0,2},{1,15},{2,4},{3,1},{4,6},{5,3},{6,8},{7,5},{8,10},{9,7},{10,... | collective-permute-start | bytes 1425416 | tf_op jit(solution)/shard_map/ppermute | solution.py:217
  7.2 16.1 %collective-permute-start.3 = (bf16[1856,128]{1,0:T(8,128)(2,1)}, bf16[1856,128]{1,0:T(8,128)(2,1)}, u32[]{:S(2)}, u32[]{:S(2)}) collective-permute-start(bf16[1856,128]{1,0:T(8,128)(2,1)} %collective-permute-done.other), channel_id=1, source_target_pairs={{0,2},{1,15},{2,4},{3,1},{4,6},{5,3},{6,8},{7,5},{8,10},{9,7},{10,... | collective-permute-start | bytes 1425416 | tf_op jit(solution)/shard_map/ppermute | solution.py:220
  10.7 9.4 %collective-permute-start.1 = (bf16[256,128]{1,0:T(8,128)(2,1)S(1)}, bf16[256,128]{1,0:T(8,128)(2,1)S(1)}, u32[]{:S(2)}, u32[]{:S(2)}) collective-permute-start(bf16[256,128]{1,0:T(8,128)(2,1)S(1)} %get-tuple-element.30.mine_top), channel_id=1, source_target_pairs={{0,1},{1,0},{2,3},{3,2},{4,5},{5,4},{6,7},{7,6},{8,9},{9,8},{10,11... | collective-permute-start | bytes 196616 | tf_op jit(solution)/shard_map/ppermute | solution.py:219
  18.2 12.1 %collective-permute-start.4 = (bf16[1856,128]{1,0:T(8,128)(2,1)}, bf16[1856,128]{1,0:T(8,128)(2,1)}, u32[]{:S(2)}, u32[]{:S(2)}) collective-permute-start(bf16[1856,128]{1,0:T(8,128)(2,1)} %collective-permute-done.2.first), channel_id=1, source_target_pairs={{0,2},{1,15},{2,4},{3,1},{4,6},{5,3},{6,8},{7,5},{8,10},{9,7},{10,... | collective-permute-start | bytes 1425416 | tf_op jit(solution)/shard_map/ppermute | solution.py:236
  22.3 0.9 copy-start.1
  23.3 13.7 %collective-permute-start.5 = (bf16[1856,128]{1,0:T(8,128)(2,1)}, bf16[1856,128]{1,0:T(8,128)(2,1)}, u32[]{:S(2)}, u32[]{:S(2)}) collective-permute-start(bf16[1856,128]{1,0:T(8,128)(2,1)} %collective-permute-done.3.second), channel_id=1, source_target_pairs={{0,2},{1,15},{2,4},{3,1},{4,6},{5,3},{6,8},{7,5},{8,10},{9,7},{10,... | collective-permute-start | bytes 1425416 | tf_op jit(solution)/shard_map/ppermute | solution.py:237
  25.2 1.2 copy-start.2
  26.4 9.8 %copy-start.18 = (f32[1,2048]{1,0:T(1,128)S(1)}, f32[1,2048]{1,0:T(1,128)}, u32[]{:S(2)}) copy-start(f32[1,2048]{1,0:T(1,128)} %param.8) | copy-start | bytes 24580
  32.0 11.2 %collective-permute-start.6 = (bf16[1344,128]{1,0:T(8,128)(2,1)}, bf16[1344,128]{1,0:T(8,128)(2,1)S(1)}, u32[]{:S(2)}, u32[]{:S(2)}) collective-permute-start(bf16[1344,128]{1,0:T(8,128)(2,1)} %slice.9), channel_id=1, source_target_pairs={{0,2},{1,15},{2,4},{3,1},{4,6},{5,3},{6,8},{7,5},{8,10},{9,7},{10,... | collective-permute-start | bytes 1032200 | tf_op jit(solution)/shard_map/ppermute | solution.py:236
  37.0 6.2 %copy-start.15 = (f32[32,64]{1,0:T(8,128)}, f32[32,64]{1,0:T(8,128)S(1)}, u32[]{:S(2)}) copy-start(f32[32,64]{1,0:T(8,128)S(1)} %reshape_squeeze.3) | copy-start | bytes 24580
  38.7 12.9 %collective-permute-start.7 = (bf16[1344,128]{1,0:T(8,128)(2,1)}, bf16[1344,128]{1,0:T(8,128)(2,1)}, u32[]{:S(2)}, u32[]{:S(2)}) collective-permute-start(bf16[1344,128]{1,0:T(8,128)(2,1)} %slice.12), channel_id=1, source_target_pairs={{0,2},{1,15},{2,4},{3,1},{4,6},{5,3},{6,8},{7,5},{8,10},{9,7},{10,... | collective-permute-start | bytes 1032200 | tf_op jit(solution)/shard_map/ppermute | solution.py:237
  43.2 12.6 %copy-start.17 = (f32[64,64]{1,0:T(8,128)S(1)}, f32[64,64]{1,0:T(8,128)}, u32[]{:S(2)}) copy-start(f32[64,64]{1,0:T(8,128)} %param.9) | copy-start | bytes 49156
  43.9 11.9 %collective-permute-start.8 = (bf16[1088,128]{1,0:T(8,128)(2,1)}, bf16[1088,128]{1,0:T(8,128)(2,1)S(1)}, u32[]{:S(2)}, u32[]{:S(2)}) collective-permute-start(bf16[1088,128]{1,0:T(8,128)(2,1)} %slice.11), channel_id=1, source_target_pairs={{0,2},{1,15},{2,4},{3,1},{4,6},{5,3},{6,8},{7,5},{8,10},{9,7},{10,... | collective-permute-start | bytes 835592 | tf_op jit(solution)/shard_map/ppermute | solution.py:236
  47.3 11.6 %collective-permute-start.9 = (f32[256,128]{1,0:T(8,128)}, f32[256,128]{1,0:T(8,128)S(1)}, u32[]{:S(2)}, u32[]{:S(2)}) collective-permute-start(f32[256,128]{1,0:T(8,128)} %get-tuple-element.47), channel_id=1, source_target_pairs={{0,1},{1,0},{2,3},{3,2},{4,5},{5,4},{6,7},{7,6},{8,9},{9,8},{10,11... | collective-permute-start | bytes 393224 | tf_op jit(solution)/shard_map/ppermute | solution.py:246
  49.2 10.3 %collective-permute-start.10 = (f32[256,128]{1,0:T(8,128)}, f32[256,128]{1,0:T(8,128)S(1)}, u32[]{:S(2)}, u32[]{:S(2)}) collective-permute-start(f32[256,128]{1,0:T(8,128)} %get-tuple-element.48), channel_id=1, source_target_pairs={{0,1},{1,0},{2,3},{3,2},{4,5},{5,4},{6,7},{7,6},{8,9},{9,8},{10,11... | collective-permute-start | bytes 393224 | tf_op jit(solution)/shard_map/ppermute | solution.py:246
  53.8 6.4 %collective-permute-start.11 = (f32[256,128]{1,0:T(8,128)}, f32[256,128]{1,0:T(8,128)S(1)}, u32[]{:S(2)}, u32[]{:S(2)}) collective-permute-start(f32[256,128]{1,0:T(8,128)} %get-tuple-element.49), channel_id=1, source_target_pairs={{0,1},{1,0},{2,3},{3,2},{4,5},{5,4},{6,7},{7,6},{8,9},{9,8},{10,11... | collective-permute-start | bytes 393224 | tf_op jit(solution)/shard_map/ppermute | solution.py:246
  56.4 3.8 %collective-permute-start.12 = (f32[192,128]{1,0:T(8,128)S(1)}, f32[192,128]{1,0:T(8,128)S(1)}, u32[]{:S(2)}, u32[]{:S(2)}) collective-permute-start(f32[192,128]{1,0:T(8,128)S(1)} %get-tuple-element.50), channel_id=1, source_target_pairs={{0,1},{1,0},{2,3},{3,2},{4,5},{5,4},{6,7},{7,6},{8,9},{9,8},{10,11... | collective-permute-start | bytes 294920 | tf_op jit(solution)/shard_map/ppermute | solution.py:252
  69.8 31.3 %all-to-all-start = ((f16[32,72,128]{2,1,0:T(8,128)(2,1)}), f16[32,72,128]{2,1,0:T(8,128)(2,1)S(1)}, u32[]{:S(2)}, u32[]{:S(2)}) async-start(f16[32,72,128]{2,1,0:T(8,128)(2,1)} %convert_element_type.16), calls=%async_computation | async-start | bytes 1179648 | tf_op jit(solution)/shard_map/all_to_all | solution.py:274
  102.2 7.0 %copy-start.16 = (f32[32,64]{1,0:T(8,128)S(1)}, f32[32,64]{1,0:T(8,128)}, u32[]{:S(2)}) copy-start(f32[32,64]{1,0:T(8,128)} %copy-done.15) | copy-start | bytes 24580
  103.1 24.6 %all-to-all-start.1 = ((f16[32,72,128]{2,1,0:T(8,128)(2,1)}), f16[32,72,128]{2,1,0:T(8,128)(2,1)}, u32[]{:S(2)}, u32[]{:S(2)}) async-start(f16[32,72,128]{2,1,0:T(8,128)(2,1)} %convert_element_type.18), calls=%async_computation.1 | async-start | bytes 1179648 | tf_op jit(solution)/shard_map/all_to_all | solution.py:274
  109.2 19.6 %copy-start.3 = (f32[32,64,128]{2,1,0:T(8,128)S(1)}, f32[32,64,128]{2,1,0:T(8,128)}, u32[]{:S(2)}) copy-start(f32[32,64,128]{2,1,0:T(8,128)} %get-tuple-element.51.refs_0_) | copy-start | bytes 3145732
  109.2 19.6 %copy-start.14 = (f32[64,128]{1,0:T(8,128)S(1)}, f32[64,128]{1,0:T(8,128)}, u32[]{:S(2)}) copy-start(f32[64,128]{1,0:T(8,128)} %get-tuple-element.52.refs_1_) | copy-start | bytes 98308
  (10 other events, 8.3 us)

commit v6 on v5

--- a/solution.py
+++ b/solution.py
@@ -58,42 +58,39 @@
     return panel, jnp.where(at < 2, rooted(tail, tail[3:4, :]), 0.0)
 
 
-def own_kernel(mine, other, mine_top, other_top, tile, both_t, total):
-    tall = mine.shape[0]
+def own_kernel(mine, other, mine_top, other_top, tile, both_t, token):
+    tall, width = mine.shape
     depth = both_t.shape[1]
     turned = jnp.concatenate([mine[:depth, :].T, other[:depth, :].T], axis=0)
     top = jnp.concatenate([mine_top[...].T, other_top[...].T], axis=0)
     both_t[...] = turned
     got = dot(turned, mine[:depth, :]) + dot(top, mine_top[...])
-    tile[...] = got
     border = jnp.concatenate([mine[depth:tall, :], other[depth:tall, :]], axis=1)
-    total[...] = jnp.concatenate([border_times(border, got), jnp.zeros(total.shape[:1] + got.shape[1:])], axis=1)
-
-
-def far_tiles(panels, both_t, before):
-    tall = panels[0].shape[0]
-    depth = tall - before.shape[0]
+    tile[: CORES * width, :] = got
+    tile[CORES * width :, :] = border_times(border, got)
+    token[...] = jnp.zeros_like(token)
+
+
+def far_tiles(panels, both_t, keep, give):
+    tall, width = panels[0].shape
+    count = width * len(panels)
+    depth = tall - (keep.shape[0] - count)
     joined = jnp.concatenate([p[:depth, :] for p in panels], axis=1)
     border = jnp.concatenate([p[depth:tall, :] for p in panels], axis=1)
     tile = dot(both_t[:, both_t.shape[1] - depth :], joined).T
-    return tile, before[...] + border_times(border, tile)
-
-
-def far_kernel(first, second, both_t, before, keep, give, total):
-    tile, total[...] = far_tiles((first, second), both_t, before)
-    width = keep.shape[1]
-    keep[...] = tile[:, :width]
-    give[...] = tile[:, width:]
-
-
-def farthest_kernel(first, both_t, before, keep, give):
-    tile, total = far_tiles((first,), both_t, before)
-    width = keep.shape[1]
-    count = tile.shape[0]
-    keep[:count, :] = tile[:, :width]
-    keep[count:, :] = total[:, :width]
-    give[:count, :] = tile[:, width:]
-    give[count:, :] = total[:, width:]
+    total = border_times(border, tile)
+    for at, part in ((0, keep), (width, give)):
+        part[:count, :] = tile[:, at : at + width]
+        part[count:, :] = total[:, at : at + width]
+
+
+def far_kernel(first, second, both_t, passed, keep, give, token):
+    far_tiles((first, second), both_t, keep, give)
+    token[...] = passed[...]
+
+
+def farthest_kernel(first, both_t, passed, keep, give):
+    far_tiles((first,), both_t, keep, give)
 
 
 def message_kernel(rows, chips, hops, at, own, *refs):
@@ -109,17 +106,20 @@
         plain[pl.ds(spot * per, per), :, :] = block.reshape(per, rows, width)
 
     put(own[:width, :], 0, core)
-    put(own[width:, :], 0, 1 - core)
+    put(own[width : CORES * width, :], 0, 1 - core)
     for s in range(hops):
         hop = (s + 1) * way
         put(kept[s][:width, :], -hop, core)
         put(given[s][:width, :], hop, 1 - core)
         if s < hops - 1:
-            put(kept[s][width:, :], -hop, 1 - core)
-            put(given[s][width:, :], hop, core)
+            put(kept[s][width : 2 * width, :], -hop, 1 - core)
+            put(given[s][width : 2 * width, :], hop, core)
     copy = pltpu.make_async_copy(plain, copied, done)
     copy.start()
-    total = kept[-1][width:, :] + given[-1][width:, :]
+    border = own_arrow.shape[0]
+    total = own[CORES * width :, :]
+    for part in (*kept, *given):
+        total = total + part[part.shape[0] - border :, :]
     arrow = -jnp.dot(tip_t[...], total, precision=lax.Precision.HIGHEST, preferred_element_type=jnp.float32)
     own_arrow[...] = arrow
     fill = jnp.zeros((PAD - 2, width), jnp.float32)
@@ -170,6 +170,9 @@
 SMEM = pl.BlockSpec(memory_space=pltpu.SMEM)
 
 
+SMALL = pltpu.CompilerParams(vmem_limit_bytes=12 << 20)
+
+
 def near(x):
     return pltpu.with_memory_space_constraint(x, pltpu.VMEM)
 
@@ -181,6 +184,7 @@
         in_specs=[VMEM] * len(operands),
         out_specs=(VMEM,) * len(results),
         scratch_shapes=scratch,
+        compiler_params=SMALL,
         name=name,
     )(*map(near, operands))
 
@@ -212,42 +216,46 @@
         out_shape=(pltpu.VMEM((tall, width), bf16), pltpu.VMEM((cut, width), bf16)),
         in_specs=[VMEM, VMEM],
         out_specs=(VMEM, VMEM),
+        compiler_params=SMALL,
         name="pack",
     )(factor_cols, arrow_factor[0])
     first = lax.ppermute(mine, "space", around)
     other = lax.ppermute(mine, "space", swapped)
     other_top = lax.ppermute(top, "space", swapped)
     second = lax.ppermute(other, "space", around)
-    own, both_t, total = pl.pallas_call(
+    mark = jax.ShapeDtypeStruct((8, width), f32)
+    own, both_t, token = pl.pallas_call(
         own_kernel,
         out_shape=(
-            jax.ShapeDtypeStruct((both, width), f32),
+            pltpu.VMEM((both + arrow, width), f32),
             pltpu.VMEM((both, depth), bf16),
-            pltpu.VMEM((arrow, both), f32),
+            mark,
         ),
         in_specs=[VMEM] * 4,
         out_specs=(VMEM,) * 3,
+        compiler_params=SMALL,
         name="own",
     )(*map(near, (mine, other, top, other_top)))
     kept, given = [], []
-    second, total = lax.optimization_barrier((second, total))
+    second, token = lax.optimization_barrier((second, token))
     for s in range(hops - 1):
         skip = cut * (s + 2) - (order + arrow - first.shape[0]) if s > 0 else 0
         next_first = lax.ppermute(first[skip:], "space", around)
         next_second = lax.ppermute(second[skip:], "space", around) if s < hops - 2 else None
-        keep, give, total = pl.pallas_call(
+        keep, give, token = pl.pallas_call(
             far_kernel,
-            out_shape=(*[jax.ShapeDtypeStruct((both, width), f32)] * 2, pltpu.VMEM((arrow, both), f32)),
+            out_shape=(*[pltpu.VMEM((both + arrow, width), f32)] * 2, mark),
             in_specs=[VMEM] * 4,
             out_specs=(VMEM,) * 3,
+            compiler_params=SMALL,
             name="far",
-        )(*map(near, (first, second, both_t, total)))
+        )(*map(near, (first, second, both_t)), token)
         kept.append(keep)
         given.append(lax.ppermute(give, "space", swapped))
         first, second = next_first, next_second
         if s < hops - 2:
-            first, total = lax.optimization_barrier((first, total))
-    keep, give = held(farthest_kernel, "farthest", (((width + arrow, width), f32),) * 2, first, both_t, total)
+            first, token = lax.optimization_barrier((first, token))
+    keep, give = held(farthest_kernel, "farthest", (((width + arrow, width), f32),) * 2, first, both_t, token)
     kept.append(keep)
     given.append(lax.ppermute(give, "space", swapped))
 
@@ -267,6 +275,7 @@
         in_specs=[SMEM] + [VMEM] * (2 * hops + 4),
         out_specs=(VMEM, pl.BlockSpec(memory_space=pl.ANY), VMEM),
         scratch_shapes=[pltpu.VMEM((pieces, rows, width), f32), pltpu.SemaphoreType.DMA],
+        compiler_params=SMALL,
         name="message",
     )(column_at.reshape(1), *map(near, (own, *kept, *given, tip_inverse.T, row_parts, col_parts)))
 
@@ -294,6 +303,7 @@
         lambda *refs: last_kernel(rows, *refs),
         out_shape=(jax.ShapeDtypeStruct((order, width), f32), jax.ShapeDtypeStruct((arrow, width), f32)),
         in_specs=[VMEM] * len(last),
+        compiler_params=SMALL,
         name="last",
     )(*map(near, last))
     return sigma[None], arrows.T[None]

time: 132 us -> 121 us (0.917)
  local copies, waits for them, and re-layouts: 16.1 us -> 7.52 us
  waiting for transfers between devices: 39.9 us -> 45.9 us
  Pallas kernels: 15.2 us -> 10.7 us
  starting transfers between devices: 54.4 us -> 52.3 us
    unnamed x40 -> x24, local copies, waits for them, and re-layouts: 11 us -> 4.43 us
    ppermute x1, waiting for transfers between devices: 0.09 us -> 2.63 us  [body(): second = lax.ppermute(other, 'space', around)]
    ppermute x3, starting transfers between devices: 8.95 us -> 6.48 us  [body(): next_first = lax.ppermute(first[skip:], 'space', around)]
    pallas_call x4, Pallas kernels: 9.14 us -> 6.95 us  [the longest x3 6.32 us: body(): pl.pallas_call(far_kernel, out_shape=(*[pltpu.VMEM((both + arrow, width),...]
    ppermute x2, waiting for transfers between devices: 0.01 us -> 1.48 us  [body(): lax.ppermute(second[skip:], 'space', around)]
  transfers between devices with their start and end apart: 15 -> 15, of which waited for: 5 -> 8; matrix products, arithmetic and copies ran while one was open for 5% -> 4% of each run, Pallas kernels for 7% -> 6%
where the time goes in v6:
time: 121 us; the launch traced here: 120 us
  starting transfers between devices  52.3 us (43%)
  waiting for transfers between devices  45.9 us (38%)
  Pallas kernels  10.7 us (9%)
  local copies, waits for them, and re-layouts  7.52 us (6%)
  other arithmetic  2.8 us (2%)
    all_to_all x2, waiting for transfers between devices, exchange(): moved = lax.all_to_all(values.astype(jnp.float16), 'tm', 0, 0, tiled=True)  36.2 us
    all_to_all x2, starting transfers between devices, exchange(): moved = lax.all_to_all(values.astype(jnp.float16), 'tm', 0, 0, tiled=True)  19 us
    ppermute x4, starting transfers between devices, body(): given.append(lax.ppermute(give, 'space', swapped))  8.9 us
    ppermute x3, starting transfers between devices, body(): next_first = lax.ppermute(first[skip:], 'space', around)  6.48 us
    pallas_call x3, Pallas kernels, body(): pl.pallas_call(far_kernel, out_shape=(*[pltpu.VMEM((both + arrow, width),...  6.32 us
    ppermute x1, starting transfers between devices, body(): other_top = lax.ppermute(top, 'space', swapped)  4.81 us
    unnamed x24, local copies, waits for them, and re-layouts  4.43 us
    ppermute x2, starting transfers between devices, body(): lax.ppermute(second[skip:], 'space', around)  4.21 us
  transfers between devices with their start and end apart: 15, of which 8 were waited for; matrix products, arithmetic and copies ran while one was open for 4% of the time, Pallas kernels for 6%

profile of v6, /device:TPU:8, one launch (start us, length us, event | category | flops | bytes accessed | tf_op | source)
XLA Modules:
  0.0 120.2 jit_solution(3029539304901067046)
XLA Ops:
  2.5 1.9 %collective-permute-start = (bf16[1856,128]{1,0:T(8,128)(2,1)S(1)}, bf16[1856,128]{1,0:T(8,128)(2,1)S(1)}, u32[]{:S(2)}, u32[]{:S(2)}) collective-permute-start(bf16[1856,128]{1,0:T(8,128)(2,1)S(1)} %get-tuple-element.29.mine), channel_id=1, source_target_pairs={{0,1},{1,0},{2,3},{3,2},{4,5},{5,4},{6,7},{7,6},{8,9},{9,8},{10,11... | collective-permute-start | bytes 1425416 | tf_op jit(solution)/shard_map/ppermute | solution.py:223
  4.5 3.5 %collective-permute-start.2 = (bf16[1856,128]{1,0:T(8,128)(2,1)S(1)}, bf16[1856,128]{1,0:T(8,128)(2,1)S(1)}, u32[]{:S(2)}, u32[]{:S(2)}) collective-permute-start(bf16[1856,128]{1,0:T(8,128)(2,1)S(1)} %get-tuple-element.29.mine), channel_id=1, source_target_pairs={{0,2},{1,15},{2,4},{3,1},{4,6},{5,3},{6,8},{7,5},{8,10},{9,7},{10,... | collective-permute-start | bytes 1425416 | tf_op jit(solution)/shard_map/ppermute | solution.py:222
  8.0 3.5 %collective-permute-start.3 = (bf16[1856,128]{1,0:T(8,128)(2,1)S(1)}, bf16[1856,128]{1,0:T(8,128)(2,1)}, u32[]{:S(2)}, u32[]{:S(2)}) collective-permute-start(bf16[1856,128]{1,0:T(8,128)(2,1)S(1)} %collective-permute-done.other), channel_id=1, source_target_pairs={{0,2},{1,15},{2,4},{3,1},{4,6},{5,3},{6,8},{7,5},{8,10},{9,7},{10,... | collective-permute-start | bytes 1425416 | tf_op jit(solution)/shard_map/ppermute | solution.py:225
  11.5 4.8 %collective-permute-start.1 = (bf16[256,128]{1,0:T(8,128)(2,1)S(1)}, bf16[256,128]{1,0:T(8,128)(2,1)S(1)}, u32[]{:S(2)}, u32[]{:S(2)}) collective-permute-start(bf16[256,128]{1,0:T(8,128)(2,1)S(1)} %get-tuple-element.30.mine_top), channel_id=1, source_target_pairs={{0,1},{1,0},{2,3},{3,2},{4,5},{5,4},{6,7},{7,6},{8,9},{9,8},{10,11... | collective-permute-start | bytes 196616 | tf_op jit(solution)/shard_map/ppermute | solution.py:224
  16.3 2.5 %collective-permute-done.2.first = bf16[1856,128]{1,0:T(8,128)(2,1)S(1)} collective-permute-done((bf16[1856,128]{1,0:T(8,128)(2,1)S(1)}, bf16[1856,128]{1,0:T(8,128)(2,1)S(1)}, u32[]{:S(2)}, u32[]{:S(2)}) %collective-permute-start.2) | collective-permute-done | bytes 475168 | tf_op jit(solution)/shard_map/ppermute | solution.py:222
  18.8 1.9 %collective-permute-start.4 = (bf16[1856,128]{1,0:T(8,128)(2,1)S(1)}, bf16[1856,128]{1,0:T(8,128)(2,1)S(1)}, u32[]{:S(2)}, u32[]{:S(2)}) collective-permute-start(bf16[1856,128]{1,0:T(8,128)(2,1)S(1)} %collective-permute-done.2.first), channel_id=1, source_target_pairs={{0,2},{1,15},{2,4},{3,1},{4,6},{5,3},{6,8},{7,5},{8,10},{9,7},{10,... | collective-permute-start | bytes 1425416 | tf_op jit(solution)/shard_map/ppermute | solution.py:243
  21.4 2.6 %collective-permute-done.3.second = bf16[1856,128]{1,0:T(8,128)(2,1)} collective-permute-done((bf16[1856,128]{1,0:T(8,128)(2,1)S(1)}, bf16[1856,128]{1,0:T(8,128)(2,1)}, u32[]{:S(2)}, u32[]{:S(2)}) %collective-permute-start.3) | collective-permute-done | bytes 475168 | tf_op jit(solution)/shard_map/ppermute | solution.py:225
  24.0 1.9 %collective-permute-start.5 = (bf16[1856,128]{1,0:T(8,128)(2,1)}, bf16[1856,128]{1,0:T(8,128)(2,1)S(1)}, u32[]{:S(2)}, u32[]{:S(2)}) collective-permute-start(bf16[1856,128]{1,0:T(8,128)(2,1)} %collective-permute-done.3.second), channel_id=1, source_target_pairs={{0,2},{1,15},{2,4},{3,1},{4,6},{5,3},{6,8},{7,5},{8,10},{9,7},{10,... | collective-permute-start | bytes 1425416 | tf_op jit(solution)/shard_map/ppermute | solution.py:244
  25.9 2.5 %far.3 = (f32[320,128]{1,0:T(8,128)S(1)}, f32[320,128]{1,0:T(8,128)}, f32[8,128]{1,0:T(8,128)S(1)}) custom-call(bf16[1856,128]{1,0:T(8,128)(2,1)S(1)} %collective-permute-done.2.first, bf16[1856,128]{1,0:T(8,128)(2,1)} %collective-permute-done.3.second, bf16[256,1792]{1,0:T(8,128)(2,1)S(1)} %get-tuple-element.34.both_t, f32[8,128]{1,0:T(8,128)S(1)} %get-tuple-element.35.passed), custom_call_target="tpu_custom_call" | custom-call | tf_op jit(solution)/shard_map/far/pallas_call | solution.py:245
  31.3 1.9 %collective-permute-start.6 = (bf16[1344,128]{1,0:T(8,128)(2,1)}, bf16[1344,128]{1,0:T(8,128)(2,1)S(1)}, u32[]{:S(2)}, u32[]{:S(2)}) collective-permute-start(bf16[1344,128]{1,0:T(8,128)(2,1)} %slice.9), channel_id=1, source_target_pairs={{0,2},{1,15},{2,4},{3,1},{4,6},{5,3},{6,8},{7,5},{8,10},{9,7},{10,... | collective-permute-start | bytes 1032200 | tf_op jit(solution)/shard_map/ppermute | solution.py:243
  34.5 1.5 %collective-permute-done.5.second = bf16[1856,128]{1,0:T(8,128)(2,1)S(1)} collective-permute-done((bf16[1856,128]{1,0:T(8,128)(2,1)}, bf16[1856,128]{1,0:T(8,128)(2,1)S(1)}, u32[]{:S(2)}, u32[]{:S(2)}) %collective-permute-start.5) | collective-permute-done | bytes 475168 | tf_op jit(solution)/shard_map/ppermute | solution.py:244
  36.7 2.3 %collective-permute-start.7 = (bf16[1344,128]{1,0:T(8,128)(2,1)}, bf16[1344,128]{1,0:T(8,128)(2,1)}, u32[]{:S(2)}, u32[]{:S(2)}) collective-permute-start(bf16[1344,128]{1,0:T(8,128)(2,1)} %slice.12), channel_id=1, source_target_pairs={{0,2},{1,15},{2,4},{3,1},{4,6},{5,3},{6,8},{7,5},{8,10},{9,7},{10,... | collective-permute-start | bytes 1032200 | tf_op jit(solution)/shard_map/ppermute | solution.py:244
  39.1 1.4 %far.4 = (f32[320,128]{1,0:T(8,128)S(1)}, f32[320,128]{1,0:T(8,128)}, f32[8,128]{1,0:T(8,128)S(1)}) custom-call(bf16[1856,128]{1,0:T(8,128)(2,1)S(1)} %collective-permute-done.4.first, bf16[1856,128]{1,0:T(8,128)(2,1)S(1)} %collective-permute-done.5.second, bf16[256,1792]{1,0:T(8,128)(2,1)S(1)} %get-tuple-element.34.both_t, ...), custom_call_target="tpu_custom_call" | custom-call | tf_op jit(solution)/shard_map/far/pallas_call | solution.py:245
  42.6 2.7 %collective-permute-start.8 = (bf16[1088,128]{1,0:T(8,128)(2,1)}, bf16[1088,128]{1,0:T(8,128)(2,1)S(1)}, u32[]{:S(2)}, u32[]{:S(2)}) collective-permute-start(bf16[1088,128]{1,0:T(8,128)(2,1)} %slice.11), channel_id=1, source_target_pairs={{0,2},{1,15},{2,4},{3,1},{4,6},{5,3},{6,8},{7,5},{8,10},{9,7},{10,... | collective-permute-start | bytes 835592 | tf_op jit(solution)/shard_map/ppermute | solution.py:243
  45.3 1.9 %collective-permute-start.9 = (f32[320,128]{1,0:T(8,128)}, f32[320,128]{1,0:T(8,128)S(1)}, u32[]{:S(2)}, u32[]{:S(2)}) collective-permute-start(f32[320,128]{1,0:T(8,128)} %get-tuple-element.47), channel_id=1, source_target_pairs={{0,1},{1,0},{2,3},{3,2},{4,5},{5,4},{6,7},{7,6},{8,9},{9,8},{10,11... | collective-permute-start | bytes 491528 | tf_op jit(solution)/shard_map/ppermute | solution.py:254
  47.2 2.5 %collective-permute-start.10 = (f32[320,128]{1,0:T(8,128)}, f32[320,128]{1,0:T(8,128)S(1)}, u32[]{:S(2)}, u32[]{:S(2)}) collective-permute-start(f32[320,128]{1,0:T(8,128)} %get-tuple-element.48), channel_id=1, source_target_pairs={{0,1},{1,0},{2,3},{3,2},{4,5},{5,4},{6,7},{7,6},{8,9},{9,8},{10,11... | collective-permute-start | bytes 491528 | tf_op jit(solution)/shard_map/ppermute | solution.py:254
  49.8 2.4 %far.5 = (f32[320,128]{1,0:T(8,128)S(1)}, f32[320,128]{1,0:T(8,128)}, f32[8,128]{1,0:T(8,128)S(1)}) custom-call(bf16[1344,128]{1,0:T(8,128)(2,1)S(1)} %collective-permute-done.6.first, bf16[1344,128]{1,0:T(8,128)(2,1)} %collective-permute-done.7.second, bf16[256,1792]{1,0:T(8,128)(2,1)S(1)} %get-tuple-element.34.both_t, f32[8,128]{1,0:T(8,128)S(1)} %get-tuple-element.43.passed), custom_call_target="tpu_custom_call" | custom-call | tf_op jit(solution)/shard_map/far/pallas_call | solution.py:245
  52.8 2.0 %collective-permute-start.11 = (f32[320,128]{1,0:T(8,128)}, f32[320,128]{1,0:T(8,128)S(1)}, u32[]{:S(2)}, u32[]{:S(2)}) collective-permute-start(f32[320,128]{1,0:T(8,128)} %get-tuple-element.49), channel_id=1, source_target_pairs={{0,1},{1,0},{2,3},{3,2},{4,5},{5,4},{6,7},{7,6},{8,9},{9,8},{10,11... | collective-permute-start | bytes 491528 | tf_op jit(solution)/shard_map/ppermute | solution.py:254
  55.6 2.4 %collective-permute-start.12 = (f32[192,128]{1,0:T(8,128)S(1)}, f32[192,128]{1,0:T(8,128)S(1)}, u32[]{:S(2)}, u32[]{:S(2)}) collective-permute-start(f32[192,128]{1,0:T(8,128)S(1)} %get-tuple-element.50), channel_id=1, source_target_pairs={{0,1},{1,0},{2,3},{3,2},{4,5},{5,4},{6,7},{7,6},{8,9},{9,8},{10,11... | collective-permute-start | bytes 294920 | tf_op jit(solution)/shard_map/ppermute | solution.py:260
  60.4 13.2 %all-to-all-start = ((f16[32,72,128]{2,1,0:T(8,128)(2,1)}), f16[32,72,128]{2,1,0:T(8,128)(2,1)S(1)}, u32[]{:S(2)}, u32[]{:S(2)}) async-start(f16[32,72,128]{2,1,0:T(8,128)(2,1)} %convert_element_type.16), calls=%async_computation | async-start | bytes 1179648 | tf_op jit(solution)/shard_map/all_to_all | solution.py:283
  74.4 17.7 %all-to-all-done = f16[32,72,128]{2,1,0:T(8,128)(2,1)S(1)} async-done(((f16[32,72,128]{2,1,0:T(8,128)(2,1)}), f16[32,72,128]{2,1,0:T(8,128)(2,1)S(1)}, u32[]{:S(2)}, u32[]{:S(2)}) %all-to-all-start) | async-done | bytes 589856 | tf_op jit(solution)/shard_map/all_to_all | solution.py:283
  94.2 5.8 %all-to-all-start.1 = ((f16[32,72,128]{2,1,0:T(8,128)(2,1)}), f16[32,72,128]{2,1,0:T(8,128)(2,1)S(1)}, u32[]{:S(2)}, u32[]{:S(2)}) async-start(f16[32,72,128]{2,1,0:T(8,128)(2,1)} %convert_element_type.18), calls=%async_computation.1 | async-start | bytes 1179648 | tf_op jit(solution)/shard_map/all_to_all | solution.py:283
  100.0 18.5 %all-to-all-done.1 = f16[32,72,128]{2,1,0:T(8,128)(2,1)S(1)} async-done(((f16[32,72,128]{2,1,0:T(8,128)(2,1)}), f16[32,72,128]{2,1,0:T(8,128)(2,1)S(1)}, u32[]{:S(2)}, u32[]{:S(2)}) %all-to-all-start.1) | async-done | bytes 589856 | tf_op jit(solution)/shard_map/all_to_all | solution.py:283
  118.5 1.6 %last.1 = (f32[2048,128]{1,0:T(8,128)}, f32[64,128]{1,0:T(8,128)}) custom-call(f32[32,64,128]{2,1,0:T(8,128)S(1)} %get-tuple-element.51.refs_0_, f32[64,128]{1,0:T(8,128)S(1)} %get-tuple-element.52.refs_1_, f32[32,72,128]{2,1,0:T(8,128)S(1)} %convert_element_type.19.refs_2_, f32[32,128]{1,0:T(8,128)S(1)} %pad.9.refs_3_, f32[1,128]{1,0:T(1,128)S(1)} %get-tuple-element.57.refs_4_), custom_call_target="tpu_custom_call" | custom-call | tf_op jit(solution)/shard_map/last/pallas_call | solution.py:302
  (59 shorter events, 16.1 us)
Async XLA Ops:
  0.6 73.7 %copy-start = (f32[2048,128]{1,0:T(8,128)S(1)}, f32[2048,128]{1,0:T(8,128)}, u32[]{:S(2)}) copy-start(f32[2048,128]{1,0:T(8,128)} %param.10) | copy-start | bytes 3145732
  0.6 1.1 copy-start.1
  1.8 0.7 copy-start.8
  2.5 5.4 %collective-permute-start = (bf16[1856,128]{1,0:T(8,128)(2,1)S(1)}, bf16[1856,128]{1,0:T(8,128)(2,1)S(1)}, u32[]{:S(2)}, u32[]{:S(2)}) collective-permute-start(bf16[1856,128]{1,0:T(8,128)(2,1)S(1)} %get-tuple-element.29.mine), channel_id=1, source_target_pairs={{0,1},{1,0},{2,3},{3,2},{4,5},{5,4},{6,7},{7,6},{8,9},{9,8},{10,11... | collective-permute-start | bytes 1425416 | tf_op jit(solution)/shard_map/ppermute | solution.py:223
  4.5 14.4 %collective-permute-start.2 = (bf16[1856,128]{1,0:T(8,128)(2,1)S(1)}, bf16[1856,128]{1,0:T(8,128)(2,1)S(1)}, u32[]{:S(2)}, u32[]{:S(2)}) collective-permute-start(bf16[1856,128]{1,0:T(8,128)(2,1)S(1)} %get-tuple-element.29.mine), channel_id=1, source_target_pairs={{0,2},{1,15},{2,4},{3,1},{4,6},{5,3},{6,8},{7,5},{8,10},{9,7},{10,... | collective-permute-start | bytes 1425416 | tf_op jit(solution)/shard_map/ppermute | solution.py:222
  8.0 16.1 %collective-permute-start.3 = (bf16[1856,128]{1,0:T(8,128)(2,1)S(1)}, bf16[1856,128]{1,0:T(8,128)(2,1)}, u32[]{:S(2)}, u32[]{:S(2)}) collective-permute-start(bf16[1856,128]{1,0:T(8,128)(2,1)S(1)} %collective-permute-done.other), channel_id=1, source_target_pairs={{0,2},{1,15},{2,4},{3,1},{4,6},{5,3},{6,8},{7,5},{8,10},{9,7},{10,... | collective-permute-start | bytes 1425416 | tf_op jit(solution)/shard_map/ppermute | solution.py:225
  11.5 9.3 %collective-permute-start.1 = (bf16[256,128]{1,0:T(8,128)(2,1)S(1)}, bf16[256,128]{1,0:T(8,128)(2,1)S(1)}, u32[]{:S(2)}, u32[]{:S(2)}) collective-permute-start(bf16[256,128]{1,0:T(8,128)(2,1)S(1)} %get-tuple-element.30.mine_top), channel_id=1, source_target_pairs={{0,1},{1,0},{2,3},{3,2},{4,5},{5,4},{6,7},{7,6},{8,9},{9,8},{10,11... | collective-permute-start | bytes 196616 | tf_op jit(solution)/shard_map/ppermute | solution.py:224
  18.8 11.7 %collective-permute-start.4 = (bf16[1856,128]{1,0:T(8,128)(2,1)S(1)}, bf16[1856,128]{1,0:T(8,128)(2,1)S(1)}, u32[]{:S(2)}, u32[]{:S(2)}) collective-permute-start(bf16[1856,128]{1,0:T(8,128)(2,1)S(1)} %collective-permute-done.2.first), channel_id=1, source_target_pairs={{0,2},{1,15},{2,4},{3,1},{4,6},{5,3},{6,8},{7,5},{8,10},{9,7},{10,... | collective-permute-start | bytes 1425416 | tf_op jit(solution)/shard_map/ppermute | solution.py:243
  24.0 12.0 %collective-permute-start.5 = (bf16[1856,128]{1,0:T(8,128)(2,1)}, bf16[1856,128]{1,0:T(8,128)(2,1)S(1)}, u32[]{:S(2)}, u32[]{:S(2)}) collective-permute-start(bf16[1856,128]{1,0:T(8,128)(2,1)} %collective-permute-done.3.second), channel_id=1, source_target_pairs={{0,2},{1,15},{2,4},{3,1},{4,6},{5,3},{6,8},{7,5},{8,10},{9,7},{10,... | collective-permute-start | bytes 1425416 | tf_op jit(solution)/shard_map/ppermute | solution.py:244
  25.9 7.8 %copy-start.10 = (f32[1,2048]{1,0:T(1,128)S(1)}, f32[1,2048]{1,0:T(1,128)}, u32[]{:S(2)}) copy-start(f32[1,2048]{1,0:T(1,128)} %param.8) | copy-start | bytes 24580
  28.5 0.7 copy-start.2
  31.3 10.6 %collective-permute-start.6 = (bf16[1344,128]{1,0:T(8,128)(2,1)}, bf16[1344,128]{1,0:T(8,128)(2,1)S(1)}, u32[]{:S(2)}, u32[]{:S(2)}) collective-permute-start(bf16[1344,128]{1,0:T(8,128)(2,1)} %slice.9), channel_id=1, source_target_pairs={{0,2},{1,15},{2,4},{3,1},{4,6},{5,3},{6,8},{7,5},{8,10},{9,7},{10,... | collective-permute-start | bytes 1032200 | tf_op jit(solution)/shard_map/ppermute | solution.py:243
  36.7 13.0 %collective-permute-start.7 = (bf16[1344,128]{1,0:T(8,128)(2,1)}, bf16[1344,128]{1,0:T(8,128)(2,1)}, u32[]{:S(2)}, u32[]{:S(2)}) collective-permute-start(bf16[1344,128]{1,0:T(8,128)(2,1)} %slice.12), channel_id=1, source_target_pairs={{0,2},{1,15},{2,4},{3,1},{4,6},{5,3},{6,8},{7,5},{8,10},{9,7},{10,... | collective-permute-start | bytes 1032200 | tf_op jit(solution)/shard_map/ppermute | solution.py:244
  41.2 13.7 %copy-start.9 = (f32[64,64]{1,0:T(8,128)S(1)}, f32[64,64]{1,0:T(8,128)}, u32[]{:S(2)}) copy-start(f32[64,64]{1,0:T(8,128)} %param.9) | copy-start | bytes 49156
  42.6 12.4 %collective-permute-start.8 = (bf16[1088,128]{1,0:T(8,128)(2,1)}, bf16[1088,128]{1,0:T(8,128)(2,1)S(1)}, u32[]{:S(2)}, u32[]{:S(2)}) collective-permute-start(bf16[1088,128]{1,0:T(8,128)(2,1)} %slice.11), channel_id=1, source_target_pairs={{0,2},{1,15},{2,4},{3,1},{4,6},{5,3},{6,8},{7,5},{8,10},{9,7},{10,... | collective-permute-start | bytes 835592 | tf_op jit(solution)/shard_map/ppermute | solution.py:243
  45.3 12.7 %collective-permute-start.9 = (f32[320,128]{1,0:T(8,128)}, f32[320,128]{1,0:T(8,128)S(1)}, u32[]{:S(2)}, u32[]{:S(2)}) collective-permute-start(f32[320,128]{1,0:T(8,128)} %get-tuple-element.47), channel_id=1, source_target_pairs={{0,1},{1,0},{2,3},{3,2},{4,5},{5,4},{6,7},{7,6},{8,9},{9,8},{10,11... | collective-permute-start | bytes 491528 | tf_op jit(solution)/shard_map/ppermute | solution.py:254
  47.2 11.7 %copy-start.3 = (f32[320,128]{1,0:T(8,128)S(1)}, f32[320,128]{1,0:T(8,128)}, u32[]{:S(2)}) copy-start(f32[320,128]{1,0:T(8,128)} %copy-done.2) | copy-start | bytes 491524
  47.2 11.7 %copy-start.5 = (f32[320,128]{1,0:T(8,128)S(1)}, f32[320,128]{1,0:T(8,128)}, u32[]{:S(2)}) copy-start(f32[320,128]{1,0:T(8,128)} %copy-done.4) | copy-start | bytes 491524
  47.2 10.8 %collective-permute-start.10 = (f32[320,128]{1,0:T(8,128)}, f32[320,128]{1,0:T(8,128)S(1)}, u32[]{:S(2)}, u32[]{:S(2)}) collective-permute-start(f32[320,128]{1,0:T(8,128)} %get-tuple-element.48), channel_id=1, source_target_pairs={{0,1},{1,0},{2,3},{3,2},{4,5},{5,4},{6,7},{7,6},{8,9},{9,8},{10,11... | collective-permute-start | bytes 491528 | tf_op jit(solution)/shard_map/ppermute | solution.py:254
  52.8 6.1 %copy-start.7 = (f32[320,128]{1,0:T(8,128)S(1)}, f32[320,128]{1,0:T(8,128)}, u32[]{:S(2)}) copy-start(f32[320,128]{1,0:T(8,128)} %copy-done.6) | copy-start | bytes 491524
  52.8 6.1 %collective-permute-start.11 = (f32[320,128]{1,0:T(8,128)}, f32[320,128]{1,0:T(8,128)S(1)}, u32[]{:S(2)}, u32[]{:S(2)}) collective-permute-start(f32[320,128]{1,0:T(8,128)} %get-tuple-element.49), channel_id=1, source_target_pairs={{0,1},{1,0},{2,3},{3,2},{4,5},{5,4},{6,7},{7,6},{8,9},{9,8},{10,11... | collective-permute-start | bytes 491528 | tf_op jit(solution)/shard_map/ppermute | solution.py:254
  55.6 3.3 %collective-permute-start.12 = (f32[192,128]{1,0:T(8,128)S(1)}, f32[192,128]{1,0:T(8,128)S(1)}, u32[]{:S(2)}, u32[]{:S(2)}) collective-permute-start(f32[192,128]{1,0:T(8,128)S(1)} %get-tuple-element.50), channel_id=1, source_target_pairs={{0,1},{1,0},{2,3},{3,2},{4,5},{5,4},{6,7},{7,6},{8,9},{9,8},{10,11... | collective-permute-start | bytes 294920 | tf_op jit(solution)/shard_map/ppermute | solution.py:260
  60.4 31.8 %all-to-all-start = ((f16[32,72,128]{2,1,0:T(8,128)(2,1)}), f16[32,72,128]{2,1,0:T(8,128)(2,1)S(1)}, u32[]{:S(2)}, u32[]{:S(2)}) async-start(f16[32,72,128]{2,1,0:T(8,128)(2,1)} %convert_element_type.16), calls=%async_computation | async-start | bytes 1179648 | tf_op jit(solution)/shard_map/all_to_all | solution.py:283
  94.2 24.3 %all-to-all-start.1 = ((f16[32,72,128]{2,1,0:T(8,128)(2,1)}), f16[32,72,128]{2,1,0:T(8,128)(2,1)S(1)}, u32[]{:S(2)}, u32[]{:S(2)}) async-start(f16[32,72,128]{2,1,0:T(8,128)(2,1)} %convert_element_type.18), calls=%async_computation.1 | async-start | bytes 1179648 | tf_op jit(solution)/shard_map/all_to_all | solution.py:283
  (2 other events, 1.3 us)

commit v7 on v6

--- a/solution.py
+++ b/solution.py
@@ -206,16 +206,23 @@
     tall, hops = depth + arrow, chips // 2
     f32, bf16 = jnp.float32, jnp.bfloat16
 
-    def pack_kernel(cols, border, out, top):
-        out[:depth, :] = cols[cut:, :]
-        out[depth:, :] = border[...]
-        top[...] = cols[:cut, :]
+    def pack_kernel(cols, border, out, top, done):
+        copies = [
+            pltpu.make_async_copy(cols.at[pl.ds(cut, depth)], out.at[pl.ds(0, depth)], done.at[0]),
+            pltpu.make_async_copy(border, out.at[pl.ds(depth, arrow)], done.at[1]),
+            pltpu.make_async_copy(cols.at[pl.ds(0, cut)], top, done.at[2]),
+        ]
+        for copy in copies:
+            copy.start()
+        for copy in copies:
+            copy.wait()
 
     mine, top = pl.pallas_call(
         pack_kernel,
         out_shape=(pltpu.VMEM((tall, width), bf16), pltpu.VMEM((cut, width), bf16)),
-        in_specs=[VMEM, VMEM],
+        in_specs=[pl.BlockSpec(memory_space=pltpu.HBM)] * 2,
         out_specs=(VMEM, VMEM),
+        scratch_shapes=[pltpu.SemaphoreType.DMA((3,))],
         compiler_params=SMALL,
         name="pack",
     )(factor_cols, arrow_factor[0])
@@ -236,15 +243,31 @@
         compiler_params=SMALL,
         name="own",
     )(*map(near, (mine, other, top, other_top)))
+    by_col = lax.dynamic_slice_in_dim(decay, column_at * width, width, axis=1)
+    decay_rows = decay[0].reshape(pieces, rows)
+    row_parts = jnp.concatenate(two_parts(decay_rows), axis=1)
+    row_parts = jnp.pad(row_parts, ((0, 0), (0, width - 2 * rows)))
+    col_parts = jnp.pad(jnp.concatenate(two_parts(by_col), axis=0), ((5, PAD - 7), (0, 0)))
+    all_rows = jnp.pad(decay_rows, ((0, 0), (0, width - rows)))
+    end = jnp.concatenate(
+        [
+            lax.dynamic_slice_in_dim(sigma_end, piece_at * rows, rows, axis=0),
+            lax.dynamic_slice_in_dim(arrow_end.T, piece_at * share, share, axis=0),
+            jnp.zeros((PAD - share, width), jnp.float32),
+        ],
+        axis=0,
+    )
+    small = (row_parts, col_parts, tip_inverse.T, all_rows, by_col, end)
     kept, given = [], []
-    second, token = lax.optimization_barrier((second, token))
+    second, token, small = lax.optimization_barrier((second, token, small))
+    row_parts, col_parts, tip_t, all_rows, by_col, end = small
     for s in range(hops - 1):
         skip = cut * (s + 2) - (order + arrow - first.shape[0]) if s > 0 else 0
         next_first = lax.ppermute(first[skip:], "space", around)
         next_second = lax.ppermute(second[skip:], "space", around) if s < hops - 2 else None
         keep, give, token = pl.pallas_call(
             far_kernel,
-            out_shape=(*[pltpu.VMEM((both + arrow, width), f32)] * 2, mark),
+            out_shape=(*[jax.ShapeDtypeStruct((both + arrow, width), f32)] * 2, mark),
             in_specs=[VMEM] * 4,
             out_specs=(VMEM,) * 3,
             compiler_params=SMALL,
@@ -259,11 +282,6 @@
     kept.append(keep)
     given.append(lax.ppermute(give, "space", swapped))
 
-    by_col = lax.dynamic_slice_in_dim(decay, column_at * width, width, axis=1)
-    decay_rows = decay[0].reshape(pieces, rows)
-    row_parts = jnp.concatenate(two_parts(decay_rows), axis=1)
-    row_parts = jnp.pad(row_parts, ((0, 0), (0, width - 2 * rows)))
-    col_parts = jnp.pad(jnp.concatenate(two_parts(by_col), axis=0), ((5, PAD - 7), (0, 0)))
     message = ((pieces, rows + PAD, width), f32)
     sent, plain, own_arrow = pl.pallas_call(
         lambda *refs: message_kernel(rows, chips, hops, *refs),
@@ -277,20 +295,12 @@
         scratch_shapes=[pltpu.VMEM((pieces, rows, width), f32), pltpu.SemaphoreType.DMA],
         compiler_params=SMALL,
         name="message",
-    )(column_at.reshape(1), *map(near, (own, *kept, *given, tip_inverse.T, row_parts, col_parts)))
+    )(column_at.reshape(1), *map(near, (own, *kept, *given, tip_t, row_parts, col_parts)))
 
     def exchange(values):
         moved = lax.all_to_all(values.astype(jnp.float16), "tm", 0, 0, tiled=True)
         return moved.astype(jnp.float32)
 
-    end = jnp.concatenate(
-        [
-            lax.dynamic_slice_in_dim(sigma_end, piece_at * rows, rows, axis=0),
-            lax.dynamic_slice_in_dim(arrow_end.T, piece_at * share, share, axis=0),
-            jnp.zeros((PAD - share, width), jnp.float32),
-        ],
-        axis=0,
-    )
     (ahead,) = held(
         lambda *refs: scan_kernel(rows, *refs),
         "suffix",
@@ -298,7 +308,7 @@
         *(exchange(sent), end),
         scratch=[pltpu.VMEM((pieces, width), f32)],
     )
-    last = (plain, own_arrow, exchange(ahead), jnp.pad(decay_rows, ((0, 0), (0, width - rows))), by_col)
+    last = (plain, own_arrow, exchange(ahead), all_rows, by_col)
     sigma, arrows = pl.pallas_call(
         lambda *refs: last_kernel(rows, *refs),
         out_shape=(jax.ShapeDtypeStruct((order, width), f32), jax.ShapeDtypeStruct((arrow, width), f32)),

time: 121 us -> 115 us (0.950)
  the two profiles are of different devices: /device:TPU:8 before, /device:TPU:16 now
where the time goes in v7:
time: 115 us; the launch traced here: 114 us
  blocking collectives  55.7 us (48%)
  starting transfers between devices  37.7 us (33%)
  Pallas kernels  7.06 us (6%)
  waiting for transfers between devices  6.09 us (5%)
  local copies, waits for them, and re-layouts  4.11 us (4%)
  other arithmetic  2.52 us (2%)
    all_to_all x2, blocking collectives, exchange(): moved = lax.all_to_all(values.astype(jnp.float16), 'tm', 0, 0, tiled=True)  55.7 us
    ppermute x3, starting transfers between devices, body(): next_first = lax.ppermute(first[skip:], 'space', around)  9.55 us
    ppermute x4, starting transfers between devices, body(): given.append(lax.ppermute(give, 'space', swapped))  8.65 us
    ppermute x2, starting transfers between devices, body(): lax.ppermute(second[skip:], 'space', around)  6.95 us
    ppermute x1, starting transfers between devices, body(): second = lax.ppermute(other, 'space', around)  4.68 us
    ppermute x1, starting transfers between devices, body(): first = lax.ppermute(mine, 'space', around)  3.48 us
    unnamed x8, local copies, waits for them, and re-layouts  3.19 us
    ppermute x3, waiting for transfers between devices, body(): next_first = lax.ppermute(first[skip:], 'space', around)  2.7 us
  transfers between devices with their start and end apart: 13, of which 4 were waited for; matrix products, arithmetic and copies ran while one was open for 4% of the time, Pallas kernels for 3%

profile of v7, /device:TPU:16, one launch (start us, length us, event | category | flops | bytes accessed | tf_op | source)
XLA Modules:
  0.0 114.1 jit_solution(8427091976898996581)
XLA Ops:
  0.7 1.1 copy-done.1
  2.9 3.5 %collective-permute-start.2 = (bf16[1856,128]{1,0:T(8,128)(2,1)S(1)}, bf16[1856,128]{1,0:T(8,128)(2,1)S(1)}, u32[]{:S(2)}, u32[]{:S(2)}) collective-permute-start(bf16[1856,128]{1,0:T(8,128)(2,1)S(1)} %get-tuple-element.35.mine), channel_id=1, source_target_pairs={{0,2},{1,15},{2,4},{3,1},{4,6},{5,3},{6,8},{7,5},{8,10},{9,7},{10,... | collective-permute-start | bytes 1425416 | tf_op jit(solution)/shard_map/ppermute | solution.py:229
  6.4 1.9 %collective-permute-start = (bf16[1856,128]{1,0:T(8,128)(2,1)S(1)}, bf16[1856,128]{1,0:T(8,128)(2,1)S(1)}, u32[]{:S(2)}, u32[]{:S(2)}) collective-permute-start(bf16[1856,128]{1,0:T(8,128)(2,1)S(1)} %get-tuple-element.35.mine), channel_id=1, source_target_pairs={{0,1},{1,0},{2,3},{3,2},{4,5},{5,4},{6,7},{7,6},{8,9},{9,8},{10,11... | collective-permute-start | bytes 1425416 | tf_op jit(solution)/shard_map/ppermute | solution.py:230
  8.3 2.4 %collective-permute-start.1 = (bf16[256,128]{1,0:T(8,128)(2,1)S(1)}, bf16[256,128]{1,0:T(8,128)(2,1)S(1)}, u32[]{:S(2)}, u32[]{:S(2)}) collective-permute-start(bf16[256,128]{1,0:T(8,128)(2,1)S(1)} %get-tuple-element.36.mine_top), channel_id=1, source_target_pairs={{0,1},{1,0},{2,3},{3,2},{4,5},{5,4},{6,7},{7,6},{8,9},{9,8},{10,11... | collective-permute-start | bytes 196616 | tf_op jit(solution)/shard_map/ppermute | solution.py:231
  12.3 4.7 %collective-permute-start.3 = (bf16[1856,128]{1,0:T(8,128)(2,1)S(1)}, bf16[1856,128]{1,0:T(8,128)(2,1)S(1)}, u32[]{:S(2)}, u32[]{:S(2)}) collective-permute-start(bf16[1856,128]{1,0:T(8,128)(2,1)S(1)} %collective-permute-done.other), channel_id=1, source_target_pairs={{0,2},{1,15},{2,4},{3,1},{4,6},{5,3},{6,8},{7,5},{8,10},{9,7},{10,... | collective-permute-start | bytes 1425416 | tf_op jit(solution)/shard_map/ppermute | solution.py:232
  17.5 1.4 %reduce.3 = f32[2048]{0:T(1024)S(1)} reduce(f32[1,2048]{1,0:T(1,128)} %param.8, f32[]{:T(128)} %broadcast.18), dimensions={0}, to_apply=%param.8.reduce_sub_computation.3 | reduce | bytes 16388 | tf_op args[2]
  18.9 0.8 copy.8
  19.8 2.6 %collective-permute-start.4 = (bf16[1856,128]{1,0:T(8,128)(2,1)S(1)}, bf16[1856,128]{1,0:T(8,128)(2,1)S(1)}, u32[]{:S(2)}, u32[]{:S(2)}) collective-permute-start(bf16[1856,128]{1,0:T(8,128)(2,1)S(1)} %collective-permute-done.2.first), channel_id=1, source_target_pairs={{0,2},{1,15},{2,4},{3,1},{4,6},{5,3},{6,8},{7,5},{8,10},{9,7},{10,... | collective-permute-start | bytes 1425416 | tf_op jit(solution)/shard_map/ppermute | solution.py:266
  23.1 4.3 %collective-permute-start.5 = (bf16[1856,128]{1,0:T(8,128)(2,1)S(1)}, bf16[1856,128]{1,0:T(8,128)(2,1)S(1)}, u32[]{:S(2)}, u32[]{:S(2)}) collective-permute-start(bf16[1856,128]{1,0:T(8,128)(2,1)S(1)} %collective-permute-done.3.second), channel_id=1, source_target_pairs={{0,2},{1,15},{2,4},{3,1},{4,6},{5,3},{6,8},{7,5},{8,10},{9,7},{10,... | collective-permute-start | bytes 1425416 | tf_op jit(solution)/shard_map/ppermute | solution.py:267
  28.3 2.1 %collective-permute-done.4.first = bf16[1856,128]{1,0:T(8,128)(2,1)S(1)} collective-permute-done((bf16[1856,128]{1,0:T(8,128)(2,1)S(1)}, bf16[1856,128]{1,0:T(8,128)(2,1)S(1)}, u32[]{:S(2)}, u32[]{:S(2)}) %collective-permute-start.4) | collective-permute-done | bytes 475168 | tf_op jit(solution)/shard_map/ppermute | solution.py:266
  30.4 2.6 %collective-permute-start.6 = (bf16[1344,128]{1,0:T(8,128)(2,1)S(1)}, bf16[1344,128]{1,0:T(8,128)(2,1)S(1)}, u32[]{:S(2)}, u32[]{:S(2)}) collective-permute-start(bf16[1344,128]{1,0:T(8,128)(2,1)S(1)} %slice.9), channel_id=1, source_target_pairs={{0,2},{1,15},{2,4},{3,1},{4,6},{5,3},{6,8},{7,5},{8,10},{9,7},{10,... | collective-permute-start | bytes 1032200 | tf_op jit(solution)/shard_map/ppermute | solution.py:266
  33.0 2.5 %collective-permute-done.5.second = bf16[1856,128]{1,0:T(8,128)(2,1)S(1)} collective-permute-done((bf16[1856,128]{1,0:T(8,128)(2,1)S(1)}, bf16[1856,128]{1,0:T(8,128)(2,1)S(1)}, u32[]{:S(2)}, u32[]{:S(2)}) %collective-permute-start.5) | collective-permute-done | bytes 475168 | tf_op jit(solution)/shard_map/ppermute | solution.py:267
  35.5 2.6 %collective-permute-start.7 = (bf16[1344,128]{1,0:T(8,128)(2,1)S(1)}, bf16[1344,128]{1,0:T(8,128)(2,1)S(1)}, u32[]{:S(2)}, u32[]{:S(2)}) collective-permute-start(bf16[1344,128]{1,0:T(8,128)(2,1)S(1)} %slice.12), channel_id=1, source_target_pairs={{0,2},{1,15},{2,4},{3,1},{4,6},{5,3},{6,8},{7,5},{8,10},{9,7},{10,... | collective-permute-start | bytes 1032200 | tf_op jit(solution)/shard_map/ppermute | solution.py:267
  38.1 0.8 far.4
  39.5 4.4 %collective-permute-start.8 = (bf16[1088,128]{1,0:T(8,128)(2,1)S(1)}, bf16[1088,128]{1,0:T(8,128)(2,1)S(1)}, u32[]{:S(2)}, u32[]{:S(2)}) collective-permute-start(bf16[1088,128]{1,0:T(8,128)(2,1)S(1)} %slice.11), channel_id=1, source_target_pairs={{0,2},{1,15},{2,4},{3,1},{4,6},{5,3},{6,8},{7,5},{8,10},{9,7},{10,... | collective-permute-start | bytes 835592 | tf_op jit(solution)/shard_map/ppermute | solution.py:266
  43.9 1.9 %collective-permute-start.9 = (f32[320,128]{1,0:T(8,128)S(1)}, f32[320,128]{1,0:T(8,128)S(1)}, u32[]{:S(2)}, u32[]{:S(2)}) collective-permute-start(f32[320,128]{1,0:T(8,128)S(1)} %get-tuple-element.53), channel_id=1, source_target_pairs={{0,1},{1,0},{2,3},{3,2},{4,5},{5,4},{6,7},{7,6},{8,9},{9,8},{10,11... | collective-permute-start | bytes 491528 | tf_op jit(solution)/shard_map/ppermute | solution.py:277
  45.9 2.4 %collective-permute-start.10 = (f32[320,128]{1,0:T(8,128)S(1)}, f32[320,128]{1,0:T(8,128)S(1)}, u32[]{:S(2)}, u32[]{:S(2)}) collective-permute-start(f32[320,128]{1,0:T(8,128)S(1)} %get-tuple-element.54), channel_id=1, source_target_pairs={{0,1},{1,0},{2,3},{3,2},{4,5},{5,4},{6,7},{7,6},{8,9},{9,8},{10,11... | collective-permute-start | bytes 491528 | tf_op jit(solution)/shard_map/ppermute | solution.py:277
  49.0 1.9 %collective-permute-start.11 = (f32[320,128]{1,0:T(8,128)S(1)}, f32[320,128]{1,0:T(8,128)S(1)}, u32[]{:S(2)}, u32[]{:S(2)}) collective-permute-start(f32[320,128]{1,0:T(8,128)S(1)} %get-tuple-element.55), channel_id=1, source_target_pairs={{0,1},{1,0},{2,3},{3,2},{4,5},{5,4},{6,7},{7,6},{8,9},{9,8},{10,11... | collective-permute-start | bytes 491528 | tf_op jit(solution)/shard_map/ppermute | solution.py:277
  51.5 2.4 %collective-permute-start.12 = (f32[192,128]{1,0:T(8,128)S(1)}, f32[192,128]{1,0:T(8,128)S(1)}, u32[]{:S(2)}, u32[]{:S(2)}) collective-permute-start(f32[192,128]{1,0:T(8,128)S(1)} %get-tuple-element.56), channel_id=1, source_target_pairs={{0,1},{1,0},{2,3},{3,2},{4,5},{5,4},{6,7},{7,6},{8,9},{9,8},{10,11... | collective-permute-start | bytes 294920 | tf_op jit(solution)/shard_map/ppermute | solution.py:283
  53.9 0.9 collective-permute-done.12.refs_9_
  55.4 31.6 %all_to_all.10 = f16[32,72,128]{2,1,0:T(8,128)(2,1)S(1)} all-to-all(f16[32,72,128]{2,1,0:T(8,128)(2,1)S(1)} %convert_element_type.16), channel_id=1, replica_groups=mesh['tm'=32,'space'=16] {'tm'}, dimensions={0} | all-to-all | bytes 1179648 | tf_op jit(solution)/shard_map/all_to_all | solution.py:301
  87.1 1.0 suffix.1
  88.2 24.1 %all_to_all.11 = f16[32,72,128]{2,1,0:T(8,128)(2,1)S(1)} all-to-all(f16[32,72,128]{2,1,0:T(8,128)(2,1)S(1)} %convert_element_type.18), channel_id=1, replica_groups=mesh['tm'=32,'space'=16] {'tm'}, dimensions={0} | all-to-all | bytes 1179648 | tf_op jit(solution)/shard_map/all_to_all | solution.py:301
  112.4 1.6 %last.1 = (f32[2048,128]{1,0:T(8,128)}, f32[64,128]{1,0:T(8,128)}) custom-call(f32[32,64,128]{2,1,0:T(8,128)S(1)} %get-tuple-element.60.refs_0_, f32[64,128]{1,0:T(8,128)S(1)} %get-tuple-element.61.refs_1_, f32[32,72,128]{2,1,0:T(8,128)S(1)} %convert_element_type.19.refs_2_, f32[32,128]{1,0:T(8,128)S(1)} %pad.9.refs_3_, f32[1,128]{1,0:T(1,128)S(1)} %get-tuple-element.65.refs_4_), custom_call_target="tpu_custom_call" | custom-call | tf_op jit(solution)/shard_map/last/pallas_call | solution.py:312
  (41 shorter events, 7.6 us)
Async XLA Ops:
  0.6 10.9 %copy-start = (f32[2048,128]{1,0:T(8,128)S(1)}, f32[2048,128]{1,0:T(8,128)}, u32[]{:S(2)}) copy-start(f32[2048,128]{1,0:T(8,128)} %param.10) | copy-start | bytes 3145732
  0.6 1.1 copy-start.1
  1.8 0.7 copy-start.2
  2.9 16.9 %collective-permute-start.2 = (bf16[1856,128]{1,0:T(8,128)(2,1)S(1)}, bf16[1856,128]{1,0:T(8,128)(2,1)S(1)}, u32[]{:S(2)}, u32[]{:S(2)}) collective-permute-start(bf16[1856,128]{1,0:T(8,128)(2,1)S(1)} %get-tuple-element.35.mine), channel_id=1, source_target_pairs={{0,2},{1,15},{2,4},{3,1},{4,6},{5,3},{6,8},{7,5},{8,10},{9,7},{10,... | collective-permute-start | bytes 1425416 | tf_op jit(solution)/shard_map/ppermute | solution.py:229
  6.4 5.9 %collective-permute-start = (bf16[1856,128]{1,0:T(8,128)(2,1)S(1)}, bf16[1856,128]{1,0:T(8,128)(2,1)S(1)}, u32[]{:S(2)}, u32[]{:S(2)}) collective-permute-start(bf16[1856,128]{1,0:T(8,128)(2,1)S(1)} %get-tuple-element.35.mine), channel_id=1, source_target_pairs={{0,1},{1,0},{2,3},{3,2},{4,5},{5,4},{6,7},{7,6},{8,9},{9,8},{10,11... | collective-permute-start | bytes 1425416 | tf_op jit(solution)/shard_map/ppermute | solution.py:230
  8.3 14.2 %collective-permute-start.1 = (bf16[256,128]{1,0:T(8,128)(2,1)S(1)}, bf16[256,128]{1,0:T(8,128)(2,1)S(1)}, u32[]{:S(2)}, u32[]{:S(2)}) collective-permute-start(bf16[256,128]{1,0:T(8,128)(2,1)S(1)} %get-tuple-element.36.mine_top), channel_id=1, source_target_pairs={{0,1},{1,0},{2,3},{3,2},{4,5},{5,4},{6,7},{7,6},{8,9},{9,8},{10,11... | collective-permute-start | bytes 196616 | tf_op jit(solution)/shard_map/ppermute | solution.py:231
  12.3 10.9 %collective-permute-start.3 = (bf16[1856,128]{1,0:T(8,128)(2,1)S(1)}, bf16[1856,128]{1,0:T(8,128)(2,1)S(1)}, u32[]{:S(2)}, u32[]{:S(2)}) collective-permute-start(bf16[1856,128]{1,0:T(8,128)(2,1)S(1)} %collective-permute-done.other), channel_id=1, source_target_pairs={{0,2},{1,15},{2,4},{3,1},{4,6},{5,3},{6,8},{7,5},{8,10},{9,7},{10,... | collective-permute-start | bytes 1425416 | tf_op jit(solution)/shard_map/ppermute | solution.py:232
  19.8 10.5 %collective-permute-start.4 = (bf16[1856,128]{1,0:T(8,128)(2,1)S(1)}, bf16[1856,128]{1,0:T(8,128)(2,1)S(1)}, u32[]{:S(2)}, u32[]{:S(2)}) collective-permute-start(bf16[1856,128]{1,0:T(8,128)(2,1)S(1)} %collective-permute-done.2.first), channel_id=1, source_target_pairs={{0,2},{1,15},{2,4},{3,1},{4,6},{5,3},{6,8},{7,5},{8,10},{9,7},{10,... | collective-permute-start | bytes 1425416 | tf_op jit(solution)/shard_map/ppermute | solution.py:266
  23.1 12.3 %collective-permute-start.5 = (bf16[1856,128]{1,0:T(8,128)(2,1)S(1)}, bf16[1856,128]{1,0:T(8,128)(2,1)S(1)}, u32[]{:S(2)}, u32[]{:S(2)}) collective-permute-start(bf16[1856,128]{1,0:T(8,128)(2,1)S(1)} %collective-permute-done.3.second), channel_id=1, source_target_pairs={{0,2},{1,15},{2,4},{3,1},{4,6},{5,3},{6,8},{7,5},{8,10},{9,7},{10,... | collective-permute-start | bytes 1425416 | tf_op jit(solution)/shard_map/ppermute | solution.py:267
  30.4 9.1 %collective-permute-start.6 = (bf16[1344,128]{1,0:T(8,128)(2,1)S(1)}, bf16[1344,128]{1,0:T(8,128)(2,1)S(1)}, u32[]{:S(2)}, u32[]{:S(2)}) collective-permute-start(bf16[1344,128]{1,0:T(8,128)(2,1)S(1)} %slice.9), channel_id=1, source_target_pairs={{0,2},{1,15},{2,4},{3,1},{4,6},{5,3},{6,8},{7,5},{8,10},{9,7},{10,... | collective-permute-start | bytes 1032200 | tf_op jit(solution)/shard_map/ppermute | solution.py:266
  35.5 12.8 %collective-permute-start.7 = (bf16[1344,128]{1,0:T(8,128)(2,1)S(1)}, bf16[1344,128]{1,0:T(8,128)(2,1)S(1)}, u32[]{:S(2)}, u32[]{:S(2)}) collective-permute-start(bf16[1344,128]{1,0:T(8,128)(2,1)S(1)} %slice.12), channel_id=1, source_target_pairs={{0,2},{1,15},{2,4},{3,1},{4,6},{5,3},{6,8},{7,5},{8,10},{9,7},{10,... | collective-permute-start | bytes 1032200 | tf_op jit(solution)/shard_map/ppermute | solution.py:267
  39.5 11.4 %collective-permute-start.8 = (bf16[1088,128]{1,0:T(8,128)(2,1)S(1)}, bf16[1088,128]{1,0:T(8,128)(2,1)S(1)}, u32[]{:S(2)}, u32[]{:S(2)}) collective-permute-start(bf16[1088,128]{1,0:T(8,128)(2,1)S(1)} %slice.11), channel_id=1, source_target_pairs={{0,2},{1,15},{2,4},{3,1},{4,6},{5,3},{6,8},{7,5},{8,10},{9,7},{10,... | collective-permute-start | bytes 835592 | tf_op jit(solution)/shard_map/ppermute | solution.py:266
  43.9 10.0 %collective-permute-start.9 = (f32[320,128]{1,0:T(8,128)S(1)}, f32[320,128]{1,0:T(8,128)S(1)}, u32[]{:S(2)}, u32[]{:S(2)}) collective-permute-start(f32[320,128]{1,0:T(8,128)S(1)} %get-tuple-element.53), channel_id=1, source_target_pairs={{0,1},{1,0},{2,3},{3,2},{4,5},{5,4},{6,7},{7,6},{8,9},{9,8},{10,11... | collective-permute-start | bytes 491528 | tf_op jit(solution)/shard_map/ppermute | solution.py:277
  45.9 8.1 %collective-permute-start.10 = (f32[320,128]{1,0:T(8,128)S(1)}, f32[320,128]{1,0:T(8,128)S(1)}, u32[]{:S(2)}, u32[]{:S(2)}) collective-permute-start(f32[320,128]{1,0:T(8,128)S(1)} %get-tuple-element.54), channel_id=1, source_target_pairs={{0,1},{1,0},{2,3},{3,2},{4,5},{5,4},{6,7},{7,6},{8,9},{9,8},{10,11... | collective-permute-start | bytes 491528 | tf_op jit(solution)/shard_map/ppermute | solution.py:277
  49.0 5.8 %collective-permute-start.11 = (f32[320,128]{1,0:T(8,128)S(1)}, f32[320,128]{1,0:T(8,128)S(1)}, u32[]{:S(2)}, u32[]{:S(2)}) collective-permute-start(f32[320,128]{1,0:T(8,128)S(1)} %get-tuple-element.55), channel_id=1, source_target_pairs={{0,1},{1,0},{2,3},{3,2},{4,5},{5,4},{6,7},{7,6},{8,9},{9,8},{10,11... | collective-permute-start | bytes 491528 | tf_op jit(solution)/shard_map/ppermute | solution.py:277
  51.5 3.3 %collective-permute-start.12 = (f32[192,128]{1,0:T(8,128)S(1)}, f32[192,128]{1,0:T(8,128)S(1)}, u32[]{:S(2)}, u32[]{:S(2)}) collective-permute-start(f32[192,128]{1,0:T(8,128)S(1)} %get-tuple-element.56), channel_id=1, source_target_pairs={{0,1},{1,0},{2,3},{3,2},{4,5},{5,4},{6,7},{7,6},{8,9},{9,8},{10,11... | collective-permute-start | bytes 294920 | tf_op jit(solution)/shard_map/ppermute | solution.py:283

commit v8 on v7

--- a/solution.py
+++ b/solution.py
@@ -89,13 +89,20 @@
     token[...] = passed[...]
 
 
-def farthest_kernel(first, both_t, passed, keep, give):
-    far_tiles((first,), both_t, keep, give)
+def farthest_kernel(first, second, straight, both_t, token, keep, give, near_part, far_part):
+    count = CORES * first.shape[1]
+    far_tiles((first, second), both_t, near_part.at[0], near_part.at[1])
+    far_tiles((straight,), both_t, far_part.at[0], far_part.at[1])
+    single = straight.shape[1]
+    for at, out in enumerate((keep, give)):
+        out[:count, :] = near_part[at, :count, :]
+        out[count : count + single, :] = far_part[at, :single, :]
+        out[count + single :, :] = near_part[at, count:, :] + far_part[at, single:, :]
 
 
 def message_kernel(rows, chips, hops, at, own, *refs):
-    kept, given = refs[:hops], refs[hops : 2 * hops]
-    tip_t, decay_rows, decay_cols, out, copied, own_arrow, plain, done = refs[2 * hops :]
+    kept, given = refs[: hops - 1], refs[hops - 1 : 2 * hops - 2]
+    tip_t, decay_rows, decay_cols, out, copied, own_arrow, plain, done = refs[2 * hops - 2 :]
     width = own.shape[1]
     per = width // rows
     chip, core = at[0] // CORES, at[0] % CORES
@@ -107,13 +114,14 @@
 
     put(own[:width, :], 0, core)
     put(own[width : CORES * width, :], 0, 1 - core)
-    for s in range(hops):
+    for s in range(hops - 1):
         hop = (s + 1) * way
         put(kept[s][:width, :], -hop, core)
         put(given[s][:width, :], hop, 1 - core)
-        if s < hops - 1:
-            put(kept[s][width : 2 * width, :], -hop, 1 - core)
-            put(given[s][width : 2 * width, :], hop, core)
+        put(kept[s][width : 2 * width, :], -hop, 1 - core)
+        put(given[s][width : 2 * width, :], hop, core)
+    put(kept[-1][2 * width : 3 * width, :], hops, core)
+    put(given[-1][2 * width : 3 * width, :], hops, 1 - core)
     copy = pltpu.make_async_copy(plain, copied, done)
     copy.start()
     border = own_arrow.shape[0]
@@ -150,14 +158,24 @@
         pair = arrow + by_col * pair
 
 
-def last_kernel(rows, plain, own_arrow, got, decay_rows, by_col, sigma, arrows):
+def last_kernel(rows, plain, own_arrow, got, decay_rows, by_col, sigma, arrows, whole, done):
     columns = decay_rows[...].T[:rows, :]
-    for r in range(plain.shape[0]):
+    pieces, parts = plain.shape[0], done.shape[0]
+    span = pieces // parts * rows
+    copies = []
+    for r in range(pieces):
         later, later_arrow = decode(got[r], rows)
         by_row = jnp.broadcast_to(columns[:, r : r + 1], later.shape)
-        sigma[r * rows : (r + 1) * rows, :] = plain[r] + by_row * by_col[...] * later
+        whole[r * rows : (r + 1) * rows, :] = plain[r] + by_row * by_col[...] * later
         pair = slice(2 * r, 2 * r + 2)
         arrows[pair, :] = own_arrow[pair, :] + by_col[...] * later_arrow[:2, :]
+        if (r + 1) % (pieces // parts) == 0:
+            part = len(copies)
+            spot = pl.ds(part * span, span)
+            copies.append(pltpu.make_async_copy(whole.at[spot], sigma.at[spot], done.at[part]))
+            copies[-1].start()
+    for copy in copies:
+        copy.wait()
 
 
 def two_parts(decay):
@@ -199,9 +217,6 @@
     column_at = lax.axis_index("space")
     piece_at = lax.axis_index("tm")
     swapped = [(p, p ^ 1) for p in range(devices)]
-    around = [
-        (p, (p // CORES + 1 - 2 * (p % CORES)) % chips * CORES + p % CORES) for p in range(devices)
-    ]
     depth, both = order - cut, CORES * width
     tall, hops = depth + arrow, chips // 2
     f32, bf16 = jnp.float32, jnp.bfloat16
@@ -225,11 +240,22 @@
         scratch_shapes=[pltpu.SemaphoreType.DMA((3,))],
         compiler_params=SMALL,
         name="pack",
-    )(factor_cols, arrow_factor[0])
-    first = lax.ppermute(mine, "space", around)
+    )(*[pltpu.with_memory_space_constraint(x, pltpu.HBM) for x in (factor_cols, arrow_factor[0])])
+
+    def hop(panel, count=1):
+        pairs = []
+        for p in range(devices):
+            chip, core = p // CORES, p % CORES
+            pairs.append((p, (chip + count * (1 - 2 * core)) % chips * CORES + core))
+        return lax.ppermute(panel, "space", pairs)
+
+    def shared(panel, count):
+        return panel[cut * count - (order + arrow - panel.shape[0]) :]
+
+    first = hop(mine)
     other = lax.ppermute(mine, "space", swapped)
     other_top = lax.ppermute(top, "space", swapped)
-    second = lax.ppermute(other, "space", around)
+    second = hop(other)
     mark = jax.ShapeDtypeStruct((8, width), f32)
     own, both_t, token = pl.pallas_call(
         own_kernel,
@@ -258,14 +284,9 @@
         axis=0,
     )
     small = (row_parts, col_parts, tip_inverse.T, all_rows, by_col, end)
-    kept, given = [], []
-    second, token, small = lax.optimization_barrier((second, token, small))
-    row_parts, col_parts, tip_t, all_rows, by_col, end = small
-    for s in range(hops - 1):
-        skip = cut * (s + 2) - (order + arrow - first.shape[0]) if s > 0 else 0
-        next_first = lax.ppermute(first[skip:], "space", around)
-        next_second = lax.ppermute(second[skip:], "space", around) if s < hops - 2 else None
-        keep, give, token = pl.pallas_call(
+
+    def far(first, second, token):
+        return pl.pallas_call(
             far_kernel,
             out_shape=(*[jax.ShapeDtypeStruct((both + arrow, width), f32)] * 2, mark),
             in_specs=[VMEM] * 4,
@@ -273,14 +294,32 @@
             compiler_params=SMALL,
             name="far",
         )(*map(near, (first, second, both_t)), token)
-        kept.append(keep)
-        given.append(lax.ppermute(give, "space", swapped))
-        first, second = next_first, next_second
-        if s < hops - 2:
-            first, token = lax.optimization_barrier((first, token))
-    keep, give = held(farthest_kernel, "farthest", (((width + arrow, width), f32),) * 2, first, both_t, token)
-    kept.append(keep)
-    given.append(lax.ppermute(give, "space", swapped))
+
+    def swap(tile):
+        return lax.ppermute(tile, "space", swapped)
+
+    first_2 = hop(shared(first, 2))
+    second, token, small = lax.optimization_barrier((second, token, small))
+    second_2 = hop(shared(second, 2))
+    second_3 = hop(shared(second_2, 3))
+    keep_1, give_1, token = far(first, second, token)
+    first_2, token = lax.optimization_barrier((first_2, token))
+    first_4 = hop(shared(first_2, 4), 2)
+    first_3 = hop(shared(first_2, 3))
+    given_1 = swap(give_1)
+    keep_2, give_2, token = far(first_2, second_2, token)
+    given_2 = swap(give_2)
+    token, given_1, given_2 = lax.optimization_barrier((token, given_1, given_2))
+    stacked = (3 * width + arrow, width)
+    keep, give = held(
+        farthest_kernel,
+        "farthest",
+        ((stacked, f32),) * 2,
+        *(first_3, second_3, first_4, both_t, token),
+        scratch=[pltpu.VMEM((2, both + arrow, width), f32), pltpu.VMEM((2, width + arrow, width), f32)],
+    )
+    kept, given = (keep_1, keep_2, keep), (given_1, given_2, swap(give))
+    row_parts, col_parts, tip_t, all_rows, by_col, end = small
 
     message = ((pieces, rows + PAD, width), f32)
     sent, plain, own_arrow = pl.pallas_call(
@@ -290,7 +329,7 @@
             jax.ShapeDtypeStruct((pieces, rows, width), f32),
             jax.ShapeDtypeStruct((arrow, width), f32),
         ),
-        in_specs=[SMEM] + [VMEM] * (2 * hops + 4),
+        in_specs=[SMEM] + [VMEM] * (2 * hops + 2),
         out_specs=(VMEM, pl.BlockSpec(memory_space=pl.ANY), VMEM),
         scratch_shapes=[pltpu.VMEM((pieces, rows, width), f32), pltpu.SemaphoreType.DMA],
         compiler_params=SMALL,
@@ -313,6 +352,8 @@
         lambda *refs: last_kernel(rows, *refs),
         out_shape=(jax.ShapeDtypeStruct((order, width), f32), jax.ShapeDtypeStruct((arrow, width), f32)),
         in_specs=[VMEM] * len(last),
+        out_specs=(pl.BlockSpec(memory_space=pltpu.HBM), VMEM),
+        scratch_shapes=[pltpu.VMEM((order, width), f32), pltpu.SemaphoreType.DMA((4,))],
         compiler_params=SMALL,
         name="last",
     )(*map(near, last))

time: 115 us -> 117 us (1.017)
  the two profiles are of different devices: /device:TPU:16 before, /device:TPU:8 now
where the time goes in v8:
time: 117 us; the launch traced here: 116 us
  blocking collectives  52.6 us (45%)
  starting transfers between devices  34.1 us (29%)
  waiting for transfers between devices  15.9 us (14%)
  Pallas kernels  8.1 us (7%)
  other arithmetic  2.52 us (2%)
  local copies, waits for them, and re-layouts  2.33 us (2%)
    all_to_all x2, blocking collectives, exchange(): moved = lax.all_to_all(values.astype(jnp.float16), 'tm', 0, 0, tiled=True)  52.6 us
    ppermute x7, starting transfers between devices, hop(): return lax.ppermute(panel, 'space', pairs)  23.5 us
    ppermute x7, waiting for transfers between devices, hop(): return lax.ppermute(panel, 'space', pairs)  13.5 us
    ppermute x3, starting transfers between devices, swap(): return lax.ppermute(tile, 'space', swapped)  6.27 us
    ppermute x3, waiting for transfers between devices, swap(): return lax.ppermute(tile, 'space', swapped)  2.45 us
    ppermute x1, starting transfers between devices, body(): other_top = lax.ppermute(top, 'space', swapped)  2.41 us
  transfers between devices with their start and end apart: 12, of which 6 were waited for; matrix products, arithmetic and copies ran while one was open for 4% of the time, Pallas kernels for 2%

profile of v8, /device:TPU:8, one launch (start us, length us, event | category | flops | bytes accessed | tf_op | source)
XLA Modules:
  0.0 116.5 jit_solution(12842477114428366512)
XLA Ops:
  0.6 1.1 pack.1
  1.8 3.5 %collective-permute-start.2 = (bf16[1856,128]{1,0:T(8,128)(2,1)S(1)}, bf16[1856,128]{1,0:T(8,128)(2,1)S(1)}, u32[]{:S(2)}, u32[]{:S(2)}) collective-permute-start(bf16[1856,128]{1,0:T(8,128)(2,1)S(1)} %get-tuple-element.33.mine), channel_id=1, source_target_pairs={{0,2},{1,15},{2,4},{3,1},{4,6},{5,3},{6,8},{7,5},{8,10},{9,7},{10,... | collective-permute-start | bytes 1425416 | tf_op jit(solution)/shard_map/ppermute | solution.py:250
  5.3 1.9 %collective-permute-start = (bf16[1856,128]{1,0:T(8,128)(2,1)S(1)}, bf16[1856,128]{1,0:T(8,128)(2,1)S(1)}, u32[]{:S(2)}, u32[]{:S(2)}) collective-permute-start(bf16[1856,128]{1,0:T(8,128)(2,1)S(1)} %get-tuple-element.33.mine), channel_id=1, source_target_pairs={{0,1},{1,0},{2,3},{3,2},{4,5},{5,4},{6,7},{7,6},{8,9},{9,8},{10,11... | collective-permute-start | bytes 1425416 | tf_op jit(solution)/shard_map/ppermute | solution.py:256
  7.2 2.4 %collective-permute-start.1 = (bf16[256,128]{1,0:T(8,128)(2,1)S(1)}, bf16[256,128]{1,0:T(8,128)(2,1)S(1)}, u32[]{:S(2)}, u32[]{:S(2)}) collective-permute-start(bf16[256,128]{1,0:T(8,128)(2,1)S(1)} %get-tuple-element.34.mine_top), channel_id=1, source_target_pairs={{0,1},{1,0},{2,3},{3,2},{4,5},{5,4},{6,7},{7,6},{8,9},{9,8},{10,11... | collective-permute-start | bytes 196616 | tf_op jit(solution)/shard_map/ppermute | solution.py:257
  10.1 1.4 %reduce.3 = f32[2048]{0:T(1024)S(1)} reduce(f32[1,2048]{1,0:T(1,128)} %param.8, f32[]{:T(128)} %broadcast.18), dimensions={0}, to_apply=%param.8.reduce_sub_computation.3 | reduce | bytes 16388 | tf_op args[2]
  12.3 3.5 %collective-permute-start.3 = (bf16[1856,128]{1,0:T(8,128)(2,1)S(1)}, bf16[1856,128]{1,0:T(8,128)(2,1)S(1)}, u32[]{:S(2)}, u32[]{:S(2)}) collective-permute-start(bf16[1856,128]{1,0:T(8,128)(2,1)S(1)} %collective-permute-done.other), channel_id=1, source_target_pairs={{0,2},{1,15},{2,4},{3,1},{4,6},{5,3},{6,8},{7,5},{8,10},{9,7},{10,... | collective-permute-start | bytes 1425416 | tf_op jit(solution)/shard_map/ppermute | solution.py:250
  17.6 4.7 %collective-permute-start.4 = (bf16[1600,128]{1,0:T(8,128)(2,1)S(1)}, bf16[1600,128]{1,0:T(8,128)(2,1)S(1)}, u32[]{:S(2)}, u32[]{:S(2)}) collective-permute-start(bf16[1600,128]{1,0:T(8,128)(2,1)S(1)} %slice.20), channel_id=1, source_target_pairs={{0,2},{1,15},{2,4},{3,1},{4,6},{5,3},{6,8},{7,5},{8,10},{9,7},{10,... | collective-permute-start | bytes 1228808 | tf_op jit(solution)/shard_map/ppermute | solution.py:250
  22.9 2.2 %collective-permute-done.3.second = bf16[1856,128]{1,0:T(8,128)(2,1)S(1)} collective-permute-done((bf16[1856,128]{1,0:T(8,128)(2,1)S(1)}, bf16[1856,128]{1,0:T(8,128)(2,1)S(1)}, u32[]{:S(2)}, u32[]{:S(2)}) %collective-permute-start.3) | collective-permute-done | bytes 475168 | tf_op jit(solution)/shard_map/ppermute | solution.py:250
  25.2 1.9 %collective-permute-start.5 = (bf16[1600,128]{1,0:T(8,128)(2,1)S(1)}, bf16[1600,128]{1,0:T(8,128)(2,1)S(1)}, u32[]{:S(2)}, u32[]{:S(2)}) collective-permute-start(bf16[1600,128]{1,0:T(8,128)(2,1)S(1)} %slice.16), channel_id=1, source_target_pairs={{0,2},{1,15},{2,4},{3,1},{4,6},{5,3},{6,8},{7,5},{8,10},{9,7},{10,... | collective-permute-start | bytes 1228808 | tf_op jit(solution)/shard_map/ppermute | solution.py:250
  27.9 1.6 %collective-permute-done.4.first = bf16[1600,128]{1,0:T(8,128)(2,1)S(1)} collective-permute-done((bf16[1600,128]{1,0:T(8,128)(2,1)S(1)}, bf16[1600,128]{1,0:T(8,128)(2,1)S(1)}, u32[]{:S(2)}, u32[]{:S(2)}) %collective-permute-start.4) | collective-permute-done | bytes 409632 | tf_op jit(solution)/shard_map/ppermute | solution.py:250
  29.5 2.6 %collective-permute-start.6 = (bf16[1344,128]{1,0:T(8,128)(2,1)S(1)}, bf16[1344,128]{1,0:T(8,128)(2,1)S(1)}, u32[]{:S(2)}, u32[]{:S(2)}) collective-permute-start(bf16[1344,128]{1,0:T(8,128)(2,1)S(1)} %slice.17), channel_id=1, source_target_pairs={{0,2},{1,15},{2,4},{3,1},{4,6},{5,3},{6,8},{7,5},{8,10},{9,7},{10,... | collective-permute-start | bytes 1032200 | tf_op jit(solution)/shard_map/ppermute | solution.py:250
  32.2 4.0 %collective-permute-done.5.second = bf16[1600,128]{1,0:T(8,128)(2,1)S(1)} collective-permute-done((bf16[1600,128]{1,0:T(8,128)(2,1)S(1)}, bf16[1600,128]{1,0:T(8,128)(2,1)S(1)}, u32[]{:S(2)}, u32[]{:S(2)}) %collective-permute-start.5) | collective-permute-done | bytes 409632 | tf_op jit(solution)/shard_map/ppermute | solution.py:250
  36.2 1.9 %collective-permute-start.7 = (bf16[1344,128]{1,0:T(8,128)(2,1)S(1)}, bf16[1344,128]{1,0:T(8,128)(2,1)S(1)}, u32[]{:S(2)}, u32[]{:S(2)}) collective-permute-start(bf16[1344,128]{1,0:T(8,128)(2,1)S(1)} %slice.21), channel_id=1, source_target_pairs={{0,2},{1,15},{2,4},{3,1},{4,6},{5,3},{6,8},{7,5},{8,10},{9,7},{10,... | collective-permute-start | bytes 1032200 | tf_op jit(solution)/shard_map/ppermute | solution.py:250
  38.2 5.3 %collective-permute-start.8 = (bf16[1088,128]{1,0:T(8,128)(2,1)S(1)}, bf16[1088,128]{1,0:T(8,128)(2,1)S(1)}, u32[]{:S(2)}, u32[]{:S(2)}) collective-permute-start(bf16[1088,128]{1,0:T(8,128)(2,1)S(1)} %slice.19), channel_id=1, source_target_pairs={{0,4},{1,13},{2,6},{3,15},{4,8},{5,1},{6,10},{7,3},{8,12},{9,5},{1... | collective-permute-start | bytes 835592 | tf_op jit(solution)/shard_map/ppermute | solution.py:250
  43.5 1.9 %collective-permute-start.9 = (f32[320,128]{1,0:T(8,128)S(1)}, f32[320,128]{1,0:T(8,128)S(1)}, u32[]{:S(2)}, u32[]{:S(2)}) collective-permute-start(f32[320,128]{1,0:T(8,128)S(1)} %get-tuple-element.46), channel_id=1, source_target_pairs={{0,1},{1,0},{2,3},{3,2},{4,5},{5,4},{6,7},{7,6},{8,9},{9,8},{10,11... | collective-permute-start | bytes 491528 | tf_op jit(solution)/shard_map/ppermute | solution.py:299
  46.2 2.4 %collective-permute-start.10 = (f32[320,128]{1,0:T(8,128)S(1)}, f32[320,128]{1,0:T(8,128)S(1)}, u32[]{:S(2)}, u32[]{:S(2)}) collective-permute-start(f32[320,128]{1,0:T(8,128)S(1)} %get-tuple-element.47), channel_id=1, source_target_pairs={{0,1},{1,0},{2,3},{3,2},{4,5},{5,4},{6,7},{7,6},{8,9},{9,8},{10,11... | collective-permute-start | bytes 491528 | tf_op jit(solution)/shard_map/ppermute | solution.py:299
  49.6 5.6 %collective-permute-done.8.straight = bf16[1088,128]{1,0:T(8,128)(2,1)S(1)} collective-permute-done((bf16[1088,128]{1,0:T(8,128)(2,1)S(1)}, bf16[1088,128]{1,0:T(8,128)(2,1)S(1)}, u32[]{:S(2)}, u32[]{:S(2)}) %collective-permute-start.8) | collective-permute-done | bytes 278560 | tf_op jit(solution)/shard_map/ppermute | solution.py:250
  55.2 1.3 %farthest.1 = (f32[448,128]{1,0:T(8,128)S(1)}, f32[448,128]{1,0:T(8,128)S(1)}) custom-call(bf16[1344,128]{1,0:T(8,128)(2,1)S(1)} %collective-permute-done.6.first, bf16[1344,128]{1,0:T(8,128)(2,1)S(1)} %collective-permute-done.7.second, bf16[1088,128]{1,0:T(8,128)(2,1)S(1)} %collective-permute-done.8.straight, ...), custom_call_target="tpu_custom_call" | custom-call | tf_op jit(solution)/shard_map/farthest/pallas_call | solution.py:199
  56.5 1.9 %collective-permute-start.11 = (f32[448,128]{1,0:T(8,128)S(1)}, f32[448,128]{1,0:T(8,128)S(1)}, u32[]{:S(2)}, u32[]{:S(2)}) collective-permute-start(f32[448,128]{1,0:T(8,128)S(1)} %get-tuple-element.52), channel_id=1, source_target_pairs={{0,1},{1,0},{2,3},{3,2},{4,5},{5,4},{6,7},{7,6},{8,9},{9,8},{10,11... | collective-permute-start | bytes 688136 | tf_op jit(solution)/shard_map/ppermute | solution.py:299
  58.4 1.5 %collective-permute-done.11.refs_7_ = f32[448,128]{1,0:T(8,128)S(1)} collective-permute-done((f32[448,128]{1,0:T(8,128)S(1)}, f32[448,128]{1,0:T(8,128)S(1)}, u32[]{:S(2)}, u32[]{:S(2)}) %collective-permute-start.11) | collective-permute-done | bytes 229408 | tf_op jit(solution)/shard_map/ppermute | solution.py:299
  60.5 28.4 %all_to_all.10 = f16[32,72,128]{2,1,0:T(8,128)(2,1)S(1)} all-to-all(f16[32,72,128]{2,1,0:T(8,128)(2,1)S(1)} %convert_element_type.16), channel_id=1, replica_groups=mesh['tm'=32,'space'=16] {'tm'}, dimensions={0} | all-to-all | bytes 1179648 | tf_op jit(solution)/shard_map/all_to_all | solution.py:340
  89.0 1.0 suffix.1
  90.1 24.2 %all_to_all.11 = f16[32,72,128]{2,1,0:T(8,128)(2,1)S(1)} all-to-all(f16[32,72,128]{2,1,0:T(8,128)(2,1)S(1)} %convert_element_type.18), channel_id=1, replica_groups=mesh['tm'=32,'space'=16] {'tm'}, dimensions={0} | all-to-all | bytes 1179648 | tf_op jit(solution)/shard_map/all_to_all | solution.py:340
  114.4 2.1 %last.1 = (f32[2048,128]{1,0:T(8,128)}, f32[64,128]{1,0:T(8,128)}) custom-call(f32[32,64,128]{2,1,0:T(8,128)S(1)} %get-tuple-element.56.refs_0_, f32[64,128]{1,0:T(8,128)S(1)} %get-tuple-element.57.refs_1_, f32[32,72,128]{2,1,0:T(8,128)S(1)} %convert_element_type.19.refs_2_, f32[32,128]{1,0:T(8,128)S(1)} %pad.9.refs_3_, f32[1,128]{1,0:T(1,128)S(1)} %get-tuple-element.61.refs_4_), custom_call_target="tpu_custom_call" | custom-call | tf_op jit(solution)/shard_map/last/pallas_call | solution.py:351
  (36 shorter events, 7.1 us)
Async XLA Ops:
  0.6 16.8 %copy-start = (f32[2048,128]{1,0:T(8,128)S(1)}, f32[2048,128]{1,0:T(8,128)}, u32[]{:S(2)}) copy-start(f32[2048,128]{1,0:T(8,128)} %param.10) | copy-start | bytes 3145732
  1.8 15.8 %collective-permute-start.2 = (bf16[1856,128]{1,0:T(8,128)(2,1)S(1)}, bf16[1856,128]{1,0:T(8,128)(2,1)S(1)}, u32[]{:S(2)}, u32[]{:S(2)}) collective-permute-start(bf16[1856,128]{1,0:T(8,128)(2,1)S(1)} %get-tuple-element.33.mine), channel_id=1, source_target_pairs={{0,2},{1,15},{2,4},{3,1},{4,6},{5,3},{6,8},{7,5},{8,10},{9,7},{10,... | collective-permute-start | bytes 1425416 | tf_op jit(solution)/shard_map/ppermute | solution.py:250
  5.3 7.1 %collective-permute-start = (bf16[1856,128]{1,0:T(8,128)(2,1)S(1)}, bf16[1856,128]{1,0:T(8,128)(2,1)S(1)}, u32[]{:S(2)}, u32[]{:S(2)}) collective-permute-start(bf16[1856,128]{1,0:T(8,128)(2,1)S(1)} %get-tuple-element.33.mine), channel_id=1, source_target_pairs={{0,1},{1,0},{2,3},{3,2},{4,5},{5,4},{6,7},{7,6},{8,9},{9,8},{10,11... | collective-permute-start | bytes 1425416 | tf_op jit(solution)/shard_map/ppermute | solution.py:256
  7.2 15.1 %collective-permute-start.1 = (bf16[256,128]{1,0:T(8,128)(2,1)S(1)}, bf16[256,128]{1,0:T(8,128)(2,1)S(1)}, u32[]{:S(2)}, u32[]{:S(2)}) collective-permute-start(bf16[256,128]{1,0:T(8,128)(2,1)S(1)} %get-tuple-element.34.mine_top), channel_id=1, source_target_pairs={{0,1},{1,0},{2,3},{3,2},{4,5},{5,4},{6,7},{7,6},{8,9},{9,8},{10,11... | collective-permute-start | bytes 196616 | tf_op jit(solution)/shard_map/ppermute | solution.py:257
  12.3 12.8 %collective-permute-start.3 = (bf16[1856,128]{1,0:T(8,128)(2,1)S(1)}, bf16[1856,128]{1,0:T(8,128)(2,1)S(1)}, u32[]{:S(2)}, u32[]{:S(2)}) collective-permute-start(bf16[1856,128]{1,0:T(8,128)(2,1)S(1)} %collective-permute-done.other), channel_id=1, source_target_pairs={{0,2},{1,15},{2,4},{3,1},{4,6},{5,3},{6,8},{7,5},{8,10},{9,7},{10,... | collective-permute-start | bytes 1425416 | tf_op jit(solution)/shard_map/ppermute | solution.py:250
  17.6 11.9 %collective-permute-start.4 = (bf16[1600,128]{1,0:T(8,128)(2,1)S(1)}, bf16[1600,128]{1,0:T(8,128)(2,1)S(1)}, u32[]{:S(2)}, u32[]{:S(2)}) collective-permute-start(bf16[1600,128]{1,0:T(8,128)(2,1)S(1)} %slice.20), channel_id=1, source_target_pairs={{0,2},{1,15},{2,4},{3,1},{4,6},{5,3},{6,8},{7,5},{8,10},{9,7},{10,... | collective-permute-start | bytes 1228808 | tf_op jit(solution)/shard_map/ppermute | solution.py:250
  25.2 11.1 %collective-permute-start.5 = (bf16[1600,128]{1,0:T(8,128)(2,1)S(1)}, bf16[1600,128]{1,0:T(8,128)(2,1)S(1)}, u32[]{:S(2)}, u32[]{:S(2)}) collective-permute-start(bf16[1600,128]{1,0:T(8,128)(2,1)S(1)} %slice.16), channel_id=1, source_target_pairs={{0,2},{1,15},{2,4},{3,1},{4,6},{5,3},{6,8},{7,5},{8,10},{9,7},{10,... | collective-permute-start | bytes 1228808 | tf_op jit(solution)/shard_map/ppermute | solution.py:250
  29.5 25.7 %collective-permute-start.6 = (bf16[1344,128]{1,0:T(8,128)(2,1)S(1)}, bf16[1344,128]{1,0:T(8,128)(2,1)S(1)}, u32[]{:S(2)}, u32[]{:S(2)}) collective-permute-start(bf16[1344,128]{1,0:T(8,128)(2,1)S(1)} %slice.17), channel_id=1, source_target_pairs={{0,2},{1,15},{2,4},{3,1},{4,6},{5,3},{6,8},{7,5},{8,10},{9,7},{10,... | collective-permute-start | bytes 1032200 | tf_op jit(solution)/shard_map/ppermute | solution.py:250
  36.2 19.0 %collective-permute-start.7 = (bf16[1344,128]{1,0:T(8,128)(2,1)S(1)}, bf16[1344,128]{1,0:T(8,128)(2,1)S(1)}, u32[]{:S(2)}, u32[]{:S(2)}) collective-permute-start(bf16[1344,128]{1,0:T(8,128)(2,1)S(1)} %slice.21), channel_id=1, source_target_pairs={{0,2},{1,15},{2,4},{3,1},{4,6},{5,3},{6,8},{7,5},{8,10},{9,7},{10,... | collective-permute-start | bytes 1032200 | tf_op jit(solution)/shard_map/ppermute | solution.py:250
  38.2 17.0 %collective-permute-start.8 = (bf16[1088,128]{1,0:T(8,128)(2,1)S(1)}, bf16[1088,128]{1,0:T(8,128)(2,1)S(1)}, u32[]{:S(2)}, u32[]{:S(2)}) collective-permute-start(bf16[1088,128]{1,0:T(8,128)(2,1)S(1)} %slice.19), channel_id=1, source_target_pairs={{0,4},{1,13},{2,6},{3,15},{4,8},{5,1},{6,10},{7,3},{8,12},{9,5},{1... | collective-permute-start | bytes 835592 | tf_op jit(solution)/shard_map/ppermute | solution.py:250
  43.5 5.1 %collective-permute-start.9 = (f32[320,128]{1,0:T(8,128)S(1)}, f32[320,128]{1,0:T(8,128)S(1)}, u32[]{:S(2)}, u32[]{:S(2)}) collective-permute-start(f32[320,128]{1,0:T(8,128)S(1)} %get-tuple-element.46), channel_id=1, source_target_pairs={{0,1},{1,0},{2,3},{3,2},{4,5},{5,4},{6,7},{7,6},{8,9},{9,8},{10,11... | collective-permute-start | bytes 491528 | tf_op jit(solution)/shard_map/ppermute | solution.py:299
  46.2 3.4 %collective-permute-start.10 = (f32[320,128]{1,0:T(8,128)S(1)}, f32[320,128]{1,0:T(8,128)S(1)}, u32[]{:S(2)}, u32[]{:S(2)}) collective-permute-start(f32[320,128]{1,0:T(8,128)S(1)} %get-tuple-element.47), channel_id=1, source_target_pairs={{0,1},{1,0},{2,3},{3,2},{4,5},{5,4},{6,7},{7,6},{8,9},{9,8},{10,11... | collective-permute-start | bytes 491528 | tf_op jit(solution)/shard_map/ppermute | solution.py:299
  56.5 3.4 %collective-permute-start.11 = (f32[448,128]{1,0:T(8,128)S(1)}, f32[448,128]{1,0:T(8,128)S(1)}, u32[]{:S(2)}, u32[]{:S(2)}) collective-permute-start(f32[448,128]{1,0:T(8,128)S(1)} %get-tuple-element.52), channel_id=1, source_target_pairs={{0,1},{1,0},{2,3},{3,2},{4,5},{5,4},{6,7},{7,6},{8,9},{9,8},{10,11... | collective-permute-start | bytes 688136 | tf_op jit(solution)/shard_map/ppermute | solution.py:299

commit v9 on v8

v9 whole, which is shorter than its diff:
```python
import jax
import jax.numpy as jnp
from jax import lax
from jax.experimental import pallas as pl
from jax.experimental.pallas import tpu as pltpu
from jax.sharding import PartitionSpec as P

CORES = 2
PAD = 8
TOP = 14.0
DECAY = 1024.0


def split3(x):
    hi = x.astype(jnp.bfloat16)
    rest = x - hi.astype(jnp.float32)
    mid = rest.astype(jnp.bfloat16)
    low = (rest - mid.astype(jnp.float32)).astype(jnp.bfloat16)
    return hi, mid, low


def dot(a, b):
    return jnp.dot(a, b, preferred_element_type=jnp.float32)


def border_times(border, tile):
    hi, mid, low = split3(tile)
    return dot(border, hi) + dot(border, mid) + dot(border, low)


def exponent(x):
    largest = jnp.max(jnp.abs(x), axis=0, keepdims=True)
    return jnp.ceil(jnp.log2(jnp.maximum(largest, 2.0**-100)))


def squared(x, level):
    unit = x * jnp.exp2(TOP / 2 - level)
    return unit * jnp.abs(unit)


def rooted(x, level):
    root = jnp.sqrt(jnp.abs(x))
    return jnp.where(x < 0, -root, root) * jnp.exp2(level - TOP / 2)


def encode(panel, pair, extra):
    at = lax.broadcasted_iota(jnp.int32, pair.shape, 0)
    level, pair_level = exponent(panel), exponent(pair)
    tail = jnp.where(at < 2, squared(pair, pair_level), extra)
    tail = jnp.where(at == 2, level, jnp.where(at == 3, pair_level, tail))
    return squared(panel, level), tail


def decode(message, rows):
    tail = message[rows:, :]
    at = lax.broadcasted_iota(jnp.int32, tail.shape, 0)
    panel = rooted(message[:rows, :], tail[2:3, :])
    return panel, jnp.where(at < 2, rooted(tail, tail[3:4, :]), 0.0)


def own_kernel(mine, other, tile, both_t, token):
    width = mine.shape[1]
    depth = both_t.shape[1]
    turned = jnp.concatenate([mine[:depth, :].T, other[:depth, :].T], axis=0)
    both_t[...] = turned
    got = dot(turned, mine[:depth, :])
    border = jnp.concatenate([mine[depth:, :], other[depth:, :]], axis=1)
    tile[: CORES * width, :] = got
    tile[CORES * width :, :] = border_times(border, got)
    token[...] = jnp.zeros_like(token)


def far_tiles(panels, both_t, keep, give):
    tall, width = panels[0].shape
    count = width * len(panels)
    depth = tall - (keep.shape[0] - count)
    joined = jnp.concatenate([p[:depth, :] for p in panels], axis=1)
    border = jnp.concatenate([p[depth:tall, :] for p in panels], axis=1)
    tile = dot(both_t[:, both_t.shape[1] - depth :], joined).T
    total = border_times(border, tile)
    for at, part in ((0, keep), (width, give)):
        part[:count, :] = tile[:, at : at + width]
        part[count:, :] = total[:, at : at + width]


def far_kernel(first, second, both_t, passed, keep, give, token):
    far_tiles((first, second), both_t, keep, give)
    token[...] = passed[...]


def three_kernel(first, second, straight, both_t, passed, keep, give, token, pair, single):
    count, width = CORES * first.shape[1], straight.shape[1]
    far_tiles((first, second), both_t, pair.at[0], pair.at[1])
    far_tiles((straight,), both_t, single.at[0], single.at[1])
    for at, out in enumerate((keep, give)):
        out[:count, :] = pair[at, :count, :]
        out[count : count + width, :] = single[at, :width, :]
        out[count + width :, :] = pair[at, count:, :] + single[at, width:, :]
    token[...] = passed[...]


def two_parts(decay):
    scaled = decay * DECAY
    high = scaled.astype(jnp.bfloat16).astype(jnp.float32)
    return high, (scaled - high) * 256


def message_kernel(rows, chips, hops, at, own, *refs):
    kept, given = refs[: hops - 1], refs[hops - 1 : 2 * hops - 2]
    tip, decay, out, copied, own_arrow, plain, done = refs[2 * hops - 2 :]
    width = own.shape[1]
    per = width // rows
    chip, core = at[0] // CORES, at[0] % CORES
    way = 1 - 2 * core

    def put(block, hop, parity):
        spot = lax.rem(chip + hop + chips, chips) * CORES + parity
        plain[pl.ds(spot * per, per), :, :] = block.reshape(per, rows, width)

    put(own[:width, :], 0, core)
    put(own[width : CORES * width, :], 0, 1 - core)
    for s in range(hops - 1):
        hop = (s + 1) * way
        put(kept[s][:width, :], -hop, core)
        put(given[s][:width, :], hop, 1 - core)
        put(kept[s][width : 2 * width, :], -hop, 1 - core)
        put(given[s][width : 2 * width, :], hop, core)
        if kept[s].shape[0] > 3 * width:
            put(kept[s][2 * width : 3 * width, :], hops, core)
            put(given[s][2 * width : 3 * width, :], hops, 1 - core)
    copy = pltpu.make_async_copy(plain, copied, done)
    copy.start()
    border = own_arrow.shape[0]
    total = own[CORES * width :, :]
    for part in (*kept, *given):
        total = total + part[part.shape[0] - border :, :]
    arrow = -lax.dot_general(
        tip[...],
        total,
        (((0,), (0,)), ((), ())),
        precision=lax.Precision.HIGHEST,
        preferred_element_type=jnp.float32,
    )
    own_arrow[...] = arrow
    fill = jnp.zeros((PAD - 2, width), jnp.float32)
    place = lax.broadcasted_iota(jnp.int32, (PAD, width), 0)
    by_col = decay[:, pl.ds(pl.multiple_of(at[0] * width, width), width)]
    col_high, col_low = two_parts(by_col)
    cols = jnp.where(place == 5, col_high, jnp.where(place == 6, col_low, 0.0))
    for r in range(out.shape[0]):
        by_row = jnp.concatenate(two_parts(decay[:, r * rows : (r + 1) * rows]), axis=1)
        extra = jnp.where(place == 4, by_row, cols)
        pair = jnp.concatenate([arrow[2 * r : 2 * r + 2, :], fill], axis=0)
        out[r, :rows, :], out[r, rows:, :] = encode(plain[r], pair, extra)
    copy.wait()


def scan_kernel(rows, at, got, sigma_end, arrow_end, out, turned):
    pieces, _, width = got.shape
    share = arrow_end.shape[0] // pieces
    for s in range(pieces):
        turned[s : s + 1, :] = got[s, rows + 4 : rows + 5, :]
    columns = turned[...].T
    columns = (columns[:rows, :] + columns[rows : 2 * rows, :] * (1 / 256)) * (1 / DECAY)
    carry = sigma_end[pl.ds(pl.multiple_of(at[0] * rows, rows), rows), :]
    place = lax.broadcasted_iota(jnp.int32, (PAD, width), 0)
    pair = jnp.zeros((PAD, width), jnp.float32)
    for r in range(share):
        pair = jnp.where(place == r, arrow_end[pl.ds(at[0] * share + r, 1), :], pair)
    for s in range(pieces - 1, -1, -1):
        out[s, :rows, :], out[s, rows:, :] = encode(carry, pair, jnp.zeros_like(pair))
        if s == 0:
            break
        panel, arrow = decode(got[s], rows)
        by_col = (got[s, rows + 5 : rows + 6, :] + got[s, rows + 6 : rows + 7, :] * (1 / 256)) * (1 / DECAY)
        by_row = jnp.broadcast_to(columns[:, s : s + 1], (rows, width))
        carry = panel + by_row * by_col * carry
        pair = arrow + by_col * pair


def last_kernel(rows, at, plain, own_arrow, got, decay, sigma, arrows, turned):
    pieces, _, width = plain.shape
    for r in range(pieces):
        turned[r : r + 1, :rows] = decay[:, r * rows : (r + 1) * rows]
        turned[r : r + 1, rows:] = jnp.zeros((1, width - rows), jnp.float32)
    columns = turned[...].T[:rows, :]
    by_col = decay[:, pl.ds(pl.multiple_of(at[0] * width, width), width)]
    for r in range(pieces):
        later, later_arrow = decode(got[r], rows)
        by_row = jnp.broadcast_to(columns[:, r : r + 1], later.shape)
        sigma[r * rows : (r + 1) * rows, :] = plain[r] + by_row * by_col * later
        pair = slice(2 * r, 2 * r + 2)
        arrows[pair, :] = own_arrow[pair, :] + by_col * later_arrow[:2, :]


VMEM = pl.BlockSpec(memory_space=pltpu.VMEM)
SMEM = pl.BlockSpec(memory_space=pltpu.SMEM)


SMALL = pltpu.CompilerParams(vmem_limit_bytes=12 << 20)


def near(x):
    return pltpu.with_memory_space_constraint(x, pltpu.VMEM)


def body(inverse_factor, arrow_factor, decay, tip_inverse, sigma_end, arrow_end):
    factor_cols = inverse_factor[0]
    order, width = factor_cols.shape
    arrow = tip_inverse.shape[0]
    pieces, devices = lax.axis_size("tm"), lax.axis_size("space")
    chips, cut = devices // CORES, CORES * width
    rows, both, hops = order // pieces, CORES * width, chips // 2
    f32, bf16 = jnp.float32, jnp.bfloat16
    column_at = lax.axis_index("space").reshape(1)
    piece_at = lax.axis_index("tm").reshape(1)
    hbm = pl.BlockSpec(memory_space=pltpu.HBM)

    def pack_kernel(cols, border, out, done):
        copies = [
            pltpu.make_async_copy(cols, out.at[pl.ds(0, order)], done.at[0]),
            pltpu.make_async_copy(border, out.at[pl.ds(order, arrow)], done.at[1]),
        ]
        for copy in copies:
            copy.start()
        for copy in copies:
            copy.wait()

    mine = pl.pallas_call(
        pack_kernel,
        out_shape=pltpu.VMEM((order + arrow, width), bf16),
        in_specs=[hbm, hbm],
        out_specs=VMEM,
        scratch_shapes=[pltpu.SemaphoreType.DMA((2,))],
        compiler_params=SMALL,
        name="pack",
    )(*[pltpu.with_memory_space_constraint(x, pltpu.HBM) for x in (factor_cols, arrow_factor[0])])

    def hop(panel, count=1):
        pairs = []
        for p in range(devices):
            chip, core = p // CORES, p % CORES
            pairs.append((p, (chip + count * (1 - 2 * core)) % chips * CORES + core))
        return lax.ppermute(panel, "space", pairs)

    def swap(tile):
        return lax.ppermute(tile, "space", [(p, p ^ 1) for p in range(devices)])

    def shared(panel, count):
        return panel[cut * count - (order + arrow - panel.shape[0]) :]

    def product(kernel, name, count, panels, token, scratch=()):
        tall = count * width + arrow
        return pl.pallas_call(
            kernel,
            out_shape=(*[jax.ShapeDtypeStruct((tall, width), f32)] * 2, mark),
            in_specs=[VMEM] * (len(panels) + 2),
            out_specs=(VMEM,) * 3,
            scratch_shapes=scratch,
            compiler_params=SMALL,
            name=name,
        )(*map(near, panels), near(both_t), token)

    first = hop(shared(mine, 1))
    other = swap(mine)
    second = hop(shared(other, 1))
    mark = jax.ShapeDtypeStruct((8, width), f32)
    own, both_t, token = pl.pallas_call(
        own_kernel,
        out_shape=(pltpu.VMEM((both + arrow, width), f32), pltpu.VMEM((both, order), bf16), mark),
        in_specs=[VMEM] * 2,
        out_specs=(VMEM,) * 3,
        compiler_params=SMALL,
        name="own",
    )(near(mine), near(other))

    first_2 = hop(shared(first, 2))
    second, token = lax.optimization_barrier((second, token))
    second_2 = hop(shared(second, 2))
    keep_1, give_1, token = product(far_kernel, "far", 2, (first, second), token)
    first_2, token = lax.optimization_barrier((first_2, token))
    first_4 = hop(shared(first_2, 4), 2)
    first_3 = hop(shared(first_2, 3))
    second_3 = hop(shared(second_2, 3))
    given_1 = swap(give_1)
    token, given_1 = lax.optimization_barrier((token, given_1))
    keep_2, give_2, token = product(
        three_kernel,
        "three",
        3,
        (first_2, second_2, first_4),
        token,
        [pltpu.VMEM((2, both + arrow, width), f32), pltpu.VMEM((2, width + arrow, width), f32)],
    )
    given_2 = swap(give_2)
    keep_3, give_3, token = product(far_kernel, "far", 2, (first_3, second_3), token)
    kept, given = (keep_1, keep_2, keep_3), (given_1, given_2, swap(give_3))

    message = (pieces, rows + PAD, width)
    sent, plain, own_arrow = pl.pallas_call(
        lambda *refs: message_kernel(rows, chips, hops, *refs),
        out_shape=(
            pltpu.VMEM(message, f32),
            jax.ShapeDtypeStruct((pieces, rows, width), f32),
            jax.ShapeDtypeStruct((arrow, width), f32),
        ),
        in_specs=[SMEM] + [VMEM] * (2 * hops + 1),
        out_specs=(VMEM, pl.BlockSpec(memory_space=pl.ANY), VMEM),
        scratch_shapes=[pltpu.VMEM((pieces, rows, width), f32), pltpu.SemaphoreType.DMA],
        compiler_params=SMALL,
        name="message",
    )(column_at, *map(near, (own, *kept, *given, tip_inverse, decay)))

    def exchange(values):
        moved = lax.all_to_all(values.astype(jnp.float16), "tm", 0, 0, tiled=True)
        return moved.astype(jnp.float32)

    ahead = pl.pallas_call(
        lambda *refs: scan_kernel(rows, *refs),
        out_shape=pltpu.VMEM(message, f32),
        in_specs=[SMEM] + [VMEM] * 3,
        out_specs=VMEM,
        scratch_shapes=[pltpu.VMEM((pieces, width), f32)],
        compiler_params=SMALL,
        name="suffix",
    )(piece_at, *map(near, (exchange(sent), sigma_end, arrow_end.T)))
    sigma, arrows = pl.pallas_call(
        lambda *refs: last_kernel(rows, *refs),
        out_shape=(jax.ShapeDtypeStruct((order, width), f32), jax.ShapeDtypeStruct((arrow, width), f32)),
        in_specs=[SMEM] + [VMEM] * 4,
        scratch_shapes=[pltpu.VMEM((pieces, width), f32)],
        compiler_params=SMALL,
        name="last",
    )(column_at, *map(near, (plain, own_arrow, exchange(ahead), decay)))
    return sigma[None], arrows.T[None]


def solution(mesh):
    placed = (
        P("tm", None, "space"),
        P("tm", None, "space"),
        P("tm", None),
        P(),
        P(None, "space"),
        P("space", None),
    )
    return jax.shard_map(
        body,
        mesh=mesh,
        in_specs=placed,
        out_specs=(P("tm", None, "space"), P("tm", "space", None)),
        check_vma=False,
    )
```

time: 117 us -> 111 us (0.949)
  the two profiles are of different devices: /device:TPU:8 before, /device:TPU:64 now
where the time goes in v9:
time: 111 us
  starting transfers between devices  44 us (40%)
  waiting for transfers between devices  32.5 us (29%)
  blocking collectives  23.4 us (21%)
  Pallas kernels  8.38 us (8%)
  other arithmetic  1.13 us (1%)
    ppermute x7, starting transfers between devices, hop(): return lax.ppermute(panel, 'space', pairs)  23.5 us
    all_to_all x1, blocking collectives, exchange(): moved = lax.all_to_all(values.astype(jnp.float16), 'tm', 0, 0, tiled=True)  23.4 us
    all_to_all x1, waiting for transfers between devices, exchange(): moved = lax.all_to_all(values.astype(jnp.float16), 'tm', 0, 0, tiled=True)  19.3 us
    all_to_all x1, starting transfers between devices, exchange(): moved = lax.all_to_all(values.astype(jnp.float16), 'tm', 0, 0, tiled=True)  12.6 us
    ppermute x7, waiting for transfers between devices, hop(): return lax.ppermute(panel, 'space', pairs)  10.7 us
    ppermute x4, starting transfers between devices, swap(): return lax.ppermute(tile, 'space', [(p, p ^ 1) for p in range(devices)])  7.96 us
    pallas_call x3, Pallas kernels, product(): pl.pallas_call(kernel, out_shape=(*[jax.ShapeDtypeStruct((tall, width), f...  3.33 us
    ppermute x4, waiting for transfers between devices, swap(): return lax.ppermute(tile, 'space', [(p, p ^ 1) for p in range(devices)])  2.56 us
  transfers between devices with their start and end apart: 12, of which 7 were waited for; matrix products, arithmetic and copies ran while one was open for 0% of the time, Pallas kernels for 4%

profile of v9, /device:TPU:64, one launch (start us, length us, event | category | flops | bytes accessed | tf_op | source)
XLA Modules:
  0.0 110.6 jit_solution(6821153086219091782)
XLA Ops:
  0.6 1.1 pack.1.mine
  1.7 1.9 %collective-permute-start = (bf16[2112,128]{1,0:T(8,128)(2,1)S(1)}, bf16[2112,128]{1,0:T(8,128)(2,1)S(1)}, u32[]{:S(2)}, u32[]{:S(2)}) collective-permute-start(bf16[2112,128]{1,0:T(8,128)(2,1)S(1)} %pack.1.mine), channel_id=1, source_target_pairs={{0,1},{1,0},{2,3},{3,2},{4,5},{5,4},{6,7},{7,6},{8,9},{9,8},{10,11... | collective-permute-start | bytes 1622024 | tf_op jit(solution)/shard_map/ppermute | solution.py:247
  3.7 3.5 %collective-permute-start.1 = (bf16[1856,128]{1,0:T(8,128)(2,1)S(1)}, bf16[1856,128]{1,0:T(8,128)(2,1)S(1)}, u32[]{:S(2)}, u32[]{:S(2)}) collective-permute-start(bf16[1856,128]{1,0:T(8,128)(2,1)S(1)} %slice.28), channel_id=1, source_target_pairs={{0,2},{1,15},{2,4},{3,1},{4,6},{5,3},{6,8},{7,5},{8,10},{9,7},{10,... | collective-permute-start | bytes 1425416 | tf_op jit(solution)/shard_map/ppermute | solution.py:244
  7.2 3.5 %collective-permute-start.2 = (bf16[1856,128]{1,0:T(8,128)(2,1)S(1)}, bf16[1856,128]{1,0:T(8,128)(2,1)S(1)}, u32[]{:S(2)}, u32[]{:S(2)}) collective-permute-start(bf16[1856,128]{1,0:T(8,128)(2,1)S(1)} %slice.29), channel_id=1, source_target_pairs={{0,2},{1,15},{2,4},{3,1},{4,6},{5,3},{6,8},{7,5},{8,10},{9,7},{10,... | collective-permute-start | bytes 1425416 | tf_op jit(solution)/shard_map/ppermute | solution.py:244
  10.7 5.0 %collective-permute-done.1.first = bf16[1856,128]{1,0:T(8,128)(2,1)S(1)} collective-permute-done((bf16[1856,128]{1,0:T(8,128)(2,1)S(1)}, bf16[1856,128]{1,0:T(8,128)(2,1)S(1)}, u32[]{:S(2)}, u32[]{:S(2)}) %collective-permute-start.1) | collective-permute-done | bytes 475168 | tf_op jit(solution)/shard_map/ppermute | solution.py:244
  15.7 2.0 %collective-permute-start.3 = (bf16[1600,128]{1,0:T(8,128)(2,1)S(1)}, bf16[1600,128]{1,0:T(8,128)(2,1)S(1)}, u32[]{:S(2)}, u32[]{:S(2)}) collective-permute-start(bf16[1600,128]{1,0:T(8,128)(2,1)S(1)} %slice.30), channel_id=1, source_target_pairs={{0,2},{1,15},{2,4},{3,1},{4,6},{5,3},{6,8},{7,5},{8,10},{9,7},{10,... | collective-permute-start | bytes 1228808 | tf_op jit(solution)/shard_map/ppermute | solution.py:244
  18.4 2.4 %collective-permute-done.2.second = bf16[1856,128]{1,0:T(8,128)(2,1)S(1)} collective-permute-done((bf16[1856,128]{1,0:T(8,128)(2,1)S(1)}, bf16[1856,128]{1,0:T(8,128)(2,1)S(1)}, u32[]{:S(2)}, u32[]{:S(2)}) %collective-permute-start.2) | collective-permute-done | bytes 475168 | tf_op jit(solution)/shard_map/ppermute | solution.py:244
  20.8 2.0 %collective-permute-start.4 = (bf16[1600,128]{1,0:T(8,128)(2,1)S(1)}, bf16[1600,128]{1,0:T(8,128)(2,1)S(1)}, u32[]{:S(2)}, u32[]{:S(2)}) collective-permute-start(bf16[1600,128]{1,0:T(8,128)(2,1)S(1)} %slice.24), channel_id=1, source_target_pairs={{0,2},{1,15},{2,4},{3,1},{4,6},{5,3},{6,8},{7,5},{8,10},{9,7},{10,... | collective-permute-start | bytes 1228808 | tf_op jit(solution)/shard_map/ppermute | solution.py:244
  23.6 3.1 %collective-permute-done.3.first = bf16[1600,128]{1,0:T(8,128)(2,1)S(1)} collective-permute-done((bf16[1600,128]{1,0:T(8,128)(2,1)S(1)}, bf16[1600,128]{1,0:T(8,128)(2,1)S(1)}, u32[]{:S(2)}, u32[]{:S(2)}) %collective-permute-start.3) | collective-permute-done | bytes 409632 | tf_op jit(solution)/shard_map/ppermute | solution.py:244
  26.8 2.9 %collective-permute-start.5 = (bf16[1088,128]{1,0:T(8,128)(2,1)S(1)}, bf16[1088,128]{1,0:T(8,128)(2,1)S(1)}, u32[]{:S(2)}, u32[]{:S(2)}) collective-permute-start(bf16[1088,128]{1,0:T(8,128)(2,1)S(1)} %slice.25), channel_id=1, source_target_pairs={{0,4},{1,13},{2,6},{3,15},{4,8},{5,1},{6,10},{7,3},{8,12},{9,5},{1... | collective-permute-start | bytes 835592 | tf_op jit(solution)/shard_map/ppermute | solution.py:244
  29.7 4.4 %collective-permute-start.7 = (bf16[1344,128]{1,0:T(8,128)(2,1)S(1)}, bf16[1344,128]{1,0:T(8,128)(2,1)S(1)}, u32[]{:S(2)}, u32[]{:S(2)}) collective-permute-start(bf16[1344,128]{1,0:T(8,128)(2,1)S(1)} %slice.26), channel_id=1, source_target_pairs={{0,2},{1,15},{2,4},{3,1},{4,6},{5,3},{6,8},{7,5},{8,10},{9,7},{10,... | collective-permute-start | bytes 1032200 | tf_op jit(solution)/shard_map/ppermute | solution.py:244
  34.2 5.2 %collective-permute-start.8 = (bf16[1344,128]{1,0:T(8,128)(2,1)S(1)}, bf16[1344,128]{1,0:T(8,128)(2,1)S(1)}, u32[]{:S(2)}, u32[]{:S(2)}) collective-permute-start(bf16[1344,128]{1,0:T(8,128)(2,1)S(1)} %slice.31), channel_id=1, source_target_pairs={{0,2},{1,15},{2,4},{3,1},{4,6},{5,3},{6,8},{7,5},{8,10},{9,7},{10,... | collective-permute-start | bytes 1032200 | tf_op jit(solution)/shard_map/ppermute | solution.py:244
  39.3 1.9 %collective-permute-start.6 = (f32[320,128]{1,0:T(8,128)S(1)}, f32[320,128]{1,0:T(8,128)S(1)}, u32[]{:S(2)}, u32[]{:S(2)}) collective-permute-start(f32[320,128]{1,0:T(8,128)S(1)} %get-tuple-element.33), channel_id=1, source_target_pairs={{0,1},{1,0},{2,3},{3,2},{4,5},{5,4},{6,7},{7,6},{8,9},{9,8},{10,11... | collective-permute-start | bytes 491528 | tf_op jit(solution)/shard_map/ppermute | solution.py:247
  41.2 1.4 %collective-permute-done.6.refs_5_ = f32[320,128]{1,0:T(8,128)S(1)} collective-permute-done((f32[320,128]{1,0:T(8,128)S(1)}, f32[320,128]{1,0:T(8,128)S(1)}, u32[]{:S(2)}, u32[]{:S(2)}) %collective-permute-start.6) | collective-permute-done | bytes 163872 | tf_op jit(solution)/shard_map/ppermute | solution.py:247
  42.6 1.4 %three.1 = (f32[448,128]{1,0:T(8,128)S(1)}, f32[448,128]{1,0:T(8,128)S(1)}, f32[8,128]{1,0:T(8,128)S(1)}) custom-call(bf16[1600,128]{1,0:T(8,128)(2,1)S(1)} %collective-permute-done.3.first, bf16[1600,128]{1,0:T(8,128)(2,1)S(1)} %collective-permute-done.4.second, bf16[1088,128]{1,0:T(8,128)(2,1)S(1)} %collective-permute-done.5.straight, ...), custom_call_target="tpu_custom_call" | custom-call | tf_op jit(solution)/shard_map/three/pallas_call | solution.py:254
  44.0 2.1 %collective-permute-start.9 = (f32[448,128]{1,0:T(8,128)S(1)}, f32[448,128]{1,0:T(8,128)S(1)}, u32[]{:S(2)}, u32[]{:S(2)}) collective-permute-start(f32[448,128]{1,0:T(8,128)S(1)} %get-tuple-element.39), channel_id=1, source_target_pairs={{0,1},{1,0},{2,3},{3,2},{4,5},{5,4},{6,7},{7,6},{8,9},{9,8},{10,11... | collective-permute-start | bytes 688136 | tf_op jit(solution)/shard_map/ppermute | solution.py:247
  46.3 1.2 %far.3 = (f32[320,128]{1,0:T(8,128)S(1)}, f32[320,128]{1,0:T(8,128)S(1)}, f32[8,128]{1,0:T(8,128)}) custom-call(bf16[1344,128]{1,0:T(8,128)(2,1)S(1)} %collective-permute-done.7.first, bf16[1344,128]{1,0:T(8,128)(2,1)S(1)} %collective-permute-done.8.second, bf16[256,2048]{1,0:T(8,128)(2,1)S(1)} %get-tuple-element.27.both_t, ...), custom_call_target="tpu_custom_call" | custom-call | tf_op jit(solution)/shard_map/far/pallas_call | solution.py:254
  47.5 2.1 %collective-permute-start.10 = (f32[320,128]{1,0:T(8,128)S(1)}, f32[320,128]{1,0:T(8,128)S(1)}, u32[]{:S(2)}, u32[]{:S(2)}) collective-permute-start(f32[320,128]{1,0:T(8,128)S(1)} %get-tuple-element.40), channel_id=1, source_target_pairs={{0,1},{1,0},{2,3},{3,2},{4,5},{5,4},{6,7},{7,6},{8,9},{9,8},{10,11... | collective-permute-start | bytes 491528 | tf_op jit(solution)/shard_map/ppermute | solution.py:247
  49.6 1.2 %collective-permute-done.10.refs_7_ = f32[320,128]{1,0:T(8,128)S(1)} collective-permute-done((f32[320,128]{1,0:T(8,128)S(1)}, f32[320,128]{1,0:T(8,128)S(1)}, u32[]{:S(2)}, u32[]{:S(2)}) %collective-permute-start.10) | collective-permute-done | bytes 163872 | tf_op jit(solution)/shard_map/ppermute | solution.py:247
  52.2 12.6 %all-to-all-start = ((f16[32,72,128]{2,1,0:T(8,128)(2,1)}), f16[32,72,128]{2,1,0:T(8,128)(2,1)S(1)}, u32[]{:S(2)}, u32[]{:S(2)}) async-start(f16[32,72,128]{2,1,0:T(8,128)(2,1)} %convert_element_type.12), calls=%async_computation | async-start | bytes 1179648 | tf_op jit(solution)/shard_map/all_to_all | solution.py:315
  64.9 19.3 %all-to-all-done = f16[32,72,128]{2,1,0:T(8,128)(2,1)S(1)} async-done(((f16[32,72,128]{2,1,0:T(8,128)(2,1)}), f16[32,72,128]{2,1,0:T(8,128)(2,1)S(1)}, u32[]{:S(2)}, u32[]{:S(2)}) %all-to-all-start) | async-done | bytes 589856 | tf_op jit(solution)/shard_map/all_to_all | solution.py:315
  84.3 1.0 suffix.1
  85.4 23.4 %all_to_all.10 = f16[32,72,128]{2,1,0:T(8,128)(2,1)S(1)} all-to-all(f16[32,72,128]{2,1,0:T(8,128)(2,1)S(1)} %convert_element_type.14), channel_id=1, replica_groups=mesh['tm'=32,'space'=16] {'tm'}, dimensions={0} | all-to-all | bytes 1179648 | tf_op jit(solution)/shard_map/all_to_all | solution.py:315
  108.9 1.7 %last.1 = (f32[2048,128]{1,0:T(8,128)}, f32[64,128]{1,0:T(8,128)}) custom-call(s32[1]{0:T(128)} %bitcast.refs_0_, f32[32,64,128]{2,1,0:T(8,128)S(1)} %get-tuple-element.41.refs_1_, f32[64,128]{1,0:T(8,128)S(1)} %get-tuple-element.42.refs_2_, f32[32,72,128]{2,1,0:T(8,128)S(1)} %convert_element_type.15.refs_3_, f32[1,2048]{1,0:T(1,128)S(1)} %copy-done.2), custom_call_target="tpu_custom_call" | custom-call | tf_op jit(solution)/shard_map/last/pallas_call | solution.py:327
  (28 shorter events, 3.6 us)
Async XLA Ops:
  1.7 5.5 %collective-permute-start = (bf16[2112,128]{1,0:T(8,128)(2,1)S(1)}, bf16[2112,128]{1,0:T(8,128)(2,1)S(1)}, u32[]{:S(2)}, u32[]{:S(2)}) collective-permute-start(bf16[2112,128]{1,0:T(8,128)(2,1)S(1)} %pack.1.mine), channel_id=1, source_target_pairs={{0,1},{1,0},{2,3},{3,2},{4,5},{5,4},{6,7},{7,6},{8,9},{9,8},{10,11... | collective-permute-start | bytes 1622024 | tf_op jit(solution)/shard_map/ppermute | solution.py:247
  3.7 12.0 %collective-permute-start.1 = (bf16[1856,128]{1,0:T(8,128)(2,1)S(1)}, bf16[1856,128]{1,0:T(8,128)(2,1)S(1)}, u32[]{:S(2)}, u32[]{:S(2)}) collective-permute-start(bf16[1856,128]{1,0:T(8,128)(2,1)S(1)} %slice.28), channel_id=1, source_target_pairs={{0,2},{1,15},{2,4},{3,1},{4,6},{5,3},{6,8},{7,5},{8,10},{9,7},{10,... | collective-permute-start | bytes 1425416 | tf_op jit(solution)/shard_map/ppermute | solution.py:244
  7.2 13.6 %collective-permute-start.2 = (bf16[1856,128]{1,0:T(8,128)(2,1)S(1)}, bf16[1856,128]{1,0:T(8,128)(2,1)S(1)}, u32[]{:S(2)}, u32[]{:S(2)}) collective-permute-start(bf16[1856,128]{1,0:T(8,128)(2,1)S(1)} %slice.29), channel_id=1, source_target_pairs={{0,2},{1,15},{2,4},{3,1},{4,6},{5,3},{6,8},{7,5},{8,10},{9,7},{10,... | collective-permute-start | bytes 1425416 | tf_op jit(solution)/shard_map/ppermute | solution.py:244
  15.7 11.1 %collective-permute-start.3 = (bf16[1600,128]{1,0:T(8,128)(2,1)S(1)}, bf16[1600,128]{1,0:T(8,128)(2,1)S(1)}, u32[]{:S(2)}, u32[]{:S(2)}) collective-permute-start(bf16[1600,128]{1,0:T(8,128)(2,1)S(1)} %slice.30), channel_id=1, source_target_pairs={{0,2},{1,15},{2,4},{3,1},{4,6},{5,3},{6,8},{7,5},{8,10},{9,7},{10,... | collective-permute-start | bytes 1228808 | tf_op jit(solution)/shard_map/ppermute | solution.py:244
  20.8 13.3 %collective-permute-start.4 = (bf16[1600,128]{1,0:T(8,128)(2,1)S(1)}, bf16[1600,128]{1,0:T(8,128)(2,1)S(1)}, u32[]{:S(2)}, u32[]{:S(2)}) collective-permute-start(bf16[1600,128]{1,0:T(8,128)(2,1)S(1)} %slice.24), channel_id=1, source_target_pairs={{0,2},{1,15},{2,4},{3,1},{4,6},{5,3},{6,8},{7,5},{8,10},{9,7},{10,... | collective-permute-start | bytes 1228808 | tf_op jit(solution)/shard_map/ppermute | solution.py:244
  26.8 15.8 %collective-permute-start.5 = (bf16[1088,128]{1,0:T(8,128)(2,1)S(1)}, bf16[1088,128]{1,0:T(8,128)(2,1)S(1)}, u32[]{:S(2)}, u32[]{:S(2)}) collective-permute-start(bf16[1088,128]{1,0:T(8,128)(2,1)S(1)} %slice.25), channel_id=1, source_target_pairs={{0,4},{1,13},{2,6},{3,15},{4,8},{5,1},{6,10},{7,3},{8,12},{9,5},{1... | collective-permute-start | bytes 835592 | tf_op jit(solution)/shard_map/ppermute | solution.py:244
  29.7 16.4 %collective-permute-start.7 = (bf16[1344,128]{1,0:T(8,128)(2,1)S(1)}, bf16[1344,128]{1,0:T(8,128)(2,1)S(1)}, u32[]{:S(2)}, u32[]{:S(2)}) collective-permute-start(bf16[1344,128]{1,0:T(8,128)(2,1)S(1)} %slice.26), channel_id=1, source_target_pairs={{0,2},{1,15},{2,4},{3,1},{4,6},{5,3},{6,8},{7,5},{8,10},{9,7},{10,... | collective-permute-start | bytes 1032200 | tf_op jit(solution)/shard_map/ppermute | solution.py:244
  34.2 12.1 %collective-permute-start.8 = (bf16[1344,128]{1,0:T(8,128)(2,1)S(1)}, bf16[1344,128]{1,0:T(8,128)(2,1)S(1)}, u32[]{:S(2)}, u32[]{:S(2)}) collective-permute-start(bf16[1344,128]{1,0:T(8,128)(2,1)S(1)} %slice.31), channel_id=1, source_target_pairs={{0,2},{1,15},{2,4},{3,1},{4,6},{5,3},{6,8},{7,5},{8,10},{9,7},{10,... | collective-permute-start | bytes 1032200 | tf_op jit(solution)/shard_map/ppermute | solution.py:244
  39.3 3.3 %collective-permute-start.6 = (f32[320,128]{1,0:T(8,128)S(1)}, f32[320,128]{1,0:T(8,128)S(1)}, u32[]{:S(2)}, u32[]{:S(2)}) collective-permute-start(f32[320,128]{1,0:T(8,128)S(1)} %get-tuple-element.33), channel_id=1, source_target_pairs={{0,1},{1,0},{2,3},{3,2},{4,5},{5,4},{6,7},{7,6},{8,9},{9,8},{10,11... | collective-permute-start | bytes 491528 | tf_op jit(solution)/shard_map/ppermute | solution.py:247
  44.0 6.8 %copy-start.2 = (f32[1,2048]{1,0:T(1,128)S(1)}, f32[1,2048]{1,0:T(1,128)}, u32[]{:S(2)}) copy-start(f32[1,2048]{1,0:T(1,128)} %refs_4_.1) | copy-start | bytes 24580
  44.0 6.8 %copy-start.3 = (f32[64,64]{1,0:T(8,128)S(1)}, f32[64,64]{1,0:T(8,128)}, u32[]{:S(2)}) copy-start(f32[64,64]{1,0:T(8,128)} %refs_8_.1) | copy-start | bytes 49156
  44.0 5.5 %collective-permute-start.9 = (f32[448,128]{1,0:T(8,128)S(1)}, f32[448,128]{1,0:T(8,128)S(1)}, u32[]{:S(2)}, u32[]{:S(2)}) collective-permute-start(f32[448,128]{1,0:T(8,128)S(1)} %get-tuple-element.39), channel_id=1, source_target_pairs={{0,1},{1,0},{2,3},{3,2},{4,5},{5,4},{6,7},{7,6},{8,9},{9,8},{10,11... | collective-permute-start | bytes 688136 | tf_op jit(solution)/shard_map/ppermute | solution.py:247
  47.5 3.3 %collective-permute-start.10 = (f32[320,128]{1,0:T(8,128)S(1)}, f32[320,128]{1,0:T(8,128)S(1)}, u32[]{:S(2)}, u32[]{:S(2)}) collective-permute-start(f32[320,128]{1,0:T(8,128)S(1)} %get-tuple-element.40), channel_id=1, source_target_pairs={{0,1},{1,0},{2,3},{3,2},{4,5},{5,4},{6,7},{7,6},{8,9},{9,8},{10,11... | collective-permute-start | bytes 491528 | tf_op jit(solution)/shard_map/ppermute | solution.py:247
  52.2 31.9 %all-to-all-start = ((f16[32,72,128]{2,1,0:T(8,128)(2,1)}), f16[32,72,128]{2,1,0:T(8,128)(2,1)S(1)}, u32[]{:S(2)}, u32[]{:S(2)}) async-start(f16[32,72,128]{2,1,0:T(8,128)(2,1)} %convert_element_type.12), calls=%async_computation | async-start | bytes 1179648 | tf_op jit(solution)/shard_map/all_to_all | solution.py:315
  64.8 19.4 %copy-start = (f32[2048,128]{1,0:T(8,128)S(1)}, f32[2048,128]{1,0:T(8,128)}, u32[]{:S(2)}) copy-start(f32[2048,128]{1,0:T(8,128)} %refs_2_.1) | copy-start | bytes 3145732
  64.9 19.4 %copy-start.1 = (f32[128,64]{0,1:T(8,128)S(1)}, f32[128,64]{0,1:T(8,128)}, u32[]{:S(2)}) copy-start(f32[128,64]{0,1:T(8,128)} %param.11) | copy-start | bytes 98308

commit v10 on v9

--- a/solution.py
+++ b/solution.py
@@ -39,8 +39,7 @@
 
 
 def rooted(x, level):
-    root = jnp.sqrt(jnp.abs(x))
-    return jnp.where(x < 0, -root, root) * jnp.exp2(level - TOP / 2)
+    return x * (lax.rsqrt(jnp.maximum(jnp.abs(x), 2.0**-60)) * jnp.exp2(level - TOP / 2))
 
 
 def encode(panel, pair, extra):
@@ -58,9 +57,19 @@
     return panel, jnp.where(at < 2, rooted(tail, tail[3:4, :]), 0.0)
 
 
-def own_kernel(mine, other, tile, both_t, token):
+def own_kernel(at, mine, other, sigma_end, arrow_end, tile, both_t, end, token, done):
     width = mine.shape[1]
     depth = both_t.shape[1]
+    rows = end.shape[0] - PAD
+    share = arrow_end.shape[0] * rows // depth
+    spot = pl.ds(pl.multiple_of(at[0] * rows, rows), rows)
+    copy = pltpu.make_async_copy(sigma_end.at[spot], end.at[pl.ds(0, rows)], done)
+    copy.start()
+    place = lax.broadcasted_iota(jnp.int32, (PAD, width), 0)
+    pair = jnp.zeros((PAD, width), jnp.float32)
+    for r in range(share):
+        pair = jnp.where(place == r, arrow_end[pl.ds(at[0] * share + r, 1), :], pair)
+    end[rows:, :] = pair
     turned = jnp.concatenate([mine[:depth, :].T, other[:depth, :].T], axis=0)
     both_t[...] = turned
     got = dot(turned, mine[:depth, :])
@@ -68,6 +77,7 @@
     tile[: CORES * width, :] = got
     tile[CORES * width :, :] = border_times(border, got)
     token[...] = jnp.zeros_like(token)
+    copy.wait()
 
 
 def far_tiles(panels, both_t, keep, give):
@@ -155,18 +165,13 @@
     copy.wait()
 
 
-def scan_kernel(rows, at, got, sigma_end, arrow_end, out, turned):
+def scan_kernel(rows, got, end, out, turned):
     pieces, _, width = got.shape
-    share = arrow_end.shape[0] // pieces
     for s in range(pieces):
         turned[s : s + 1, :] = got[s, rows + 4 : rows + 5, :]
     columns = turned[...].T
     columns = (columns[:rows, :] + columns[rows : 2 * rows, :] * (1 / 256)) * (1 / DECAY)
-    carry = sigma_end[pl.ds(pl.multiple_of(at[0] * rows, rows), rows), :]
-    place = lax.broadcasted_iota(jnp.int32, (PAD, width), 0)
-    pair = jnp.zeros((PAD, width), jnp.float32)
-    for r in range(share):
-        pair = jnp.where(place == r, arrow_end[pl.ds(at[0] * share + r, 1), :], pair)
+    carry, pair = end[:rows, :], end[rows:, :]
     for s in range(pieces - 1, -1, -1):
         out[s, :rows, :], out[s, rows:, :] = encode(carry, pair, jnp.zeros_like(pair))
         if s == 0:
@@ -204,6 +209,10 @@
     return pltpu.with_memory_space_constraint(x, pltpu.VMEM)
 
 
+def far_off(x):
+    return pltpu.with_memory_space_constraint(x, pltpu.HBM)
+
+
 def body(inverse_factor, arrow_factor, decay, tip_inverse, sigma_end, arrow_end):
     factor_cols = inverse_factor[0]
     order, width = factor_cols.shape
@@ -234,12 +243,12 @@
         scratch_shapes=[pltpu.SemaphoreType.DMA((2,))],
         compiler_params=SMALL,
         name="pack",
-    )(*[pltpu.with_memory_space_constraint(x, pltpu.HBM) for x in (factor_cols, arrow_factor[0])])
-
-    def hop(panel, count=1):
+    )(far_off(factor_cols), far_off(arrow_factor[0]))
+
+    def hop(panel, count=1, cross=0):
         pairs = []
         for p in range(devices):
-            chip, core = p // CORES, p % CORES
+            chip, core = p // CORES, p % CORES ^ cross
             pairs.append((p, (chip + count * (1 - 2 * core)) % chips * CORES + core))
         return lax.ppermute(panel, "space", pairs)
 
@@ -261,18 +270,24 @@
             name=name,
         )(*map(near, panels), near(both_t), token)
 
-    first = hop(shared(mine, 1))
+    start = shared(mine, 1)
+    first, second = hop(start), hop(start, cross=1)
     other = swap(mine)
-    second = hop(shared(other, 1))
     mark = jax.ShapeDtypeStruct((8, width), f32)
-    own, both_t, token = pl.pallas_call(
+    own, both_t, end, token = pl.pallas_call(
         own_kernel,
-        out_shape=(pltpu.VMEM((both + arrow, width), f32), pltpu.VMEM((both, order), bf16), mark),
-        in_specs=[VMEM] * 2,
-        out_specs=(VMEM,) * 3,
+        out_shape=(
+            pltpu.VMEM((both + arrow, width), f32),
+            pltpu.VMEM((both, order), bf16),
+            pltpu.VMEM((rows + PAD, width), f32),
+            mark,
+        ),
+        in_specs=[SMEM, VMEM, VMEM, hbm, VMEM],
+        out_specs=(VMEM,) * 4,
+        scratch_shapes=[pltpu.SemaphoreType.DMA],
         compiler_params=SMALL,
         name="own",
-    )(near(mine), near(other))
+    )(piece_at, near(mine), near(other), far_off(sigma_end), near(arrow_end.T))
 
     first_2 = hop(shared(first, 2))
     second, token = lax.optimization_barrier((second, token))
@@ -318,12 +333,12 @@
     ahead = pl.pallas_call(
         lambda *refs: scan_kernel(rows, *refs),
         out_shape=pltpu.VMEM(message, f32),
-        in_specs=[SMEM] + [VMEM] * 3,
+        in_specs=[VMEM] * 2,
         out_specs=VMEM,
         scratch_shapes=[pltpu.VMEM((pieces, width), f32)],
         compiler_params=SMALL,
         name="suffix",
-    )(piece_at, *map(near, (exchange(sent), sigma_end, arrow_end.T)))
+    )(near(exchange(sent)), near(end))
     sigma, arrows = pl.pallas_call(
         lambda *refs: last_kernel(rows, *refs),
         out_shape=(jax.ShapeDtypeStruct((order, width), f32), jax.ShapeDtypeStruct((arrow, width), f32)),

time: 111 us -> 113 us (1.018)
  blocking collectives: 23.4 us -> 55.1 us
  waiting for transfers between devices: 32.5 us -> 12.1 us
  starting transfers between devices: 44 us -> 35.1 us
    all_to_all x1 -> x2, blocking collectives: 23.4 us -> 55.1 us  [exchange(): moved = lax.all_to_all(values.astype(jnp.float16), 'tm', 0, 0, tiled=True)]
    all_to_all x1 -> x0, waiting for transfers between devices: 19.3 us -> none  [exchange(): moved = lax.all_to_all(values.astype(jnp.float16), 'tm', 0, 0, tiled=True)]
    all_to_all x1 -> x0, starting transfers between devices: 12.6 us -> none  [exchange(): moved = lax.all_to_all(values.astype(jnp.float16), 'tm', 0, 0, tiled=True)]
    ppermute x7, starting transfers between devices: 23.5 us -> 27.1 us  [hop(): return lax.ppermute(panel, 'space', pairs)]
  transfers between devices with their start and end apart: 12 -> 11, of which waited for: 7 -> 5; matrix products, arithmetic and copies ran while one was open for 0% -> 0% of each run, Pallas kernels for 4% -> 4%
where the time goes in v10:
time: 113 us; the launch traced here: 112 us
  blocking collectives  55.1 us (49%)
  starting transfers between devices  35.1 us (31%)
  waiting for transfers between devices  12.1 us (11%)
  Pallas kernels  8.49 us (8%)
    all_to_all x2, blocking collectives, exchange(): moved = lax.all_to_all(values.astype(jnp.float16), 'tm', 0, 0, tiled=True)  55.1 us
    ppermute x7, starting transfers between devices, hop(): return lax.ppermute(panel, 'space', pairs)  27.1 us
    ppermute x7, waiting for transfers between devices, hop(): return lax.ppermute(panel, 'space', pairs)  9.59 us
    ppermute x4, starting transfers between devices, swap(): return lax.ppermute(tile, 'space', [(p, p ^ 1) for p in range(devices)])  8 us
    pallas_call x3, Pallas kernels, product(): pl.pallas_call(kernel, out_shape=(*[jax.ShapeDtypeStruct((tall, width), f...  3.33 us
    ppermute x4, waiting for transfers between devices, swap(): return lax.ppermute(tile, 'space', [(p, p ^ 1) for p in range(devices)])  2.52 us
  transfers between devices with their start and end apart: 11, of which 5 were waited for; matrix products, arithmetic and copies ran while one was open for 0% of the time, Pallas kernels for 4%

profile of v10, /device:TPU:64, one launch (start us, length us, event | category | flops | bytes accessed | tf_op | source)
XLA Modules:
  0.0 112.2 jit_solution(9758877900230100917)
XLA Ops:
  0.6 1.1 pack.1.mine
  1.7 1.9 %collective-permute-start = (bf16[2112,128]{1,0:T(8,128)(2,1)S(1)}, bf16[2112,128]{1,0:T(8,128)(2,1)S(1)}, u32[]{:S(2)}, u32[]{:S(2)}) collective-permute-start(bf16[2112,128]{1,0:T(8,128)(2,1)S(1)} %pack.1.mine), channel_id=1, source_target_pairs={{0,1},{1,0},{2,3},{3,2},{4,5},{5,4},{6,7},{7,6},{8,9},{9,8},{10,11... | collective-permute-start | bytes 1622024 | tf_op jit(solution)/shard_map/ppermute | solution.py:256
  3.7 3.5 %collective-permute-start.1 = (bf16[1856,128]{1,0:T(8,128)(2,1)S(1)}, bf16[1856,128]{1,0:T(8,128)(2,1)S(1)}, u32[]{:S(2)}, u32[]{:S(2)}) collective-permute-start(bf16[1856,128]{1,0:T(8,128)(2,1)S(1)} %slice.24), channel_id=1, source_target_pairs={{0,2},{1,15},{2,4},{3,1},{4,6},{5,3},{6,8},{7,5},{8,10},{9,7},{10,... | collective-permute-start | bytes 1425416 | tf_op jit(solution)/shard_map/ppermute | solution.py:253
  7.2 5.0 %collective-permute-start.2 = (bf16[1856,128]{1,0:T(8,128)(2,1)S(1)}, bf16[1856,128]{1,0:T(8,128)(2,1)S(1)}, u32[]{:S(2)}, u32[]{:S(2)}) collective-permute-start(bf16[1856,128]{1,0:T(8,128)(2,1)S(1)} %slice.24), channel_id=1, source_target_pairs={{0,15},{1,2},{2,1},{3,4},{4,3},{5,6},{6,5},{7,8},{8,7},{9,10},{10,... | collective-permute-start | bytes 1425416 | tf_op jit(solution)/shard_map/ppermute | solution.py:253
  12.2 5.8 %collective-permute-done.1.first = bf16[1856,128]{1,0:T(8,128)(2,1)S(1)} collective-permute-done((bf16[1856,128]{1,0:T(8,128)(2,1)S(1)}, bf16[1856,128]{1,0:T(8,128)(2,1)S(1)}, u32[]{:S(2)}, u32[]{:S(2)}) %collective-permute-start.1) | collective-permute-done | bytes 475168 | tf_op jit(solution)/shard_map/ppermute | solution.py:253
  17.9 1.9 %collective-permute-start.3 = (bf16[1600,128]{1,0:T(8,128)(2,1)S(1)}, bf16[1600,128]{1,0:T(8,128)(2,1)S(1)}, u32[]{:S(2)}, u32[]{:S(2)}) collective-permute-start(bf16[1600,128]{1,0:T(8,128)(2,1)S(1)} %slice.25), channel_id=1, source_target_pairs={{0,2},{1,15},{2,4},{3,1},{4,6},{5,3},{6,8},{7,5},{8,10},{9,7},{10,... | collective-permute-start | bytes 1228808 | tf_op jit(solution)/shard_map/ppermute | solution.py:253
  19.9 1.1 %own.1 = (f32[320,128]{1,0:T(8,128)S(1)}, bf16[256,2048]{1,0:T(8,128)(2,1)S(1)}, f32[72,128]{1,0:T(8,128)S(1)}, f32[8,128]{1,0:T(8,128)S(1)}) custom-call(s32[1]{0:T(128)} %bitcast.1.at, bf16[2112,128]{1,0:T(8,128)(2,1)S(1)} %pack.1.mine, bf16[2112,128]{1,0:T(8,128)(2,1)S(1)} %collective-permute-done.other, f32[2048,128]{1,0:T(8,128)} %sigma_end.1, ...), custom_call_target="tpu_custom_call" | custom-call | tf_op jit(solution)/shard_map/own/pallas_call | solution.py:277
  21.1 3.5 %collective-permute-start.4 = (bf16[1600,128]{1,0:T(8,128)(2,1)S(1)}, bf16[1600,128]{1,0:T(8,128)(2,1)S(1)}, u32[]{:S(2)}, u32[]{:S(2)}) collective-permute-start(bf16[1600,128]{1,0:T(8,128)(2,1)S(1)} %slice.20), channel_id=1, source_target_pairs={{0,2},{1,15},{2,4},{3,1},{4,6},{5,3},{6,8},{7,5},{8,10},{9,7},{10,... | collective-permute-start | bytes 1228808 | tf_op jit(solution)/shard_map/ppermute | solution.py:253
  24.6 0.8 far.2
  25.3 3.7 %collective-permute-done.3.first = bf16[1600,128]{1,0:T(8,128)(2,1)S(1)} collective-permute-done((bf16[1600,128]{1,0:T(8,128)(2,1)S(1)}, bf16[1600,128]{1,0:T(8,128)(2,1)S(1)}, u32[]{:S(2)}, u32[]{:S(2)}) %collective-permute-start.3) | collective-permute-done | bytes 409632 | tf_op jit(solution)/shard_map/ppermute | solution.py:253
  29.1 4.2 %collective-permute-start.5 = (bf16[1088,128]{1,0:T(8,128)(2,1)S(1)}, bf16[1088,128]{1,0:T(8,128)(2,1)S(1)}, u32[]{:S(2)}, u32[]{:S(2)}) collective-permute-start(bf16[1088,128]{1,0:T(8,128)(2,1)S(1)} %slice.21), channel_id=1, source_target_pairs={{0,4},{1,13},{2,6},{3,15},{4,8},{5,1},{6,10},{7,3},{8,12},{9,5},{1... | collective-permute-start | bytes 835592 | tf_op jit(solution)/shard_map/ppermute | solution.py:253
  33.2 3.4 %collective-permute-start.7 = (bf16[1344,128]{1,0:T(8,128)(2,1)S(1)}, bf16[1344,128]{1,0:T(8,128)(2,1)S(1)}, u32[]{:S(2)}, u32[]{:S(2)}) collective-permute-start(bf16[1344,128]{1,0:T(8,128)(2,1)S(1)} %slice.22), channel_id=1, source_target_pairs={{0,2},{1,15},{2,4},{3,1},{4,6},{5,3},{6,8},{7,5},{8,10},{9,7},{10,... | collective-permute-start | bytes 1032200 | tf_op jit(solution)/shard_map/ppermute | solution.py:253
  36.7 5.6 %collective-permute-start.8 = (bf16[1344,128]{1,0:T(8,128)(2,1)S(1)}, bf16[1344,128]{1,0:T(8,128)(2,1)S(1)}, u32[]{:S(2)}, u32[]{:S(2)}) collective-permute-start(bf16[1344,128]{1,0:T(8,128)(2,1)S(1)} %slice.26), channel_id=1, source_target_pairs={{0,2},{1,15},{2,4},{3,1},{4,6},{5,3},{6,8},{7,5},{8,10},{9,7},{10,... | collective-permute-start | bytes 1032200 | tf_op jit(solution)/shard_map/ppermute | solution.py:253
  42.3 1.9 %collective-permute-start.6 = (f32[320,128]{1,0:T(8,128)S(1)}, f32[320,128]{1,0:T(8,128)S(1)}, u32[]{:S(2)}, u32[]{:S(2)}) collective-permute-start(f32[320,128]{1,0:T(8,128)S(1)} %get-tuple-element.34), channel_id=1, source_target_pairs={{0,1},{1,0},{2,3},{3,2},{4,5},{5,4},{6,7},{7,6},{8,9},{9,8},{10,11... | collective-permute-start | bytes 491528 | tf_op jit(solution)/shard_map/ppermute | solution.py:256
  44.3 1.4 %collective-permute-done.6.refs_5_ = f32[320,128]{1,0:T(8,128)S(1)} collective-permute-done((f32[320,128]{1,0:T(8,128)S(1)}, f32[320,128]{1,0:T(8,128)S(1)}, u32[]{:S(2)}, u32[]{:S(2)}) %collective-permute-start.6) | collective-permute-done | bytes 163872 | tf_op jit(solution)/shard_map/ppermute | solution.py:256
  45.6 1.4 %three.1 = (f32[448,128]{1,0:T(8,128)S(1)}, f32[448,128]{1,0:T(8,128)S(1)}, f32[8,128]{1,0:T(8,128)S(1)}) custom-call(bf16[1600,128]{1,0:T(8,128)(2,1)S(1)} %collective-permute-done.3.first, bf16[1600,128]{1,0:T(8,128)(2,1)S(1)} %collective-permute-done.4.second, bf16[1088,128]{1,0:T(8,128)(2,1)S(1)} %collective-permute-done.5.straight, ...), custom_call_target="tpu_custom_call" | custom-call | tf_op jit(solution)/shard_map/three/pallas_call | solution.py:263
  47.0 2.1 %collective-permute-start.9 = (f32[448,128]{1,0:T(8,128)S(1)}, f32[448,128]{1,0:T(8,128)S(1)}, u32[]{:S(2)}, u32[]{:S(2)}) collective-permute-start(f32[448,128]{1,0:T(8,128)S(1)} %get-tuple-element.40), channel_id=1, source_target_pairs={{0,1},{1,0},{2,3},{3,2},{4,5},{5,4},{6,7},{7,6},{8,9},{9,8},{10,11... | collective-permute-start | bytes 688136 | tf_op jit(solution)/shard_map/ppermute | solution.py:256
  49.3 1.2 %far.3 = (f32[320,128]{1,0:T(8,128)S(1)}, f32[320,128]{1,0:T(8,128)S(1)}, f32[8,128]{1,0:T(8,128)}) custom-call(bf16[1344,128]{1,0:T(8,128)(2,1)S(1)} %collective-permute-done.7.first, bf16[1344,128]{1,0:T(8,128)(2,1)S(1)} %collective-permute-done.8.second, bf16[256,2048]{1,0:T(8,128)(2,1)S(1)} %get-tuple-element.28.both_t, ...), custom_call_target="tpu_custom_call" | custom-call | tf_op jit(solution)/shard_map/far/pallas_call | solution.py:263
  50.4 2.1 %collective-permute-start.10 = (f32[320,128]{1,0:T(8,128)S(1)}, f32[320,128]{1,0:T(8,128)S(1)}, u32[]{:S(2)}, u32[]{:S(2)}) collective-permute-start(f32[320,128]{1,0:T(8,128)S(1)} %get-tuple-element.41), channel_id=1, source_target_pairs={{0,1},{1,0},{2,3},{3,2},{4,5},{5,4},{6,7},{7,6},{8,9},{9,8},{10,11... | collective-permute-start | bytes 491528 | tf_op jit(solution)/shard_map/ppermute | solution.py:256
  52.6 1.2 %collective-permute-done.10.refs_7_ = f32[320,128]{1,0:T(8,128)S(1)} collective-permute-done((f32[320,128]{1,0:T(8,128)S(1)}, f32[320,128]{1,0:T(8,128)S(1)}, u32[]{:S(2)}, u32[]{:S(2)}) %collective-permute-start.10) | collective-permute-done | bytes 163872 | tf_op jit(solution)/shard_map/ppermute | solution.py:256
  54.4 31.8 %all_to_all.10 = f16[32,72,128]{2,1,0:T(8,128)(2,1)S(1)} all-to-all(f16[32,72,128]{2,1,0:T(8,128)(2,1)S(1)} %convert_element_type.12), channel_id=1, replica_groups=mesh['tm'=32,'space'=16] {'tm'}, dimensions={0} | all-to-all | bytes 1179648 | tf_op jit(solution)/shard_map/all_to_all | solution.py:330
  86.2 0.8 suffix.1
  87.1 23.4 %all_to_all.11 = f16[32,72,128]{2,1,0:T(8,128)(2,1)S(1)} all-to-all(f16[32,72,128]{2,1,0:T(8,128)(2,1)S(1)} %convert_element_type.14), channel_id=1, replica_groups=mesh['tm'=32,'space'=16] {'tm'}, dimensions={0} | all-to-all | bytes 1179648 | tf_op jit(solution)/shard_map/all_to_all | solution.py:330
  110.6 1.6 %last.1 = (f32[2048,128]{1,0:T(8,128)}, f32[64,128]{1,0:T(8,128)}) custom-call(s32[1]{0:T(128)} %bitcast.refs_0_, f32[32,64,128]{2,1,0:T(8,128)S(1)} %get-tuple-element.42.refs_1_, f32[64,128]{1,0:T(8,128)S(1)} %get-tuple-element.43.refs_2_, f32[32,72,128]{2,1,0:T(8,128)S(1)} %convert_element_type.15.refs_3_, f32[1,2048]{1,0:T(1,128)S(1)} %copy-done.1), custom_call_target="tpu_custom_call" | custom-call | tf_op jit(solution)/shard_map/last/pallas_call | solution.py:342
  (24 shorter events, 1.3 us)
Async XLA Ops:
  0.6 19.3 %copy-start = (f32[128,64]{0,1:T(8,128)S(1)}, f32[128,64]{0,1:T(8,128)}, u32[]{:S(2)}) copy-start(f32[128,64]{0,1:T(8,128)} %param.11) | copy-start | bytes 98308
  1.7 18.2 %collective-permute-start = (bf16[2112,128]{1,0:T(8,128)(2,1)S(1)}, bf16[2112,128]{1,0:T(8,128)(2,1)S(1)}, u32[]{:S(2)}, u32[]{:S(2)}) collective-permute-start(bf16[2112,128]{1,0:T(8,128)(2,1)S(1)} %pack.1.mine), channel_id=1, source_target_pairs={{0,1},{1,0},{2,3},{3,2},{4,5},{5,4},{6,7},{7,6},{8,9},{9,8},{10,11... | collective-permute-start | bytes 1622024 | tf_op jit(solution)/shard_map/ppermute | solution.py:256
  3.7 14.2 %collective-permute-start.1 = (bf16[1856,128]{1,0:T(8,128)(2,1)S(1)}, bf16[1856,128]{1,0:T(8,128)(2,1)S(1)}, u32[]{:S(2)}, u32[]{:S(2)}) collective-permute-start(bf16[1856,128]{1,0:T(8,128)(2,1)S(1)} %slice.24), channel_id=1, source_target_pairs={{0,2},{1,15},{2,4},{3,1},{4,6},{5,3},{6,8},{7,5},{8,10},{9,7},{10,... | collective-permute-start | bytes 1425416 | tf_op jit(solution)/shard_map/ppermute | solution.py:253
  7.2 13.9 %collective-permute-start.2 = (bf16[1856,128]{1,0:T(8,128)(2,1)S(1)}, bf16[1856,128]{1,0:T(8,128)(2,1)S(1)}, u32[]{:S(2)}, u32[]{:S(2)}) collective-permute-start(bf16[1856,128]{1,0:T(8,128)(2,1)S(1)} %slice.24), channel_id=1, source_target_pairs={{0,15},{1,2},{2,1},{3,4},{4,3},{5,6},{6,5},{7,8},{8,7},{9,10},{10,... | collective-permute-start | bytes 1425416 | tf_op jit(solution)/shard_map/ppermute | solution.py:253
  17.9 11.1 %collective-permute-start.3 = (bf16[1600,128]{1,0:T(8,128)(2,1)S(1)}, bf16[1600,128]{1,0:T(8,128)(2,1)S(1)}, u32[]{:S(2)}, u32[]{:S(2)}) collective-permute-start(bf16[1600,128]{1,0:T(8,128)(2,1)S(1)} %slice.25), channel_id=1, source_target_pairs={{0,2},{1,15},{2,4},{3,1},{4,6},{5,3},{6,8},{7,5},{8,10},{9,7},{10,... | collective-permute-start | bytes 1228808 | tf_op jit(solution)/shard_map/ppermute | solution.py:253
  21.1 15.6 %collective-permute-start.4 = (bf16[1600,128]{1,0:T(8,128)(2,1)S(1)}, bf16[1600,128]{1,0:T(8,128)(2,1)S(1)}, u32[]{:S(2)}, u32[]{:S(2)}) collective-permute-start(bf16[1600,128]{1,0:T(8,128)(2,1)S(1)} %slice.20), channel_id=1, source_target_pairs={{0,2},{1,15},{2,4},{3,1},{4,6},{5,3},{6,8},{7,5},{8,10},{9,7},{10,... | collective-permute-start | bytes 1228808 | tf_op jit(solution)/shard_map/ppermute | solution.py:253
  29.1 16.6 %collective-permute-start.5 = (bf16[1088,128]{1,0:T(8,128)(2,1)S(1)}, bf16[1088,128]{1,0:T(8,128)(2,1)S(1)}, u32[]{:S(2)}, u32[]{:S(2)}) collective-permute-start(bf16[1088,128]{1,0:T(8,128)(2,1)S(1)} %slice.21), channel_id=1, source_target_pairs={{0,4},{1,13},{2,6},{3,15},{4,8},{5,1},{6,10},{7,3},{8,12},{9,5},{1... | collective-permute-start | bytes 835592 | tf_op jit(solution)/shard_map/ppermute | solution.py:253
  33.2 15.9 %collective-permute-start.7 = (bf16[1344,128]{1,0:T(8,128)(2,1)S(1)}, bf16[1344,128]{1,0:T(8,128)(2,1)S(1)}, u32[]{:S(2)}, u32[]{:S(2)}) collective-permute-start(bf16[1344,128]{1,0:T(8,128)(2,1)S(1)} %slice.22), channel_id=1, source_target_pairs={{0,2},{1,15},{2,4},{3,1},{4,6},{5,3},{6,8},{7,5},{8,10},{9,7},{10,... | collective-permute-start | bytes 1032200 | tf_op jit(solution)/shard_map/ppermute | solution.py:253
  36.7 12.5 %collective-permute-start.8 = (bf16[1344,128]{1,0:T(8,128)(2,1)S(1)}, bf16[1344,128]{1,0:T(8,128)(2,1)S(1)}, u32[]{:S(2)}, u32[]{:S(2)}) collective-permute-start(bf16[1344,128]{1,0:T(8,128)(2,1)S(1)} %slice.26), channel_id=1, source_target_pairs={{0,2},{1,15},{2,4},{3,1},{4,6},{5,3},{6,8},{7,5},{8,10},{9,7},{10,... | collective-permute-start | bytes 1032200 | tf_op jit(solution)/shard_map/ppermute | solution.py:253
  42.3 3.3 %collective-permute-start.6 = (f32[320,128]{1,0:T(8,128)S(1)}, f32[320,128]{1,0:T(8,128)S(1)}, u32[]{:S(2)}, u32[]{:S(2)}) collective-permute-start(f32[320,128]{1,0:T(8,128)S(1)} %get-tuple-element.34), channel_id=1, source_target_pairs={{0,1},{1,0},{2,3},{3,2},{4,5},{5,4},{6,7},{7,6},{8,9},{9,8},{10,11... | collective-permute-start | bytes 491528 | tf_op jit(solution)/shard_map/ppermute | solution.py:256
  47.0 6.7 %copy-start.1 = (f32[1,2048]{1,0:T(1,128)S(1)}, f32[1,2048]{1,0:T(1,128)}, u32[]{:S(2)}) copy-start(f32[1,2048]{1,0:T(1,128)} %refs_4_.1) | copy-start | bytes 24580
  47.0 6.7 %copy-start.2 = (f32[64,64]{1,0:T(8,128)S(1)}, f32[64,64]{1,0:T(8,128)}, u32[]{:S(2)}) copy-start(f32[64,64]{1,0:T(8,128)} %refs_8_.1) | copy-start | bytes 49156
  47.0 5.5 %collective-permute-start.9 = (f32[448,128]{1,0:T(8,128)S(1)}, f32[448,128]{1,0:T(8,128)S(1)}, u32[]{:S(2)}, u32[]{:S(2)}) collective-permute-start(f32[448,128]{1,0:T(8,128)S(1)} %get-tuple-element.40), channel_id=1, source_target_pairs={{0,1},{1,0},{2,3},{3,2},{4,5},{5,4},{6,7},{7,6},{8,9},{9,8},{10,11... | collective-permute-start | bytes 688136 | tf_op jit(solution)/shard_map/ppermute | solution.py:256
  50.4 3.3 %collective-permute-start.10 = (f32[320,128]{1,0:T(8,128)S(1)}, f32[320,128]{1,0:T(8,128)S(1)}, u32[]{:S(2)}, u32[]{:S(2)}) collective-permute-start(f32[320,128]{1,0:T(8,128)S(1)} %get-tuple-element.41), channel_id=1, source_target_pairs={{0,1},{1,0},{2,3},{3,2},{4,5},{5,4},{6,7},{7,6},{8,9},{9,8},{10,11... | collective-permute-start | bytes 491528 | tf_op jit(solution)/shard_map/ppermute | solution.py:256

commit v11 on v10

--- a/solution.py
+++ b/solution.py
@@ -245,10 +245,10 @@
         name="pack",
     )(far_off(factor_cols), far_off(arrow_factor[0]))
 
-    def hop(panel, count=1, cross=0):
+    def hop(panel, count=1):
         pairs = []
         for p in range(devices):
-            chip, core = p // CORES, p % CORES ^ cross
+            chip, core = p // CORES, p % CORES
             pairs.append((p, (chip + count * (1 - 2 * core)) % chips * CORES + core))
         return lax.ppermute(panel, "space", pairs)
 
@@ -270,9 +270,9 @@
             name=name,
         )(*map(near, panels), near(both_t), token)
 
-    start = shared(mine, 1)
-    first, second = hop(start), hop(start, cross=1)
+    first = hop(shared(mine, 1))
     other = swap(mine)
+    second = hop(shared(other, 1))
     mark = jax.ShapeDtypeStruct((8, width), f32)
     own, both_t, end, token = pl.pallas_call(
         own_kernel,

time: 113 us -> 110 us (0.973)
  starting transfers between devices: 35.1 us -> 31.4 us
    ppermute x7, starting transfers between devices: 27.1 us -> 23.5 us  [hop(): return lax.ppermute(panel, 'space', pairs)]
  transfers between devices with their start and end apart: 11 -> 11, of which waited for: 5 -> 6; matrix products, arithmetic and copies ran while one was open for 0% -> 0% of each run, Pallas kernels for 4% -> 4%
where the time goes in v11:
time: 110 us; the launch traced here: 109 us
  blocking collectives  55.1 us (50%)
  starting transfers between devices  31.4 us (29%)
  waiting for transfers between devices  12.8 us (12%)
  Pallas kernels  8.49 us (8%)
    all_to_all x2, blocking collectives, exchange(): moved = lax.all_to_all(values.astype(jnp.float16), 'tm', 0, 0, tiled=True)  55.1 us
    ppermute x7, starting transfers between devices, hop(): return lax.ppermute(panel, 'space', pairs)  23.5 us
    ppermute x7, waiting for transfers between devices, hop(): return lax.ppermute(panel, 'space', pairs)  10.2 us
    ppermute x4, starting transfers between devices, swap(): return lax.ppermute(tile, 'space', [(p, p ^ 1) for p in range(devices)])  7.95 us
    pallas_call x3, Pallas kernels, product(): pl.pallas_call(kernel, out_shape=(*[jax.ShapeDtypeStruct((tall, width), f...  3.33 us
    ppermute x4, waiting for transfers between devices, swap(): return lax.ppermute(tile, 'space', [(p, p ^ 1) for p in range(devices)])  2.56 us
  transfers between devices with their start and end apart: 11, of which 6 were waited for; matrix products, arithmetic and copies ran while one was open for 0% of the time, Pallas kernels for 4%

profile of v11, /device:TPU:64, one launch (start us, length us, event | category | flops | bytes accessed | tf_op | source)
XLA Modules:
  0.0 109.2 jit_solution(985105886054924296)
XLA Ops:
  0.6 1.1 pack.1.mine
  1.7 1.9 %collective-permute-start = (bf16[2112,128]{1,0:T(8,128)(2,1)S(1)}, bf16[2112,128]{1,0:T(8,128)(2,1)S(1)}, u32[]{:S(2)}, u32[]{:S(2)}) collective-permute-start(bf16[2112,128]{1,0:T(8,128)(2,1)S(1)} %pack.1.mine), channel_id=1, source_target_pairs={{0,1},{1,0},{2,3},{3,2},{4,5},{5,4},{6,7},{7,6},{8,9},{9,8},{10,11... | collective-permute-start | bytes 1622024 | tf_op jit(solution)/shard_map/ppermute | solution.py:256
  3.7 3.5 %collective-permute-start.1 = (bf16[1856,128]{1,0:T(8,128)(2,1)S(1)}, bf16[1856,128]{1,0:T(8,128)(2,1)S(1)}, u32[]{:S(2)}, u32[]{:S(2)}) collective-permute-start(bf16[1856,128]{1,0:T(8,128)(2,1)S(1)} %slice.28), channel_id=1, source_target_pairs={{0,2},{1,15},{2,4},{3,1},{4,6},{5,3},{6,8},{7,5},{8,10},{9,7},{10,... | collective-permute-start | bytes 1425416 | tf_op jit(solution)/shard_map/ppermute | solution.py:253
  7.2 3.5 %collective-permute-start.2 = (bf16[1856,128]{1,0:T(8,128)(2,1)S(1)}, bf16[1856,128]{1,0:T(8,128)(2,1)S(1)}, u32[]{:S(2)}, u32[]{:S(2)}) collective-permute-start(bf16[1856,128]{1,0:T(8,128)(2,1)S(1)} %slice.29), channel_id=1, source_target_pairs={{0,2},{1,15},{2,4},{3,1},{4,6},{5,3},{6,8},{7,5},{8,10},{9,7},{10,... | collective-permute-start | bytes 1425416 | tf_op jit(solution)/shard_map/ppermute | solution.py:253
  10.7 5.0 %collective-permute-done.1.first = bf16[1856,128]{1,0:T(8,128)(2,1)S(1)} collective-permute-done((bf16[1856,128]{1,0:T(8,128)(2,1)S(1)}, bf16[1856,128]{1,0:T(8,128)(2,1)S(1)}, u32[]{:S(2)}, u32[]{:S(2)}) %collective-permute-start.1) | collective-permute-done | bytes 475168 | tf_op jit(solution)/shard_map/ppermute | solution.py:253
  15.7 2.0 %collective-permute-start.3 = (bf16[1600,128]{1,0:T(8,128)(2,1)S(1)}, bf16[1600,128]{1,0:T(8,128)(2,1)S(1)}, u32[]{:S(2)}, u32[]{:S(2)}) collective-permute-start(bf16[1600,128]{1,0:T(8,128)(2,1)S(1)} %slice.30), channel_id=1, source_target_pairs={{0,2},{1,15},{2,4},{3,1},{4,6},{5,3},{6,8},{7,5},{8,10},{9,7},{10,... | collective-permute-start | bytes 1228808 | tf_op jit(solution)/shard_map/ppermute | solution.py:253
  17.8 1.1 %own.1 = (f32[320,128]{1,0:T(8,128)S(1)}, bf16[256,2048]{1,0:T(8,128)(2,1)S(1)}, f32[72,128]{1,0:T(8,128)S(1)}, f32[8,128]{1,0:T(8,128)S(1)}) custom-call(s32[1]{0:T(128)} %bitcast.1.at, bf16[2112,128]{1,0:T(8,128)(2,1)S(1)} %pack.1.mine, bf16[2112,128]{1,0:T(8,128)(2,1)S(1)} %collective-permute-done.other, f32[2048,128]{1,0:T(8,128)} %sigma_end.1, ...), custom_call_target="tpu_custom_call" | custom-call | tf_op jit(solution)/shard_map/own/pallas_call | solution.py:277
  18.9 1.9 %collective-permute-done.2.second = bf16[1856,128]{1,0:T(8,128)(2,1)S(1)} collective-permute-done((bf16[1856,128]{1,0:T(8,128)(2,1)S(1)}, bf16[1856,128]{1,0:T(8,128)(2,1)S(1)}, u32[]{:S(2)}, u32[]{:S(2)}) %collective-permute-start.2) | collective-permute-done | bytes 475168 | tf_op jit(solution)/shard_map/ppermute | solution.py:253
  20.8 2.0 %collective-permute-start.4 = (bf16[1600,128]{1,0:T(8,128)(2,1)S(1)}, bf16[1600,128]{1,0:T(8,128)(2,1)S(1)}, u32[]{:S(2)}, u32[]{:S(2)}) collective-permute-start(bf16[1600,128]{1,0:T(8,128)(2,1)S(1)} %slice.24), channel_id=1, source_target_pairs={{0,2},{1,15},{2,4},{3,1},{4,6},{5,3},{6,8},{7,5},{8,10},{9,7},{10,... | collective-permute-start | bytes 1228808 | tf_op jit(solution)/shard_map/ppermute | solution.py:253
  23.6 3.1 %collective-permute-done.3.first = bf16[1600,128]{1,0:T(8,128)(2,1)S(1)} collective-permute-done((bf16[1600,128]{1,0:T(8,128)(2,1)S(1)}, bf16[1600,128]{1,0:T(8,128)(2,1)S(1)}, u32[]{:S(2)}, u32[]{:S(2)}) %collective-permute-start.3) | collective-permute-done | bytes 409632 | tf_op jit(solution)/shard_map/ppermute | solution.py:253
  26.8 3.4 %collective-permute-start.5 = (bf16[1088,128]{1,0:T(8,128)(2,1)S(1)}, bf16[1088,128]{1,0:T(8,128)(2,1)S(1)}, u32[]{:S(2)}, u32[]{:S(2)}) collective-permute-start(bf16[1088,128]{1,0:T(8,128)(2,1)S(1)} %slice.25), channel_id=1, source_target_pairs={{0,4},{1,13},{2,6},{3,15},{4,8},{5,1},{6,10},{7,3},{8,12},{9,5},{1... | collective-permute-start | bytes 835592 | tf_op jit(solution)/shard_map/ppermute | solution.py:253
  30.2 3.9 %collective-permute-start.7 = (bf16[1344,128]{1,0:T(8,128)(2,1)S(1)}, bf16[1344,128]{1,0:T(8,128)(2,1)S(1)}, u32[]{:S(2)}, u32[]{:S(2)}) collective-permute-start(bf16[1344,128]{1,0:T(8,128)(2,1)S(1)} %slice.26), channel_id=1, source_target_pairs={{0,2},{1,15},{2,4},{3,1},{4,6},{5,3},{6,8},{7,5},{8,10},{9,7},{10,... | collective-permute-start | bytes 1032200 | tf_op jit(solution)/shard_map/ppermute | solution.py:253
  34.2 5.2 %collective-permute-start.8 = (bf16[1344,128]{1,0:T(8,128)(2,1)S(1)}, bf16[1344,128]{1,0:T(8,128)(2,1)S(1)}, u32[]{:S(2)}, u32[]{:S(2)}) collective-permute-start(bf16[1344,128]{1,0:T(8,128)(2,1)S(1)} %slice.31), channel_id=1, source_target_pairs={{0,2},{1,15},{2,4},{3,1},{4,6},{5,3},{6,8},{7,5},{8,10},{9,7},{10,... | collective-permute-start | bytes 1032200 | tf_op jit(solution)/shard_map/ppermute | solution.py:253
  39.3 1.9 %collective-permute-start.6 = (f32[320,128]{1,0:T(8,128)S(1)}, f32[320,128]{1,0:T(8,128)S(1)}, u32[]{:S(2)}, u32[]{:S(2)}) collective-permute-start(f32[320,128]{1,0:T(8,128)S(1)} %get-tuple-element.34), channel_id=1, source_target_pairs={{0,1},{1,0},{2,3},{3,2},{4,5},{5,4},{6,7},{7,6},{8,9},{9,8},{10,11... | collective-permute-start | bytes 491528 | tf_op jit(solution)/shard_map/ppermute | solution.py:256
  41.3 1.4 %collective-permute-done.6.refs_5_ = f32[320,128]{1,0:T(8,128)S(1)} collective-permute-done((f32[320,128]{1,0:T(8,128)S(1)}, f32[320,128]{1,0:T(8,128)S(1)}, u32[]{:S(2)}, u32[]{:S(2)}) %collective-permute-start.6) | collective-permute-done | bytes 163872 | tf_op jit(solution)/shard_map/ppermute | solution.py:256
  42.6 1.4 %three.1 = (f32[448,128]{1,0:T(8,128)S(1)}, f32[448,128]{1,0:T(8,128)S(1)}, f32[8,128]{1,0:T(8,128)S(1)}) custom-call(bf16[1600,128]{1,0:T(8,128)(2,1)S(1)} %collective-permute-done.3.first, bf16[1600,128]{1,0:T(8,128)(2,1)S(1)} %collective-permute-done.4.second, bf16[1088,128]{1,0:T(8,128)(2,1)S(1)} %collective-permute-done.5.straight, ...), custom_call_target="tpu_custom_call" | custom-call | tf_op jit(solution)/shard_map/three/pallas_call | solution.py:263
  44.0 2.0 %collective-permute-start.9 = (f32[448,128]{1,0:T(8,128)S(1)}, f32[448,128]{1,0:T(8,128)S(1)}, u32[]{:S(2)}, u32[]{:S(2)}) collective-permute-start(f32[448,128]{1,0:T(8,128)S(1)} %get-tuple-element.40), channel_id=1, source_target_pairs={{0,1},{1,0},{2,3},{3,2},{4,5},{5,4},{6,7},{7,6},{8,9},{9,8},{10,11... | collective-permute-start | bytes 688136 | tf_op jit(solution)/shard_map/ppermute | solution.py:256
  46.3 1.2 %far.3 = (f32[320,128]{1,0:T(8,128)S(1)}, f32[320,128]{1,0:T(8,128)S(1)}, f32[8,128]{1,0:T(8,128)}) custom-call(bf16[1344,128]{1,0:T(8,128)(2,1)S(1)} %collective-permute-done.7.first, bf16[1344,128]{1,0:T(8,128)(2,1)S(1)} %collective-permute-done.8.second, bf16[256,2048]{1,0:T(8,128)(2,1)S(1)} %get-tuple-element.28.both_t, ...), custom_call_target="tpu_custom_call" | custom-call | tf_op jit(solution)/shard_map/far/pallas_call | solution.py:263
  47.5 2.1 %collective-permute-start.10 = (f32[320,128]{1,0:T(8,128)S(1)}, f32[320,128]{1,0:T(8,128)S(1)}, u32[]{:S(2)}, u32[]{:S(2)}) collective-permute-start(f32[320,128]{1,0:T(8,128)S(1)} %get-tuple-element.41), channel_id=1, source_target_pairs={{0,1},{1,0},{2,3},{3,2},{4,5},{5,4},{6,7},{7,6},{8,9},{9,8},{10,11... | collective-permute-start | bytes 491528 | tf_op jit(solution)/shard_map/ppermute | solution.py:256
  49.6 1.2 %collective-permute-done.10.refs_7_ = f32[320,128]{1,0:T(8,128)S(1)} collective-permute-done((f32[320,128]{1,0:T(8,128)S(1)}, f32[320,128]{1,0:T(8,128)S(1)}, u32[]{:S(2)}, u32[]{:S(2)}) %collective-permute-start.10) | collective-permute-done | bytes 163872 | tf_op jit(solution)/shard_map/ppermute | solution.py:256
  51.5 31.7 %all_to_all.10 = f16[32,72,128]{2,1,0:T(8,128)(2,1)S(1)} all-to-all(f16[32,72,128]{2,1,0:T(8,128)(2,1)S(1)} %convert_element_type.12), channel_id=1, replica_groups=mesh['tm'=32,'space'=16] {'tm'}, dimensions={0} | all-to-all | bytes 1179648 | tf_op jit(solution)/shard_map/all_to_all | solution.py:330
  83.2 0.8 suffix.1
  84.1 23.4 %all_to_all.11 = f16[32,72,128]{2,1,0:T(8,128)(2,1)S(1)} all-to-all(f16[32,72,128]{2,1,0:T(8,128)(2,1)S(1)} %convert_element_type.14), channel_id=1, replica_groups=mesh['tm'=32,'space'=16] {'tm'}, dimensions={0} | all-to-all | bytes 1179648 | tf_op jit(solution)/shard_map/all_to_all | solution.py:330
  107.6 1.6 %last.1 = (f32[2048,128]{1,0:T(8,128)}, f32[64,128]{1,0:T(8,128)}) custom-call(s32[1]{0:T(128)} %bitcast.refs_0_, f32[32,64,128]{2,1,0:T(8,128)S(1)} %get-tuple-element.42.refs_1_, f32[64,128]{1,0:T(8,128)S(1)} %get-tuple-element.43.refs_2_, f32[32,72,128]{2,1,0:T(8,128)S(1)} %convert_element_type.15.refs_3_, f32[1,2048]{1,0:T(1,128)S(1)} %copy-done.1), custom_call_target="tpu_custom_call" | custom-call | tf_op jit(solution)/shard_map/last/pallas_call | solution.py:342
  (25 shorter events, 2.1 us)
Async XLA Ops:
  1.7 16.1 %copy-start = (f32[128,64]{0,1:T(8,128)S(1)}, f32[128,64]{0,1:T(8,128)}, u32[]{:S(2)}) copy-start(f32[128,64]{0,1:T(8,128)} %param.11) | copy-start | bytes 98308
  1.7 5.5 %collective-permute-start = (bf16[2112,128]{1,0:T(8,128)(2,1)S(1)}, bf16[2112,128]{1,0:T(8,128)(2,1)S(1)}, u32[]{:S(2)}, u32[]{:S(2)}) collective-permute-start(bf16[2112,128]{1,0:T(8,128)(2,1)S(1)} %pack.1.mine), channel_id=1, source_target_pairs={{0,1},{1,0},{2,3},{3,2},{4,5},{5,4},{6,7},{7,6},{8,9},{9,8},{10,11... | collective-permute-start | bytes 1622024 | tf_op jit(solution)/shard_map/ppermute | solution.py:256
  3.7 12.0 %collective-permute-start.1 = (bf16[1856,128]{1,0:T(8,128)(2,1)S(1)}, bf16[1856,128]{1,0:T(8,128)(2,1)S(1)}, u32[]{:S(2)}, u32[]{:S(2)}) collective-permute-start(bf16[1856,128]{1,0:T(8,128)(2,1)S(1)} %slice.28), channel_id=1, source_target_pairs={{0,2},{1,15},{2,4},{3,1},{4,6},{5,3},{6,8},{7,5},{8,10},{9,7},{10,... | collective-permute-start | bytes 1425416 | tf_op jit(solution)/shard_map/ppermute | solution.py:253
  7.2 13.6 %collective-permute-start.2 = (bf16[1856,128]{1,0:T(8,128)(2,1)S(1)}, bf16[1856,128]{1,0:T(8,128)(2,1)S(1)}, u32[]{:S(2)}, u32[]{:S(2)}) collective-permute-start(bf16[1856,128]{1,0:T(8,128)(2,1)S(1)} %slice.29), channel_id=1, source_target_pairs={{0,2},{1,15},{2,4},{3,1},{4,6},{5,3},{6,8},{7,5},{8,10},{9,7},{10,... | collective-permute-start | bytes 1425416 | tf_op jit(solution)/shard_map/ppermute | solution.py:253
  15.7 11.1 %collective-permute-start.3 = (bf16[1600,128]{1,0:T(8,128)(2,1)S(1)}, bf16[1600,128]{1,0:T(8,128)(2,1)S(1)}, u32[]{:S(2)}, u32[]{:S(2)}) collective-permute-start(bf16[1600,128]{1,0:T(8,128)(2,1)S(1)} %slice.30), channel_id=1, source_target_pairs={{0,2},{1,15},{2,4},{3,1},{4,6},{5,3},{6,8},{7,5},{8,10},{9,7},{10,... | collective-permute-start | bytes 1228808 | tf_op jit(solution)/shard_map/ppermute | solution.py:253
  20.8 13.3 %collective-permute-start.4 = (bf16[1600,128]{1,0:T(8,128)(2,1)S(1)}, bf16[1600,128]{1,0:T(8,128)(2,1)S(1)}, u32[]{:S(2)}, u32[]{:S(2)}) collective-permute-start(bf16[1600,128]{1,0:T(8,128)(2,1)S(1)} %slice.24), channel_id=1, source_target_pairs={{0,2},{1,15},{2,4},{3,1},{4,6},{5,3},{6,8},{7,5},{8,10},{9,7},{10,... | collective-permute-start | bytes 1228808 | tf_op jit(solution)/shard_map/ppermute | solution.py:253
  26.8 15.8 %collective-permute-start.5 = (bf16[1088,128]{1,0:T(8,128)(2,1)S(1)}, bf16[1088,128]{1,0:T(8,128)(2,1)S(1)}, u32[]{:S(2)}, u32[]{:S(2)}) collective-permute-start(bf16[1088,128]{1,0:T(8,128)(2,1)S(1)} %slice.25), channel_id=1, source_target_pairs={{0,4},{1,13},{2,6},{3,15},{4,8},{5,1},{6,10},{7,3},{8,12},{9,5},{1... | collective-permute-start | bytes 835592 | tf_op jit(solution)/shard_map/ppermute | solution.py:253
  30.2 15.9 %collective-permute-start.7 = (bf16[1344,128]{1,0:T(8,128)(2,1)S(1)}, bf16[1344,128]{1,0:T(8,128)(2,1)S(1)}, u32[]{:S(2)}, u32[]{:S(2)}) collective-permute-start(bf16[1344,128]{1,0:T(8,128)(2,1)S(1)} %slice.26), channel_id=1, source_target_pairs={{0,2},{1,15},{2,4},{3,1},{4,6},{5,3},{6,8},{7,5},{8,10},{9,7},{10,... | collective-permute-start | bytes 1032200 | tf_op jit(solution)/shard_map/ppermute | solution.py:253
  34.2 12.1 %collective-permute-start.8 = (bf16[1344,128]{1,0:T(8,128)(2,1)S(1)}, bf16[1344,128]{1,0:T(8,128)(2,1)S(1)}, u32[]{:S(2)}, u32[]{:S(2)}) collective-permute-start(bf16[1344,128]{1,0:T(8,128)(2,1)S(1)} %slice.31), channel_id=1, source_target_pairs={{0,2},{1,15},{2,4},{3,1},{4,6},{5,3},{6,8},{7,5},{8,10},{9,7},{10,... | collective-permute-start | bytes 1032200 | tf_op jit(solution)/shard_map/ppermute | solution.py:253
  39.3 3.3 %collective-permute-start.6 = (f32[320,128]{1,0:T(8,128)S(1)}, f32[320,128]{1,0:T(8,128)S(1)}, u32[]{:S(2)}, u32[]{:S(2)}) collective-permute-start(f32[320,128]{1,0:T(8,128)S(1)} %get-tuple-element.34), channel_id=1, source_target_pairs={{0,1},{1,0},{2,3},{3,2},{4,5},{5,4},{6,7},{7,6},{8,9},{9,8},{10,11... | collective-permute-start | bytes 491528 | tf_op jit(solution)/shard_map/ppermute | solution.py:256
  44.0 6.8 %copy-start.1 = (f32[1,2048]{1,0:T(1,128)S(1)}, f32[1,2048]{1,0:T(1,128)}, u32[]{:S(2)}) copy-start(f32[1,2048]{1,0:T(1,128)} %refs_4_.1) | copy-start | bytes 24580
  44.0 6.8 %copy-start.2 = (f32[64,64]{1,0:T(8,128)S(1)}, f32[64,64]{1,0:T(8,128)}, u32[]{:S(2)}) copy-start(f32[64,64]{1,0:T(8,128)} %refs_8_.1) | copy-start | bytes 49156
  44.0 5.5 %collective-permute-start.9 = (f32[448,128]{1,0:T(8,128)S(1)}, f32[448,128]{1,0:T(8,128)S(1)}, u32[]{:S(2)}, u32[]{:S(2)}) collective-permute-start(f32[448,128]{1,0:T(8,128)S(1)} %get-tuple-element.40), channel_id=1, source_target_pairs={{0,1},{1,0},{2,3},{3,2},{4,5},{5,4},{6,7},{7,6},{8,9},{9,8},{10,11... | collective-permute-start | bytes 688136 | tf_op jit(solution)/shard_map/ppermute | solution.py:256
  47.5 3.3 %collective-permute-start.10 = (f32[320,128]{1,0:T(8,128)S(1)}, f32[320,128]{1,0:T(8,128)S(1)}, u32[]{:S(2)}, u32[]{:S(2)}) collective-permute-start(f32[320,128]{1,0:T(8,128)S(1)} %get-tuple-element.41), channel_id=1, source_target_pairs={{0,1},{1,0},{2,3},{3,2},{4,5},{5,4},{6,7},{7,6},{8,9},{9,8},{10,11... | collective-permute-start | bytes 491528 | tf_op jit(solution)/shard_map/ppermute | solution.py:256

commit v12 on v11

--- a/solution.py
+++ b/solution.py
@@ -98,14 +98,8 @@
     token[...] = passed[...]
 
 
-def three_kernel(first, second, straight, both_t, passed, keep, give, token, pair, single):
-    count, width = CORES * first.shape[1], straight.shape[1]
-    far_tiles((first, second), both_t, pair.at[0], pair.at[1])
-    far_tiles((straight,), both_t, single.at[0], single.at[1])
-    for at, out in enumerate((keep, give)):
-        out[:count, :] = pair[at, :count, :]
-        out[count : count + width, :] = single[at, :width, :]
-        out[count + width :, :] = pair[at, count:, :] + single[at, width:, :]
+def farthest_kernel(straight, both_t, passed, keep, give, token):
+    far_tiles((straight,), both_t, keep, give)
     token[...] = passed[...]
 
 
@@ -116,8 +110,8 @@
 
 
 def message_kernel(rows, chips, hops, at, own, *refs):
-    kept, given = refs[: hops - 1], refs[hops - 1 : 2 * hops - 2]
-    tip, decay, out, copied, own_arrow, plain, done = refs[2 * hops - 2 :]
+    kept, given = refs[:hops], refs[hops : 2 * hops]
+    tip, decay, out, copied, own_arrow, plain, done = refs[2 * hops :]
     width = own.shape[1]
     per = width // rows
     chip, core = at[0] // CORES, at[0] % CORES
@@ -129,15 +123,13 @@
 
     put(own[:width, :], 0, core)
     put(own[width : CORES * width, :], 0, 1 - core)
-    for s in range(hops - 1):
+    for s in range(hops):
         hop = (s + 1) * way
         put(kept[s][:width, :], -hop, core)
         put(given[s][:width, :], hop, 1 - core)
-        put(kept[s][width : 2 * width, :], -hop, 1 - core)
-        put(given[s][width : 2 * width, :], hop, core)
-        if kept[s].shape[0] > 3 * width:
-            put(kept[s][2 * width : 3 * width, :], hops, core)
-            put(given[s][2 * width : 3 * width, :], hops, 1 - core)
+        if s < hops - 1:
+            put(kept[s][width : 2 * width, :], -hop, 1 - core)
+            put(given[s][width : 2 * width, :], hop, core)
     copy = pltpu.make_async_copy(plain, copied, done)
     copy.start()
     border = own_arrow.shape[0]
@@ -258,14 +250,13 @@
     def shared(panel, count):
         return panel[cut * count - (order + arrow - panel.shape[0]) :]
 
-    def product(kernel, name, count, panels, token, scratch=()):
+    def product(kernel, name, count, panels, token):
         tall = count * width + arrow
         return pl.pallas_call(
             kernel,
             out_shape=(*[jax.ShapeDtypeStruct((tall, width), f32)] * 2, mark),
             in_specs=[VMEM] * (len(panels) + 2),
             out_specs=(VMEM,) * 3,
-            scratch_shapes=scratch,
             compiler_params=SMALL,
             name=name,
         )(*map(near, panels), near(both_t), token)
@@ -294,22 +285,16 @@
     second_2 = hop(shared(second, 2))
     keep_1, give_1, token = product(far_kernel, "far", 2, (first, second), token)
     first_2, token = lax.optimization_barrier((first_2, token))
-    first_4 = hop(shared(first_2, 4), 2)
     first_3 = hop(shared(first_2, 3))
     second_3 = hop(shared(second_2, 3))
+    first_4 = hop(shared(first_2, 4), 2)
     given_1 = swap(give_1)
-    token, given_1 = lax.optimization_barrier((token, given_1))
-    keep_2, give_2, token = product(
-        three_kernel,
-        "three",
-        3,
-        (first_2, second_2, first_4),
-        token,
-        [pltpu.VMEM((2, both + arrow, width), f32), pltpu.VMEM((2, width + arrow, width), f32)],
-    )
+    keep_2, give_2, token = product(far_kernel, "far", 2, (first_2, second_2), token)
     given_2 = swap(give_2)
+    token, given_1, given_2 = lax.optimization_barrier((token, given_1, given_2))
     keep_3, give_3, token = product(far_kernel, "far", 2, (first_3, second_3), token)
-    kept, given = (keep_1, keep_2, keep_3), (given_1, given_2, swap(give_3))
+    keep_4, give_4, token = product(farthest_kernel, "farthest", 1, (first_4,), token)
+    kept, given = (keep_1, keep_2, keep_3, keep_4), (given_1, given_2, swap(give_3), swap(give_4))
 
     message = (pieces, rows + PAD, width)
     sent, plain, own_arrow = pl.pallas_call(
@@ -319,7 +304,7 @@
             jax.ShapeDtypeStruct((pieces, rows, width), f32),
             jax.ShapeDtypeStruct((arrow, width), f32),
         ),
-        in_specs=[SMEM] + [VMEM] * (2 * hops + 1),
+        in_specs=[SMEM] + [VMEM] * (2 * hops + 3),
         out_specs=(VMEM, pl.BlockSpec(memory_space=pl.ANY), VMEM),
         scratch_shapes=[pltpu.VMEM((pieces, rows, width), f32), pltpu.SemaphoreType.DMA],
         compiler_params=SMALL,

time: 110 us -> 114 us (1.036)
  the two profiles are of different devices: /device:TPU:64 before, /device:TPU:8 now
where the time goes in v12:
time: 114 us; the launch traced here: 113 us
  blocking collectives  52.2 us (46%)
  starting transfers between devices  29.8 us (26%)
  waiting for transfers between devices  21.2 us (19%)
  Pallas kernels  8.34 us (7%)
    all_to_all x2, blocking collectives, exchange(): moved = lax.all_to_all(values.astype(jnp.float16), 'tm', 0, 0, tiled=True)  52.2 us
    ppermute x7, starting transfers between devices, hop(): return lax.ppermute(panel, 'space', pairs)  19.3 us
    ppermute x7, waiting for transfers between devices, hop(): return lax.ppermute(panel, 'space', pairs)  19 us
    ppermute x5, starting transfers between devices, swap(): return lax.ppermute(tile, 'space', [(p, p ^ 1) for p in range(devices)])  10.4 us
    pallas_call x4, Pallas kernels, product(): pl.pallas_call(kernel, out_shape=(*[jax.ShapeDtypeStruct((tall, width), f...  3.17 us
  transfers between devices with their start and end apart: 12, of which 7 were waited for; matrix products, arithmetic and copies ran while one was open for 0% of the time, Pallas kernels for 4%

profile of v12, /device:TPU:8, one launch (start us, length us, event | category | flops | bytes accessed | tf_op | source)
XLA Modules:
  0.0 113.0 jit_solution(12868227026049582494)
XLA Ops:
  0.6 1.1 pack.1.mine
  1.7 1.9 %collective-permute-start = (bf16[2112,128]{1,0:T(8,128)(2,1)S(1)}, bf16[2112,128]{1,0:T(8,128)(2,1)S(1)}, u32[]{:S(2)}, u32[]{:S(2)}) collective-permute-start(bf16[2112,128]{1,0:T(8,128)(2,1)S(1)} %pack.1.mine), channel_id=1, source_target_pairs={{0,1},{1,0},{2,3},{3,2},{4,5},{5,4},{6,7},{7,6},{8,9},{9,8},{10,11... | collective-permute-start | bytes 1622024 | tf_op jit(solution)/shard_map/ppermute | solution.py:248
  3.7 3.5 %collective-permute-start.1 = (bf16[1856,128]{1,0:T(8,128)(2,1)S(1)}, bf16[1856,128]{1,0:T(8,128)(2,1)S(1)}, u32[]{:S(2)}, u32[]{:S(2)}) collective-permute-start(bf16[1856,128]{1,0:T(8,128)(2,1)S(1)} %slice.28), channel_id=1, source_target_pairs={{0,2},{1,15},{2,4},{3,1},{4,6},{5,3},{6,8},{7,5},{8,10},{9,7},{10,... | collective-permute-start | bytes 1425416 | tf_op jit(solution)/shard_map/ppermute | solution.py:245
  7.2 3.5 %collective-permute-start.2 = (bf16[1856,128]{1,0:T(8,128)(2,1)S(1)}, bf16[1856,128]{1,0:T(8,128)(2,1)S(1)}, u32[]{:S(2)}, u32[]{:S(2)}) collective-permute-start(bf16[1856,128]{1,0:T(8,128)(2,1)S(1)} %slice.29), channel_id=1, source_target_pairs={{0,2},{1,15},{2,4},{3,1},{4,6},{5,3},{6,8},{7,5},{8,10},{9,7},{10,... | collective-permute-start | bytes 1425416 | tf_op jit(solution)/shard_map/ppermute | solution.py:245
  10.7 7.3 %collective-permute-done.1.first = bf16[1856,128]{1,0:T(8,128)(2,1)S(1)} collective-permute-done((bf16[1856,128]{1,0:T(8,128)(2,1)S(1)}, bf16[1856,128]{1,0:T(8,128)(2,1)S(1)}, u32[]{:S(2)}, u32[]{:S(2)}) %collective-permute-start.1) | collective-permute-done | bytes 475168 | tf_op jit(solution)/shard_map/ppermute | solution.py:245
  18.1 1.9 %collective-permute-start.3 = (bf16[1600,128]{1,0:T(8,128)(2,1)S(1)}, bf16[1600,128]{1,0:T(8,128)(2,1)S(1)}, u32[]{:S(2)}, u32[]{:S(2)}) collective-permute-start(bf16[1600,128]{1,0:T(8,128)(2,1)S(1)} %slice.30), channel_id=1, source_target_pairs={{0,2},{1,15},{2,4},{3,1},{4,6},{5,3},{6,8},{7,5},{8,10},{9,7},{10,... | collective-permute-start | bytes 1228808 | tf_op jit(solution)/shard_map/ppermute | solution.py:245
  20.0 1.1 own.1
  21.1 2.0 %collective-permute-done.2.second = bf16[1856,128]{1,0:T(8,128)(2,1)S(1)} collective-permute-done((bf16[1856,128]{1,0:T(8,128)(2,1)S(1)}, bf16[1856,128]{1,0:T(8,128)(2,1)S(1)}, u32[]{:S(2)}, u32[]{:S(2)}) %collective-permute-start.2) | collective-permute-done | bytes 475168 | tf_op jit(solution)/shard_map/ppermute | solution.py:245
  23.2 1.9 %collective-permute-start.4 = (bf16[1600,128]{1,0:T(8,128)(2,1)S(1)}, bf16[1600,128]{1,0:T(8,128)(2,1)S(1)}, u32[]{:S(2)}, u32[]{:S(2)}) collective-permute-start(bf16[1600,128]{1,0:T(8,128)(2,1)S(1)} %slice.24), channel_id=1, source_target_pairs={{0,2},{1,15},{2,4},{3,1},{4,6},{5,3},{6,8},{7,5},{8,10},{9,7},{10,... | collective-permute-start | bytes 1228808 | tf_op jit(solution)/shard_map/ppermute | solution.py:245
  25.9 3.2 %collective-permute-done.3.first = bf16[1600,128]{1,0:T(8,128)(2,1)S(1)} collective-permute-done((bf16[1600,128]{1,0:T(8,128)(2,1)S(1)}, bf16[1600,128]{1,0:T(8,128)(2,1)S(1)}, u32[]{:S(2)}, u32[]{:S(2)}) %collective-permute-start.3) | collective-permute-done | bytes 409632 | tf_op jit(solution)/shard_map/ppermute | solution.py:245
  29.2 1.9 %collective-permute-start.5 = (bf16[1344,128]{1,0:T(8,128)(2,1)S(1)}, bf16[1344,128]{1,0:T(8,128)(2,1)S(1)}, u32[]{:S(2)}, u32[]{:S(2)}) collective-permute-start(bf16[1344,128]{1,0:T(8,128)(2,1)S(1)} %slice.25), channel_id=1, source_target_pairs={{0,2},{1,15},{2,4},{3,1},{4,6},{5,3},{6,8},{7,5},{8,10},{9,7},{10,... | collective-permute-start | bytes 1032200 | tf_op jit(solution)/shard_map/ppermute | solution.py:245
  31.1 3.1 %collective-permute-done.4.second = bf16[1600,128]{1,0:T(8,128)(2,1)S(1)} collective-permute-done((bf16[1600,128]{1,0:T(8,128)(2,1)S(1)}, bf16[1600,128]{1,0:T(8,128)(2,1)S(1)}, u32[]{:S(2)}, u32[]{:S(2)}) %collective-permute-start.4) | collective-permute-done | bytes 409632 | tf_op jit(solution)/shard_map/ppermute | solution.py:245
  34.2 1.9 %collective-permute-start.6 = (bf16[1344,128]{1,0:T(8,128)(2,1)S(1)}, bf16[1344,128]{1,0:T(8,128)(2,1)S(1)}, u32[]{:S(2)}, u32[]{:S(2)}) collective-permute-start(bf16[1344,128]{1,0:T(8,128)(2,1)S(1)} %slice.31), channel_id=1, source_target_pairs={{0,2},{1,15},{2,4},{3,1},{4,6},{5,3},{6,8},{7,5},{8,10},{9,7},{10,... | collective-permute-start | bytes 1032200 | tf_op jit(solution)/shard_map/ppermute | solution.py:245
  36.2 4.7 %collective-permute-start.9 = (bf16[1088,128]{1,0:T(8,128)(2,1)S(1)}, bf16[1088,128]{1,0:T(8,128)(2,1)S(1)}, u32[]{:S(2)}, u32[]{:S(2)}) collective-permute-start(bf16[1088,128]{1,0:T(8,128)(2,1)S(1)} %slice.27), channel_id=1, source_target_pairs={{0,4},{1,13},{2,6},{3,15},{4,8},{5,1},{6,10},{7,3},{8,12},{9,5},{1... | collective-permute-start | bytes 835592 | tf_op jit(solution)/shard_map/ppermute | solution.py:245
  40.9 1.9 %collective-permute-start.7 = (f32[320,128]{1,0:T(8,128)S(1)}, f32[320,128]{1,0:T(8,128)S(1)}, u32[]{:S(2)}, u32[]{:S(2)}) collective-permute-start(f32[320,128]{1,0:T(8,128)S(1)} %get-tuple-element.40), channel_id=1, source_target_pairs={{0,1},{1,0},{2,3},{3,2},{4,5},{5,4},{6,7},{7,6},{8,9},{9,8},{10,11... | collective-permute-start | bytes 491528 | tf_op jit(solution)/shard_map/ppermute | solution.py:248
  43.5 2.4 %collective-permute-start.8 = (f32[320,128]{1,0:T(8,128)S(1)}, f32[320,128]{1,0:T(8,128)S(1)}, u32[]{:S(2)}, u32[]{:S(2)}) collective-permute-start(f32[320,128]{1,0:T(8,128)S(1)} %get-tuple-element.41), channel_id=1, source_target_pairs={{0,1},{1,0},{2,3},{3,2},{4,5},{5,4},{6,7},{7,6},{8,9},{9,8},{10,11... | collective-permute-start | bytes 491528 | tf_op jit(solution)/shard_map/ppermute | solution.py:248
  45.9 1.0 collective-permute-done.8.refs_7_
  47.7 2.3 %collective-permute-start.10 = (f32[320,128]{1,0:T(8,128)S(1)}, f32[320,128]{1,0:T(8,128)S(1)}, u32[]{:S(2)}, u32[]{:S(2)}) collective-permute-start(f32[320,128]{1,0:T(8,128)S(1)} %get-tuple-element.48), channel_id=1, source_target_pairs={{0,1},{1,0},{2,3},{3,2},{4,5},{5,4},{6,7},{7,6},{8,9},{9,8},{10,11... | collective-permute-start | bytes 491528 | tf_op jit(solution)/shard_map/ppermute | solution.py:248
  50.0 3.3 %collective-permute-done.9.straight = bf16[1088,128]{1,0:T(8,128)(2,1)S(1)} collective-permute-done((bf16[1088,128]{1,0:T(8,128)(2,1)S(1)}, bf16[1088,128]{1,0:T(8,128)(2,1)S(1)}, u32[]{:S(2)}, u32[]{:S(2)}) %collective-permute-start.9) | collective-permute-done | bytes 278560 | tf_op jit(solution)/shard_map/ppermute | solution.py:245
  54.2 1.9 %collective-permute-start.11 = (f32[192,128]{1,0:T(8,128)S(1)}, f32[192,128]{1,0:T(8,128)S(1)}, u32[]{:S(2)}, u32[]{:S(2)}) collective-permute-start(f32[192,128]{1,0:T(8,128)S(1)} %get-tuple-element.49), channel_id=1, source_target_pairs={{0,1},{1,0},{2,3},{3,2},{4,5},{5,4},{6,7},{7,6},{8,9},{9,8},{10,11... | collective-permute-start | bytes 294920 | tf_op jit(solution)/shard_map/ppermute | solution.py:248
  56.1 1.3 %collective-permute-done.11.refs_9_ = f32[192,128]{1,0:T(8,128)S(1)} collective-permute-done((f32[192,128]{1,0:T(8,128)S(1)}, f32[192,128]{1,0:T(8,128)S(1)}, u32[]{:S(2)}, u32[]{:S(2)}) %collective-permute-start.11) | collective-permute-done | bytes 98336 | tf_op jit(solution)/shard_map/ppermute | solution.py:248
  58.1 28.0 %all_to_all.10 = f16[32,72,128]{2,1,0:T(8,128)(2,1)S(1)} all-to-all(f16[32,72,128]{2,1,0:T(8,128)(2,1)S(1)} %convert_element_type.12), channel_id=1, replica_groups=mesh['tm'=32,'space'=16] {'tm'}, dimensions={0} | all-to-all | bytes 1179648 | tf_op jit(solution)/shard_map/all_to_all | solution.py:315
  87.1 24.2 %all_to_all.11 = f16[32,72,128]{2,1,0:T(8,128)(2,1)S(1)} all-to-all(f16[32,72,128]{2,1,0:T(8,128)(2,1)S(1)} %convert_element_type.14), channel_id=1, replica_groups=mesh['tm'=32,'space'=16] {'tm'}, dimensions={0} | all-to-all | bytes 1179648 | tf_op jit(solution)/shard_map/all_to_all | solution.py:315
  111.4 1.6 %last.1 = (f32[2048,128]{1,0:T(8,128)}, f32[64,128]{1,0:T(8,128)}) custom-call(s32[1]{0:T(128)} %bitcast.refs_0_, f32[32,64,128]{2,1,0:T(8,128)S(1)} %get-tuple-element.50.refs_1_, f32[64,128]{1,0:T(8,128)S(1)} %get-tuple-element.51.refs_2_, f32[32,72,128]{2,1,0:T(8,128)S(1)} %convert_element_type.15.refs_3_, f32[1,2048]{1,0:T(1,128)S(1)} %copy-done.1), custom_call_target="tpu_custom_call" | custom-call | tf_op jit(solution)/shard_map/last/pallas_call | solution.py:327
  (28 shorter events, 5.1 us)
Async XLA Ops:
  1.7 18.3 %copy-start = (f32[128,64]{0,1:T(8,128)S(1)}, f32[128,64]{0,1:T(8,128)}, u32[]{:S(2)}) copy-start(f32[128,64]{0,1:T(8,128)} %param.11) | copy-start | bytes 98308
  1.7 5.5 %collective-permute-start = (bf16[2112,128]{1,0:T(8,128)(2,1)S(1)}, bf16[2112,128]{1,0:T(8,128)(2,1)S(1)}, u32[]{:S(2)}, u32[]{:S(2)}) collective-permute-start(bf16[2112,128]{1,0:T(8,128)(2,1)S(1)} %pack.1.mine), channel_id=1, source_target_pairs={{0,1},{1,0},{2,3},{3,2},{4,5},{5,4},{6,7},{7,6},{8,9},{9,8},{10,11... | collective-permute-start | bytes 1622024 | tf_op jit(solution)/shard_map/ppermute | solution.py:248
  3.7 14.4 %collective-permute-start.1 = (bf16[1856,128]{1,0:T(8,128)(2,1)S(1)}, bf16[1856,128]{1,0:T(8,128)(2,1)S(1)}, u32[]{:S(2)}, u32[]{:S(2)}) collective-permute-start(bf16[1856,128]{1,0:T(8,128)(2,1)S(1)} %slice.28), channel_id=1, source_target_pairs={{0,2},{1,15},{2,4},{3,1},{4,6},{5,3},{6,8},{7,5},{8,10},{9,7},{10,... | collective-permute-start | bytes 1425416 | tf_op jit(solution)/shard_map/ppermute | solution.py:245
  7.2 15.9 %collective-permute-start.2 = (bf16[1856,128]{1,0:T(8,128)(2,1)S(1)}, bf16[1856,128]{1,0:T(8,128)(2,1)S(1)}, u32[]{:S(2)}, u32[]{:S(2)}) collective-permute-start(bf16[1856,128]{1,0:T(8,128)(2,1)S(1)} %slice.29), channel_id=1, source_target_pairs={{0,2},{1,15},{2,4},{3,1},{4,6},{5,3},{6,8},{7,5},{8,10},{9,7},{10,... | collective-permute-start | bytes 1425416 | tf_op jit(solution)/shard_map/ppermute | solution.py:245
  18.1 11.1 %collective-permute-start.3 = (bf16[1600,128]{1,0:T(8,128)(2,1)S(1)}, bf16[1600,128]{1,0:T(8,128)(2,1)S(1)}, u32[]{:S(2)}, u32[]{:S(2)}) collective-permute-start(bf16[1600,128]{1,0:T(8,128)(2,1)S(1)} %slice.30), channel_id=1, source_target_pairs={{0,2},{1,15},{2,4},{3,1},{4,6},{5,3},{6,8},{7,5},{8,10},{9,7},{10,... | collective-permute-start | bytes 1228808 | tf_op jit(solution)/shard_map/ppermute | solution.py:245
  23.2 11.1 %collective-permute-start.4 = (bf16[1600,128]{1,0:T(8,128)(2,1)S(1)}, bf16[1600,128]{1,0:T(8,128)(2,1)S(1)}, u32[]{:S(2)}, u32[]{:S(2)}) collective-permute-start(bf16[1600,128]{1,0:T(8,128)(2,1)S(1)} %slice.24), channel_id=1, source_target_pairs={{0,2},{1,15},{2,4},{3,1},{4,6},{5,3},{6,8},{7,5},{8,10},{9,7},{10,... | collective-permute-start | bytes 1228808 | tf_op jit(solution)/shard_map/ppermute | solution.py:245
  29.2 17.8 %collective-permute-start.5 = (bf16[1344,128]{1,0:T(8,128)(2,1)S(1)}, bf16[1344,128]{1,0:T(8,128)(2,1)S(1)}, u32[]{:S(2)}, u32[]{:S(2)}) collective-permute-start(bf16[1344,128]{1,0:T(8,128)(2,1)S(1)} %slice.25), channel_id=1, source_target_pairs={{0,2},{1,15},{2,4},{3,1},{4,6},{5,3},{6,8},{7,5},{8,10},{9,7},{10,... | collective-permute-start | bytes 1032200 | tf_op jit(solution)/shard_map/ppermute | solution.py:245
  34.2 12.7 %collective-permute-start.6 = (bf16[1344,128]{1,0:T(8,128)(2,1)S(1)}, bf16[1344,128]{1,0:T(8,128)(2,1)S(1)}, u32[]{:S(2)}, u32[]{:S(2)}) collective-permute-start(bf16[1344,128]{1,0:T(8,128)(2,1)S(1)} %slice.31), channel_id=1, source_target_pairs={{0,2},{1,15},{2,4},{3,1},{4,6},{5,3},{6,8},{7,5},{8,10},{9,7},{10,... | collective-permute-start | bytes 1032200 | tf_op jit(solution)/shard_map/ppermute | solution.py:245
  36.2 17.0 %collective-permute-start.9 = (bf16[1088,128]{1,0:T(8,128)(2,1)S(1)}, bf16[1088,128]{1,0:T(8,128)(2,1)S(1)}, u32[]{:S(2)}, u32[]{:S(2)}) collective-permute-start(bf16[1088,128]{1,0:T(8,128)(2,1)S(1)} %slice.27), channel_id=1, source_target_pairs={{0,4},{1,13},{2,6},{3,15},{4,8},{5,1},{6,10},{7,3},{8,12},{9,5},{1... | collective-permute-start | bytes 835592 | tf_op jit(solution)/shard_map/ppermute | solution.py:245
  40.9 5.1 %collective-permute-start.7 = (f32[320,128]{1,0:T(8,128)S(1)}, f32[320,128]{1,0:T(8,128)S(1)}, u32[]{:S(2)}, u32[]{:S(2)}) collective-permute-start(f32[320,128]{1,0:T(8,128)S(1)} %get-tuple-element.40), channel_id=1, source_target_pairs={{0,1},{1,0},{2,3},{3,2},{4,5},{5,4},{6,7},{7,6},{8,9},{9,8},{10,11... | collective-permute-start | bytes 491528 | tf_op jit(solution)/shard_map/ppermute | solution.py:248
  43.5 3.4 %collective-permute-start.8 = (f32[320,128]{1,0:T(8,128)S(1)}, f32[320,128]{1,0:T(8,128)S(1)}, u32[]{:S(2)}, u32[]{:S(2)}) collective-permute-start(f32[320,128]{1,0:T(8,128)S(1)} %get-tuple-element.41), channel_id=1, source_target_pairs={{0,1},{1,0},{2,3},{3,2},{4,5},{5,4},{6,7},{7,6},{8,9},{9,8},{10,11... | collective-permute-start | bytes 491528 | tf_op jit(solution)/shard_map/ppermute | solution.py:248
  46.9 10.5 %copy-start.1 = (f32[1,2048]{1,0:T(1,128)S(1)}, f32[1,2048]{1,0:T(1,128)}, u32[]{:S(2)}) copy-start(f32[1,2048]{1,0:T(1,128)} %refs_4_.1) | copy-start | bytes 24580
  46.9 10.5 %copy-start.2 = (f32[64,64]{1,0:T(8,128)S(1)}, f32[64,64]{1,0:T(8,128)}, u32[]{:S(2)}) copy-start(f32[64,64]{1,0:T(8,128)} %refs_10_.1) | copy-start | bytes 49156
  47.7 9.7 %collective-permute-start.10 = (f32[320,128]{1,0:T(8,128)S(1)}, f32[320,128]{1,0:T(8,128)S(1)}, u32[]{:S(2)}, u32[]{:S(2)}) collective-permute-start(f32[320,128]{1,0:T(8,128)S(1)} %get-tuple-element.48), channel_id=1, source_target_pairs={{0,1},{1,0},{2,3},{3,2},{4,5},{5,4},{6,7},{7,6},{8,9},{9,8},{10,11... | collective-permute-start | bytes 491528 | tf_op jit(solution)/shard_map/ppermute | solution.py:248
  54.2 3.2 %collective-permute-start.11 = (f32[192,128]{1,0:T(8,128)S(1)}, f32[192,128]{1,0:T(8,128)S(1)}, u32[]{:S(2)}, u32[]{:S(2)}) collective-permute-start(f32[192,128]{1,0:T(8,128)S(1)} %get-tuple-element.49), channel_id=1, source_target_pairs={{0,1},{1,0},{2,3},{3,2},{4,5},{5,4},{6,7},{7,6},{8,9},{9,8},{10,11... | collective-permute-start | bytes 294920 | tf_op jit(solution)/shard_map/ppermute | solution.py:248

commit v13 on v11

--- a/solution.py
+++ b/solution.py
@@ -57,11 +57,12 @@
     return panel, jnp.where(at < 2, rooted(tail, tail[3:4, :]), 0.0)
 
 
-def own_kernel(at, mine, other, sigma_end, arrow_end, tile, both_t, end, token, done):
-    width = mine.shape[1]
+def own_kernel(at, mine, other, mine_top, other_top, sigma_end, arrow_end, tile, both_t, end, token, done):
+    tall, width = mine.shape
     depth = both_t.shape[1]
+    order = depth + mine_top.shape[0]
     rows = end.shape[0] - PAD
-    share = arrow_end.shape[0] * rows // depth
+    share = arrow_end.shape[0] * rows // order
     spot = pl.ds(pl.multiple_of(at[0] * rows, rows), rows)
     copy = pltpu.make_async_copy(sigma_end.at[spot], end.at[pl.ds(0, rows)], done)
     copy.start()
@@ -71,9 +72,10 @@
         pair = jnp.where(place == r, arrow_end[pl.ds(at[0] * share + r, 1), :], pair)
     end[rows:, :] = pair
     turned = jnp.concatenate([mine[:depth, :].T, other[:depth, :].T], axis=0)
+    top = jnp.concatenate([mine_top[...].T, other_top[...].T], axis=0)
     both_t[...] = turned
-    got = dot(turned, mine[:depth, :])
-    border = jnp.concatenate([mine[depth:, :], other[depth:, :]], axis=1)
+    got = dot(turned, mine[:depth, :]) + dot(top, mine_top[...])
+    border = jnp.concatenate([mine[depth:tall, :], other[depth:tall, :]], axis=1)
     tile[: CORES * width, :] = got
     tile[CORES * width :, :] = border_times(border, got)
     token[...] = jnp.zeros_like(token)
@@ -96,6 +98,17 @@
 def far_kernel(first, second, both_t, passed, keep, give, token):
     far_tiles((first, second), both_t, keep, give)
     token[...] = passed[...]
+
+
+def half_kernel(low, first, second, both_t, passed, out):
+    tall, width = first.shape
+    count = CORES * width
+    depth = tall - (out.shape[0] - count)
+    joined = jnp.concatenate([first[:depth, :], second[:depth, :]], axis=1)
+    border = jnp.concatenate([first[depth:tall, :], second[depth:tall, :]], axis=1)
+    tile = dot(both_t[low : low + width, both_t.shape[1] - depth :], joined).T
+    out[:count, :] = tile
+    out[count:, :] = border_times(border, tile)
 
 
 def three_kernel(first, second, straight, both_t, passed, keep, give, token, pair, single):
@@ -225,22 +238,24 @@
     piece_at = lax.axis_index("tm").reshape(1)
     hbm = pl.BlockSpec(memory_space=pltpu.HBM)
 
-    def pack_kernel(cols, border, out, done):
+    def pack_kernel(cols, border, out, top, done):
+        depth = order - cut
         copies = [
-            pltpu.make_async_copy(cols, out.at[pl.ds(0, order)], done.at[0]),
-            pltpu.make_async_copy(border, out.at[pl.ds(order, arrow)], done.at[1]),
+            pltpu.make_async_copy(cols.at[pl.ds(cut, depth)], out.at[pl.ds(0, depth)], done.at[0]),
+            pltpu.make_async_copy(border, out.at[pl.ds(depth, arrow)], done.at[1]),
+            pltpu.make_async_copy(cols.at[pl.ds(0, cut)], top, done.at[2]),
         ]
         for copy in copies:
             copy.start()
         for copy in copies:
             copy.wait()
 
-    mine = pl.pallas_call(
+    mine, top = pl.pallas_call(
         pack_kernel,
-        out_shape=pltpu.VMEM((order + arrow, width), bf16),
+        out_shape=(pltpu.VMEM((order - cut + arrow, width), bf16), pltpu.VMEM((cut, width), bf16)),
         in_specs=[hbm, hbm],
-        out_specs=VMEM,
-        scratch_shapes=[pltpu.SemaphoreType.DMA((2,))],
+        out_specs=(VMEM, VMEM),
+        scratch_shapes=[pltpu.SemaphoreType.DMA((3,))],
         compiler_params=SMALL,
         name="pack",
     )(far_off(factor_cols), far_off(arrow_factor[0]))
@@ -270,24 +285,24 @@
             name=name,
         )(*map(near, panels), near(both_t), token)
 
-    first = hop(shared(mine, 1))
-    other = swap(mine)
-    second = hop(shared(other, 1))
+    first = hop(mine)
+    other, other_top = swap(mine), swap(top)
+    second = hop(other)
     mark = jax.ShapeDtypeStruct((8, width), f32)
     own, both_t, end, token = pl.pallas_call(
         own_kernel,
         out_shape=(
             pltpu.VMEM((both + arrow, width), f32),
-            pltpu.VMEM((both, order), bf16),
+            pltpu.VMEM((both, order - cut), bf16),
             pltpu.VMEM((rows + PAD, width), f32),
             mark,
         ),
-        in_specs=[SMEM, VMEM, VMEM, hbm, VMEM],
+        in_specs=[SMEM, VMEM, VMEM, VMEM, VMEM, hbm, VMEM],
         out_specs=(VMEM,) * 4,
         scratch_shapes=[pltpu.SemaphoreType.DMA],
         compiler_params=SMALL,
         name="own",
-    )(piece_at, near(mine), near(other), far_off(sigma_end), near(arrow_end.T))
+    )(piece_at, *map(near, (mine, other, top, other_top)), far_off(sigma_end), near(arrow_end.T))
 
     first_2 = hop(shared(first, 2))
     second, token = lax.optimization_barrier((second, token))
@@ -308,7 +323,17 @@
         [pltpu.VMEM((2, both + arrow, width), f32), pltpu.VMEM((2, width + arrow, width), f32)],
     )
     given_2 = swap(give_2)
-    keep_3, give_3, token = product(far_kernel, "far", 2, (first_3, second_3), token)
+    give_3, keep_3 = [
+        pl.pallas_call(
+            lambda *refs, low=low: half_kernel(low, *refs),
+            out_shape=jax.ShapeDtypeStruct((both + arrow, width), f32),
+            in_specs=[VMEM] * 4,
+            out_specs=VMEM,
+            compiler_params=SMALL,
+            name=name,
+        )(near(first_3), near(second_3), near(both_t), token)
+        for name, low in (("give", width), ("keep", 0))
+    ]
     kept, given = (keep_1, keep_2, keep_3), (given_1, given_2, swap(give_3))
 
     message = (pieces, rows + PAD, width)

time: 110 us -> 109 us (level)
  waiting for transfers between devices: 12.8 us -> 8.76 us
  starting transfers between devices: 31.4 us -> 34.9 us
    ppermute x4 -> x5, starting transfers between devices: 7.95 us -> 11.5 us  [swap(): return lax.ppermute(tile, 'space', [(p, p ^ 1) for p in range(devices)])]
    ppermute x7, waiting for transfers between devices: 10.2 us -> 6.73 us  [hop(): return lax.ppermute(panel, 'space', pairs)]
    pallas_call x3 -> x2, Pallas kernels: 3.33 us -> 2.16 us  [product(): pl.pallas_call(kernel, out_shape=(*[jax.ShapeDtypeStruct((tall, width), f...]
    ppermute x4 -> x5, waiting for transfers between devices: 2.56 us -> 2.03 us  [swap(): return lax.ppermute(tile, 'space', [(p, p ^ 1) for p in range(devices)])]
  transfers between devices with their start and end apart: 11 -> 12, of which waited for: 6 -> 6; matrix products, arithmetic and copies ran while one was open for 0% -> 0% of each run, Pallas kernels for 4% -> 4%
where the time goes in v13:
time: 109 us
  blocking collectives  55.1 us (51%)
  starting transfers between devices  34.9 us (32%)
  waiting for transfers between devices  8.76 us (8%)
  Pallas kernels  8.39 us (8%)
    all_to_all x2, blocking collectives, exchange(): moved = lax.all_to_all(values.astype(jnp.float16), 'tm', 0, 0, tiled=True)  55.1 us
    ppermute x7, starting transfers between devices, hop(): return lax.ppermute(panel, 'space', pairs)  23.5 us
    ppermute x5, starting transfers between devices, swap(): return lax.ppermute(tile, 'space', [(p, p ^ 1) for p in range(devices)])  11.5 us
    ppermute x7, waiting for transfers between devices, hop(): return lax.ppermute(panel, 'space', pairs)  6.73 us
  transfers between devices with their start and end apart: 12, of which 6 were waited for; matrix products, arithmetic and copies ran while one was open for 0% of the time, Pallas kernels for 4%

profile of v13, /device:TPU:64, one launch (start us, length us, event | category | flops | bytes accessed | tf_op | source)
XLA Modules:
  0.0 108.5 jit_solution(8067737839146646912)
XLA Ops:
  0.6 1.1 pack.1
  1.7 1.9 %collective-permute-start = (bf16[1856,128]{1,0:T(8,128)(2,1)S(1)}, bf16[1856,128]{1,0:T(8,128)(2,1)S(1)}, u32[]{:S(2)}, u32[]{:S(2)}) collective-permute-start(bf16[1856,128]{1,0:T(8,128)(2,1)S(1)} %get-tuple-element.25.mine), channel_id=1, source_target_pairs={{0,1},{1,0},{2,3},{3,2},{4,5},{5,4},{6,7},{7,6},{8,9},{9,8},{10,11... | collective-permute-start | bytes 1425416 | tf_op jit(solution)/shard_map/ppermute | solution.py:271
  3.6 3.5 %collective-permute-start.2 = (bf16[1856,128]{1,0:T(8,128)(2,1)S(1)}, bf16[1856,128]{1,0:T(8,128)(2,1)S(1)}, u32[]{:S(2)}, u32[]{:S(2)}) collective-permute-start(bf16[1856,128]{1,0:T(8,128)(2,1)S(1)} %get-tuple-element.25.mine), channel_id=1, source_target_pairs={{0,2},{1,15},{2,4},{3,1},{4,6},{5,3},{6,8},{7,5},{8,10},{9,7},{10,... | collective-permute-start | bytes 1425416 | tf_op jit(solution)/shard_map/ppermute | solution.py:268
  7.1 3.5 %collective-permute-start.3 = (bf16[1856,128]{1,0:T(8,128)(2,1)S(1)}, bf16[1856,128]{1,0:T(8,128)(2,1)S(1)}, u32[]{:S(2)}, u32[]{:S(2)}) collective-permute-start(bf16[1856,128]{1,0:T(8,128)(2,1)S(1)} %collective-permute-done.other), channel_id=1, source_target_pairs={{0,2},{1,15},{2,4},{3,1},{4,6},{5,3},{6,8},{7,5},{8,10},{9,7},{10,... | collective-permute-start | bytes 1425416 | tf_op jit(solution)/shard_map/ppermute | solution.py:268
  10.6 3.5 %collective-permute-start.1 = (bf16[256,128]{1,0:T(8,128)(2,1)S(1)}, bf16[256,128]{1,0:T(8,128)(2,1)S(1)}, u32[]{:S(2)}, u32[]{:S(2)}) collective-permute-start(bf16[256,128]{1,0:T(8,128)(2,1)S(1)} %get-tuple-element.26.mine_top), channel_id=1, source_target_pairs={{0,1},{1,0},{2,3},{3,2},{4,5},{5,4},{6,7},{7,6},{8,9},{9,8},{10,11... | collective-permute-start | bytes 196616 | tf_op jit(solution)/shard_map/ppermute | solution.py:271
  14.2 1.5 %collective-permute-done.2.first = bf16[1856,128]{1,0:T(8,128)(2,1)S(1)} collective-permute-done((bf16[1856,128]{1,0:T(8,128)(2,1)S(1)}, bf16[1856,128]{1,0:T(8,128)(2,1)S(1)}, u32[]{:S(2)}, u32[]{:S(2)}) %collective-permute-start.2) | collective-permute-done | bytes 475168 | tf_op jit(solution)/shard_map/ppermute | solution.py:268
  15.7 2.0 %collective-permute-start.4 = (bf16[1600,128]{1,0:T(8,128)(2,1)S(1)}, bf16[1600,128]{1,0:T(8,128)(2,1)S(1)}, u32[]{:S(2)}, u32[]{:S(2)}) collective-permute-start(bf16[1600,128]{1,0:T(8,128)(2,1)S(1)} %slice.20), channel_id=1, source_target_pairs={{0,2},{1,15},{2,4},{3,1},{4,6},{5,3},{6,8},{7,5},{8,10},{9,7},{10,... | collective-permute-start | bytes 1228808 | tf_op jit(solution)/shard_map/ppermute | solution.py:268
  17.7 1.1 %own.1 = (f32[320,128]{1,0:T(8,128)S(1)}, bf16[256,1792]{1,0:T(8,128)(2,1)S(1)}, f32[72,128]{1,0:T(8,128)S(1)}, f32[8,128]{1,0:T(8,128)S(1)}) custom-call(s32[1]{0:T(128)} %bitcast.1.at, bf16[1856,128]{1,0:T(8,128)(2,1)S(1)} %get-tuple-element.25.mine, bf16[1856,128]{1,0:T(8,128)(2,1)S(1)} %collective-permute-done.other, ...), custom_call_target="tpu_custom_call" | custom-call | tf_op jit(solution)/shard_map/own/pallas_call | solution.py:292
  18.9 1.9 %collective-permute-done.3.second = bf16[1856,128]{1,0:T(8,128)(2,1)S(1)} collective-permute-done((bf16[1856,128]{1,0:T(8,128)(2,1)S(1)}, bf16[1856,128]{1,0:T(8,128)(2,1)S(1)}, u32[]{:S(2)}, u32[]{:S(2)}) %collective-permute-start.3) | collective-permute-done | bytes 475168 | tf_op jit(solution)/shard_map/ppermute | solution.py:268
  20.8 2.0 %collective-permute-start.5 = (bf16[1600,128]{1,0:T(8,128)(2,1)S(1)}, bf16[1600,128]{1,0:T(8,128)(2,1)S(1)}, u32[]{:S(2)}, u32[]{:S(2)}) collective-permute-start(bf16[1600,128]{1,0:T(8,128)(2,1)S(1)} %slice.16), channel_id=1, source_target_pairs={{0,2},{1,15},{2,4},{3,1},{4,6},{5,3},{6,8},{7,5},{8,10},{9,7},{10,... | collective-permute-start | bytes 1228808 | tf_op jit(solution)/shard_map/ppermute | solution.py:268
  22.8 0.8 far.1
  23.6 3.1 %collective-permute-done.4.first = bf16[1600,128]{1,0:T(8,128)(2,1)S(1)} collective-permute-done((bf16[1600,128]{1,0:T(8,128)(2,1)S(1)}, bf16[1600,128]{1,0:T(8,128)(2,1)S(1)}, u32[]{:S(2)}, u32[]{:S(2)}) %collective-permute-start.4) | collective-permute-done | bytes 409632 | tf_op jit(solution)/shard_map/ppermute | solution.py:268
  26.8 3.4 %collective-permute-start.6 = (bf16[1088,128]{1,0:T(8,128)(2,1)S(1)}, bf16[1088,128]{1,0:T(8,128)(2,1)S(1)}, u32[]{:S(2)}, u32[]{:S(2)}) collective-permute-start(bf16[1088,128]{1,0:T(8,128)(2,1)S(1)} %slice.17), channel_id=1, source_target_pairs={{0,4},{1,13},{2,6},{3,15},{4,8},{5,1},{6,10},{7,3},{8,12},{9,5},{1... | collective-permute-start | bytes 835592 | tf_op jit(solution)/shard_map/ppermute | solution.py:268
  30.2 3.9 %collective-permute-start.8 = (bf16[1344,128]{1,0:T(8,128)(2,1)S(1)}, bf16[1344,128]{1,0:T(8,128)(2,1)S(1)}, u32[]{:S(2)}, u32[]{:S(2)}) collective-permute-start(bf16[1344,128]{1,0:T(8,128)(2,1)S(1)} %slice.18), channel_id=1, source_target_pairs={{0,2},{1,15},{2,4},{3,1},{4,6},{5,3},{6,8},{7,5},{8,10},{9,7},{10,... | collective-permute-start | bytes 1032200 | tf_op jit(solution)/shard_map/ppermute | solution.py:268
  34.1 5.2 %collective-permute-start.9 = (bf16[1344,128]{1,0:T(8,128)(2,1)S(1)}, bf16[1344,128]{1,0:T(8,128)(2,1)S(1)}, u32[]{:S(2)}, u32[]{:S(2)}) collective-permute-start(bf16[1344,128]{1,0:T(8,128)(2,1)S(1)} %slice.21), channel_id=1, source_target_pairs={{0,2},{1,15},{2,4},{3,1},{4,6},{5,3},{6,8},{7,5},{8,10},{9,7},{10,... | collective-permute-start | bytes 1032200 | tf_op jit(solution)/shard_map/ppermute | solution.py:268
  39.3 1.9 %collective-permute-start.7 = (f32[320,128]{1,0:T(8,128)S(1)}, f32[320,128]{1,0:T(8,128)S(1)}, u32[]{:S(2)}, u32[]{:S(2)}) collective-permute-start(f32[320,128]{1,0:T(8,128)S(1)} %get-tuple-element.36), channel_id=1, source_target_pairs={{0,1},{1,0},{2,3},{3,2},{4,5},{5,4},{6,7},{7,6},{8,9},{9,8},{10,11... | collective-permute-start | bytes 491528 | tf_op jit(solution)/shard_map/ppermute | solution.py:271
  41.2 1.4 %collective-permute-done.7.refs_5_ = f32[320,128]{1,0:T(8,128)S(1)} collective-permute-done((f32[320,128]{1,0:T(8,128)S(1)}, f32[320,128]{1,0:T(8,128)S(1)}, u32[]{:S(2)}, u32[]{:S(2)}) %collective-permute-start.7) | collective-permute-done | bytes 163872 | tf_op jit(solution)/shard_map/ppermute | solution.py:271
  42.6 1.4 %three.1 = (f32[448,128]{1,0:T(8,128)S(1)}, f32[448,128]{1,0:T(8,128)S(1)}, f32[8,128]{1,0:T(8,128)S(1)}) custom-call(bf16[1600,128]{1,0:T(8,128)(2,1)S(1)} %collective-permute-done.4.first, bf16[1600,128]{1,0:T(8,128)(2,1)S(1)} %collective-permute-done.5.second, bf16[1088,128]{1,0:T(8,128)(2,1)S(1)} %collective-permute-done.6.straight, ...), custom_call_target="tpu_custom_call" | custom-call | tf_op jit(solution)/shard_map/three/pallas_call | solution.py:278
  44.0 2.1 %collective-permute-start.10 = (f32[448,128]{1,0:T(8,128)S(1)}, f32[448,128]{1,0:T(8,128)S(1)}, u32[]{:S(2)}, u32[]{:S(2)}) collective-permute-start(f32[448,128]{1,0:T(8,128)S(1)} %get-tuple-element.41), channel_id=1, source_target_pairs={{0,1},{1,0},{2,3},{3,2},{4,5},{5,4},{6,7},{7,6},{8,9},{9,8},{10,11... | collective-permute-start | bytes 688136 | tf_op jit(solution)/shard_map/ppermute | solution.py:271
  46.8 2.1 %collective-permute-start.11 = (f32[320,128]{1,0:T(8,128)S(1)}, f32[320,128]{1,0:T(8,128)S(1)}, u32[]{:S(2)}, u32[]{:S(2)}) collective-permute-start(f32[320,128]{1,0:T(8,128)S(1)} %give.1), channel_id=1, source_target_pairs={{0,1},{1,0},{2,3},{3,2},{4,5},{5,4},{6,7},{7,6},{8,9},{9,8},{10,11... | collective-permute-start | bytes 491528 | tf_op jit(solution)/shard_map/ppermute | solution.py:271
  50.8 31.7 %all_to_all.10 = f16[32,72,128]{2,1,0:T(8,128)(2,1)S(1)} all-to-all(f16[32,72,128]{2,1,0:T(8,128)(2,1)S(1)} %convert_element_type.12), channel_id=1, replica_groups=mesh['tm'=32,'space'=16] {'tm'}, dimensions={0} | all-to-all | bytes 1179648 | tf_op jit(solution)/shard_map/all_to_all | solution.py:355
  82.5 0.8 suffix.1
  83.4 23.4 %all_to_all.11 = f16[32,72,128]{2,1,0:T(8,128)(2,1)S(1)} all-to-all(f16[32,72,128]{2,1,0:T(8,128)(2,1)S(1)} %convert_element_type.14), channel_id=1, replica_groups=mesh['tm'=32,'space'=16] {'tm'}, dimensions={0} | all-to-all | bytes 1179648 | tf_op jit(solution)/shard_map/all_to_all | solution.py:355
  106.9 1.6 %last.1 = (f32[2048,128]{1,0:T(8,128)}, f32[64,128]{1,0:T(8,128)}) custom-call(s32[1]{0:T(128)} %bitcast.refs_0_, f32[32,64,128]{2,1,0:T(8,128)S(1)} %get-tuple-element.42.refs_1_, f32[64,128]{1,0:T(8,128)S(1)} %get-tuple-element.43.refs_2_, f32[32,72,128]{2,1,0:T(8,128)S(1)} %convert_element_type.15.refs_3_, f32[1,2048]{1,0:T(1,128)S(1)} %copy-done.1), custom_call_target="tpu_custom_call" | custom-call | tf_op jit(solution)/shard_map/last/pallas_call | solution.py:367
  (26 shorter events, 3.0 us)
Async XLA Ops:
  0.6 17.1 %copy-start = (f32[128,64]{0,1:T(8,128)S(1)}, f32[128,64]{0,1:T(8,128)}, u32[]{:S(2)}) copy-start(f32[128,64]{0,1:T(8,128)} %param.11) | copy-start | bytes 98308
  1.7 5.4 %collective-permute-start = (bf16[1856,128]{1,0:T(8,128)(2,1)S(1)}, bf16[1856,128]{1,0:T(8,128)(2,1)S(1)}, u32[]{:S(2)}, u32[]{:S(2)}) collective-permute-start(bf16[1856,128]{1,0:T(8,128)(2,1)S(1)} %get-tuple-element.25.mine), channel_id=1, source_target_pairs={{0,1},{1,0},{2,3},{3,2},{4,5},{5,4},{6,7},{7,6},{8,9},{9,8},{10,11... | collective-permute-start | bytes 1425416 | tf_op jit(solution)/shard_map/ppermute | solution.py:271
  3.6 12.0 %collective-permute-start.2 = (bf16[1856,128]{1,0:T(8,128)(2,1)S(1)}, bf16[1856,128]{1,0:T(8,128)(2,1)S(1)}, u32[]{:S(2)}, u32[]{:S(2)}) collective-permute-start(bf16[1856,128]{1,0:T(8,128)(2,1)S(1)} %get-tuple-element.25.mine), channel_id=1, source_target_pairs={{0,2},{1,15},{2,4},{3,1},{4,6},{5,3},{6,8},{7,5},{8,10},{9,7},{10,... | collective-permute-start | bytes 1425416 | tf_op jit(solution)/shard_map/ppermute | solution.py:268
  7.1 13.6 %collective-permute-start.3 = (bf16[1856,128]{1,0:T(8,128)(2,1)S(1)}, bf16[1856,128]{1,0:T(8,128)(2,1)S(1)}, u32[]{:S(2)}, u32[]{:S(2)}) collective-permute-start(bf16[1856,128]{1,0:T(8,128)(2,1)S(1)} %collective-permute-done.other), channel_id=1, source_target_pairs={{0,2},{1,15},{2,4},{3,1},{4,6},{5,3},{6,8},{7,5},{8,10},{9,7},{10,... | collective-permute-start | bytes 1425416 | tf_op jit(solution)/shard_map/ppermute | solution.py:268
  10.6 7.1 %collective-permute-start.1 = (bf16[256,128]{1,0:T(8,128)(2,1)S(1)}, bf16[256,128]{1,0:T(8,128)(2,1)S(1)}, u32[]{:S(2)}, u32[]{:S(2)}) collective-permute-start(bf16[256,128]{1,0:T(8,128)(2,1)S(1)} %get-tuple-element.26.mine_top), channel_id=1, source_target_pairs={{0,1},{1,0},{2,3},{3,2},{4,5},{5,4},{6,7},{7,6},{8,9},{9,8},{10,11... | collective-permute-start | bytes 196616 | tf_op jit(solution)/shard_map/ppermute | solution.py:271
  15.7 11.1 %collective-permute-start.4 = (bf16[1600,128]{1,0:T(8,128)(2,1)S(1)}, bf16[1600,128]{1,0:T(8,128)(2,1)S(1)}, u32[]{:S(2)}, u32[]{:S(2)}) collective-permute-start(bf16[1600,128]{1,0:T(8,128)(2,1)S(1)} %slice.20), channel_id=1, source_target_pairs={{0,2},{1,15},{2,4},{3,1},{4,6},{5,3},{6,8},{7,5},{8,10},{9,7},{10,... | collective-permute-start | bytes 1228808 | tf_op jit(solution)/shard_map/ppermute | solution.py:268
  20.8 13.3 %collective-permute-start.5 = (bf16[1600,128]{1,0:T(8,128)(2,1)S(1)}, bf16[1600,128]{1,0:T(8,128)(2,1)S(1)}, u32[]{:S(2)}, u32[]{:S(2)}) collective-permute-start(bf16[1600,128]{1,0:T(8,128)(2,1)S(1)} %slice.16), channel_id=1, source_target_pairs={{0,2},{1,15},{2,4},{3,1},{4,6},{5,3},{6,8},{7,5},{8,10},{9,7},{10,... | collective-permute-start | bytes 1228808 | tf_op jit(solution)/shard_map/ppermute | solution.py:268
  26.8 15.8 %collective-permute-start.6 = (bf16[1088,128]{1,0:T(8,128)(2,1)S(1)}, bf16[1088,128]{1,0:T(8,128)(2,1)S(1)}, u32[]{:S(2)}, u32[]{:S(2)}) collective-permute-start(bf16[1088,128]{1,0:T(8,128)(2,1)S(1)} %slice.17), channel_id=1, source_target_pairs={{0,4},{1,13},{2,6},{3,15},{4,8},{5,1},{6,10},{7,3},{8,12},{9,5},{1... | collective-permute-start | bytes 835592 | tf_op jit(solution)/shard_map/ppermute | solution.py:268
  30.2 15.9 %collective-permute-start.8 = (bf16[1344,128]{1,0:T(8,128)(2,1)S(1)}, bf16[1344,128]{1,0:T(8,128)(2,1)S(1)}, u32[]{:S(2)}, u32[]{:S(2)}) collective-permute-start(bf16[1344,128]{1,0:T(8,128)(2,1)S(1)} %slice.18), channel_id=1, source_target_pairs={{0,2},{1,15},{2,4},{3,1},{4,6},{5,3},{6,8},{7,5},{8,10},{9,7},{10,... | collective-permute-start | bytes 1032200 | tf_op jit(solution)/shard_map/ppermute | solution.py:268
  34.1 12.2 %collective-permute-start.9 = (bf16[1344,128]{1,0:T(8,128)(2,1)S(1)}, bf16[1344,128]{1,0:T(8,128)(2,1)S(1)}, u32[]{:S(2)}, u32[]{:S(2)}) collective-permute-start(bf16[1344,128]{1,0:T(8,128)(2,1)S(1)} %slice.21), channel_id=1, source_target_pairs={{0,2},{1,15},{2,4},{3,1},{4,6},{5,3},{6,8},{7,5},{8,10},{9,7},{10,... | collective-permute-start | bytes 1032200 | tf_op jit(solution)/shard_map/ppermute | solution.py:268
  39.3 3.3 %collective-permute-start.7 = (f32[320,128]{1,0:T(8,128)S(1)}, f32[320,128]{1,0:T(8,128)S(1)}, u32[]{:S(2)}, u32[]{:S(2)}) collective-permute-start(f32[320,128]{1,0:T(8,128)S(1)} %get-tuple-element.36), channel_id=1, source_target_pairs={{0,1},{1,0},{2,3},{3,2},{4,5},{5,4},{6,7},{7,6},{8,9},{9,8},{10,11... | collective-permute-start | bytes 491528 | tf_op jit(solution)/shard_map/ppermute | solution.py:271
  44.0 5.5 %collective-permute-start.10 = (f32[448,128]{1,0:T(8,128)S(1)}, f32[448,128]{1,0:T(8,128)S(1)}, u32[]{:S(2)}, u32[]{:S(2)}) collective-permute-start(f32[448,128]{1,0:T(8,128)S(1)} %get-tuple-element.41), channel_id=1, source_target_pairs={{0,1},{1,0},{2,3},{3,2},{4,5},{5,4},{6,7},{7,6},{8,9},{9,8},{10,11... | collective-permute-start | bytes 688136 | tf_op jit(solution)/shard_map/ppermute | solution.py:271
  46.8 3.3 %copy-start.1 = (f32[1,2048]{1,0:T(1,128)S(1)}, f32[1,2048]{1,0:T(1,128)}, u32[]{:S(2)}) copy-start(f32[1,2048]{1,0:T(1,128)} %refs_4_.1) | copy-start | bytes 24580
  46.8 3.3 %copy-start.2 = (f32[64,64]{1,0:T(8,128)S(1)}, f32[64,64]{1,0:T(8,128)}, u32[]{:S(2)}) copy-start(f32[64,64]{1,0:T(8,128)} %refs_8_.1) | copy-start | bytes 49156
  46.8 3.3 %collective-permute-start.11 = (f32[320,128]{1,0:T(8,128)S(1)}, f32[320,128]{1,0:T(8,128)S(1)}, u32[]{:S(2)}, u32[]{:S(2)}) collective-permute-start(f32[320,128]{1,0:T(8,128)S(1)} %give.1), channel_id=1, source_target_pairs={{0,1},{1,0},{2,3},{3,2},{4,5},{5,4},{6,7},{7,6},{8,9},{9,8},{10,11... | collective-permute-start | bytes 491528 | tf_op jit(solution)/shard_map/ppermute | solution.py:271

commit v14 on v13

--- a/solution.py
+++ b/solution.py
@@ -130,7 +130,7 @@
 
 def message_kernel(rows, chips, hops, at, own, *refs):
     kept, given = refs[: hops - 1], refs[hops - 1 : 2 * hops - 2]
-    tip, decay, out, copied, own_arrow, plain, done = refs[2 * hops - 2 :]
+    tip, decay, out, plain, own_arrow = refs[2 * hops - 2 :]
     width = own.shape[1]
     per = width // rows
     chip, core = at[0] // CORES, at[0] % CORES
@@ -151,8 +151,6 @@
         if kept[s].shape[0] > 3 * width:
             put(kept[s][2 * width : 3 * width, :], hops, core)
             put(given[s][2 * width : 3 * width, :], hops, 1 - core)
-    copy = pltpu.make_async_copy(plain, copied, done)
-    copy.start()
     border = own_arrow.shape[0]
     total = own[CORES * width :, :]
     for part in (*kept, *given):
@@ -175,7 +173,6 @@
         extra = jnp.where(place == 4, by_row, cols)
         pair = jnp.concatenate([arrow[2 * r : 2 * r + 2, :], fill], axis=0)
         out[r, :rows, :], out[r, rows:, :] = encode(plain[r], pair, extra)
-    copy.wait()
 
 
 def scan_kernel(rows, got, end, out, turned):
@@ -341,12 +338,11 @@
         lambda *refs: message_kernel(rows, chips, hops, *refs),
         out_shape=(
             pltpu.VMEM(message, f32),
-            jax.ShapeDtypeStruct((pieces, rows, width), f32),
-            jax.ShapeDtypeStruct((arrow, width), f32),
+            pltpu.VMEM((pieces, rows, width), f32),
+            pltpu.VMEM((arrow, width), f32),
         ),
         in_specs=[SMEM] + [VMEM] * (2 * hops + 1),
-        out_specs=(VMEM, pl.BlockSpec(memory_space=pl.ANY), VMEM),
-        scratch_shapes=[pltpu.VMEM((pieces, rows, width), f32), pltpu.SemaphoreType.DMA],
+        out_specs=(VMEM,) * 3,
         compiler_params=SMALL,
         name="message",
     )(column_at, *map(near, (own, *kept, *given, tip_inverse, decay)))

time: 109 us -> 109 us (level)
  no operation moved by 1% of the time
where the time goes in v14:
time: 109 us; the launch traced here: 108 us
  blocking collectives  55.1 us (51%)
  starting transfers between devices  34.9 us (32%)
  waiting for transfers between devices  8.76 us (8%)
  Pallas kernels  8.23 us (8%)
    all_to_all x2, blocking collectives, exchange(): moved = lax.all_to_all(values.astype(jnp.float16), 'tm', 0, 0, tiled=True)  55.1 us
    ppermute x7, starting transfers between devices, hop(): return lax.ppermute(panel, 'space', pairs)  23.5 us
    ppermute x5, starting transfers between devices, swap(): return lax.ppermute(tile, 'space', [(p, p ^ 1) for p in range(devices)])  11.5 us
    ppermute x7, waiting for transfers between devices, hop(): return lax.ppermute(panel, 'space', pairs)  6.73 us
  transfers between devices with their start and end apart: 12, of which 6 were waited for; matrix products, arithmetic and copies ran while one was open for 0% of the time, Pallas kernels for 4%

profile of v14, /device:TPU:64, one launch (start us, length us, event | category | flops | bytes accessed | tf_op | source)
XLA Modules:
  0.0 108.4 jit_solution(11176079936700729038)
XLA Ops:
  0.6 1.1 pack.1
  1.7 1.9 %collective-permute-start = (bf16[1856,128]{1,0:T(8,128)(2,1)S(1)}, bf16[1856,128]{1,0:T(8,128)(2,1)S(1)}, u32[]{:S(2)}, u32[]{:S(2)}) collective-permute-start(bf16[1856,128]{1,0:T(8,128)(2,1)S(1)} %get-tuple-element.25.mine), channel_id=1, source_target_pairs={{0,1},{1,0},{2,3},{3,2},{4,5},{5,4},{6,7},{7,6},{8,9},{9,8},{10,11... | collective-permute-start | bytes 1425416 | tf_op jit(solution)/shard_map/ppermute | solution.py:268
  3.6 3.5 %collective-permute-start.2 = (bf16[1856,128]{1,0:T(8,128)(2,1)S(1)}, bf16[1856,128]{1,0:T(8,128)(2,1)S(1)}, u32[]{:S(2)}, u32[]{:S(2)}) collective-permute-start(bf16[1856,128]{1,0:T(8,128)(2,1)S(1)} %get-tuple-element.25.mine), channel_id=1, source_target_pairs={{0,2},{1,15},{2,4},{3,1},{4,6},{5,3},{6,8},{7,5},{8,10},{9,7},{10,... | collective-permute-start | bytes 1425416 | tf_op jit(solution)/shard_map/ppermute | solution.py:265
  7.1 3.5 %collective-permute-start.3 = (bf16[1856,128]{1,0:T(8,128)(2,1)S(1)}, bf16[1856,128]{1,0:T(8,128)(2,1)S(1)}, u32[]{:S(2)}, u32[]{:S(2)}) collective-permute-start(bf16[1856,128]{1,0:T(8,128)(2,1)S(1)} %collective-permute-done.other), channel_id=1, source_target_pairs={{0,2},{1,15},{2,4},{3,1},{4,6},{5,3},{6,8},{7,5},{8,10},{9,7},{10,... | collective-permute-start | bytes 1425416 | tf_op jit(solution)/shard_map/ppermute | solution.py:265
  10.6 3.5 %collective-permute-start.1 = (bf16[256,128]{1,0:T(8,128)(2,1)S(1)}, bf16[256,128]{1,0:T(8,128)(2,1)S(1)}, u32[]{:S(2)}, u32[]{:S(2)}) collective-permute-start(bf16[256,128]{1,0:T(8,128)(2,1)S(1)} %get-tuple-element.26.mine_top), channel_id=1, source_target_pairs={{0,1},{1,0},{2,3},{3,2},{4,5},{5,4},{6,7},{7,6},{8,9},{9,8},{10,11... | collective-permute-start | bytes 196616 | tf_op jit(solution)/shard_map/ppermute | solution.py:268
  14.2 1.5 %collective-permute-done.2.first = bf16[1856,128]{1,0:T(8,128)(2,1)S(1)} collective-permute-done((bf16[1856,128]{1,0:T(8,128)(2,1)S(1)}, bf16[1856,128]{1,0:T(8,128)(2,1)S(1)}, u32[]{:S(2)}, u32[]{:S(2)}) %collective-permute-start.2) | collective-permute-done | bytes 475168 | tf_op jit(solution)/shard_map/ppermute | solution.py:265
  15.7 2.0 %collective-permute-start.4 = (bf16[1600,128]{1,0:T(8,128)(2,1)S(1)}, bf16[1600,128]{1,0:T(8,128)(2,1)S(1)}, u32[]{:S(2)}, u32[]{:S(2)}) collective-permute-start(bf16[1600,128]{1,0:T(8,128)(2,1)S(1)} %slice.20), channel_id=1, source_target_pairs={{0,2},{1,15},{2,4},{3,1},{4,6},{5,3},{6,8},{7,5},{8,10},{9,7},{10,... | collective-permute-start | bytes 1228808 | tf_op jit(solution)/shard_map/ppermute | solution.py:265
  17.7 1.1 %own.1 = (f32[320,128]{1,0:T(8,128)S(1)}, bf16[256,1792]{1,0:T(8,128)(2,1)S(1)}, f32[72,128]{1,0:T(8,128)S(1)}, f32[8,128]{1,0:T(8,128)S(1)}) custom-call(s32[1]{0:T(128)} %bitcast.1.at, bf16[1856,128]{1,0:T(8,128)(2,1)S(1)} %get-tuple-element.25.mine, bf16[1856,128]{1,0:T(8,128)(2,1)S(1)} %collective-permute-done.other, ...), custom_call_target="tpu_custom_call" | custom-call | tf_op jit(solution)/shard_map/own/pallas_call | solution.py:289
  18.9 1.9 %collective-permute-done.3.second = bf16[1856,128]{1,0:T(8,128)(2,1)S(1)} collective-permute-done((bf16[1856,128]{1,0:T(8,128)(2,1)S(1)}, bf16[1856,128]{1,0:T(8,128)(2,1)S(1)}, u32[]{:S(2)}, u32[]{:S(2)}) %collective-permute-start.3) | collective-permute-done | bytes 475168 | tf_op jit(solution)/shard_map/ppermute | solution.py:265
  20.8 2.0 %collective-permute-start.5 = (bf16[1600,128]{1,0:T(8,128)(2,1)S(1)}, bf16[1600,128]{1,0:T(8,128)(2,1)S(1)}, u32[]{:S(2)}, u32[]{:S(2)}) collective-permute-start(bf16[1600,128]{1,0:T(8,128)(2,1)S(1)} %slice.16), channel_id=1, source_target_pairs={{0,2},{1,15},{2,4},{3,1},{4,6},{5,3},{6,8},{7,5},{8,10},{9,7},{10,... | collective-permute-start | bytes 1228808 | tf_op jit(solution)/shard_map/ppermute | solution.py:265
  22.8 0.8 far.1
  23.6 3.1 %collective-permute-done.4.first = bf16[1600,128]{1,0:T(8,128)(2,1)S(1)} collective-permute-done((bf16[1600,128]{1,0:T(8,128)(2,1)S(1)}, bf16[1600,128]{1,0:T(8,128)(2,1)S(1)}, u32[]{:S(2)}, u32[]{:S(2)}) %collective-permute-start.4) | collective-permute-done | bytes 409632 | tf_op jit(solution)/shard_map/ppermute | solution.py:265
  26.8 3.4 %collective-permute-start.6 = (bf16[1088,128]{1,0:T(8,128)(2,1)S(1)}, bf16[1088,128]{1,0:T(8,128)(2,1)S(1)}, u32[]{:S(2)}, u32[]{:S(2)}) collective-permute-start(bf16[1088,128]{1,0:T(8,128)(2,1)S(1)} %slice.17), channel_id=1, source_target_pairs={{0,4},{1,13},{2,6},{3,15},{4,8},{5,1},{6,10},{7,3},{8,12},{9,5},{1... | collective-permute-start | bytes 835592 | tf_op jit(solution)/shard_map/ppermute | solution.py:265
  30.2 3.9 %collective-permute-start.8 = (bf16[1344,128]{1,0:T(8,128)(2,1)S(1)}, bf16[1344,128]{1,0:T(8,128)(2,1)S(1)}, u32[]{:S(2)}, u32[]{:S(2)}) collective-permute-start(bf16[1344,128]{1,0:T(8,128)(2,1)S(1)} %slice.18), channel_id=1, source_target_pairs={{0,2},{1,15},{2,4},{3,1},{4,6},{5,3},{6,8},{7,5},{8,10},{9,7},{10,... | collective-permute-start | bytes 1032200 | tf_op jit(solution)/shard_map/ppermute | solution.py:265
  34.1 5.2 %collective-permute-start.9 = (bf16[1344,128]{1,0:T(8,128)(2,1)S(1)}, bf16[1344,128]{1,0:T(8,128)(2,1)S(1)}, u32[]{:S(2)}, u32[]{:S(2)}) collective-permute-start(bf16[1344,128]{1,0:T(8,128)(2,1)S(1)} %slice.21), channel_id=1, source_target_pairs={{0,2},{1,15},{2,4},{3,1},{4,6},{5,3},{6,8},{7,5},{8,10},{9,7},{10,... | collective-permute-start | bytes 1032200 | tf_op jit(solution)/shard_map/ppermute | solution.py:265
  39.3 1.9 %collective-permute-start.7 = (f32[320,128]{1,0:T(8,128)S(1)}, f32[320,128]{1,0:T(8,128)S(1)}, u32[]{:S(2)}, u32[]{:S(2)}) collective-permute-start(f32[320,128]{1,0:T(8,128)S(1)} %get-tuple-element.36), channel_id=1, source_target_pairs={{0,1},{1,0},{2,3},{3,2},{4,5},{5,4},{6,7},{7,6},{8,9},{9,8},{10,11... | collective-permute-start | bytes 491528 | tf_op jit(solution)/shard_map/ppermute | solution.py:268
  41.2 1.4 %collective-permute-done.7.refs_5_ = f32[320,128]{1,0:T(8,128)S(1)} collective-permute-done((f32[320,128]{1,0:T(8,128)S(1)}, f32[320,128]{1,0:T(8,128)S(1)}, u32[]{:S(2)}, u32[]{:S(2)}) %collective-permute-start.7) | collective-permute-done | bytes 163872 | tf_op jit(solution)/shard_map/ppermute | solution.py:268
  42.6 1.4 %three.1 = (f32[448,128]{1,0:T(8,128)S(1)}, f32[448,128]{1,0:T(8,128)S(1)}, f32[8,128]{1,0:T(8,128)S(1)}) custom-call(bf16[1600,128]{1,0:T(8,128)(2,1)S(1)} %collective-permute-done.4.first, bf16[1600,128]{1,0:T(8,128)(2,1)S(1)} %collective-permute-done.5.second, bf16[1088,128]{1,0:T(8,128)(2,1)S(1)} %collective-permute-done.6.straight, ...), custom_call_target="tpu_custom_call" | custom-call | tf_op jit(solution)/shard_map/three/pallas_call | solution.py:275
  44.0 2.1 %collective-permute-start.10 = (f32[448,128]{1,0:T(8,128)S(1)}, f32[448,128]{1,0:T(8,128)S(1)}, u32[]{:S(2)}, u32[]{:S(2)}) collective-permute-start(f32[448,128]{1,0:T(8,128)S(1)} %get-tuple-element.41), channel_id=1, source_target_pairs={{0,1},{1,0},{2,3},{3,2},{4,5},{5,4},{6,7},{7,6},{8,9},{9,8},{10,11... | collective-permute-start | bytes 688136 | tf_op jit(solution)/shard_map/ppermute | solution.py:268
  46.8 2.1 %collective-permute-start.11 = (f32[320,128]{1,0:T(8,128)S(1)}, f32[320,128]{1,0:T(8,128)S(1)}, u32[]{:S(2)}, u32[]{:S(2)}) collective-permute-start(f32[320,128]{1,0:T(8,128)S(1)} %give.1), channel_id=1, source_target_pairs={{0,1},{1,0},{2,3},{3,2},{4,5},{5,4},{6,7},{7,6},{8,9},{9,8},{10,11... | collective-permute-start | bytes 491528 | tf_op jit(solution)/shard_map/ppermute | solution.py:268
  50.6 31.7 %all_to_all.10 = f16[32,72,128]{2,1,0:T(8,128)(2,1)S(1)} all-to-all(f16[32,72,128]{2,1,0:T(8,128)(2,1)S(1)} %convert_element_type.12), channel_id=1, replica_groups=mesh['tm'=32,'space'=16] {'tm'}, dimensions={0} | all-to-all | bytes 1179648 | tf_op jit(solution)/shard_map/all_to_all | solution.py:351
  82.4 0.8 suffix.1
  83.3 23.4 %all_to_all.11 = f16[32,72,128]{2,1,0:T(8,128)(2,1)S(1)} all-to-all(f16[32,72,128]{2,1,0:T(8,128)(2,1)S(1)} %convert_element_type.14), channel_id=1, replica_groups=mesh['tm'=32,'space'=16] {'tm'}, dimensions={0} | all-to-all | bytes 1179648 | tf_op jit(solution)/shard_map/all_to_all | solution.py:351
  106.8 1.6 %last.1 = (f32[2048,128]{1,0:T(8,128)}, f32[64,128]{1,0:T(8,128)}) custom-call(s32[1]{0:T(128)} %bitcast.refs_0_, f32[32,64,128]{2,1,0:T(8,128)S(1)} %get-tuple-element.42.refs_1_, f32[64,128]{1,0:T(8,128)S(1)} %get-tuple-element.43.refs_2_, f32[32,72,128]{2,1,0:T(8,128)S(1)} %convert_element_type.15.refs_3_, f32[1,2048]{1,0:T(1,128)S(1)} %copy-done.1), custom_call_target="tpu_custom_call" | custom-call | tf_op jit(solution)/shard_map/last/pallas_call | solution.py:363
  (26 shorter events, 2.9 us)
Async XLA Ops:
  0.6 17.1 %copy-start = (f32[128,64]{0,1:T(8,128)S(1)}, f32[128,64]{0,1:T(8,128)}, u32[]{:S(2)}) copy-start(f32[128,64]{0,1:T(8,128)} %param.11) | copy-start | bytes 98308
  1.7 5.4 %collective-permute-start = (bf16[1856,128]{1,0:T(8,128)(2,1)S(1)}, bf16[1856,128]{1,0:T(8,128)(2,1)S(1)}, u32[]{:S(2)}, u32[]{:S(2)}) collective-permute-start(bf16[1856,128]{1,0:T(8,128)(2,1)S(1)} %get-tuple-element.25.mine), channel_id=1, source_target_pairs={{0,1},{1,0},{2,3},{3,2},{4,5},{5,4},{6,7},{7,6},{8,9},{9,8},{10,11... | collective-permute-start | bytes 1425416 | tf_op jit(solution)/shard_map/ppermute | solution.py:268
  3.6 12.0 %collective-permute-start.2 = (bf16[1856,128]{1,0:T(8,128)(2,1)S(1)}, bf16[1856,128]{1,0:T(8,128)(2,1)S(1)}, u32[]{:S(2)}, u32[]{:S(2)}) collective-permute-start(bf16[1856,128]{1,0:T(8,128)(2,1)S(1)} %get-tuple-element.25.mine), channel_id=1, source_target_pairs={{0,2},{1,15},{2,4},{3,1},{4,6},{5,3},{6,8},{7,5},{8,10},{9,7},{10,... | collective-permute-start | bytes 1425416 | tf_op jit(solution)/shard_map/ppermute | solution.py:265
  7.1 13.6 %collective-permute-start.3 = (bf16[1856,128]{1,0:T(8,128)(2,1)S(1)}, bf16[1856,128]{1,0:T(8,128)(2,1)S(1)}, u32[]{:S(2)}, u32[]{:S(2)}) collective-permute-start(bf16[1856,128]{1,0:T(8,128)(2,1)S(1)} %collective-permute-done.other), channel_id=1, source_target_pairs={{0,2},{1,15},{2,4},{3,1},{4,6},{5,3},{6,8},{7,5},{8,10},{9,7},{10,... | collective-permute-start | bytes 1425416 | tf_op jit(solution)/shard_map/ppermute | solution.py:265
  10.6 7.1 %collective-permute-start.1 = (bf16[256,128]{1,0:T(8,128)(2,1)S(1)}, bf16[256,128]{1,0:T(8,128)(2,1)S(1)}, u32[]{:S(2)}, u32[]{:S(2)}) collective-permute-start(bf16[256,128]{1,0:T(8,128)(2,1)S(1)} %get-tuple-element.26.mine_top), channel_id=1, source_target_pairs={{0,1},{1,0},{2,3},{3,2},{4,5},{5,4},{6,7},{7,6},{8,9},{9,8},{10,11... | collective-permute-start | bytes 196616 | tf_op jit(solution)/shard_map/ppermute | solution.py:268
  15.7 11.1 %collective-permute-start.4 = (bf16[1600,128]{1,0:T(8,128)(2,1)S(1)}, bf16[1600,128]{1,0:T(8,128)(2,1)S(1)}, u32[]{:S(2)}, u32[]{:S(2)}) collective-permute-start(bf16[1600,128]{1,0:T(8,128)(2,1)S(1)} %slice.20), channel_id=1, source_target_pairs={{0,2},{1,15},{2,4},{3,1},{4,6},{5,3},{6,8},{7,5},{8,10},{9,7},{10,... | collective-permute-start | bytes 1228808 | tf_op jit(solution)/shard_map/ppermute | solution.py:265
  20.8 13.3 %collective-permute-start.5 = (bf16[1600,128]{1,0:T(8,128)(2,1)S(1)}, bf16[1600,128]{1,0:T(8,128)(2,1)S(1)}, u32[]{:S(2)}, u32[]{:S(2)}) collective-permute-start(bf16[1600,128]{1,0:T(8,128)(2,1)S(1)} %slice.16), channel_id=1, source_target_pairs={{0,2},{1,15},{2,4},{3,1},{4,6},{5,3},{6,8},{7,5},{8,10},{9,7},{10,... | collective-permute-start | bytes 1228808 | tf_op jit(solution)/shard_map/ppermute | solution.py:265
  26.8 15.8 %collective-permute-start.6 = (bf16[1088,128]{1,0:T(8,128)(2,1)S(1)}, bf16[1088,128]{1,0:T(8,128)(2,1)S(1)}, u32[]{:S(2)}, u32[]{:S(2)}) collective-permute-start(bf16[1088,128]{1,0:T(8,128)(2,1)S(1)} %slice.17), channel_id=1, source_target_pairs={{0,4},{1,13},{2,6},{3,15},{4,8},{5,1},{6,10},{7,3},{8,12},{9,5},{1... | collective-permute-start | bytes 835592 | tf_op jit(solution)/shard_map/ppermute | solution.py:265
  30.2 15.9 %collective-permute-start.8 = (bf16[1344,128]{1,0:T(8,128)(2,1)S(1)}, bf16[1344,128]{1,0:T(8,128)(2,1)S(1)}, u32[]{:S(2)}, u32[]{:S(2)}) collective-permute-start(bf16[1344,128]{1,0:T(8,128)(2,1)S(1)} %slice.18), channel_id=1, source_target_pairs={{0,2},{1,15},{2,4},{3,1},{4,6},{5,3},{6,8},{7,5},{8,10},{9,7},{10,... | collective-permute-start | bytes 1032200 | tf_op jit(solution)/shard_map/ppermute | solution.py:265
  34.1 12.2 %collective-permute-start.9 = (bf16[1344,128]{1,0:T(8,128)(2,1)S(1)}, bf16[1344,128]{1,0:T(8,128)(2,1)S(1)}, u32[]{:S(2)}, u32[]{:S(2)}) collective-permute-start(bf16[1344,128]{1,0:T(8,128)(2,1)S(1)} %slice.21), channel_id=1, source_target_pairs={{0,2},{1,15},{2,4},{3,1},{4,6},{5,3},{6,8},{7,5},{8,10},{9,7},{10,... | collective-permute-start | bytes 1032200 | tf_op jit(solution)/shard_map/ppermute | solution.py:265
  39.3 3.3 %collective-permute-start.7 = (f32[320,128]{1,0:T(8,128)S(1)}, f32[320,128]{1,0:T(8,128)S(1)}, u32[]{:S(2)}, u32[]{:S(2)}) collective-permute-start(f32[320,128]{1,0:T(8,128)S(1)} %get-tuple-element.36), channel_id=1, source_target_pairs={{0,1},{1,0},{2,3},{3,2},{4,5},{5,4},{6,7},{7,6},{8,9},{9,8},{10,11... | collective-permute-start | bytes 491528 | tf_op jit(solution)/shard_map/ppermute | solution.py:268
  44.0 5.5 %collective-permute-start.10 = (f32[448,128]{1,0:T(8,128)S(1)}, f32[448,128]{1,0:T(8,128)S(1)}, u32[]{:S(2)}, u32[]{:S(2)}) collective-permute-start(f32[448,128]{1,0:T(8,128)S(1)} %get-tuple-element.41), channel_id=1, source_target_pairs={{0,1},{1,0},{2,3},{3,2},{4,5},{5,4},{6,7},{7,6},{8,9},{9,8},{10,11... | collective-permute-start | bytes 688136 | tf_op jit(solution)/shard_map/ppermute | solution.py:268
  46.8 3.3 %copy-start.1 = (f32[1,2048]{1,0:T(1,128)S(1)}, f32[1,2048]{1,0:T(1,128)}, u32[]{:S(2)}) copy-start(f32[1,2048]{1,0:T(1,128)} %refs_4_.1) | copy-start | bytes 24580
  46.8 3.3 %copy-start.2 = (f32[64,64]{1,0:T(8,128)S(1)}, f32[64,64]{1,0:T(8,128)}, u32[]{:S(2)}) copy-start(f32[64,64]{1,0:T(8,128)} %refs_8_.1) | copy-start | bytes 49156
  46.8 3.3 %collective-permute-start.11 = (f32[320,128]{1,0:T(8,128)S(1)}, f32[320,128]{1,0:T(8,128)S(1)}, u32[]{:S(2)}, u32[]{:S(2)}) collective-permute-start(f32[320,128]{1,0:T(8,128)S(1)} %give.1), channel_id=1, source_target_pairs={{0,1},{1,0},{2,3},{3,2},{4,5},{5,4},{6,7},{7,6},{8,9},{9,8},{10,11... | collective-permute-start | bytes 491528 | tf_op jit(solution)/shard_map/ppermute | solution.py:268

commit v15 on v14

--- a/solution.py
+++ b/solution.py
@@ -238,10 +238,14 @@
     def pack_kernel(cols, border, out, top, done):
         depth = order - cut
         copies = [
-            pltpu.make_async_copy(cols.at[pl.ds(cut, depth)], out.at[pl.ds(0, depth)], done.at[0]),
-            pltpu.make_async_copy(border, out.at[pl.ds(depth, arrow)], done.at[1]),
-            pltpu.make_async_copy(cols.at[pl.ds(0, cut)], top, done.at[2]),
+            pltpu.make_async_copy(border, out.at[pl.ds(depth, arrow)], done.at[0]),
+            pltpu.make_async_copy(cols.at[pl.ds(0, cut)], top, done.at[1]),
         ]
+        for at in range(0, depth, cut):
+            spot = pl.ds(at, cut)
+            copies.append(
+                pltpu.make_async_copy(cols.at[pl.ds(cut + at, cut)], out.at[spot], done.at[1 + (at + cut) // cut])
+            )
         for copy in copies:
             copy.start()
         for copy in copies:
@@ -252,7 +256,7 @@
         out_shape=(pltpu.VMEM((order - cut + arrow, width), bf16), pltpu.VMEM((cut, width), bf16)),
         in_specs=[hbm, hbm],
         out_specs=(VMEM, VMEM),
-        scratch_shapes=[pltpu.SemaphoreType.DMA((3,))],
+        scratch_shapes=[pltpu.SemaphoreType.DMA((order // cut + 1,))],
         compiler_params=SMALL,
         name="pack",
     )(far_off(factor_cols), far_off(arrow_factor[0]))

time: 109 us -> 109 us (level)
  no operation moved by 1% of the time
where the time goes in v15:
time: 109 us; the launch traced here: 108 us
  blocking collectives  55.1 us (51%)
  starting transfers between devices  34.9 us (32%)
  waiting for transfers between devices  8.76 us (8%)
  Pallas kernels  8.35 us (8%)
    all_to_all x2, blocking collectives, exchange(): moved = lax.all_to_all(values.astype(jnp.float16), 'tm', 0, 0, tiled=True)  55.1 us
    ppermute x7, starting transfers between devices, hop(): return lax.ppermute(panel, 'space', pairs)  23.5 us
    ppermute x5, starting transfers between devices, swap(): return lax.ppermute(tile, 'space', [(p, p ^ 1) for p in range(devices)])  11.5 us
    ppermute x7, waiting for transfers between devices, hop(): return lax.ppermute(panel, 'space', pairs)  6.73 us
  transfers between devices with their start and end apart: 12, of which 6 were waited for; matrix products, arithmetic and copies ran while one was open for 0% of the time, Pallas kernels for 4%

profile of v15, /device:TPU:64, one launch (start us, length us, event | category | flops | bytes accessed | tf_op | source)
XLA Modules:
  0.0 108.5 jit_solution(16840923550994938952)
XLA Ops:
  0.6 1.2 %pack.1 = (bf16[1856,128]{1,0:T(8,128)(2,1)S(1)}, bf16[256,128]{1,0:T(8,128)(2,1)S(1)}) custom-call(bf16[2048,128]{1,0:T(8,128)(2,1)} %bitcast.10, bf16[64,128]{1,0:T(8,128)(2,1)} %bitcast.11), custom_call_target="tpu_custom_call" | custom-call | tf_op jit(solution)/shard_map/pack/pallas_call | solution.py:254
  1.8 1.9 %collective-permute-start = (bf16[1856,128]{1,0:T(8,128)(2,1)S(1)}, bf16[1856,128]{1,0:T(8,128)(2,1)S(1)}, u32[]{:S(2)}, u32[]{:S(2)}) collective-permute-start(bf16[1856,128]{1,0:T(8,128)(2,1)S(1)} %get-tuple-element.25.mine), channel_id=1, source_target_pairs={{0,1},{1,0},{2,3},{3,2},{4,5},{5,4},{6,7},{7,6},{8,9},{9,8},{10,11... | collective-permute-start | bytes 1425416 | tf_op jit(solution)/shard_map/ppermute | solution.py:272
  3.7 3.5 %collective-permute-start.2 = (bf16[1856,128]{1,0:T(8,128)(2,1)S(1)}, bf16[1856,128]{1,0:T(8,128)(2,1)S(1)}, u32[]{:S(2)}, u32[]{:S(2)}) collective-permute-start(bf16[1856,128]{1,0:T(8,128)(2,1)S(1)} %get-tuple-element.25.mine), channel_id=1, source_target_pairs={{0,2},{1,15},{2,4},{3,1},{4,6},{5,3},{6,8},{7,5},{8,10},{9,7},{10,... | collective-permute-start | bytes 1425416 | tf_op jit(solution)/shard_map/ppermute | solution.py:269
  7.2 3.5 %collective-permute-start.3 = (bf16[1856,128]{1,0:T(8,128)(2,1)S(1)}, bf16[1856,128]{1,0:T(8,128)(2,1)S(1)}, u32[]{:S(2)}, u32[]{:S(2)}) collective-permute-start(bf16[1856,128]{1,0:T(8,128)(2,1)S(1)} %collective-permute-done.other), channel_id=1, source_target_pairs={{0,2},{1,15},{2,4},{3,1},{4,6},{5,3},{6,8},{7,5},{8,10},{9,7},{10,... | collective-permute-start | bytes 1425416 | tf_op jit(solution)/shard_map/ppermute | solution.py:269
  10.7 3.5 %collective-permute-start.1 = (bf16[256,128]{1,0:T(8,128)(2,1)S(1)}, bf16[256,128]{1,0:T(8,128)(2,1)S(1)}, u32[]{:S(2)}, u32[]{:S(2)}) collective-permute-start(bf16[256,128]{1,0:T(8,128)(2,1)S(1)} %get-tuple-element.26.mine_top), channel_id=1, source_target_pairs={{0,1},{1,0},{2,3},{3,2},{4,5},{5,4},{6,7},{7,6},{8,9},{9,8},{10,11... | collective-permute-start | bytes 196616 | tf_op jit(solution)/shard_map/ppermute | solution.py:272
  14.3 1.5 %collective-permute-done.2.first = bf16[1856,128]{1,0:T(8,128)(2,1)S(1)} collective-permute-done((bf16[1856,128]{1,0:T(8,128)(2,1)S(1)}, bf16[1856,128]{1,0:T(8,128)(2,1)S(1)}, u32[]{:S(2)}, u32[]{:S(2)}) %collective-permute-start.2) | collective-permute-done | bytes 475168 | tf_op jit(solution)/shard_map/ppermute | solution.py:269
  15.8 2.0 %collective-permute-start.4 = (bf16[1600,128]{1,0:T(8,128)(2,1)S(1)}, bf16[1600,128]{1,0:T(8,128)(2,1)S(1)}, u32[]{:S(2)}, u32[]{:S(2)}) collective-permute-start(bf16[1600,128]{1,0:T(8,128)(2,1)S(1)} %slice.20), channel_id=1, source_target_pairs={{0,2},{1,15},{2,4},{3,1},{4,6},{5,3},{6,8},{7,5},{8,10},{9,7},{10,... | collective-permute-start | bytes 1228808 | tf_op jit(solution)/shard_map/ppermute | solution.py:269
  17.8 1.1 %own.1 = (f32[320,128]{1,0:T(8,128)S(1)}, bf16[256,1792]{1,0:T(8,128)(2,1)S(1)}, f32[72,128]{1,0:T(8,128)S(1)}, f32[8,128]{1,0:T(8,128)S(1)}) custom-call(s32[1]{0:T(128)} %bitcast.1.at, bf16[1856,128]{1,0:T(8,128)(2,1)S(1)} %get-tuple-element.25.mine, bf16[1856,128]{1,0:T(8,128)(2,1)S(1)} %collective-permute-done.other, ...), custom_call_target="tpu_custom_call" | custom-call | tf_op jit(solution)/shard_map/own/pallas_call | solution.py:293
  19.0 1.9 %collective-permute-done.3.second = bf16[1856,128]{1,0:T(8,128)(2,1)S(1)} collective-permute-done((bf16[1856,128]{1,0:T(8,128)(2,1)S(1)}, bf16[1856,128]{1,0:T(8,128)(2,1)S(1)}, u32[]{:S(2)}, u32[]{:S(2)}) %collective-permute-start.3) | collective-permute-done | bytes 475168 | tf_op jit(solution)/shard_map/ppermute | solution.py:269
  20.9 2.0 %collective-permute-start.5 = (bf16[1600,128]{1,0:T(8,128)(2,1)S(1)}, bf16[1600,128]{1,0:T(8,128)(2,1)S(1)}, u32[]{:S(2)}, u32[]{:S(2)}) collective-permute-start(bf16[1600,128]{1,0:T(8,128)(2,1)S(1)} %slice.16), channel_id=1, source_target_pairs={{0,2},{1,15},{2,4},{3,1},{4,6},{5,3},{6,8},{7,5},{8,10},{9,7},{10,... | collective-permute-start | bytes 1228808 | tf_op jit(solution)/shard_map/ppermute | solution.py:269
  22.9 0.8 far.1
  23.7 3.1 %collective-permute-done.4.first = bf16[1600,128]{1,0:T(8,128)(2,1)S(1)} collective-permute-done((bf16[1600,128]{1,0:T(8,128)(2,1)S(1)}, bf16[1600,128]{1,0:T(8,128)(2,1)S(1)}, u32[]{:S(2)}, u32[]{:S(2)}) %collective-permute-start.4) | collective-permute-done | bytes 409632 | tf_op jit(solution)/shard_map/ppermute | solution.py:269
  26.9 3.4 %collective-permute-start.6 = (bf16[1088,128]{1,0:T(8,128)(2,1)S(1)}, bf16[1088,128]{1,0:T(8,128)(2,1)S(1)}, u32[]{:S(2)}, u32[]{:S(2)}) collective-permute-start(bf16[1088,128]{1,0:T(8,128)(2,1)S(1)} %slice.17), channel_id=1, source_target_pairs={{0,4},{1,13},{2,6},{3,15},{4,8},{5,1},{6,10},{7,3},{8,12},{9,5},{1... | collective-permute-start | bytes 835592 | tf_op jit(solution)/shard_map/ppermute | solution.py:269
  30.3 3.9 %collective-permute-start.8 = (bf16[1344,128]{1,0:T(8,128)(2,1)S(1)}, bf16[1344,128]{1,0:T(8,128)(2,1)S(1)}, u32[]{:S(2)}, u32[]{:S(2)}) collective-permute-start(bf16[1344,128]{1,0:T(8,128)(2,1)S(1)} %slice.18), channel_id=1, source_target_pairs={{0,2},{1,15},{2,4},{3,1},{4,6},{5,3},{6,8},{7,5},{8,10},{9,7},{10,... | collective-permute-start | bytes 1032200 | tf_op jit(solution)/shard_map/ppermute | solution.py:269
  34.2 5.2 %collective-permute-start.9 = (bf16[1344,128]{1,0:T(8,128)(2,1)S(1)}, bf16[1344,128]{1,0:T(8,128)(2,1)S(1)}, u32[]{:S(2)}, u32[]{:S(2)}) collective-permute-start(bf16[1344,128]{1,0:T(8,128)(2,1)S(1)} %slice.21), channel_id=1, source_target_pairs={{0,2},{1,15},{2,4},{3,1},{4,6},{5,3},{6,8},{7,5},{8,10},{9,7},{10,... | collective-permute-start | bytes 1032200 | tf_op jit(solution)/shard_map/ppermute | solution.py:269
  39.4 1.9 %collective-permute-start.7 = (f32[320,128]{1,0:T(8,128)S(1)}, f32[320,128]{1,0:T(8,128)S(1)}, u32[]{:S(2)}, u32[]{:S(2)}) collective-permute-start(f32[320,128]{1,0:T(8,128)S(1)} %get-tuple-element.36), channel_id=1, source_target_pairs={{0,1},{1,0},{2,3},{3,2},{4,5},{5,4},{6,7},{7,6},{8,9},{9,8},{10,11... | collective-permute-start | bytes 491528 | tf_op jit(solution)/shard_map/ppermute | solution.py:272
  41.3 1.4 %collective-permute-done.7.refs_5_ = f32[320,128]{1,0:T(8,128)S(1)} collective-permute-done((f32[320,128]{1,0:T(8,128)S(1)}, f32[320,128]{1,0:T(8,128)S(1)}, u32[]{:S(2)}, u32[]{:S(2)}) %collective-permute-start.7) | collective-permute-done | bytes 163872 | tf_op jit(solution)/shard_map/ppermute | solution.py:272
  42.7 1.4 %three.1 = (f32[448,128]{1,0:T(8,128)S(1)}, f32[448,128]{1,0:T(8,128)S(1)}, f32[8,128]{1,0:T(8,128)S(1)}) custom-call(bf16[1600,128]{1,0:T(8,128)(2,1)S(1)} %collective-permute-done.4.first, bf16[1600,128]{1,0:T(8,128)(2,1)S(1)} %collective-permute-done.5.second, bf16[1088,128]{1,0:T(8,128)(2,1)S(1)} %collective-permute-done.6.straight, ...), custom_call_target="tpu_custom_call" | custom-call | tf_op jit(solution)/shard_map/three/pallas_call | solution.py:279
  44.1 2.0 %collective-permute-start.10 = (f32[448,128]{1,0:T(8,128)S(1)}, f32[448,128]{1,0:T(8,128)S(1)}, u32[]{:S(2)}, u32[]{:S(2)}) collective-permute-start(f32[448,128]{1,0:T(8,128)S(1)} %get-tuple-element.41), channel_id=1, source_target_pairs={{0,1},{1,0},{2,3},{3,2},{4,5},{5,4},{6,7},{7,6},{8,9},{9,8},{10,11... | collective-permute-start | bytes 688136 | tf_op jit(solution)/shard_map/ppermute | solution.py:272
  46.9 2.1 %collective-permute-start.11 = (f32[320,128]{1,0:T(8,128)S(1)}, f32[320,128]{1,0:T(8,128)S(1)}, u32[]{:S(2)}, u32[]{:S(2)}) collective-permute-start(f32[320,128]{1,0:T(8,128)S(1)} %give.1), channel_id=1, source_target_pairs={{0,1},{1,0},{2,3},{3,2},{4,5},{5,4},{6,7},{7,6},{8,9},{9,8},{10,11... | collective-permute-start | bytes 491528 | tf_op jit(solution)/shard_map/ppermute | solution.py:272
  50.8 31.7 %all_to_all.10 = f16[32,72,128]{2,1,0:T(8,128)(2,1)S(1)} all-to-all(f16[32,72,128]{2,1,0:T(8,128)(2,1)S(1)} %convert_element_type.12), channel_id=1, replica_groups=mesh['tm'=32,'space'=16] {'tm'}, dimensions={0} | all-to-all | bytes 1179648 | tf_op jit(solution)/shard_map/all_to_all | solution.py:355
  82.5 0.8 suffix.1
  83.4 23.4 %all_to_all.11 = f16[32,72,128]{2,1,0:T(8,128)(2,1)S(1)} all-to-all(f16[32,72,128]{2,1,0:T(8,128)(2,1)S(1)} %convert_element_type.14), channel_id=1, replica_groups=mesh['tm'=32,'space'=16] {'tm'}, dimensions={0} | all-to-all | bytes 1179648 | tf_op jit(solution)/shard_map/all_to_all | solution.py:355
  106.9 1.6 %last.1 = (f32[2048,128]{1,0:T(8,128)}, f32[64,128]{1,0:T(8,128)}) custom-call(s32[1]{0:T(128)} %bitcast.refs_0_, f32[32,64,128]{2,1,0:T(8,128)S(1)} %get-tuple-element.42.refs_1_, f32[64,128]{1,0:T(8,128)S(1)} %get-tuple-element.43.refs_2_, f32[32,72,128]{2,1,0:T(8,128)S(1)} %convert_element_type.15.refs_3_, f32[1,2048]{1,0:T(1,128)S(1)} %copy-done.1), custom_call_target="tpu_custom_call" | custom-call | tf_op jit(solution)/shard_map/last/pallas_call | solution.py:367
  (26 shorter events, 2.9 us)
Async XLA Ops:
  0.6 17.2 %copy-start = (f32[128,64]{0,1:T(8,128)S(1)}, f32[128,64]{0,1:T(8,128)}, u32[]{:S(2)}) copy-start(f32[128,64]{0,1:T(8,128)} %param.11) | copy-start | bytes 98308
  1.8 5.4 %collective-permute-start = (bf16[1856,128]{1,0:T(8,128)(2,1)S(1)}, bf16[1856,128]{1,0:T(8,128)(2,1)S(1)}, u32[]{:S(2)}, u32[]{:S(2)}) collective-permute-start(bf16[1856,128]{1,0:T(8,128)(2,1)S(1)} %get-tuple-element.25.mine), channel_id=1, source_target_pairs={{0,1},{1,0},{2,3},{3,2},{4,5},{5,4},{6,7},{7,6},{8,9},{9,8},{10,11... | collective-permute-start | bytes 1425416 | tf_op jit(solution)/shard_map/ppermute | solution.py:272
  3.7 12.0 %collective-permute-start.2 = (bf16[1856,128]{1,0:T(8,128)(2,1)S(1)}, bf16[1856,128]{1,0:T(8,128)(2,1)S(1)}, u32[]{:S(2)}, u32[]{:S(2)}) collective-permute-start(bf16[1856,128]{1,0:T(8,128)(2,1)S(1)} %get-tuple-element.25.mine), channel_id=1, source_target_pairs={{0,2},{1,15},{2,4},{3,1},{4,6},{5,3},{6,8},{7,5},{8,10},{9,7},{10,... | collective-permute-start | bytes 1425416 | tf_op jit(solution)/shard_map/ppermute | solution.py:269
  7.2 13.6 %collective-permute-start.3 = (bf16[1856,128]{1,0:T(8,128)(2,1)S(1)}, bf16[1856,128]{1,0:T(8,128)(2,1)S(1)}, u32[]{:S(2)}, u32[]{:S(2)}) collective-permute-start(bf16[1856,128]{1,0:T(8,128)(2,1)S(1)} %collective-permute-done.other), channel_id=1, source_target_pairs={{0,2},{1,15},{2,4},{3,1},{4,6},{5,3},{6,8},{7,5},{8,10},{9,7},{10,... | collective-permute-start | bytes 1425416 | tf_op jit(solution)/shard_map/ppermute | solution.py:269
  10.7 7.1 %collective-permute-start.1 = (bf16[256,128]{1,0:T(8,128)(2,1)S(1)}, bf16[256,128]{1,0:T(8,128)(2,1)S(1)}, u32[]{:S(2)}, u32[]{:S(2)}) collective-permute-start(bf16[256,128]{1,0:T(8,128)(2,1)S(1)} %get-tuple-element.26.mine_top), channel_id=1, source_target_pairs={{0,1},{1,0},{2,3},{3,2},{4,5},{5,4},{6,7},{7,6},{8,9},{9,8},{10,11... | collective-permute-start | bytes 196616 | tf_op jit(solution)/shard_map/ppermute | solution.py:272
  15.8 11.1 %collective-permute-start.4 = (bf16[1600,128]{1,0:T(8,128)(2,1)S(1)}, bf16[1600,128]{1,0:T(8,128)(2,1)S(1)}, u32[]{:S(2)}, u32[]{:S(2)}) collective-permute-start(bf16[1600,128]{1,0:T(8,128)(2,1)S(1)} %slice.20), channel_id=1, source_target_pairs={{0,2},{1,15},{2,4},{3,1},{4,6},{5,3},{6,8},{7,5},{8,10},{9,7},{10,... | collective-permute-start | bytes 1228808 | tf_op jit(solution)/shard_map/ppermute | solution.py:269
  20.9 13.3 %collective-permute-start.5 = (bf16[1600,128]{1,0:T(8,128)(2,1)S(1)}, bf16[1600,128]{1,0:T(8,128)(2,1)S(1)}, u32[]{:S(2)}, u32[]{:S(2)}) collective-permute-start(bf16[1600,128]{1,0:T(8,128)(2,1)S(1)} %slice.16), channel_id=1, source_target_pairs={{0,2},{1,15},{2,4},{3,1},{4,6},{5,3},{6,8},{7,5},{8,10},{9,7},{10,... | collective-permute-start | bytes 1228808 | tf_op jit(solution)/shard_map/ppermute | solution.py:269
  26.9 15.8 %collective-permute-start.6 = (bf16[1088,128]{1,0:T(8,128)(2,1)S(1)}, bf16[1088,128]{1,0:T(8,128)(2,1)S(1)}, u32[]{:S(2)}, u32[]{:S(2)}) collective-permute-start(bf16[1088,128]{1,0:T(8,128)(2,1)S(1)} %slice.17), channel_id=1, source_target_pairs={{0,4},{1,13},{2,6},{3,15},{4,8},{5,1},{6,10},{7,3},{8,12},{9,5},{1... | collective-permute-start | bytes 835592 | tf_op jit(solution)/shard_map/ppermute | solution.py:269
  30.3 15.8 %collective-permute-start.8 = (bf16[1344,128]{1,0:T(8,128)(2,1)S(1)}, bf16[1344,128]{1,0:T(8,128)(2,1)S(1)}, u32[]{:S(2)}, u32[]{:S(2)}) collective-permute-start(bf16[1344,128]{1,0:T(8,128)(2,1)S(1)} %slice.18), channel_id=1, source_target_pairs={{0,2},{1,15},{2,4},{3,1},{4,6},{5,3},{6,8},{7,5},{8,10},{9,7},{10,... | collective-permute-start | bytes 1032200 | tf_op jit(solution)/shard_map/ppermute | solution.py:269
  34.2 12.2 %collective-permute-start.9 = (bf16[1344,128]{1,0:T(8,128)(2,1)S(1)}, bf16[1344,128]{1,0:T(8,128)(2,1)S(1)}, u32[]{:S(2)}, u32[]{:S(2)}) collective-permute-start(bf16[1344,128]{1,0:T(8,128)(2,1)S(1)} %slice.21), channel_id=1, source_target_pairs={{0,2},{1,15},{2,4},{3,1},{4,6},{5,3},{6,8},{7,5},{8,10},{9,7},{10,... | collective-permute-start | bytes 1032200 | tf_op jit(solution)/shard_map/ppermute | solution.py:269
  39.4 3.3 %collective-permute-start.7 = (f32[320,128]{1,0:T(8,128)S(1)}, f32[320,128]{1,0:T(8,128)S(1)}, u32[]{:S(2)}, u32[]{:S(2)}) collective-permute-start(f32[320,128]{1,0:T(8,128)S(1)} %get-tuple-element.36), channel_id=1, source_target_pairs={{0,1},{1,0},{2,3},{3,2},{4,5},{5,4},{6,7},{7,6},{8,9},{9,8},{10,11... | collective-permute-start | bytes 491528 | tf_op jit(solution)/shard_map/ppermute | solution.py:272
  44.1 5.5 %collective-permute-start.10 = (f32[448,128]{1,0:T(8,128)S(1)}, f32[448,128]{1,0:T(8,128)S(1)}, u32[]{:S(2)}, u32[]{:S(2)}) collective-permute-start(f32[448,128]{1,0:T(8,128)S(1)} %get-tuple-element.41), channel_id=1, source_target_pairs={{0,1},{1,0},{2,3},{3,2},{4,5},{5,4},{6,7},{7,6},{8,9},{9,8},{10,11... | collective-permute-start | bytes 688136 | tf_op jit(solution)/shard_map/ppermute | solution.py:272
  46.9 3.3 %copy-start.1 = (f32[1,2048]{1,0:T(1,128)S(1)}, f32[1,2048]{1,0:T(1,128)}, u32[]{:S(2)}) copy-start(f32[1,2048]{1,0:T(1,128)} %refs_4_.1) | copy-start | bytes 24580
  46.9 3.3 %copy-start.2 = (f32[64,64]{1,0:T(8,128)S(1)}, f32[64,64]{1,0:T(8,128)}, u32[]{:S(2)}) copy-start(f32[64,64]{1,0:T(8,128)} %refs_8_.1) | copy-start | bytes 49156
  46.9 3.3 %collective-permute-start.11 = (f32[320,128]{1,0:T(8,128)S(1)}, f32[320,128]{1,0:T(8,128)S(1)}, u32[]{:S(2)}, u32[]{:S(2)}) collective-permute-start(f32[320,128]{1,0:T(8,128)S(1)} %give.1), channel_id=1, source_target_pairs={{0,1},{1,0},{2,3},{3,2},{4,5},{5,4},{6,7},{7,6},{8,9},{9,8},{10,11... | collective-permute-start | bytes 491528 | tf_op jit(solution)/shard_map/ppermute | solution.py:272
